TPU v7x, 32 devices: a whole 2x2x4 slice. The times are simulated.
32 devices in a mesh: seq: 8 (over z, core), fsdp: 4 (over y, x).
Axes of the slice: x: 2, y: 2, z: 4, core: 2. Of those that a mesh axis runs over, the one named last changes fastest.
Arguments:
- tokens: bfloat16 [4, 4, 1024, 768], P(None, 'fsdp', 'seq'), may hold values from -6 to 6
- segments: int32 [4, 4, 1024], P(None, 'fsdp', 'seq'), may hold values from 0 to 3, never falling along the last dimension, each value on 1 to 512 neighbouring positions
- w_query: bfloat16 [768, 768], P('fsdp'), may hold values from -0.4375 to 0.4375
- w_key: bfloat16 [768, 768], P('fsdp'), may hold values from -0.21875 to 0.21875
- w_value: bfloat16 [768, 768], P('fsdp'), may hold values from -0.21875 to 0.21875
- w_out: bfloat16 [768, 768], P('fsdp'), may hold values from -0.625 to 0.625
- w_gate: bfloat16 [768, 2048], P('fsdp'), may hold values from -0.21875 to 0.21875
- w_up: bfloat16 [768, 2048], P('fsdp'), may hold values from -0.21875 to 0.21875
- w_down: bfloat16 [2048, 768], P('fsdp'), may hold values from -0.125 to 0.125
- gain_attn: bfloat16 [768], P('fsdp'), may hold values from 0.099609375 to 1.8984375
- gain_ffn: bfloat16 [768], P('fsdp'), may hold values from 0.099609375 to 1.8984375
- cotangent: bfloat16 [4, 4, 1024, 768], P(None, 'fsdp', 'seq'), may hold values from -6 to 6
Outputs:
- output: bfloat16 [4, 4, 1024, 768], P(None, 'fsdp', 'seq')
- input_grad: bfloat16 [4, 4, 1024, 768], P(None, 'fsdp', 'seq')
- w_query_grad: float32 [768, 768], P('fsdp')
- w_key_grad: float32 [768, 768], P('fsdp')
- w_value_grad: float32 [768, 768], P('fsdp')
- w_out_grad: float32 [768, 768], P('fsdp')
- w_gate_grad: float32 [768, 2048], P('fsdp')
- w_up_grad: float32 [768, 2048], P('fsdp')
- w_down_grad: float32 [2048, 768], P('fsdp')
- gain_attn_grad: float32 [768], P('fsdp')
- gain_ffn_grad: float32 [768], P('fsdp')
Inputs may be any that keep to these rules, and one draw needn't show every extreme that they name: `segments`: along each sequence the document number never falls; every document of 0 to 3 holds 1 to 512 tokens, and one holds exactly 512.
All inputs are finite; a program needn't handle non-finite values.
Results may differ from a plain program's by a relative error of at most 0.024.
Values may be sent and summed in bfloat16 or wider, within the bound.
No kernel may reach another device: no remote copies, remote signals or barrier semaphores. Data moves between devices by JAX's collectives and lax.ppermute only.
A program may use at most 192 MiB of HBM per device.

v0:
```python
import math

import jax
import jax.numpy as jnp
from jax import lax
from jax.experimental import pallas as pl
from jax.experimental.pallas import tpu as pltpu
from jax.sharding import Mesh, PartitionSpec as P

HEADS = 12
DOCS = 4
EPS = 1e-06
NEGATIVE = -1e30
BF = jnp.bfloat16
F32 = jnp.float32


def dot(left, right, dims=((1,), (0,))):
    return lax.dot_general(left, right, (dims, ((), ())), preferred_element_type=F32)


def rotary_tables(seq_tokens, head_size, copies):
    half = head_size // 2
    frequency = 10000.0 ** (-jnp.arange(half, dtype=F32) / half)
    angle = jnp.arange(seq_tokens, dtype=jnp.int32).astype(F32)[:, None] * frequency[None, :]
    cosine, sine = jnp.cos(angle), jnp.sin(angle)
    return (
        jnp.concatenate([cosine, cosine] * copies, axis=1),
        jnp.concatenate([-sine, sine] * copies, axis=1),
    )


def turn(rows, half):
    lanes = rows.shape[1]
    lane = lax.broadcasted_iota(jnp.int32, (1, lanes), 1)
    low = (lane // half) % 2 == 0
    return jnp.where(low, pltpu.roll(rows, lanes - half, 1), pltpu.roll(rows, half, 1))


def first_key(query_first, block, window):
    return max(0, (query_first - window + 1) // block * block)


def start_row(seg_ref):
    seg = seg_ref[...]
    starts = jnp.zeros_like(seg)
    for doc in range(1, DOCS):
        before = jnp.sum(jnp.where(seg < doc, 1.0, 0.0), axis=1, keepdims=True)
        starts = jnp.maximum(starts, jnp.where(seg >= doc, before, 0.0))
    return starts


def place(target, refs, pieces, me, shard):
    for ref, (offset, first, rows) in zip(refs, pieces):
        if offset is None:
            target[...] = ref[...]
        else:
            start = pl.multiple_of((me ^ offset) * shard + first, 16)
            target[pl.ds(start, rows), :] = ref[0:rows, 0:target.shape[1]]


def place_tokens(target, refs, where_ref, ranks):
    if len(refs) == 1:
        target[...] = refs[0][...]
        return
    groups = len(refs) // ranks
    span = target.shape[0] // (groups * ranks)
    for n, ref in enumerate(refs):
        rank = where_ref[2] if n < groups else 1 - where_ref[2]
        chunk = (where_ref[1] ^ (n % groups)) * ranks + rank
        target[pl.ds(pl.multiple_of(chunk * span, span), span), :] = ref[0:span, :]


def place_segments(target, refs, where_ref, ranks):
    groups = len(refs) // ranks
    span = target.shape[1] // (groups * ranks)
    for n, ref in enumerate(refs):
        rank = where_ref[2] if n < groups else 1 - where_ref[2]
        chunk = (where_ref[1] ^ (n % groups)) * ranks + rank
        row = ref[span:span + 16, 0:span].astype(F32)[0:1, :]
        target[:, pl.ds(pl.multiple_of(chunk * span, span), span)] = row


def place_stack(gu, down, stack_ref, shard, part_rows):
    chunks = gu.shape[1] // 256
    for j in range(stack_ref.shape[0]):
        for c in range(chunks):
            gu[j * shard:(j + 1) * shard, c * 256:(c + 1) * 256] = (
                stack_ref[j, c * shard:(c + 1) * shard, :])
        for c in range(down.shape[1] // 256):
            at = chunks * shard + c * part_rows
            down[j * part_rows:(j + 1) * part_rows, c * 256:(c + 1) * 256] = (
                stack_ref[j, at:at + part_rows, :])


def attend_kernel(where_ref, cos_ref, sin_ref, *refs, pieces, token_count, ranks, shard, block,
                  window, scale, head_size):
    inputs, refs = refs[:-9], refs[-9:]
    q_ref, k_ref, v_ref, att_ref, lse_ref, w_ref, x_ref, seg_ref, col_ref = refs
    token_refs, w_refs = inputs[:token_count], inputs[token_count:]
    tokens = x_ref.shape[0]
    lanes = 2 * head_size
    lane = lax.broadcasted_iota(jnp.int32, (1, lanes), 1)
    first = lane < head_size
    pair = pl.program_id(0)

    @pl.when(pair == 0)
    def _():
        place(w_ref, w_refs, pieces, where_ref[0], shard)
        place_tokens(x_ref, token_refs[:1] if token_count == 2 else token_refs, where_ref, ranks)
        if token_count == 2:
            seg_ref[...] = token_refs[1][...]
        else:
            place_segments(seg_ref, token_refs, where_ref, ranks)
        starts = start_row(seg_ref)
        col_ref[...] = jnp.broadcast_to(starts, (128, tokens)).T

    w = w_ref[:, pl.ds(pl.multiple_of(pair * 3 * lanes, lanes), 3 * lanes)]
    for low in range(0, tokens, block):
        rows = pl.ds(low, block)
        lin = dot(x_ref[rows, :], w)
        cosine, sine = cos_ref[rows, :], sin_ref[rows, :]
        half = head_size // 2
        q_lin, k_lin = lin[:, :lanes], lin[:, lanes:2 * lanes]
        q_ref[rows, :] = (q_lin * cosine + turn(q_lin, half) * sine).astype(BF)
        k_ref[rows, :] = (k_lin * cosine + turn(k_lin, half) * sine).astype(BF)
        v_ref[rows, :] = lin[:, 2 * lanes:].astype(BF)
    for low in range(0, tokens, block):
        begin = first_key(low, block, window)
        end = low + block
        q = q_ref[low:end, :] * jnp.asarray(scale, BF)
        zero = jnp.zeros_like(q)
        stacked = jnp.concatenate([jnp.where(first, q, zero), jnp.where(first, zero, q)], axis=0)
        scores = dot(stacked, k_ref[begin:end, :], ((1,), (1,)))
        key_index = lax.broadcasted_iota(jnp.int32, (block, end - begin), 1) + begin
        query_index = lax.broadcasted_iota(jnp.int32, (block, end - begin), 0) + low
        visible = (key_index.astype(F32) >= col_ref[low:end, 0:1]) & (key_index <= query_index)
        parts = []
        for head in range(2):
            own = jnp.where(visible, scores[head * block:(head + 1) * block], NEGATIVE)
            top = jnp.max(own, axis=1, keepdims=True)
            weights = jnp.exp(own - top)
            total = jnp.sum(weights, axis=1, keepdims=True)
            out = dot(weights.astype(BF), v_ref[begin:end, :]) / total
            parts.append(out)
            lse = jnp.broadcast_to(top + jnp.log(total), (block, 128))
            lse_ref[0, head:head + 1, low:end] = lse.T[0:1, :]
        att_ref[low:end, :] = jnp.where(first, parts[0], parts[1]).astype(BF)


SMALL_COST = pl.CostEstimate(flops=1, bytes_accessed=1, transcendentals=0)
VMEM_SPEC = pl.BlockSpec(memory_space=pltpu.VMEM)
SMEM_SPEC = pl.BlockSpec(memory_space=pltpu.SMEM)


def attend(where, cosine, sine, token_refs, ranks, weights, pieces, shard, lanes_all, window,
           head_size, width):
    tokens = cosine.shape[0]
    lanes = 2 * head_size
    pairs = lanes_all // lanes
    kernel = lambda *refs: attend_kernel(
        *refs, pieces=pieces, token_count=len(token_refs), ranks=ranks, shard=shard, block=256,
        window=window, scale=1.0 / math.sqrt(head_size), head_size=head_size)
    column = pl.BlockSpec((tokens, lanes), lambda p: (0, p))
    whole = lambda *shape: pl.BlockSpec(shape, lambda p: (0, 0))
    return pl.pallas_call(
        kernel,
        grid=(pairs,),
        in_specs=[SMEM_SPEC] + [VMEM_SPEC] * (2 + len(token_refs) + len(weights)),
        out_specs=[column, column, column, column,
                   pl.BlockSpec((1, 8, tokens), lambda p: (p, 0, 0)),
                   whole(width, 3 * lanes_all), whole(tokens, width), whole(1, tokens)],
        out_shape=[jax.ShapeDtypeStruct((tokens, lanes_all), BF)] * 4
        + [jax.ShapeDtypeStruct((pairs, 8, tokens), F32),
           jax.ShapeDtypeStruct((width, 3 * lanes_all), BF),
           jax.ShapeDtypeStruct((tokens, width), BF),
           jax.ShapeDtypeStruct((1, tokens), F32)],
        scratch_shapes=[pltpu.VMEM((tokens, 128), F32)],
        compiler_params=pltpu.CompilerParams(vmem_limit_bytes=40 << 20),
        cost_estimate=SMALL_COST,
        name="attend",
    )(where, cosine, sine, *token_refs, *weights)


def unit_of(rows):
    factor = lax.rsqrt(jnp.mean(rows * rows, axis=1, keepdims=True) + EPS)
    return rows * factor, factor


def forward_kernel(x_ref, own_ref, got_ref, gain_ref, stack_ref, sum_ref, low_ref, hidden_ref,
                   gate_ref, silu_ref, part_ref, gu, down, *, shard, part_rows):
    @pl.when(pl.program_id(0) == 0)
    def _():
        place_stack(gu, down, stack_ref, shard, part_rows)

    total = x_ref[...].astype(F32) + own_ref[...].astype(F32) + got_ref[...].astype(F32)
    sum_ref[...] = total
    middle_low = (unit_of(total)[0] * gain_ref[...]).astype(BF)
    low_ref[...] = middle_low
    ff = down.shape[0]
    for c in range(0, ff, 256):
        gate = dot(middle_low, gu[:, c:c + 256])
        up = dot(middle_low, gu[:, ff + c:ff + c + 256])
        sigmoid = jax.nn.sigmoid(gate)
        silu = gate * sigmoid
        hidden_ref[:, c:c + 256] = (silu * up).astype(BF)
        gate_ref[:, c:c + 256] = (up * sigmoid * (1.0 + gate * (1.0 - sigmoid))).astype(BF)
        silu_ref[:, c:c + 256] = silu.astype(BF)
    part_ref[...] = dot(hidden_ref[...], down[...]).astype(BF)


def forward(x, own, got, gain, stack, shard, part_rows, ff, block):
    tokens, width = x.shape
    row = lambda cols: pl.BlockSpec((block, cols), lambda i: (i, 0))
    return pl.pallas_call(
        lambda *refs: forward_kernel(*refs, shard=shard, part_rows=part_rows),
        grid=(tokens // block,),
        in_specs=[row(width), row(width), row(width), VMEM_SPEC, VMEM_SPEC],
        out_specs=[row(width), row(width), row(ff), row(ff), row(ff), row(width)],
        out_shape=[jax.ShapeDtypeStruct((tokens, width), F32),
                   jax.ShapeDtypeStruct((tokens, width), BF)]
        + [jax.ShapeDtypeStruct((tokens, ff), BF)] * 3
        + [jax.ShapeDtypeStruct((tokens, width), BF)],
        scratch_shapes=[pltpu.VMEM((width, 2 * ff), BF), pltpu.VMEM((ff, width), BF)],
        compiler_params=pltpu.CompilerParams(vmem_limit_bytes=40 << 20),
        cost_estimate=pl.CostEstimate(
            flops=6 * tokens * width * ff, bytes_accessed=24 << 20, transcendentals=0),
        name="ffn_forward",
    )(x, own, got, gain, stack)


def backward_kernel(where_ref, sum_ref, own_ref, got_ref, gate_ref, silu_ref, gains_ref, *refs,
                    cot_count, shard, part_rows, groups, ranks):
    cot_refs, stack_ref, refs = refs[:cot_count], refs[cot_count], refs[cot_count + 1:]
    out_refs, refs = refs[:groups], refs[groups:]
    grad_ref, low_ref, gu_grad_ref, part_ref, gain_ref, gu, down, cot_ref, rows_ref = refs
    step = pl.program_id(0)

    @pl.when(step == 0)
    def _():
        place_stack(gu, down, stack_ref, shard, part_rows)
        place_tokens(cot_ref, cot_refs, where_ref, ranks)
        gain_ref[...] = jnp.zeros_like(gain_ref)

    gain_two = gains_ref[1:2, :]
    middle = unit_of(sum_ref[...])[0] * gains_ref[0:1, :]
    unit, factor = unit_of(middle + own_ref[...].astype(F32) + got_ref[...].astype(F32))
    block, span = rows_ref.shape[0], out_refs[0].shape[0]
    rows_ref[...] = unit * gain_two
    kept = rows_ref[pl.ds(pl.multiple_of(where_ref[2] * span, span), span), :].astype(BF)
    for k, out_ref in enumerate(out_refs):
        @pl.when(step == (where_ref[1] ^ k))
        def _(out_ref=out_ref):
            out_ref[...] = kept
    cot = cot_ref[pl.ds(pl.multiple_of(step * block, block), block), :].astype(F32)
    gain_ref[...] += jnp.sum(cot * unit, axis=0, keepdims=True)
    scaled = cot * gain_two
    grad = factor * (scaled - unit * jnp.mean(scaled * unit, axis=1, keepdims=True))
    grad_ref[...] = grad
    grad_low = grad.astype(BF)
    low_ref[...] = grad_low
    ff = down.shape[0]
    for c in range(0, ff, 256):
        hidden_grad = dot(grad_low, down[c:c + 256, :], ((1,), (1,)))
        gu_grad_ref[:, c:c + 256] = (hidden_grad * gate_ref[:, c:c + 256].astype(F32)).astype(BF)
        gu_grad_ref[:, ff + c:ff + c + 256] = (
            hidden_grad * silu_ref[:, c:c + 256].astype(F32)).astype(BF)
    part_ref[...] = dot(gu_grad_ref[...], gu[...], ((1,), (1,))).astype(BF)


def backward(where, total, own, got, gate, silu, gains, cot, stack, shard, part_rows, block,
             groups, ranks):
    tokens, width = total.shape
    ff = gate.shape[1]
    kernel = lambda *refs: backward_kernel(
        *refs, cot_count=len(cot), shard=shard, part_rows=part_rows, groups=groups, ranks=ranks)
    row = lambda cols: pl.BlockSpec((block, cols), lambda i: (i, 0))
    slab = pl.BlockSpec((block // ranks, width), lambda i: (0, 0))
    return pl.pallas_call(
        kernel,
        grid=(tokens // block,),
        in_specs=[SMEM_SPEC] + [row(width)] * 3 + [row(ff)] * 2
        + [VMEM_SPEC] * (2 + len(cot)),
        out_specs=[slab] * groups + [row(width), row(width), row(2 * ff), row(width),
                                     pl.BlockSpec((1, width), lambda i: (0, 0))],
        out_shape=[jax.ShapeDtypeStruct((block // ranks, width), BF)] * groups
        + [jax.ShapeDtypeStruct((tokens, width), F32),
           jax.ShapeDtypeStruct((tokens, width), BF),
           jax.ShapeDtypeStruct((tokens, 2 * ff), BF),
           jax.ShapeDtypeStruct((tokens, width), BF),
           jax.ShapeDtypeStruct((1, width), F32)],
        scratch_shapes=[pltpu.VMEM((width, 2 * ff), BF), pltpu.VMEM((ff, width), BF),
                        pltpu.VMEM((tokens, width), BF), pltpu.VMEM((block, width), F32)],
        compiler_params=pltpu.CompilerParams(vmem_limit_bytes=44 << 20),
        cost_estimate=SMALL_COST,
        name="ffn_backward",
    )(where, total, own, got, gate, silu, gains, *cot, stack)


def norm_back_kernel(rank_ref, sum_ref, grad_ref, own_ref, got_ref, gain_ref,
                     low_ref, keep_ref, gain_grad_ref, rows_ref):
    @pl.when(pl.program_id(0) == 0)
    def _():
        gain_grad_ref[...] = jnp.zeros_like(gain_grad_ref)

    unit, factor = unit_of(sum_ref[...])
    grad = grad_ref[...] + own_ref[...].astype(F32) + got_ref[...].astype(F32)
    gain_grad_ref[...] += jnp.sum(grad * unit, axis=0, keepdims=True)
    scaled = grad * gain_ref[...]
    branch_grad = factor * (scaled - unit * jnp.mean(scaled * unit, axis=1, keepdims=True))
    low_ref[...] = branch_grad.astype(BF)
    rows_ref[...] = branch_grad
    span = keep_ref.shape[1]
    keep_ref[0] = rows_ref[pl.ds(pl.multiple_of(rank_ref[0] * span, span), span), :]


def norm_back(rank, total, grad, own, got, gain, block, span):
    tokens, width = total.shape
    row = pl.BlockSpec((block, width), lambda i: (i, 0))
    return pl.pallas_call(
        norm_back_kernel,
        grid=(tokens // block,),
        in_specs=[SMEM_SPEC, row, row, row, row, VMEM_SPEC],
        out_specs=[row, pl.BlockSpec((1, span, width), lambda i: (i, 0, 0)),
                   pl.BlockSpec((1, width), lambda i: (0, 0))],
        out_shape=[jax.ShapeDtypeStruct((tokens, width), BF),
                   jax.ShapeDtypeStruct((tokens // block, span, width), F32),
                   jax.ShapeDtypeStruct((1, width), F32)],
        scratch_shapes=[pltpu.VMEM((block, width), F32)],
        compiler_params=pltpu.CompilerParams(vmem_limit_bytes=24 << 20),
        cost_estimate=SMALL_COST,
        name="norm_back",
    )(rank, total, grad, own, got, gain)


def pick(rank, parts):
    value = parts[0]
    for r in range(1, len(parts)):
        value = jnp.where(rank == r, parts[r], value)
    return value


def pack_small_kernel(where_ref, query_ref, key_ref, value_ref, out_ref, gain_ref, tokens_ref,
                      seg_ref, cot_ref, small_ref, *slab_refs, ranks, lanes, lanes_all):
    slab_refs, cot_slabs = slab_refs[:len(slab_refs) // 2], slab_refs[len(slab_refs) // 2:]
    for k, ref in enumerate(cot_slabs):
        ref[...] = cot_ref[where_ref[1] ^ k, 0]
    rank, m = where_ref[2], where_ref[1]
    shard, width = query_ref.shape
    own_cols = width // ranks
    if lanes_all != own_cols:
        small_ref[...] = jnp.zeros_like(small_ref)
    for n, ref in enumerate((query_ref, key_ref, value_ref)):
        for low in range(0, own_cols, lanes):
            size = min(lanes, own_cols - low)
            at = (low // lanes * 3 + n) * lanes
            small_ref[0:shard, at:at + size] = pick(
                rank, [ref[:, r * own_cols + low:r * own_cols + low + size] for r in range(ranks)])
    small_ref[0:shard, 3 * lanes_all:] = pick(
        rank, [out_ref[:, r * own_cols:(r + 1) * own_cols] for r in range(ranks)])
    small_ref[shard:, :] = jnp.zeros_like(small_ref[shard:, :])
    small_ref[shard:, 0:shard] = gain_ref[...]
    span = tokens_ref.shape[2]
    for k, ref in enumerate(slab_refs):
        ref[0:span, :] = tokens_ref[m ^ k, 0]
        ref[span:, :] = jnp.zeros_like(ref[span:, :])
        row = seg_ref[pl.ds(m ^ k, 1), :].astype(F32)
        ref[span:, 0:span] = jnp.broadcast_to(row, (16, span)).astype(BF)


def pack_small(where, query, key, value, out, gains, tokens, segments, cot, ranks, lanes,
               lanes_all):
    shard, width = query.shape
    groups, _, span, _ = tokens.shape
    cols = 3 * lanes_all + width // ranks
    return pl.pallas_call(
        lambda *refs: pack_small_kernel(*refs, ranks=ranks, lanes=lanes, lanes_all=lanes_all),
        in_specs=[SMEM_SPEC] + [VMEM_SPEC] * 8,
        out_specs=[VMEM_SPEC] * (1 + 2 * groups),
        out_shape=[jax.ShapeDtypeStruct((shard + 16, cols), BF)]
        + [jax.ShapeDtypeStruct((span + 16, width), BF)] * groups
        + [jax.ShapeDtypeStruct((span, width), BF)] * groups,
        compiler_params=pltpu.CompilerParams(vmem_limit_bytes=24 << 20),
        cost_estimate=SMALL_COST,
        name="pack_small",
    )(where, query, key, value, out, gains, tokens, segments, cot)


def pack_kernel(where_ref, gate_ref, up_ref, down_ref, out_ref, gu, *, fsdp, ranks):
    rank = where_ref[2]
    shard, cols = gu.shape
    part = down_ref.shape[0] // ranks
    for n, ref in enumerate((gate_ref, up_ref)):
        for j in range(fsdp):
            low = (n * fsdp + j) * part
            gu[:, low:low + part] = pick(
                rank, [ref[:, (j * ranks + r) * part:(j * ranks + r + 1) * part]
                       for r in range(ranks)])
    chunks = cols // 256
    for c in range(chunks):
        out_ref[c * shard:(c + 1) * shard, :] = gu[:, c * 256:(c + 1) * 256]
    rows = pl.ds(pl.multiple_of(rank * part, 16), part)
    for c in range(down_ref.shape[1] // 256):
        at = chunks * shard + c * part
        out_ref[at:at + part, :] = down_ref[rows, c * 256:(c + 1) * 256]


def pack(where, gate, up, down, fsdp, ranks):
    shard, ff = gate.shape
    cols = 2 * ff // ranks
    rows = cols // 256 * shard + down.shape[1] // 256 * (down.shape[0] // ranks)
    return pl.pallas_call(
        lambda *refs: pack_kernel(*refs, fsdp=fsdp, ranks=ranks),
        in_specs=[SMEM_SPEC] + [VMEM_SPEC] * 3,
        out_specs=VMEM_SPEC,
        out_shape=jax.ShapeDtypeStruct((rows, 256), BF),
        scratch_shapes=[pltpu.VMEM((shard, cols), BF)],
        compiler_params=pltpu.CompilerParams(vmem_limit_bytes=24 << 20),
        cost_estimate=SMALL_COST,
        name="pack",
    )(where, gate, up, down)


def arrange_kernel(gu_ref, down_ref, out_ref):
    shard, part = gu_ref.shape[0], down_ref.shape[0]
    chunks = gu_ref.shape[1] // 256
    for c in range(chunks):
        out_ref[0, c * shard:(c + 1) * shard, :] = gu_ref[:, c * 256:(c + 1) * 256]
    for c in range(down_ref.shape[1] // 256):
        at = chunks * shard + c * part
        out_ref[0, at:at + part, :] = down_ref[:, c * 256:(c + 1) * 256]


def arrange(gu, down, fsdp):
    shard, part = gu.shape[0] // fsdp, down.shape[0] // fsdp
    rows = gu.shape[1] // 256 * shard + down.shape[1] // 256 * part
    return pl.pallas_call(
        arrange_kernel,
        grid=(fsdp,),
        in_specs=[pl.BlockSpec((shard, gu.shape[1]), lambda j: (j, 0)),
                  pl.BlockSpec((part, down.shape[1]), lambda j: (j, 0))],
        out_specs=pl.BlockSpec((1, rows, 256), lambda j: (j, 0, 0)),
        out_shape=jax.ShapeDtypeStruct((fsdp, rows, 256), BF),
        compiler_params=pltpu.CompilerParams(vmem_limit_bytes=24 << 20),
        cost_estimate=SMALL_COST,
        name="arrange",
    )(gu, down)


def finish_kernel(where_ref, keep_ref, part_ref, got_ref, *out_refs, ranks):
    groups, span, _ = keep_ref.shape
    for k, ref in enumerate(out_refs):
        group = where_ref[1] ^ k
        row = (group * ranks + where_ref[2]) * span
        own = part_ref[pl.ds(pl.multiple_of(row, span), span), :].astype(F32)
        ref[...] = (keep_ref[group] + own + got_ref[group].astype(F32)).astype(BF)


def finish(where, keep, part, got, ranks):
    groups, span, width = keep.shape
    return pl.pallas_call(
        lambda *refs: finish_kernel(*refs, ranks=ranks),
        in_specs=[SMEM_SPEC] + [VMEM_SPEC] * 3,
        out_specs=[VMEM_SPEC] * groups,
        out_shape=[jax.ShapeDtypeStruct((span, width), BF)] * groups,
        compiler_params=pltpu.CompilerParams(vmem_limit_bytes=24 << 20),
        cost_estimate=SMALL_COST,
        name="finish",
    )(where, keep, part, got)


def stack_kernel(where_ref, *refs):
    out_ref = refs[-1]
    for k, ref in enumerate(refs[:-1]):
        out_ref[where_ref[1] ^ k, 0] = ref[...]


def stack(where, slabs):
    span, width = slabs[0].shape
    return pl.pallas_call(
        stack_kernel,
        in_specs=[SMEM_SPEC] + [VMEM_SPEC] * len(slabs),
        out_specs=VMEM_SPEC,
        out_shape=jax.ShapeDtypeStruct((len(slabs), 1, span, width), BF),
        compiler_params=pltpu.CompilerParams(vmem_limit_bytes=16 << 20),
        cost_estimate=SMALL_COST,
        name="stack",
    )(where, *slabs)


def attend_back_kernel(seg_ref, g_ref, w_out_ref, q_ref, k_ref, v_ref, att_ref, lse_ref,
                       cos_ref, sin_ref, d_ref, grad_ref, k_sum, v_sum,
                       *, block, window, scale, head_size):
    tokens = g_ref.shape[0]
    half = head_size // 2
    lanes = 2 * head_size
    lane = lax.broadcasted_iota(jnp.int32, (1, lanes), 1)
    first = lane < head_size
    starts = start_row(seg_ref)
    k_sum[...] = jnp.zeros_like(k_sum)
    v_sum[...] = jnp.zeros_like(v_sum)
    for low in range(0, tokens, block):
        rows = pl.ds(low, block)
        grad_ref[rows, :] = dot(g_ref[rows, :], w_out_ref[...], ((1,), (1,))).astype(BF)
    for low in range(0, tokens, block):
        begin = first_key(low, block, window)
        end = low + block
        count = end - begin
        q = q_ref[low:end, :] * jnp.asarray(scale, BF)
        grad = grad_ref[low:end, :]
        product = (grad.astype(F32) * att_ref[low:end, :].astype(F32)).T
        k = k_ref[begin:end, :]
        v = v_ref[begin:end, :]
        zero = jnp.zeros_like(k)
        k_two = jnp.concatenate([jnp.where(first, k, zero), jnp.where(first, zero, k)], axis=0)
        v_two = jnp.concatenate([jnp.where(first, v, zero), jnp.where(first, zero, v)], axis=0)
        scores = dot(k_two, q, ((1,), (1,)))
        prob_grad = dot(v_two, grad, ((1,), (1,)))
        key_index = lax.broadcasted_iota(jnp.int32, (count, block), 0) + begin
        query_index = lax.broadcasted_iota(jnp.int32, (count, block), 1) + low
        visible = (key_index.astype(F32) >= starts[:, low:end]) & (key_index <= query_index)
        weights_low, score_low = [], []
        for head in range(2):
            part = slice(head * count, (head + 1) * count)
            weights = jnp.where(
                visible, jnp.exp(scores[part] - lse_ref[0, head:head + 1, low:end]), 0.0)
            row_dots = jnp.sum(
                product[head * head_size:(head + 1) * head_size], axis=0, keepdims=True)
            weights_low.append(weights.astype(BF))
            score_low.append((weights * (prob_grad[part] - row_dots)).astype(BF))
        weights_low = jnp.concatenate(weights_low, axis=0)
        score_low = jnp.concatenate(score_low, axis=0)
        v_part = dot(weights_low, grad)
        k_part = dot(score_low, q)
        v_sum[begin:end, :] += jnp.where(first, v_part[:count], v_part[count:])
        k_sum[begin:end, :] += jnp.where(first, k_part[:count], k_part[count:])
        dq = dot(score_low, k_two, ((0,), (0,))) * scale
        d_ref[low:end, :lanes] = (
            dq * cos_ref[low:end, :] - turn(dq, half) * sin_ref[low:end, :]).astype(BF)
    for low in range(0, tokens, block):
        rows = pl.ds(low, block)
        dk = k_sum[rows, :]
        d_ref[rows, lanes:2 * lanes] = (
            dk * cos_ref[rows, :] - turn(dk, half) * sin_ref[rows, :]).astype(BF)
        d_ref[rows, 2 * lanes:] = v_sum[rows, :].astype(BF)

def attend_back(seg, g, w_out, q, k, v, att, lse, cosine, sine, window, head_size):
    tokens, width = g.shape
    lanes = 2 * head_size
    pairs = q.shape[1] // lanes
    kernel = lambda *refs: attend_back_kernel(
        *refs, block=256, window=window, scale=1.0 / math.sqrt(head_size), head_size=head_size)
    column = pl.BlockSpec((tokens, lanes), lambda p: (0, p))
    return pl.pallas_call(
        kernel,
        grid=(pairs,),
        in_specs=[
            VMEM_SPEC, VMEM_SPEC,
            pl.BlockSpec((lanes, width), lambda p: (p, 0)),
            column, column, column, column,
            pl.BlockSpec((1, 8, tokens), lambda p: (p, 0, 0)),
            VMEM_SPEC, VMEM_SPEC,
        ],
        out_specs=pl.BlockSpec((tokens, 3 * lanes), lambda p: (0, p)),
        out_shape=jax.ShapeDtypeStruct((tokens, 3 * lanes * pairs), BF),
        scratch_shapes=[
            pltpu.VMEM((tokens, lanes), BF),
            pltpu.VMEM((tokens, lanes), F32),
            pltpu.VMEM((tokens, lanes), F32),
        ],
        compiler_params=pltpu.CompilerParams(vmem_limit_bytes=48 << 20),
        cost_estimate=SMALL_COST,
        name="attend_back",
    )(seg, g, w_out, q, k, v, att, lse, cosine, sine)


def join_kernel(rank_ref, own_ref, other_ref, *out_refs, moves, plain):
    swapped = rank_ref[0] == 1
    own, other = own_ref[...], other_ref[...]
    halves = (jnp.where(swapped, other, own), jnp.where(swapped, own, other))
    for out, half, (rows, cols), (to_rows, to_cols) in moves:
        out_refs[out][to_rows, to_cols] = halves[half][rows, cols].astype(F32)
    for out, (rows, cols) in plain:
        out_refs[out][...] = own[rows, cols].astype(F32)


def join(rank, own, other, moves, plain, shapes):
    kernel = lambda *refs: join_kernel(*refs, moves=moves, plain=plain)
    return pl.pallas_call(
        kernel,
        in_specs=[
            pl.BlockSpec(memory_space=pltpu.SMEM),
            pl.BlockSpec(memory_space=pltpu.VMEM),
            pl.BlockSpec(memory_space=pltpu.VMEM),
        ],
        out_specs=[pl.BlockSpec(memory_space=pltpu.VMEM)] * len(shapes),
        out_shape=[jax.ShapeDtypeStruct(shape, F32) for shape in shapes],
        compiler_params=pltpu.CompilerParams(vmem_limit_bytes=32 << 20),
        name="join",
    )(rank.reshape(1), own, other)


def join_all_kernel(all_ref, *refs, moves):
    out_refs, whole_ref = refs[:-1], refs[-1]
    groups, ranks, rows, _ = all_ref.shape
    for h in range(ranks):
        for m in range(groups):
            whole_ref[h, m * rows:(m + 1) * rows, :] = all_ref[m, h]
    for out, half, (rows, cols), (to_rows, to_cols) in moves:
        out_refs[out][to_rows, to_cols] = whole_ref[half, rows, cols].astype(F32)


def join_all(parts, moves, shapes):
    groups, ranks, rows, cols = parts.shape
    return pl.pallas_call(
        lambda *refs: join_all_kernel(*refs, moves=moves),
        in_specs=[VMEM_SPEC],
        out_specs=[VMEM_SPEC] * len(shapes),
        out_shape=[jax.ShapeDtypeStruct(shape, F32) for shape in shapes],
        scratch_shapes=[pltpu.VMEM((ranks, groups * rows, cols), BF)],
        compiler_params=pltpu.CompilerParams(vmem_limit_bytes=32 << 20),
        cost_estimate=SMALL_COST,
        name="join_all",
    )(parts)


def make_body(groups, ranks, fsdp, square):
    F = ("y", "x") if square else ("f",)
    swap = [(0, 1), (1, 0)]
    pairs = square and ranks == 2 and groups == 4

    def hop(value, k):
        return lax.ppermute(value, "m", [(i, i ^ k) for i in range(groups)])

    def after(value, *earlier):
        return lax.optimization_barrier((value,) + earlier)[0]

    def between(slabs, value):
        hops, value = lax.optimization_barrier((slabs[1:], value))
        return slabs[:1] + hops, value

    def spread(slabs):
        return [hop(slab, k) if k else slab for k, slab in enumerate(slabs)]

    def both_ranks(where, slabs, span):
        if ranks == 2:
            return slabs + [lax.ppermute(slab, "r", swap) for slab in slabs]
        rows = lax.all_gather(stack(where, slabs)[:, 0], "r", axis=1)
        return [rows[:, :, :span].reshape(-1, rows.shape[-1]), rows]

    def share(part):
        if ranks == 2:
            other = lax.ppermute(part, "r", swap)
            mine_first = lax.axis_index("r") == 0
            return jnp.stack(
                [jnp.where(mine_first, part, other), jnp.where(mine_first, other, part)], axis=1)
        return lax.all_gather(part, "r", axis=1)

    def exchange(part):
        if ranks == 2:
            return part, lax.ppermute(part, "r", swap)
        return lax.psum(part, "r"), jnp.zeros_like(part)

    def gather_rows(part, wait=()):
        if not square:
            whole = lax.all_gather(part, F, axis=0, tiled=True)
            return [whole], [(None, 0, 0)], (), ()
        count = part.shape[0]
        rows = (count // 2) // 16 * 16
        send = after(part, *wait) if wait else part
        from_x = lax.ppermute(send, "x", swap)
        from_y = lax.ppermute(send, "y", swap)
        far_a = lax.ppermute(from_y[:rows], "x", swap)
        far_b = lax.ppermute(from_x[rows:], "y", swap)
        pieces = [(0, 0, count), (1, 0, count), (2, 0, count), (3, 0, rows), (3, rows, count - rows)]
        return [part, from_x, from_y, far_a, far_b], pieces, (from_x, from_y), (far_a, far_b)

    def add(*parts):
        return sum(part.astype(F32) for part in parts).astype(BF)

    def take(grad, k):
        return lax.dynamic_index_in_dim(grad, lax.axis_index(F) ^ k, 0, keepdims=False)

    def half_rows(grad):
        return (grad.shape[1] // 2) // 16 * 16

    def round_one(grad):
        far, rows = take(grad, 3), half_rows(grad)
        return lax.ppermute(far[:rows], "x", swap), lax.ppermute(far[rows:], "y", swap)

    def second_terms(grad, low, high):
        to_x, to_y, rows = take(grad, 1), take(grad, 2), half_rows(grad)
        to_x = jnp.concatenate([to_x[:rows], add(to_x[rows:], high)], axis=0)
        to_y = jnp.concatenate([add(to_y[:rows], low), to_y[rows:]], axis=0)
        return to_x, to_y

    def round_two(to_x, to_y):
        return lax.ppermute(to_x, "x", swap), lax.ppermute(to_y, "y", swap)

    def halve(owned, bit, axis):
        half = owned.shape[axis] // 2
        side = (lax.axis_index("m") // bit) % 2
        return (lax.dynamic_slice_in_dim(owned, (1 - side) * half, half, axis),
                lax.dynamic_slice_in_dim(owned, side * half, half, axis))

    def join_halves(owned, other, bit, axis):
        first = (lax.axis_index("m") // bit) % 2 == 0
        return jnp.concatenate(
            [jnp.where(first, owned, other), jnp.where(first, other, owned)], axis=axis)

    def reduce(grad):
        return lax.psum(lax.psum_scatter(grad, F, scatter_dimension=0, tiled=False), "m")

    def body(tokens, segments, w_query, w_key, w_value, w_out, w_gate, w_up, w_down,
             gain_attn, gain_ffn, cotangent):
        micro, _, span, width = tokens.shape
        head_size = width // HEADS
        seq_tokens = span * groups * ranks
        window = seq_tokens // 2
        rank = lax.axis_index("r")
        own_cols = width // ranks
        shard = w_query.shape[0]
        down_rows = w_down.shape[0]
        part_rows = down_rows // ranks
        ff = w_gate.shape[1]
        half_ff = ff // ranks

        lanes = 2 * head_size
        lanes_all = -(-own_cols // lanes) * lanes
        spare = lanes_all - own_cols
        block = span * ranks
        f_index = lax.axis_index(F)
        where = jnp.stack([f_index, lax.axis_index("m"), rank])
        small_cols = 3 * lanes_all + own_cols
        gains_in = jnp.pad(jnp.stack([gain_attn, gain_ffn]), ((0, 14), (0, 0)))
        stack_own = pack(where, w_gate, w_up, w_down, fsdp, ranks)
        stack_all = lax.all_gather(stack_own, F, axis=0)
        cosine, sine = rotary_tables(seq_tokens, head_size, 2)
        small, *slabs = pack_small(
            after(where, stack_own), w_query, w_key, w_value, w_out, gains_in, tokens,
            segments[:, 0], cotangent, ranks, lanes, lanes_all)
        token_slabs, cot_slabs = slabs[:groups], slabs[groups:]
        token_slabs = spread(token_slabs)
        small_refs, small_pieces, near, far = gather_rows(small)
        if square:
            cot_slabs = cot_slabs[:1] + [after(slab, *token_slabs) for slab in cot_slabs[1:]]
        cot_slabs = spread(cot_slabs)
        if square:
            token_slabs = token_slabs[:1] + [
                after(slab, cosine, sine) for slab in token_slabs[1:]]
        token_refs = both_ranks(where, token_slabs, span)
        if ranks != 2:
            seg = token_refs[1][:, :, span, :span].reshape(1, seq_tokens).astype(F32)
            token_refs = [token_refs[0], seg]
        if square:
            own, from_x, from_y, far_a, far_b = small_refs
            at = far_a.shape[0]
            ends = [own, from_x, from_y, jnp.concatenate([far_a, far_b[:shard - at]], axis=0)]
            tails = [v[shard:shard + 2, :shard] for v in (own, from_x, from_y)]
            tails.append(far_b[shard - at:shard - at + 2, :shard])
            gains = jnp.zeros((fsdp, 2, shard), BF)
            out_cols = jnp.zeros((width, own_cols), BF)
            for offset in range(4):
                to = (f_index ^ offset) * shard
                gains = lax.dynamic_update_index_in_dim(gains, tails[offset], f_index ^ offset, 0)
                out_cols = lax.dynamic_update_slice_in_dim(
                    out_cols, ends[offset][:shard, 3 * lanes_all:], to, 0)
            gains = gains.transpose(1, 0, 2).reshape(2, width)
            small_pieces = [(o, f, min(n, shard - f)) for o, f, n in small_pieces]
            qkv_refs = small_refs
        else:
            whole = small_refs[0].reshape(fsdp, shard + 16, small_cols)
            gains = whole[:, shard:shard + 2, :shard].transpose(1, 0, 2).reshape(2, width)
            out_cols = whole[:, :shard, 3 * lanes_all:].reshape(width, own_cols)
            qkv_refs = [whole[:, :shard, :3 * lanes_all].reshape(width, 3 * lanes_all)]
        gains = gains.astype(F32)
        if ranks == 2:
            give = lax.dynamic_slice_in_dim(out_cols, (1 - rank) * own_cols, own_cols, 0)
            keep = lax.dynamic_slice_in_dim(out_cols, rank * own_cols, own_cols, 0)
            got = lax.ppermute(give, "r", swap)
            w_out_own = jnp.where(rank == 0, jnp.concatenate([keep, got], 1),
                                  jnp.concatenate([got, keep], 1))
        else:
            pieces = lax.all_to_all(out_cols, "r", 0, 0, tiled=True)
            pieces = pieces.reshape(ranks, own_cols, own_cols)
            w_out_own = jnp.concatenate([pieces[i] for i in range(ranks)], axis=1)
        w_out_even = jnp.pad(w_out_own, ((0, spare), (0, 0)))

        q, k, v, att, lse, w_qkv, x, seg = attend(
            where, cosine, sine, token_refs, ranks, qkv_refs, small_pieces, shard, lanes_all,
            window, head_size, width)
        if square:
            cot_slabs, att = between(cot_slabs, att)
        own, got = exchange(dot(att, w_out_even).astype(BF))
        cot_refs = both_ranks(where, cot_slabs, span)
        if ranks != 2:
            cot_refs = cot_refs[:1]
        total, middle_low, hidden_low, gate_back, silu, part = forward(
            x, own, got, gains[0:1], stack_all, shard, part_rows, half_ff, block)
        own, got = exchange(part)

        *out_slabs, ffn_grad, ffn_grad_low, gu_grad_low, part, gain_ffn_grad = backward(
            where, total, own, got, gate_back, silu, gains, cot_refs, stack_all, shard, part_rows,
            block, groups, ranks)
        own, got = exchange(part)
        down_w_grad = dot(hidden_low, ffn_grad_low, ((0,), (0,))).astype(BF)
        gu_w_grad = dot(middle_low, gu_grad_low, ((0,), (0,))).astype(BF)
        stack_grad = arrange(gu_w_grad, down_w_grad, fsdp)
        stack_owned = lax.psum_scatter(stack_grad, F, scatter_dimension=0, tiled=False)
        own = after(own, stack_grad)
        branch_grad_low, branch_keep, gain_attn_grad = norm_back(
            where[2:], total, ffn_grad, own, got, gains[0:1], block, span)
        out_w_grad = dot(att, branch_grad_low, ((0,), (0,)))[:own_cols].astype(BF)
        if ranks == 2:
            give = lax.dynamic_slice_in_dim(out_w_grad, (1 - rank) * own_cols, own_cols, 1)
            keep = lax.dynamic_slice_in_dim(out_w_grad, rank * own_cols, own_cols, 1)
            got = lax.ppermute(give, "r", swap)
            out_cols_grad = jnp.where(rank == 0, jnp.concatenate([keep, got], 0),
                                      jnp.concatenate([got, keep], 0))
        else:
            rows = out_w_grad.reshape(own_cols, ranks, own_cols).transpose(1, 0, 2)
            out_cols_grad = lax.all_to_all(rows, "r", 0, 0, tiled=True).reshape(width, own_cols)
        gain_grads = jnp.concatenate([gain_attn_grad, gain_ffn_grad], axis=0).astype(BF)
        gain_grads = gain_grads.reshape(2, fsdp, shard).transpose(1, 0, 2)
        gain_grads = jnp.pad(gain_grads, ((0, 0), (0, 14), (0, small_cols - shard)))
        branch_grad_low = after(branch_grad_low, out_cols_grad, gain_grads)
        d_qkv = attend_back(
            seg, branch_grad_low, w_out_even, q, k, v, att, lse, cosine, sine, window, head_size)
        if square:
            out_slabs, d_qkv = between(spread(out_slabs), d_qkv)
        else:
            out_slabs = spread(out_slabs)
        output = stack(where, out_slabs)
        qkv_w_grad = dot(x, d_qkv, ((0,), (0,))).astype(BF)
        small_grad = jnp.concatenate([qkv_w_grad, out_cols_grad], axis=1)
        small_grad = jnp.concatenate(
            [small_grad.reshape(fsdp, shard, small_cols), gain_grads], axis=1)
        if pairs:
            small_one = round_one(small_grad)
            d_qkv = after(d_qkv, small_grad)
        part = dot(d_qkv, w_qkv, ((1,), (1,))).astype(BF)
        if ranks == 2:
            rows = part.reshape(groups, ranks, span, width)
            give = lax.dynamic_index_in_dim(rows, 1 - rank, 1, keepdims=False)
            got = lax.ppermute(give, "r", swap)
        else:
            part = lax.psum(part, "r")
            got = jnp.zeros_like(branch_keep, BF)
        grad_slabs = list(finish(where, branch_keep, part, got, ranks))
        if pairs:
            grad_slabs, small_one = between(spread(grad_slabs), small_one)
        else:
            grad_slabs = spread(grad_slabs)
        if pairs:
            terms = second_terms(small_grad, *small_one)
            small_two = round_two(*terms)
            stack_owned = after(stack_owned, *terms)
            quarter = lax.psum_scatter(stack_owned, "m", scatter_dimension=0, tiled=True)
            give, keep = halve(add(take(small_grad, 0), *small_two), 1, 1)
            got, quarter = lax.optimization_barrier((hop(give, 1), quarter))
            stack_parts = lax.all_gather(quarter, ("m", "r"), axis=0)
            stack_parts = stack_parts.reshape((groups, ranks) + quarter.shape)
            give, keep = halve(add(keep, got), 2, 1)
            owned = add(keep, hop(give, 2))
            owned = join_halves(owned, hop(owned, 2), 2, 1)
            small_sum = join_halves(owned, hop(owned, 1), 1, 1)
        else:
            stack_sum = lax.psum(stack_owned, "m")
            small_sum = reduce(small_grad)
        input_grad = stack(where, grad_slabs)
        if pairs:
            everything = slice(None)
            chunks = 2 * half_ff // 256
            stack_moves = [
                (n, h, (slice((n * fsdp + j) * shard, (n * fsdp + j + 1) * shard), everything),
                 (everything, slice(j * down_rows + h * part_rows, j * down_rows + (h + 1) * part_rows)))
                for n in range(2) for h in range(2) for j in range(fsdp)]
            stack_moves += [
                (2, h, (slice(chunks * shard + c * part_rows, chunks * shard + (c + 1) * part_rows),
                        everything),
                 (slice(h * part_rows, (h + 1) * part_rows), slice(c * 256, (c + 1) * 256)))
                for h in range(2) for c in range(width // 256)]
            small_moves = [
                (n, h, (slice(0, shard), slice((3 * p + n) * lanes, (3 * p + n + 1) * lanes)),
                 (everything, slice(h * own_cols + p * lanes, h * own_cols + (p + 1) * lanes)))
                for n in range(3) for h in range(2) for p in range(own_cols // lanes)]
            small_moves += [
                (3, h, (slice(0, shard), slice(3 * lanes_all, small_cols)),
                 (everything, slice(h * own_cols, (h + 1) * own_cols))) for h in range(2)]
            small_plain = [
                (4 + n, (slice(shard + n, shard + n + 1), slice(0, shard))) for n in range(2)]
            gate_w, up_w, down_grad = join_all(
                stack_parts, stack_moves, [(shard, ff)] * 2 + [(down_rows, width)])
            query_w, key_w, value_w, out_w, gain_a, gain_f = join(
                rank, small_sum, lax.ppermute(small_sum, "r", swap), small_moves, small_plain,
                [(shard, width)] * 4 + [(1, shard)] * 2)
        else:
            at = 2 * half_ff // 256 * shard
            down_sum = jnp.moveaxis(stack_sum[at:].reshape(-1, part_rows, 256), 0, 1)
            down_grad = jnp.moveaxis(share(down_sum.reshape(part_rows, width)), 1, 0)
            down_grad = down_grad.reshape(down_rows, width).astype(F32)
            gu_sum = jnp.moveaxis(stack_sum[:at].reshape(-1, shard, 256), 0, 1)
            gu_both = share(gu_sum.reshape(shard, 2 * fsdp, part_rows))
            gu_both = gu_both.reshape(shard, ranks, 2, fsdp, part_rows).astype(F32)
            gate_w, up_w = (
                gu_both[:, :, n].transpose(0, 2, 1, 3).reshape(shard, ff) for n in range(2))
            small_both = share(small_sum)[:shard].astype(F32)
            three = small_both[:, :, :3 * lanes_all].reshape(shard, ranks, -1, 3, lanes)
            query_w, key_w, value_w = (
                three[:, :, :, n].reshape(shard, ranks, lanes_all)[:, :, :own_cols].reshape(shard, width)
                for n in range(3))
            out_w = small_both[:, :, 3 * lanes_all:].reshape(shard, width)
            gain_a, gain_f = small_sum[shard, :shard].astype(F32), small_sum[shard + 1, :shard].astype(F32)
        return (output, input_grad, query_w, key_w, value_w, out_w,
                gate_w, up_w, down_grad, gain_a.reshape(shard), gain_f.reshape(shard))

    return body


def solution(mesh):
    def run(*args):
        groups = args[0].shape[0]
        seq, fsdp = mesh.shape["seq"], mesh.shape["fsdp"]
        ranks = seq // groups
        square = fsdp == 4
        names = ("m", "r") + (("y", "x") if square else ("f",))
        sizes = (groups, ranks) + ((2, 2) if square else (fsdp,))
        order = [mesh.axis_names.index(name) for name in ("seq", "fsdp")]
        inner = Mesh(mesh.devices.transpose(order).reshape(sizes), names)
        f = ("y", "x") if square else "f"
        s = ("m", "r")
        rows = P(f, None)
        data = P(None, f, s, None)
        in_specs = (data, P(None, f, s)) + (rows,) * 7 + (P(f), P(f), data)
        out_specs = (data, data) + (rows,) * 7 + (P(f), P(f))
        body = make_body(groups, ranks, fsdp, square)
        return jax.shard_map(
            body, mesh=inner, in_specs=in_specs, out_specs=out_specs, check_vma=False)(*args)

    return run
```

profile of v0, /device:TPU:0, one launch (start us, length us, event | category | flops | bytes accessed | tf_op | source)
XLA Modules:
  0.0 307.6 jit_solution(1325593339495177757)
XLA Ops:
  10.8 1.7 pack.1
  13.6 1.7 pack_small.1
  16.0 2.9 collective-permute-start.7
  18.9 1.5 collective-permute-start.8
  20.4 3.6 %collective-permute-start.2 = (bf16[144,768]{1,0:T(8,128)(2,1)}, bf16[144,768]{1,0:T(8,128)(2,1)}, u32[]{:S(2)}, u32[]{:S(2)}) collective-permute-start(bf16[144,768]{1,0:T(8,128)(2,1)} %get-tuple-element.91), channel_id=1, source_target_pairs={{0,24},{8,16},{16,8},{24,0},{1,25},{9,17},{17,9},{25,1},{2,26},{10... | collective-permute-start | bytes 663560 | tf_op jit(solution)/shard_map/ppermute | solution.py:633
  24.9 1.9 fusion.9
  27.8 3.2 %collective-permute-done.2.refs_6_ = bf16[144,768]{1,0:T(8,128)(2,1)} collective-permute-done((bf16[144,768]{1,0:T(8,128)(2,1)}, bf16[144,768]{1,0:T(8,128)(2,1)}, u32[]{:S(2)}, u32[]{:S(2)}) %collective-permute-start.2) | collective-permute-done | bytes 221216 | tf_op jit(solution)/shard_map/ppermute | solution.py:633
  31.0 11.5 %collective-permute-done.1.refs_5_ = bf16[144,768]{1,0:T(8,128)(2,1)S(1)} collective-permute-done((bf16[144,768]{1,0:T(8,128)(2,1)}, bf16[144,768]{1,0:T(8,128)(2,1)S(1)}, u32[]{:S(2)}, u32[]{:S(2)}) %collective-permute-start.1) | collective-permute-done | bytes 221216 | tf_op jit(solution)/shard_map/ppermute | solution.py:633
  46.4 8.3 %collective-permute-done.10.refs_15_ = bf16[112,1536]{1,0:T(8,128)(2,1)S(1)} collective-permute-done((bf16[112,1536]{1,0:T(8,128)(2,1)S(1)}, bf16[112,1536]{1,0:T(8,128)(2,1)S(1)}, u32[]{:S(2)}, u32[]{:S(2)}) %collective-permute-start.10) | collective-permute-done | bytes 344096 | tf_op jit(solution)/shard_map/ppermute | solution.py:674
  57.0 3.6 %collective-permute-start.13 = (bf16[128,768]{1,0:T(8,128)(2,1)}, bf16[128,768]{1,0:T(8,128)(2,1)}, u32[]{:S(2)}, u32[]{:S(2)}) collective-permute-start(bf16[128,768]{1,0:T(8,128)(2,1)} %get-tuple-element.100), channel_id=1, source_target_pairs={{0,24},{8,16},{16,8},{24,0},{1,25},{9,17},{17,9},{25,1},{2,26},{10... | collective-permute-start | bytes 589832 | tf_op jit(solution)/shard_map/ppermute | solution.py:633
  67.6 13.8 %attend.1 = (bf16[1024,384]{1,0:T(8,128)(2,1)S(1)}, bf16[1024,384]{1,0:T(8,128)(2,1)S(1)}, bf16[1024,384]{1,0:T(8,128)(2,1)S(1)}, bf16[1024,384]{1,0:T(8,128)(2,...) custom-call(s32[3]{0:T(128)S(1)} %pad_add_fusion.refs_0_.where_ref, ...), custom_call_target="tpu_custom_call" | custom-call | flops 1 | bytes 1 | tf_op jit(solution)/shard_map/attend/pallas_call | solution.py:166
  83.9 1.7 maximum_select_fusion.refs_2_
  85.5 2.1 convolution_convert_fusion.2.refs_1_
  90.1 2.1 collective-permute-done.15.refs_2_
  93.7 10.8 %ffn_forward.1 = (f32[1024,768]{1,0:T(8,128)}, bf16[1024,768]{1,0:T(8,128)(2,1)S(1)}, bf16[1024,1024]{1,0:T(8,128)(2,1)S(1)}, bf16[1024,1024]{1,0:T(8,128)(2,1)S...) custom-call(bf16[1024,768]{1,0:T(8,128)(2,1)S(1)} %copy-done.59, ...), custom_call_target="tpu_custom_call" | custom-call | flops 4831838208 | bytes 25165824 | tf_op jit(solution)/shard_map/ffn_forward/pallas_call | solution.py:215
  111.6 2.0 collective-permute-done.17.refs_11_
  114.5 14.4 %ffn_backward.1 = (bf16[128,768]{1,0:T(8,128)(2,1)S(1)}, bf16[128,768]{1,0:T(8,128)(2,1)S(1)}, bf16[128,768]{1,0:T(8,128)(2,1)S(1)}, bf16[128,768]{1,0:T(8,128)(...) custom-call(s32[3]{0:T(128)S(1)} %pad_add_fusion.refs_0_.where_ref, ...), custom_call_target="tpu_custom_call" | custom-call | flops 1 | bytes 1 | tf_op jit(solution)/shard_map/ffn_backward/pallas_call | solution.py:279
  131.0 6.6 %convolution_convert_fusion.1.gu_ref = bf16[768,2048]{1,0:T(8,128)(2,1)S(1)} fusion(bf16[1024,768]{1,0:T(8,128)(2,1)S(1)} %copy-done.65, bf16[1024,2048]{1,0:T(8,128)(2,1)} %get-tuple-element.119), kind=kOutput, calls=%fused_computation.6 | convolution fusion | flops 3222798336 | bytes 8912896 | tf_op jit(solution)/shard_map/dot_general | solution.py:19
  137.7 1.9 convolution_convert_fusion.4.down_ref
  140.0 2.1 copy-done
  142.6 3.6 %collective-permute-done.24.got_ref = bf16[1024,768]{1,0:T(8,128)(2,1)} collective-permute-done((bf16[1024,768]{1,0:T(8,128)(2,1)}, bf16[1024,768]{1,0:T(8,128)(2,1)}, u32[]{:S(2)}, u32[]{:S(2)}) %collective-permute-start.24) | collective-permute-done | bytes 1572896 | tf_op jit(solution)/shard_map/ppermute | solution.py:661
  146.3 1.9 copy-done.7
  148.2 1.8 copy-done.19
  150.0 3.6 %norm_back.1 = (bf16[1024,768]{1,0:T(8,128)(2,1)S(1)}, f32[4,128,768]{2,1,0:T(8,128)S(1)}, f32[1,768]{1,0:T(1,128)S(1)}) custom-call(s32[1]{0:T(128)} %bitcast.2.rank_ref.refs_0_, f32[1024,768]{1,0:T(8,128)S(1)} %copy-done.1, f32[1024,768]{1,0:T(8,128)S(1)} %copy-done.7, bf16[1024,768]{1,0:T(8,128)(2,1)S(1)} %copy-done.19, ...), custom_call_target="tpu_custom_call" | custom-call | flops 1 | bytes 1 | tf_op jit(solution)/shard_map/norm_back/pallas_call | solution.py:320
  156.7 3.2 %collective-permute-start.22 = (bf16[128,768]{1,0:T(8,128)(2,1)}, bf16[128,768]{1,0:T(8,128)(2,1)}, u32[]{:S(2)}, u32[]{:S(2)}) collective-permute-start(bf16[128,768]{1,0:T(8,128)(2,1)} %copy-done.62), channel_id=1, source_target_pairs={{0,16},{8,24},{16,0},{24,8},{1,17},{9,25},{17,1},{25,9},{2,18},{10... | collective-permute-start | bytes 589832 | tf_op jit(solution)/shard_map/ppermute | solution.py:633
  160.2 1.4 maximum_select_fusion.1
  164.1 15.2 %attend_back.1 = bf16[1024,1152]{1,0:T(8,128)(2,1)} custom-call(f32[1,1024]{1,0:T(1,128)S(1)} %copy-done.52, bf16[1024,768]{1,0:T(8,128)(2,1)} %copy-done.2, bf16[384,768]{1,0:T(8,128)(2,1)S(1)} %copy-done.13, bf16[1024,384]{1,0:T(8,128)(2,1)S(1)} %copy-done.28, bf16[1024,384]{1,0:T(8,128)(2,1)S(1)} %copy-done.30, bf16[1024,384]{1,0:T(8,128)(2,1)S(1)} %copy-done.32, ...), custom_call_target="tpu_custom_call" | custom-call | flops 1 | bytes 1 | tf_op jit(solution)/shard_map/attend_back/pallas_call | solution.py:554
  179.3 3.9 %convolution_convert_fusion = bf16[768,1152]{1,0:T(8,128)(2,1)S(1)} fusion(bf16[1024,768]{1,0:T(8,128)(2,1)S(1)} %copy-done.60, bf16[1024,1152]{1,0:T(8,128)(2,1)} %attend_back.1), kind=kOutput, calls=%fused_computation.5 | convolution fusion | flops 1812824064 | bytes 5701632 | tf_op jit(solution)/shard_map/dot_general | solution.py:19
  183.6 1.5 collective-permute-start.31
  185.7 2.2 convolution_convert_fusion.3.refs_2_
  188.8 1.6 collective-permute-done.26.refs_3_
  192.3 3.3 %collective-permute-start.28 = (bf16[128,768]{1,0:T(8,128)(2,1)S(1)}, bf16[128,768]{1,0:T(8,128)(2,1)S(1)}, u32[]{:S(2)}, u32[]{:S(2)}) collective-permute-start(bf16[128,768]{1,0:T(8,128)(2,1)S(1)} %get-tuple-element.140), channel_id=1, source_target_pairs={{0,16},{8,24},{16,0},{24,8},{1,17},{9,25},{17,1},{25,9},{2,18},{10... | collective-permute-start | bytes 589832 | tf_op jit(solution)/shard_map/ppermute | solution.py:633
  195.7 8.6 %collective-permute-done.30 = bf16[96,1536]{1,0:T(8,128)(2,1)S(1)} collective-permute-done((bf16[96,1536]{1,0:T(8,128)(2,1)S(1)}, bf16[96,1536]{1,0:T(8,128)(2,1)S(1)}, u32[]{:S(2)}, u32[]{:S(2)}) %collective-permute-start.30) | collective-permute-done | bytes 294944 | tf_op jit(solution)/shard_map/ppermute | solution.py:689
  204.3 5.5 %collective-permute-done.28.refs_2_ = bf16[128,768]{1,0:T(8,128)(2,1)S(1)} collective-permute-done((bf16[128,768]{1,0:T(8,128)(2,1)S(1)}, bf16[128,768]{1,0:T(8,128)(2,1)S(1)}, u32[]{:S(2)}, u32[]{:S(2)}) %collective-permute-start.28) | collective-permute-done | bytes 196640 | tf_op jit(solution)/shard_map/ppermute | solution.py:633
  212.6 1.7 collective-permute-start.33
  214.4 12.6 %collective-permute-done.32 = bf16[208,1536]{1,0:T(8,128)(2,1)} collective-permute-done((bf16[208,1536]{1,0:T(8,128)(2,1)}, bf16[208,1536]{1,0:T(8,128)(2,1)}, u32[]{:S(2)}, u32[]{:S(2)}) %collective-permute-start.32) | collective-permute-done | bytes 639008 | tf_op jit(solution)/shard_map/ppermute | solution.py:698
  227.5 1.6 fusion.1
  229.9 4.8 %collective-permute-start.34 = (bf16[208,768]{1,0:T(8,128)(2,1)S(1)}, bf16[208,768]{1,0:T(8,128)(2,1)S(1)}, u32[]{:S(2)}, u32[]{:S(2)}) collective-permute-start(bf16[208,768]{1,0:T(8,128)(2,1)S(1)} %constant_dynamic-slice_fusion.1), channel_id=1, source_target_pairs={{0,8},{8,0},{16,24},{24,16},{1,9},{9,1},{17,25},{25,17},{2,10},{10... | collective-permute-start | bytes 958472 | tf_op jit(solution)/shard_map/ppermute | solution.py:633
  234.7 13.0 %collective-permute-done.34 = bf16[208,768]{1,0:T(8,128)(2,1)S(1)} collective-permute-done((bf16[208,768]{1,0:T(8,128)(2,1)S(1)}, bf16[208,768]{1,0:T(8,128)(2,1)S(1)}, u32[]{:S(2)}, u32[]{:S(2)}) %collective-permute-start.34) | collective-permute-done | bytes 319520 | tf_op jit(solution)/shard_map/ppermute | solution.py:633
  249.5 1.9 collective-permute-start.35
  251.5 7.3 %collective-permute-done.35 = bf16[208,384]{1,0:T(8,128)(2,1)S(1)} collective-permute-done((bf16[208,384]{1,0:T(8,128)(2,1)S(1)}, bf16[208,384]{1,0:T(8,128)(2,1)S(1)}, u32[]{:S(2)}, u32[]{:S(2)}) %collective-permute-start.35) | collective-permute-done | bytes 159776 | tf_op jit(solution)/shard_map/ppermute | solution.py:633
  258.9 20.2 %collective-permute-done.36 = bf16[208,384]{1,0:T(8,128)(2,1)S(1)} collective-permute-done((bf16[208,384]{1,0:T(8,128)(2,1)S(1)}, bf16[208,384]{1,0:T(8,128)(2,1)S(1)}, u32[]{:S(2)}, u32[]{:S(2)}) %collective-permute-start.36) | collective-permute-done | bytes 159776 | tf_op jit(solution)/shard_map/ppermute | solution.py:633
  279.3 12.5 %collective-permute-done.37 = bf16[208,768]{1,0:T(8,128)(2,1)S(1)} collective-permute-done((bf16[208,768]{1,0:T(8,128)(2,1)S(1)}, bf16[208,768]{1,0:T(8,128)(2,1)S(1)}, u32[]{:S(2)}, u32[]{:S(2)}) %collective-permute-start.37) | collective-permute-done | bytes 319520 | tf_op jit(solution)/shard_map/ppermute | solution.py:633
  292.1 2.0 stack.30
  294.0 1.5 stack.31
  295.5 1.5 join.1
  297.0 1.7 copy-done.11
  298.7 2.4 join_all.1
  (271 shorter events, 53.3 us)
Async XLA Ops:
  7.2 85.1 %all-gather.5.cloned.1.call-start = ((), (), s32[]{:S(2)}) async-start(), calls=%async_computation.3 | async-start | bytes 5898240 | tf_op jit(solution)/shard_map/all_gather | solution.py:737
  12.5 199.2 %reduce-scatter.7.cloned.1.call-start = ((), (), s32[]{:S(2)}) async-start(), calls=%async_computation.5 | async-start | bytes 5898240
  16.0 26.5 %collective-permute-start.7 = (bf16[208,1536]{1,0:T(8,128)(2,1)S(1)}, bf16[208,1536]{1,0:T(8,128)(2,1)S(1)}, u32[]{:S(2)}, u32[]{:S(2)}) collective-permute-start(bf16[208,1536]{1,0:T(8,128)(2,1)S(1)} %get-tuple-element.93.refs_11_), channel_id=1, source_target_pairs={{0,1},{1,0},{2,3},{3,2},{4,5},{5,4},{6,7},{7,6},{8,9},{9,8},{10,11... | collective-permute-start | bytes 1916936 | tf_op jit(solution)/shard_map/ppermute | solution.py:671
  18.9 26.0 %collective-permute-start.8 = (bf16[208,1536]{1,0:T(8,128)(2,1)S(1)}, bf16[208,1536]{1,0:T(8,128)(2,1)S(1)}, u32[]{:S(2)}, u32[]{:S(2)}) collective-permute-start(bf16[208,1536]{1,0:T(8,128)(2,1)S(1)} %get-tuple-element.93.refs_11_), channel_id=1, source_target_pairs={{0,2},{2,0},{1,3},{3,1},{4,6},{6,4},{5,7},{7,5},{8,10},{10,8},{9,1... | collective-permute-start | bytes 1916936 | tf_op jit(solution)/shard_map/ppermute | solution.py:672
  20.4 10.6 %collective-permute-start.2 = (bf16[144,768]{1,0:T(8,128)(2,1)}, bf16[144,768]{1,0:T(8,128)(2,1)}, u32[]{:S(2)}, u32[]{:S(2)}) collective-permute-start(bf16[144,768]{1,0:T(8,128)(2,1)} %get-tuple-element.91), channel_id=1, source_target_pairs={{0,24},{8,16},{16,8},{24,0},{1,25},{9,17},{17,9},{25,1},{2,26},{10... | collective-permute-start | bytes 663560 | tf_op jit(solution)/shard_map/ppermute | solution.py:633
  24.1 18.4 %collective-permute-start.1 = (bf16[144,768]{1,0:T(8,128)(2,1)}, bf16[144,768]{1,0:T(8,128)(2,1)S(1)}, u32[]{:S(2)}, u32[]{:S(2)}) collective-permute-start(bf16[144,768]{1,0:T(8,128)(2,1)} %get-tuple-element.89), channel_id=1, source_target_pairs={{0,16},{8,24},{16,0},{24,8},{1,17},{9,25},{17,1},{25,9},{2,18},{10... | collective-permute-start | bytes 663560 | tf_op jit(solution)/shard_map/ppermute | solution.py:633
  24.1 32.2 %collective-permute-start = (bf16[144,768]{1,0:T(8,128)(2,1)}, bf16[144,768]{1,0:T(8,128)(2,1)}, u32[]{:S(2)}, u32[]{:S(2)}) collective-permute-start(bf16[144,768]{1,0:T(8,128)(2,1)} %get-tuple-element.87), channel_id=1, source_target_pairs={{0,8},{8,0},{16,24},{24,16},{1,9},{9,1},{17,25},{25,17},{2,10},{10... | collective-permute-start | bytes 663560 | tf_op jit(solution)/shard_map/ppermute | solution.py:633
  27.7 35.1 %copy-start.3 = (f32[1024,128]{1,0:T(8,128)}, f32[1024,128]{1,0:T(8,128)S(1)}, u32[]{:S(2)}) copy-start(f32[1024,128]{1,0:T(8,128)S(1)} %get-tuple-element.173.refs_1_.refs_8_) | copy-start | bytes 1572868
  27.7 35.1 %copy-start.5 = (f32[1024,128]{1,0:T(8,128)}, f32[1024,128]{1,0:T(8,128)S(1)}, u32[]{:S(2)}) copy-start(f32[1024,128]{1,0:T(8,128)S(1)} %get-tuple-element.174.refs_2_.refs_9_) | copy-start | bytes 1572868
  31.0 25.3 %collective-permute-start.3 = (bf16[144,768]{1,0:T(8,128)(2,1)S(1)}, bf16[144,768]{1,0:T(8,128)(2,1)S(1)}, u32[]{:S(2)}, u32[]{:S(2)}) collective-permute-start(bf16[144,768]{1,0:T(8,128)(2,1)S(1)} %get-tuple-element.86.refs_3_), channel_id=1, source_target_pairs={{0,4},{4,0},{1,5},{5,1},{2,6},{6,2},{3,7},{7,3},{8,12},{12,8},{9,1... | collective-permute-start | bytes 663560 | tf_op jit(solution)/shard_map/ppermute | solution.py:647
  42.5 18.1 %collective-permute-start.6 = (bf16[144,768]{1,0:T(8,128)(2,1)}, bf16[144,768]{1,0:T(8,128)(2,1)S(1)}, u32[]{:S(2)}, u32[]{:S(2)}) collective-permute-start(bf16[144,768]{1,0:T(8,128)(2,1)} %collective-permute-done.2.refs_6_), channel_id=1, source_target_pairs={{0,4},{4,0},{1,5},{5,1},{2,6},{6,2},{3,7},{7,3},{8,12},{12,8},{9,1... | collective-permute-start | bytes 663560 | tf_op jit(solution)/shard_map/ppermute | solution.py:647
  43.2 11.6 %collective-permute-start.10 = (bf16[112,1536]{1,0:T(8,128)(2,1)S(1)}, bf16[112,1536]{1,0:T(8,128)(2,1)S(1)}, u32[]{:S(2)}, u32[]{:S(2)}) collective-permute-start(bf16[112,1536]{1,0:T(8,128)(2,1)S(1)} %slice.96), channel_id=1, source_target_pairs={{0,2},{2,0},{1,3},{3,1},{4,6},{6,4},{5,7},{7,5},{8,10},{10,8},{9,1... | collective-permute-start | bytes 1032200 | tf_op jit(solution)/shard_map/ppermute | solution.py:674
  45.0 9.8 %collective-permute-start.9 = (bf16[96,1536]{1,0:T(8,128)(2,1)S(1)}, bf16[96,1536]{1,0:T(8,128)(2,1)S(1)}, u32[]{:S(2)}, u32[]{:S(2)}) collective-permute-start(bf16[96,1536]{1,0:T(8,128)(2,1)S(1)} %slice.95), channel_id=1, source_target_pairs={{0,1},{1,0},{2,3},{3,2},{4,5},{5,4},{6,7},{7,6},{8,9},{9,8},{10,11... | collective-permute-start | bytes 884744 | tf_op jit(solution)/shard_map/ppermute | solution.py:673
  54.8 6.5 %collective-permute-start.5 = (bf16[144,768]{1,0:T(8,128)(2,1)}, bf16[144,768]{1,0:T(8,128)(2,1)S(1)}, u32[]{:S(2)}, u32[]{:S(2)}) collective-permute-start(bf16[144,768]{1,0:T(8,128)(2,1)} %copy-done.37), channel_id=1, source_target_pairs={{0,4},{4,0},{1,5},{5,1},{2,6},{6,2},{3,7},{7,3},{8,12},{12,8},{9,1... | collective-permute-start | bytes 663560 | tf_op jit(solution)/shard_map/ppermute | solution.py:647
  55.7 28.1 %collective-permute-start.14 = (bf16[384,384]{1,0:T(8,128)(2,1)}, bf16[384,384]{1,0:T(8,128)(2,1)}, u32[]{:S(2)}, u32[]{:S(2)}) collective-permute-start(bf16[384,384]{1,0:T(8,128)(2,1)} %get-tuple-element.167), channel_id=1, source_target_pairs={{0,4},{4,0},{1,5},{5,1},{2,6},{6,2},{3,7},{7,3},{8,12},{12,8},{9,1... | collective-permute-start | bytes 884744 | tf_op jit(solution)/shard_map/ppermute | solution.py:780
  56.3 6.5 %collective-permute-start.4 = (bf16[144,768]{1,0:T(8,128)(2,1)}, bf16[144,768]{1,0:T(8,128)(2,1)}, u32[]{:S(2)}, u32[]{:S(2)}) collective-permute-start(bf16[144,768]{1,0:T(8,128)(2,1)} %collective-permute-done.refs_4_), channel_id=1, source_target_pairs={{0,4},{4,0},{1,5},{5,1},{2,6},{6,2},{3,7},{7,3},{8,12},{12,8},{9,1... | collective-permute-start | bytes 663560 | tf_op jit(solution)/shard_map/ppermute | solution.py:647
  57.0 26.8 %collective-permute-start.13 = (bf16[128,768]{1,0:T(8,128)(2,1)}, bf16[128,768]{1,0:T(8,128)(2,1)}, u32[]{:S(2)}, u32[]{:S(2)}) collective-permute-start(bf16[128,768]{1,0:T(8,128)(2,1)} %get-tuple-element.100), channel_id=1, source_target_pairs={{0,24},{8,16},{16,8},{24,0},{1,25},{9,17},{17,9},{25,1},{2,26},{10... | collective-permute-start | bytes 589832 | tf_op jit(solution)/shard_map/ppermute | solution.py:633
  61.2 22.6 %collective-permute-start.12 = (bf16[128,768]{1,0:T(8,128)(2,1)}, bf16[128,768]{1,0:T(8,128)(2,1)}, u32[]{:S(2)}, u32[]{:S(2)}) collective-permute-start(bf16[128,768]{1,0:T(8,128)(2,1)} %get-tuple-element.98), channel_id=1, source_target_pairs={{0,16},{8,24},{16,0},{24,8},{1,17},{9,25},{17,1},{25,9},{2,18},{10... | collective-permute-start | bytes 589832 | tf_op jit(solution)/shard_map/ppermute | solution.py:633
  61.9 21.9 %collective-permute-start.11 = (bf16[128,768]{1,0:T(8,128)(2,1)}, bf16[128,768]{1,0:T(8,128)(2,1)}, u32[]{:S(2)}, u32[]{:S(2)}) collective-permute-start(bf16[128,768]{1,0:T(8,128)(2,1)} %get-tuple-element.96), channel_id=1, source_target_pairs={{0,8},{8,0},{16,24},{24,16},{1,9},{9,1},{17,25},{25,17},{2,10},{10... | collective-permute-start | bytes 589832 | tf_op jit(solution)/shard_map/ppermute | solution.py:633
  88.5 3.8 %collective-permute-start.15 = (bf16[1024,768]{1,0:T(8,128)(2,1)}, bf16[1024,768]{1,0:T(8,128)(2,1)}, u32[]{:S(2)}, u32[]{:S(2)}) collective-permute-start(bf16[1024,768]{1,0:T(8,128)(2,1)} %convolution_convert_fusion.2.refs_1_), channel_id=1, source_target_pairs={{0,4},{4,0},{1,5},{5,1},{2,6},{6,2},{3,7},{7,3},{8,12},{12,8},{9,1... | collective-permute-start | bytes 4718600 | tf_op jit(solution)/shard_map/ppermute | solution.py:661
  109.6 4.9 %collective-permute-start.16 = (bf16[1024,768]{1,0:T(8,128)(2,1)S(1)}, bf16[1024,768]{1,0:T(8,128)(2,1)S(1)}, u32[]{:S(2)}, u32[]{:S(2)}) collective-permute-start(bf16[1024,768]{1,0:T(8,128)(2,1)S(1)} %get-tuple-element.104.refs_2_), channel_id=1, source_target_pairs={{0,4},{4,0},{1,5},{5,1},{2,6},{6,2},{3,7},{7,3},{8,12},{12,8},{9,1... | collective-permute-start | bytes 4718600 | tf_op jit(solution)/shard_map/ppermute | solution.py:661
  109.8 3.8 %collective-permute-start.17 = (bf16[128,768]{1,0:T(8,128)(2,1)S(1)}, bf16[128,768]{1,0:T(8,128)(2,1)S(1)}, u32[]{:S(2)}, u32[]{:S(2)}) collective-permute-start(bf16[128,768]{1,0:T(8,128)(2,1)S(1)} %copy-done.46), channel_id=1, source_target_pairs={{0,4},{4,0},{1,5},{5,1},{2,6},{6,2},{3,7},{7,3},{8,12},{12,8},{9,1... | collective-permute-start | bytes 589832 | tf_op jit(solution)/shard_map/ppermute | solution.py:647
  110.1 3.8 %collective-permute-start.18 = (bf16[128,768]{1,0:T(8,128)(2,1)}, bf16[128,768]{1,0:T(8,128)(2,1)}, u32[]{:S(2)}, u32[]{:S(2)}) collective-permute-start(bf16[128,768]{1,0:T(8,128)(2,1)} %collective-permute-done.11.refs_8_), channel_id=1, source_target_pairs={{0,4},{4,0},{1,5},{5,1},{2,6},{6,2},{3,7},{7,3},{8,12},{12,8},{9,1... | collective-permute-start | bytes 589832 | tf_op jit(solution)/shard_map/ppermute | solution.py:647
  110.3 4.0 %collective-permute-start.19 = (bf16[128,768]{1,0:T(8,128)(2,1)}, bf16[128,768]{1,0:T(8,128)(2,1)}, u32[]{:S(2)}, u32[]{:S(2)}) collective-permute-start(bf16[128,768]{1,0:T(8,128)(2,1)} %collective-permute-done.12.refs_9_), channel_id=1, source_target_pairs={{0,4},{4,0},{1,5},{5,1},{2,6},{6,2},{3,7},{7,3},{8,12},{12,8},{9,1... | collective-permute-start | bytes 589832 | tf_op jit(solution)/shard_map/ppermute | solution.py:647
  110.6 3.9 %collective-permute-start.20 = (bf16[128,768]{1,0:T(8,128)(2,1)}, bf16[128,768]{1,0:T(8,128)(2,1)}, u32[]{:S(2)}, u32[]{:S(2)}) collective-permute-start(bf16[128,768]{1,0:T(8,128)(2,1)} %collective-permute-done.13.refs_10_), channel_id=1, source_target_pairs={{0,4},{4,0},{1,5},{5,1},{2,6},{6,2},{3,7},{7,3},{8,12},{12,8},{9,1... | collective-permute-start | bytes 589832 | tf_op jit(solution)/shard_map/ppermute | solution.py:647
  114.5 16.5 %copy-start.65 = (bf16[1024,768]{1,0:T(8,128)(2,1)S(1)}, bf16[1024,768]{1,0:T(8,128)(2,1)}, u32[]{:S(2)}) copy-start(bf16[1024,768]{1,0:T(8,128)(2,1)} %copy-done.64) | copy-start | bytes 4718596
  142.2 106.2 %reduce-scatter.5.cloned.1.call-start = ((), (), s32[]{:S(2)}) async-start(), calls=%async_computation.2 | async-start | bytes 1474560 | tf_op jit(solution)/shard_map/reduce_scatter | solution.py:858
  142.4 3.8 %collective-permute-start.24 = (bf16[1024,768]{1,0:T(8,128)(2,1)}, bf16[1024,768]{1,0:T(8,128)(2,1)}, u32[]{:S(2)}, u32[]{:S(2)}) collective-permute-start(bf16[1024,768]{1,0:T(8,128)(2,1)} %copy-done.18), channel_id=1, source_target_pairs={{0,4},{4,0},{1,5},{5,1},{2,6},{6,2},{3,7},{7,3},{8,12},{12,8},{9,1... | collective-permute-start | bytes 4718600 | tf_op jit(solution)/shard_map/ppermute | solution.py:661
  155.5 4.7 %collective-permute-start.25 = (bf16[384,384]{1,0:T(8,128)(2,1)}, bf16[384,384]{1,0:T(8,128)(2,1)}, u32[]{:S(2)}, u32[]{:S(2)}) collective-permute-start(bf16[384,384]{1,0:T(8,128)(2,1)} %get-tuple-element.165), channel_id=1, source_target_pairs={{0,4},{4,0},{1,5},{5,1},{2,6},{6,2},{3,7},{7,3},{8,12},{12,8},{9,1... | collective-permute-start | bytes 884744 | tf_op jit(solution)/shard_map/ppermute | solution.py:817
  155.6 23.6 %collective-permute-start.21 = (bf16[128,768]{1,0:T(8,128)(2,1)}, bf16[128,768]{1,0:T(8,128)(2,1)S(1)}, u32[]{:S(2)}, u32[]{:S(2)}) collective-permute-start(bf16[128,768]{1,0:T(8,128)(2,1)} %copy-done.63), channel_id=1, source_target_pairs={{0,8},{8,0},{16,24},{24,16},{1,9},{9,1},{17,25},{25,17},{2,10},{10... | collective-permute-start | bytes 589832 | tf_op jit(solution)/shard_map/ppermute | solution.py:633
  156.7 22.6 %collective-permute-start.22 = (bf16[128,768]{1,0:T(8,128)(2,1)}, bf16[128,768]{1,0:T(8,128)(2,1)}, u32[]{:S(2)}, u32[]{:S(2)}) collective-permute-start(bf16[128,768]{1,0:T(8,128)(2,1)} %copy-done.62), channel_id=1, source_target_pairs={{0,16},{8,24},{16,0},{24,8},{1,17},{9,25},{17,1},{25,9},{2,18},{10... | collective-permute-start | bytes 589832 | tf_op jit(solution)/shard_map/ppermute | solution.py:633
  159.8 19.4 %collective-permute-start.23 = (bf16[128,768]{1,0:T(8,128)(2,1)}, bf16[128,768]{1,0:T(8,128)(2,1)}, u32[]{:S(2)}, u32[]{:S(2)}) collective-permute-start(bf16[128,768]{1,0:T(8,128)(2,1)} %copy-done.61), channel_id=1, source_target_pairs={{0,24},{8,16},{16,8},{24,0},{1,25},{9,17},{17,9},{25,1},{2,26},{10... | collective-permute-start | bytes 589832 | tf_op jit(solution)/shard_map/ppermute | solution.py:633
  160.2 23.2 %copy-start.70 = (bf16[4,16,1536]{2,1,0:T(8,128)(2,1)}, bf16[4,16,1536]{2,1,0:T(8,128)(2,1)S(1)}, u32[]{:S(2)}) copy-start(bf16[4,16,1536]{2,1,0:T(8,128)(2,1)S(1)} %pad.9) | copy-start | bytes 589828
  183.6 20.7 %collective-permute-start.31 = (bf16[112,1536]{1,0:T(8,128)(2,1)S(1)}, bf16[112,1536]{1,0:T(8,128)(2,1)S(1)}, u32[]{:S(2)}, u32[]{:S(2)}) collective-permute-start(bf16[112,1536]{1,0:T(8,128)(2,1)S(1)} %slice_bitcast_fusion.2), channel_id=1, source_target_pairs={{0,2},{2,0},{1,3},{3,1},{4,6},{6,4},{5,7},{7,5},{8,10},{10,8},{9,1... | collective-permute-start | bytes 1032200 | tf_op jit(solution)/shard_map/ppermute | solution.py:689
  188.0 2.4 collective-permute-start.26
  188.3 16.0 %collective-permute-start.30 = (bf16[96,1536]{1,0:T(8,128)(2,1)S(1)}, bf16[96,1536]{1,0:T(8,128)(2,1)S(1)}, u32[]{:S(2)}, u32[]{:S(2)}) collective-permute-start(bf16[96,1536]{1,0:T(8,128)(2,1)S(1)} %slice_bitcast_fusion.5), channel_id=1, source_target_pairs={{0,1},{1,0},{2,3},{3,2},{4,5},{5,4},{6,7},{7,6},{8,9},{9,8},{10,11... | collective-permute-start | bytes 884744 | tf_op jit(solution)/shard_map/ppermute | solution.py:689
  191.2 13.1 %collective-permute-start.27 = (bf16[128,768]{1,0:T(8,128)(2,1)S(1)}, bf16[128,768]{1,0:T(8,128)(2,1)S(1)}, u32[]{:S(2)}, u32[]{:S(2)}) collective-permute-start(bf16[128,768]{1,0:T(8,128)(2,1)S(1)} %get-tuple-element.139), channel_id=1, source_target_pairs={{0,8},{8,0},{16,24},{24,16},{1,9},{9,1},{17,25},{25,17},{2,10},{10... | collective-permute-start | bytes 589832 | tf_op jit(solution)/shard_map/ppermute | solution.py:633
  192.3 17.5 %collective-permute-start.28 = (bf16[128,768]{1,0:T(8,128)(2,1)S(1)}, bf16[128,768]{1,0:T(8,128)(2,1)S(1)}, u32[]{:S(2)}, u32[]{:S(2)}) collective-permute-start(bf16[128,768]{1,0:T(8,128)(2,1)S(1)} %get-tuple-element.140), channel_id=1, source_target_pairs={{0,16},{8,24},{16,0},{24,8},{1,17},{9,25},{17,1},{25,9},{2,18},{10... | collective-permute-start | bytes 589832 | tf_op jit(solution)/shard_map/ppermute | solution.py:633
  195.6 14.2 %collective-permute-start.29 = (bf16[128,768]{1,0:T(8,128)(2,1)S(1)}, bf16[128,768]{1,0:T(8,128)(2,1)S(1)}, u32[]{:S(2)}, u32[]{:S(2)}) collective-permute-start(bf16[128,768]{1,0:T(8,128)(2,1)S(1)} %get-tuple-element.141), channel_id=1, source_target_pairs={{0,24},{8,16},{16,8},{24,0},{1,25},{9,17},{17,9},{25,1},{2,26},{10... | collective-permute-start | bytes 589832 | tf_op jit(solution)/shard_map/ppermute | solution.py:633
  210.8 16.7 %copy-start.71 = (bf16[4,16,1536]{2,1,0:T(8,128)(2,1)S(1)}, bf16[4,16,1536]{2,1,0:T(8,128)(2,1)}, u32[]{:S(2)}) copy-start(bf16[4,16,1536]{2,1,0:T(8,128)(2,1)} %copy-done.70) | copy-start | bytes 589828
  211.7 85.3 %all-gather.7.cloned.1.call-start = ((), (), s32[]{:S(2)}) async-start(), calls=%async_computation.4 | async-start | bytes 2654208 | tf_op jit(solution)/shard_map/all_gather | solution.py:861
  211.8 15.2 %collective-permute-start.32 = (bf16[208,1536]{1,0:T(8,128)(2,1)}, bf16[208,1536]{1,0:T(8,128)(2,1)}, u32[]{:S(2)}, u32[]{:S(2)}) collective-permute-start(bf16[208,1536]{1,0:T(8,128)(2,1)} %pad_maximum_fusion.2), channel_id=1, source_target_pairs={{0,1},{1,0},{2,3},{3,2},{4,5},{5,4},{6,7},{7,6},{8,9},{9,8},{10,11... | collective-permute-start | bytes 1916936 | tf_op jit(solution)/shard_map/ppermute | solution.py:698
  212.6 14.9 %collective-permute-start.33 = (bf16[208,1536]{1,0:T(8,128)(2,1)}, bf16[208,1536]{1,0:T(8,128)(2,1)}, u32[]{:S(2)}, u32[]{:S(2)}) collective-permute-start(bf16[208,1536]{1,0:T(8,128)(2,1)} %pad_maximum_fusion.3), channel_id=1, source_target_pairs={{0,2},{2,0},{1,3},{3,1},{4,6},{6,4},{5,7},{7,5},{8,10},{10,8},{9,1... | collective-permute-start | bytes 1916936 | tf_op jit(solution)/shard_map/ppermute | solution.py:698
  229.9 17.9 %collective-permute-start.34 = (bf16[208,768]{1,0:T(8,128)(2,1)S(1)}, bf16[208,768]{1,0:T(8,128)(2,1)S(1)}, u32[]{:S(2)}, u32[]{:S(2)}) collective-permute-start(bf16[208,768]{1,0:T(8,128)(2,1)S(1)} %constant_dynamic-slice_fusion.1), channel_id=1, source_target_pairs={{0,8},{8,0},{16,24},{24,16},{1,9},{9,1},{17,25},{25,17},{2,10},{10... | collective-permute-start | bytes 958472 | tf_op jit(solution)/shard_map/ppermute | solution.py:633
  249.5 9.2 %collective-permute-start.35 = (bf16[208,384]{1,0:T(8,128)(2,1)S(1)}, bf16[208,384]{1,0:T(8,128)(2,1)S(1)}, u32[]{:S(2)}, u32[]{:S(2)}) collective-permute-start(bf16[208,384]{1,0:T(8,128)(2,1)S(1)} %constant_dynamic-slice_fusion), channel_id=1, source_target_pairs={{0,16},{8,24},{16,0},{24,8},{1,17},{9,25},{17,1},{25,9},{2,18},{10... | collective-permute-start | bytes 479240 | tf_op jit(solution)/shard_map/ppermute | solution.py:633
  258.8 20.3 %collective-permute-start.36 = (bf16[208,384]{1,0:T(8,128)(2,1)S(1)}, bf16[208,384]{1,0:T(8,128)(2,1)S(1)}, u32[]{:S(2)}, u32[]{:S(2)}) collective-permute-start(bf16[208,384]{1,0:T(8,128)(2,1)S(1)} %add_convert_fusion.1), channel_id=1, source_target_pairs={{0,16},{8,24},{16,0},{24,8},{1,17},{9,25},{17,1},{25,9},{2,18},{10... | collective-permute-start | bytes 479240 | tf_op jit(solution)/shard_map/ppermute | solution.py:633
  279.2 12.6 %collective-permute-start.37 = (bf16[208,768]{1,0:T(8,128)(2,1)S(1)}, bf16[208,768]{1,0:T(8,128)(2,1)S(1)}, u32[]{:S(2)}, u32[]{:S(2)}) collective-permute-start(bf16[208,768]{1,0:T(8,128)(2,1)S(1)} %pad_maximum_fusion.7), channel_id=1, source_target_pairs={{0,8},{8,0},{16,24},{24,16},{1,9},{9,1},{17,25},{25,17},{2,10},{10... | collective-permute-start | bytes 958472 | tf_op jit(solution)/shard_map/ppermute | solution.py:633
  292.0 3.5 %collective-permute-start.38 = (bf16[208,1536]{1,0:T(8,128)(2,1)S(1)}, bf16[208,1536]{1,0:T(8,128)(2,1)S(1)}, u32[]{:S(2)}, u32[]{:S(2)}) collective-permute-start(bf16[208,1536]{1,0:T(8,128)(2,1)S(1)} %pad_maximum_fusion.4.refs_1_), channel_id=1, source_target_pairs={{0,4},{4,0},{1,5},{5,1},{2,6},{6,2},{3,7},{7,3},{8,12},{12,8},{9,1... | collective-permute-start | bytes 1916936 | tf_op jit(solution)/shard_map/ppermute | solution.py:895
  (71 other events, 243.7 us)
Sparse Core Ops, SparseCore 0:
  12.6 70.8 all-gather.4
  142.3 64.6 reduce-scatter.6
  211.9 36.4 reduce-scatter.4
  249.9 39.9 all-gather.6
where the time goes:
time: 309 us; the launch traced here: 308 us
  waiting for transfers between devices  115 us (37%)
  Pallas kernels  69.6 us (23%)
  local copies, waits for them, and re-layouts  40.9 us (13%)
  starting transfers between devices  38.1 us (12%)
  matrix products  17.6 us (6%)
  between operations  14.8 us (5%)
  other arithmetic  11.2 us (4%)
    ppermute x16, waiting for transfers between devices, hop(): return lax.ppermute(value, 'm', [(i, i ^ k) for i in range(groups)])  73.3 us
    unnamed x152, local copies, waits for them, and re-layouts  36.7 us
    ppermute x16, starting transfers between devices, hop(): return lax.ppermute(value, 'm', [(i, i ^ k) for i in range(groups)])  24.5 us
    dot_general x6, matrix products, dot(): lax.dot_general(left, right, (dims, ((), ())), preferred_element_type=F32)  17.6 us
    pallas_call x1, Pallas kernels, attend_back(): pl.pallas_call(kernel, grid=(pairs,), in_specs=[VMEM_SPEC, VMEM_SPEC, pl....  15.2 us
    pallas_call x1, Pallas kernels, backward(): pl.pallas_call(kernel, grid=(tokens // block,), in_specs=[SMEM_SPEC] + [r...  14.4 us
    pallas_call x1, Pallas kernels, attend(): pl.pallas_call(kernel, grid=(pairs,), in_specs=[SMEM_SPEC] + [VMEM_SPEC]...  13.8 us
    ppermute x2, waiting for transfers between devices, round_two(): return (lax.ppermute(to_x, 'x', swap), lax.ppermute(to_y, 'y', swap))  13.1 us
  transfers between devices with their start and end apart: 43, of which 20 were waited for; matrix products, arithmetic and copies ran while one was open for 8% of the time, Pallas kernels for 13%

commit v1 on v0

--- a/solution.py
+++ b/solution.py
@@ -57,6 +57,46 @@
         else:
             start = pl.multiple_of((me ^ offset) * shard + first, 16)
             target[pl.ds(start, rows), :] = ref[0:rows, 0:target.shape[1]]
+
+
+def place_tokens(target, refs, where_ref, ranks):
+    if len(refs) == 1:
+        target[...] = refs[0][...]
+        return
+    groups = len(refs) // ranks
+    span = target.shape[0] // (groups * ranks)
+    for n, ref in enumerate(refs):
+        rank = where_ref[2] if n < groups else 1 - where_ref[2]
+        chunk = (where_ref[1] ^ (n % groups)) * ranks + rank
+        target[pl.ds(pl.multiple_of(chunk * span, span), span), :] = ref[0:span, :]
+
+
+def place_segments(target, refs, where_ref, ranks):
+    groups = len(refs) // ranks
+    span = target.shape[1] // (groups * ranks)
+    for n, ref in enumerate(refs):
+        rank = where_ref[2] if n < groups else 1 - where_ref[2]
+        chunk = (where_ref[1] ^ (n % groups)) * ranks + rank
+        row = ref[span:span + 16, 0:span].astype(F32)[0:1, :]
+        target[:, pl.ds(pl.multiple_of(chunk * span, span), span)] = row
+
+
+def stack_copies(gu, down, stack_ref, sems, shard, part_rows):
+    members, chunks, groups = stack_ref.shape[0], gu.shape[1] // 256, []
+    for c in range(chunks):
+        groups.append([
+            pltpu.make_async_copy(
+                stack_ref.at[j, c * shard:(c + 1) * shard, :],
+                gu.at[j * shard:(j + 1) * shard, c * 256:(c + 1) * 256],
+                sems.at[c, j]) for j in range(members)])
+    for c in range(down.shape[1] // 256):
+        at = chunks * shard + c * part_rows
+        groups.append([
+            pltpu.make_async_copy(
+                stack_ref.at[j, at:at + part_rows, :],
+                down.at[j * part_rows:(j + 1) * part_rows, c * 256:(c + 1) * 256],
+                sems.at[chunks + c, j]) for j in range(members)])
+    return groups
 
 
 def place_tokens(target, refs, where_ref, ranks):
@@ -148,6 +188,15 @@
         att_ref[low:end, :] = jnp.where(first, parts[0], parts[1]).astype(BF)
 
 
+def hbm(*arrays):
+    return [pltpu.with_memory_space_constraint(a, pltpu.HBM) for a in arrays]
+
+
+def whole_specs(*arrays):
+    return [pl.BlockSpec(a.shape, lambda *_, n=a.ndim: (0,) * n, pipeline_mode=pl.Buffered(1))
+            for a in arrays]
+
+
 SMALL_COST = pl.CostEstimate(flops=1, bytes_accessed=1, transcendentals=0)
 VMEM_SPEC = pl.BlockSpec(memory_space=pltpu.VMEM)
 SMEM_SPEC = pl.BlockSpec(memory_space=pltpu.SMEM)
@@ -163,23 +212,22 @@
         window=window, scale=1.0 / math.sqrt(head_size), head_size=head_size)
     column = pl.BlockSpec((tokens, lanes), lambda p: (0, p))
     whole = lambda *shape: pl.BlockSpec(shape, lambda p: (0, 0))
+    inputs = hbm(cosine, sine, *token_refs, *weights)
     return pl.pallas_call(
         kernel,
         grid=(pairs,),
-        in_specs=[SMEM_SPEC] + [VMEM_SPEC] * (2 + len(token_refs) + len(weights)),
+        in_specs=[SMEM_SPEC] + whole_specs(*inputs),
         out_specs=[column, column, column, column,
                    pl.BlockSpec((1, 8, tokens), lambda p: (p, 0, 0)),
                    whole(width, 3 * lanes_all), whole(tokens, width), whole(1, tokens)],
-        out_shape=[jax.ShapeDtypeStruct((tokens, lanes_all), BF)] * 4
-        + [jax.ShapeDtypeStruct((pairs, 8, tokens), F32),
-           jax.ShapeDtypeStruct((width, 3 * lanes_all), BF),
-           jax.ShapeDtypeStruct((tokens, width), BF),
-           jax.ShapeDtypeStruct((1, tokens), F32)],
+        out_shape=[pltpu.HBM((tokens, lanes_all), BF)] * 4
+        + [pltpu.HBM((pairs, 8, tokens), F32), pltpu.HBM((width, 3 * lanes_all), BF),
+           pltpu.HBM((tokens, width), BF), pltpu.HBM((1, tokens), F32)],
         scratch_shapes=[pltpu.VMEM((tokens, 128), F32)],
-        compiler_params=pltpu.CompilerParams(vmem_limit_bytes=40 << 20),
+        compiler_params=pltpu.CompilerParams(vmem_limit_bytes=28 << 20),
         cost_estimate=SMALL_COST,
         name="attend",
-    )(where, cosine, sine, *token_refs, *weights)
+    )(where, *inputs)
 
 
 def unit_of(rows):
@@ -188,43 +236,63 @@
 
 
 def forward_kernel(x_ref, own_ref, got_ref, gain_ref, stack_ref, sum_ref, low_ref, hidden_ref,
-                   gate_ref, silu_ref, part_ref, gu, down, *, shard, part_rows):
-    @pl.when(pl.program_id(0) == 0)
+                   gate_ref, silu_ref, part_ref, gu, down, sems, *, shard, part_rows):
+    step = pl.program_id(0)
+    ff = down.shape[0]
+    chunks = ff // 256
+    copies = stack_copies(gu, down, stack_ref, sems, shard, part_rows)
+    order = [n * chunks + c for c in range(chunks) for n in range(2)]
+    order += list(range(2 * chunks, len(copies)))
+
+    def wait_for(numbers):
+        @pl.when(step == 0)
+        def _():
+            for number in numbers:
+                for copy in copies[number]:
+                    copy.wait()
+
+    @pl.when(step == 0)
     def _():
-        place_stack(gu, down, stack_ref, shard, part_rows)
+        for number in order:
+            for copy in copies[number]:
+                copy.start()
 
     total = x_ref[...].astype(F32) + own_ref[...].astype(F32) + got_ref[...].astype(F32)
     sum_ref[...] = total
     middle_low = (unit_of(total)[0] * gain_ref[...]).astype(BF)
     low_ref[...] = middle_low
-    ff = down.shape[0]
-    for c in range(0, ff, 256):
-        gate = dot(middle_low, gu[:, c:c + 256])
-        up = dot(middle_low, gu[:, ff + c:ff + c + 256])
+    for c in range(chunks):
+        wait_for([c, chunks + c])
+        cols = slice(c * 256, (c + 1) * 256)
+        gate = dot(middle_low, gu[:, cols])
+        up = dot(middle_low, gu[:, ff + c * 256:ff + (c + 1) * 256])
         sigmoid = jax.nn.sigmoid(gate)
         silu = gate * sigmoid
-        hidden_ref[:, c:c + 256] = (silu * up).astype(BF)
-        gate_ref[:, c:c + 256] = (up * sigmoid * (1.0 + gate * (1.0 - sigmoid))).astype(BF)
-        silu_ref[:, c:c + 256] = silu.astype(BF)
+        hidden_ref[:, cols] = (silu * up).astype(BF)
+        gate_ref[:, cols] = (up * sigmoid * (1.0 + gate * (1.0 - sigmoid))).astype(BF)
+        silu_ref[:, cols] = silu.astype(BF)
+    wait_for(range(2 * chunks, len(copies)))
     part_ref[...] = dot(hidden_ref[...], down[...]).astype(BF)
+
+
+HBM_SPEC = pl.BlockSpec(memory_space=pltpu.HBM)
 
 
 def forward(x, own, got, gain, stack, shard, part_rows, ff, block):
     tokens, width = x.shape
     row = lambda cols: pl.BlockSpec((block, cols), lambda i: (i, 0))
+    x, stack = hbm(x, stack)
     return pl.pallas_call(
         lambda *refs: forward_kernel(*refs, shard=shard, part_rows=part_rows),
         grid=(tokens // block,),
-        in_specs=[row(width), row(width), row(width), VMEM_SPEC, VMEM_SPEC],
+        in_specs=[row(width), row(width), row(width)] + whole_specs(gain) + [HBM_SPEC],
         out_specs=[row(width), row(width), row(ff), row(ff), row(ff), row(width)],
-        out_shape=[jax.ShapeDtypeStruct((tokens, width), F32),
-                   jax.ShapeDtypeStruct((tokens, width), BF)]
-        + [jax.ShapeDtypeStruct((tokens, ff), BF)] * 3
-        + [jax.ShapeDtypeStruct((tokens, width), BF)],
-        scratch_shapes=[pltpu.VMEM((width, 2 * ff), BF), pltpu.VMEM((ff, width), BF)],
-        compiler_params=pltpu.CompilerParams(vmem_limit_bytes=40 << 20),
-        cost_estimate=pl.CostEstimate(
-            flops=6 * tokens * width * ff, bytes_accessed=24 << 20, transcendentals=0),
+        out_shape=[pltpu.HBM((tokens, width), F32), pltpu.HBM((tokens, width), BF)]
+        + [pltpu.HBM((tokens, ff), BF)] * 3 + [pltpu.HBM((tokens, width), BF)],
+        scratch_shapes=[pltpu.VMEM((width, 2 * ff), BF), pltpu.VMEM((ff, width), BF),
+                        pltpu.SemaphoreType.DMA(((2 * ff + width) // 256, stack.shape[0]))],
+        compiler_params=pltpu.CompilerParams(vmem_limit_bytes=28 << 20),
+        cost_estimate=SMALL_COST,
         name="ffn_forward",
     )(x, own, got, gain, stack)
 
@@ -233,12 +301,23 @@
                     cot_count, shard, part_rows, groups, ranks):
     cot_refs, stack_ref, refs = refs[:cot_count], refs[cot_count], refs[cot_count + 1:]
     out_refs, refs = refs[:groups], refs[groups:]
-    grad_ref, low_ref, gu_grad_ref, part_ref, gain_ref, gu, down, cot_ref, rows_ref = refs
+    grad_ref, low_ref, gu_grad_ref, part_ref, gain_ref, gu, down, cot_ref, rows_ref, sems = refs
     step = pl.program_id(0)
+    copies = stack_copies(gu, down, stack_ref, sems, shard, part_rows)
+    chunks = gu.shape[1] // 256
+
+    def wait_for(numbers):
+        @pl.when(step == 0)
+        def _():
+            for number in numbers:
+                for copy in copies[number]:
+                    copy.wait()
 
     @pl.when(step == 0)
     def _():
-        place_stack(gu, down, stack_ref, shard, part_rows)
+        for group in copies[chunks:] + copies[:chunks]:
+            for copy in group:
+                copy.start()
         place_tokens(cot_ref, cot_refs, where_ref, ranks)
         gain_ref[...] = jnp.zeros_like(gain_ref)
 
@@ -260,11 +339,13 @@
     grad_low = grad.astype(BF)
     low_ref[...] = grad_low
     ff = down.shape[0]
+    wait_for(range(chunks, len(copies)))
     for c in range(0, ff, 256):
         hidden_grad = dot(grad_low, down[c:c + 256, :], ((1,), (1,)))
         gu_grad_ref[:, c:c + 256] = (hidden_grad * gate_ref[:, c:c + 256].astype(F32)).astype(BF)
         gu_grad_ref[:, ff + c:ff + c + 256] = (
             hidden_grad * silu_ref[:, c:c + 256].astype(F32)).astype(BF)
+    wait_for(range(chunks))
     part_ref[...] = dot(gu_grad_ref[...], gu[...], ((1,), (1,))).astype(BF)
 
 
@@ -276,22 +357,22 @@
         *refs, cot_count=len(cot), shard=shard, part_rows=part_rows, groups=groups, ranks=ranks)
     row = lambda cols: pl.BlockSpec((block, cols), lambda i: (i, 0))
     slab = pl.BlockSpec((block // ranks, width), lambda i: (0, 0))
+    total, gate, silu, stack = hbm(total, gate, silu, stack)
     return pl.pallas_call(
         kernel,
         grid=(tokens // block,),
         in_specs=[SMEM_SPEC] + [row(width)] * 3 + [row(ff)] * 2
-        + [VMEM_SPEC] * (2 + len(cot)),
+        + whole_specs(gains, *cot) + [HBM_SPEC],
         out_specs=[slab] * groups + [row(width), row(width), row(2 * ff), row(width),
                                      pl.BlockSpec((1, width), lambda i: (0, 0))],
-        out_shape=[jax.ShapeDtypeStruct((block // ranks, width), BF)] * groups
-        + [jax.ShapeDtypeStruct((tokens, width), F32),
-           jax.ShapeDtypeStruct((tokens, width), BF),
-           jax.ShapeDtypeStruct((tokens, 2 * ff), BF),
-           jax.ShapeDtypeStruct((tokens, width), BF),
-           jax.ShapeDtypeStruct((1, width), F32)],
+        out_shape=[pltpu.HBM((block // ranks, width), BF)] * groups
+        + [pltpu.HBM((tokens, width), F32), pltpu.HBM((tokens, width), BF),
+           pltpu.HBM((tokens, 2 * ff), BF), pltpu.HBM((tokens, width), BF),
+           pltpu.HBM((1, width), F32)],
         scratch_shapes=[pltpu.VMEM((width, 2 * ff), BF), pltpu.VMEM((ff, width), BF),
-                        pltpu.VMEM((tokens, width), BF), pltpu.VMEM((block, width), F32)],
-        compiler_params=pltpu.CompilerParams(vmem_limit_bytes=44 << 20),
+                        pltpu.VMEM((tokens, width), BF), pltpu.VMEM((block, width), F32),
+                        pltpu.SemaphoreType.DMA(((2 * ff + width) // 256, stack.shape[0]))],
+        compiler_params=pltpu.CompilerParams(vmem_limit_bytes=32 << 20),
         cost_estimate=SMALL_COST,
         name="ffn_backward",
     )(where, total, own, got, gate, silu, gains, *cot, stack)
@@ -317,17 +398,18 @@
 def norm_back(rank, total, grad, own, got, gain, block, span):
     tokens, width = total.shape
     row = pl.BlockSpec((block, width), lambda i: (i, 0))
+    total, grad = hbm(total, grad)
     return pl.pallas_call(
         norm_back_kernel,
         grid=(tokens // block,),
-        in_specs=[SMEM_SPEC, row, row, row, row, VMEM_SPEC],
+        in_specs=[SMEM_SPEC, row, row, row, row] + whole_specs(gain),
         out_specs=[row, pl.BlockSpec((1, span, width), lambda i: (i, 0, 0)),
                    pl.BlockSpec((1, width), lambda i: (0, 0))],
-        out_shape=[jax.ShapeDtypeStruct((tokens, width), BF),
-                   jax.ShapeDtypeStruct((tokens // block, span, width), F32),
-                   jax.ShapeDtypeStruct((1, width), F32)],
+        out_shape=[pltpu.HBM((tokens, width), BF),
+                   pltpu.HBM((tokens // block, span, width), F32),
+                   pltpu.HBM((1, width), F32)],
         scratch_shapes=[pltpu.VMEM((block, width), F32)],
-        compiler_params=pltpu.CompilerParams(vmem_limit_bytes=24 << 20),
+        compiler_params=pltpu.CompilerParams(vmem_limit_bytes=16 << 20),
         cost_estimate=SMALL_COST,
         name="norm_back",
     )(rank, total, grad, own, got, gain)
@@ -373,17 +455,18 @@
     shard, width = query.shape
     groups, _, span, _ = tokens.shape
     cols = 3 * lanes_all + width // ranks
+    inputs = hbm(query, key, value, out, gains, tokens, segments, cot)
+    shapes = [(shard + 16, cols)] + [(span + 16, width)] * groups + [(span, width)] * groups
     return pl.pallas_call(
         lambda *refs: pack_small_kernel(*refs, ranks=ranks, lanes=lanes, lanes_all=lanes_all),
-        in_specs=[SMEM_SPEC] + [VMEM_SPEC] * 8,
-        out_specs=[VMEM_SPEC] * (1 + 2 * groups),
-        out_shape=[jax.ShapeDtypeStruct((shard + 16, cols), BF)]
-        + [jax.ShapeDtypeStruct((span + 16, width), BF)] * groups
-        + [jax.ShapeDtypeStruct((span, width), BF)] * groups,
+        grid=(1,),
+        in_specs=[SMEM_SPEC] + whole_specs(*inputs),
+        out_specs=[pl.BlockSpec(shape, lambda i: (0, 0)) for shape in shapes],
+        out_shape=[pltpu.HBM(shape, BF) for shape in shapes],
         compiler_params=pltpu.CompilerParams(vmem_limit_bytes=24 << 20),
         cost_estimate=SMALL_COST,
         name="pack_small",
-    )(where, query, key, value, out, gains, tokens, segments, cot)
+    )(where, *inputs)
 
 
 def pack_kernel(where_ref, gate_ref, up_ref, down_ref, out_ref, gu, *, fsdp, ranks):
@@ -409,16 +492,18 @@
     shard, ff = gate.shape
     cols = 2 * ff // ranks
     rows = cols // 256 * shard + down.shape[1] // 256 * (down.shape[0] // ranks)
+    inputs = hbm(gate, up, down)
     return pl.pallas_call(
         lambda *refs: pack_kernel(*refs, fsdp=fsdp, ranks=ranks),
-        in_specs=[SMEM_SPEC] + [VMEM_SPEC] * 3,
-        out_specs=VMEM_SPEC,
-        out_shape=jax.ShapeDtypeStruct((rows, 256), BF),
+        grid=(1,),
+        in_specs=[SMEM_SPEC] + whole_specs(*inputs),
+        out_specs=pl.BlockSpec((rows, 256), lambda i: (0, 0)),
+        out_shape=pltpu.HBM((rows, 256), BF),
         scratch_shapes=[pltpu.VMEM((shard, cols), BF)],
         compiler_params=pltpu.CompilerParams(vmem_limit_bytes=24 << 20),
         cost_estimate=SMALL_COST,
         name="pack",
-    )(where, gate, up, down)
+    )(where, *inputs)
 
 
 def arrange_kernel(gu_ref, down_ref, out_ref):
@@ -440,7 +525,7 @@
         in_specs=[pl.BlockSpec((shard, gu.shape[1]), lambda j: (j, 0)),
                   pl.BlockSpec((part, down.shape[1]), lambda j: (j, 0))],
         out_specs=pl.BlockSpec((1, rows, 256), lambda j: (j, 0, 0)),
-        out_shape=jax.ShapeDtypeStruct((fsdp, rows, 256), BF),
+        out_shape=pltpu.HBM((fsdp, rows, 256), BF),
         compiler_params=pltpu.CompilerParams(vmem_limit_bytes=24 << 20),
         cost_estimate=SMALL_COST,
         name="arrange",
@@ -551,27 +636,26 @@
     kernel = lambda *refs: attend_back_kernel(
         *refs, block=256, window=window, scale=1.0 / math.sqrt(head_size), head_size=head_size)
     column = pl.BlockSpec((tokens, lanes), lambda p: (0, p))
+    inputs = hbm(seg, g, w_out, q, k, v, att, lse, cosine, sine)
     return pl.pallas_call(
         kernel,
         grid=(pairs,),
-        in_specs=[
-            VMEM_SPEC, VMEM_SPEC,
+        in_specs=whole_specs(seg, g) + [
             pl.BlockSpec((lanes, width), lambda p: (p, 0)),
             column, column, column, column,
             pl.BlockSpec((1, 8, tokens), lambda p: (p, 0, 0)),
-            VMEM_SPEC, VMEM_SPEC,
-        ],
+        ] + whole_specs(cosine, sine),
         out_specs=pl.BlockSpec((tokens, 3 * lanes), lambda p: (0, p)),
-        out_shape=jax.ShapeDtypeStruct((tokens, 3 * lanes * pairs), BF),
+        out_shape=pltpu.HBM((tokens, 3 * lanes * pairs), BF),
         scratch_shapes=[
             pltpu.VMEM((tokens, lanes), BF),
             pltpu.VMEM((tokens, lanes), F32),
             pltpu.VMEM((tokens, lanes), F32),
         ],
-        compiler_params=pltpu.CompilerParams(vmem_limit_bytes=48 << 20),
+        compiler_params=pltpu.CompilerParams(vmem_limit_bytes=28 << 20),
         cost_estimate=SMALL_COST,
         name="attend_back",
-    )(seg, g, w_out, q, k, v, att, lse, cosine, sine)
+    )(*inputs)
 
 
 def join_kernel(rank_ref, own_ref, other_ref, *out_refs, moves, plain):
@@ -803,8 +887,10 @@
             where, total, own, got, gate_back, silu, gains, cot_refs, stack_all, shard, part_rows,
             block, groups, ranks)
         own, got = exchange(part)
+        gu_w_grad = dot(middle_low, gu_grad_low, ((0,), (0,))).astype(BF)
+        if ranks == 2:
+            got, gu_w_grad = lax.optimization_barrier((got, gu_w_grad))
         down_w_grad = dot(hidden_low, ffn_grad_low, ((0,), (0,))).astype(BF)
-        gu_w_grad = dot(middle_low, gu_grad_low, ((0,), (0,))).astype(BF)
         stack_grad = arrange(gu_w_grad, down_w_grad, fsdp)
         stack_owned = lax.psum_scatter(stack_grad, F, scatter_dimension=0, tiled=False)
         own = after(own, stack_grad)

time: 309 us -> 288 us (0.932)
  local copies, waits for them, and re-layouts: 40.9 us -> 11.8 us
  Pallas kernels: 69.6 us -> 83.2 us
  other arithmetic: 11.2 us -> 7.92 us
    unnamed x152 -> x56, local copies, waits for them, and re-layouts: 36.7 us -> 7.02 us
    ppermute x3, waiting for transfers between devices: 5.72 us -> 0.27 us  [exchange(): return (part, lax.ppermute(part, 'r', swap))]
    pallas_call x1, Pallas kernels: 10.8 us -> 14.7 us  [forward(): pl.pallas_call(lambda *refs: forward_kernel(*refs, shard=shard, part_rows...]
  transfers between devices with their start and end apart: 43 -> 43, of which waited for: 20 -> 20; matrix products, arithmetic and copies ran while one was open for 8% -> 11% of each run, Pallas kernels for 13% -> 16%
where the time goes in v1:
time: 288 us; the launch traced here: 287 us
  waiting for transfers between devices  113 us (39%)
  Pallas kernels  83.2 us (29%)
  starting transfers between devices  38.8 us (13%)
  matrix products  17.7 us (6%)
  between operations  14.5 us (5%)
  local copies, waits for them, and re-layouts  11.8 us (4%)
  other arithmetic  7.92 us (3%)
    ppermute x16, waiting for transfers between devices, hop(): return lax.ppermute(value, 'm', [(i, i ^ k) for i in range(groups)])  73.8 us
    ppermute x16, starting transfers between devices, hop(): return lax.ppermute(value, 'm', [(i, i ^ k) for i in range(groups)])  23.3 us
    dot_general x6, matrix products, dot(): lax.dot_general(left, right, (dims, ((), ())), preferred_element_type=F32)  17.7 us
    pallas_call x1, Pallas kernels, backward(): pl.pallas_call(kernel, grid=(tokens // block,), in_specs=[SMEM_SPEC] + [r...  15.7 us
    pallas_call x1, Pallas kernels, attend_back(): pl.pallas_call(kernel, grid=(pairs,), in_specs=whole_specs(seg, g) + [pl....  15.7 us
    pallas_call x1, Pallas kernels, attend(): pl.pallas_call(kernel, grid=(pairs,), in_specs=[SMEM_SPEC] + whole_specs(...  15 us
    pallas_call x1, Pallas kernels, forward(): pl.pallas_call(lambda *refs: forward_kernel(*refs, shard=shard, part_rows...  14.7 us
    ppermute x2, waiting for transfers between devices, round_two(): return (lax.ppermute(to_x, 'x', swap), lax.ppermute(to_y, 'y', swap))  14.1 us
  transfers between devices with their start and end apart: 43, of which 20 were waited for; matrix products, arithmetic and copies ran while one was open for 11% of the time, Pallas kernels for 16%

profile of v1, /device:TPU:0, one launch (start us, length us, event | category | flops | bytes accessed | tf_op | source)
XLA Modules:
  0.0 287.0 jit_solution(10350579108350837616)
XLA Ops:
  7.3 2.8 pack.1
  10.8 3.3 %pack_small.1 = (bf16[208,1536]{1,0:T(8,128)(2,1)}, bf16[144,768]{1,0:T(8,128)(2,1)}, bf16[144,768]{1,0:T(8,128)(2,1)}, bf16[144,768]{1,0:T(8,128)(2,1)}, bf16[1...) custom-call(s32[3]{0:T(128)S(1)} %pad_add_fusion.refs_0_.where_ref, ...), custom_call_target="tpu_custom_call" | custom-call | flops 1 | bytes 1 | tf_op jit(solution)/shard_map/pack_small/pallas_call | solution.py:460
  14.1 3.0 %collective-permute-start.7 = (bf16[208,1536]{1,0:T(8,128)(2,1)}, bf16[208,1536]{1,0:T(8,128)(2,1)S(1)}, u32[]{:S(2)}, u32[]{:S(2)}) collective-permute-start(bf16[208,1536]{1,0:T(8,128)(2,1)} %get-tuple-element.95.refs_11_), channel_id=1, source_target_pairs={{0,1},{1,0},{2,3},{3,2},{4,5},{5,4},{6,7},{7,6},{8,9},{9,8},{10,11... | collective-permute-start | bytes 1916936 | tf_op jit(solution)/shard_map/ppermute | solution.py:755
  17.1 1.5 collective-permute-start.8
  18.6 3.6 %collective-permute-start.2 = (bf16[144,768]{1,0:T(8,128)(2,1)}, bf16[144,768]{1,0:T(8,128)(2,1)}, u32[]{:S(2)}, u32[]{:S(2)}) collective-permute-start(bf16[144,768]{1,0:T(8,128)(2,1)} %get-tuple-element.93), channel_id=1, source_target_pairs={{0,24},{8,16},{16,8},{24,0},{1,25},{9,17},{17,9},{25,1},{2,26},{10... | collective-permute-start | bytes 663560 | tf_op jit(solution)/shard_map/ppermute | solution.py:717
  23.1 1.9 fusion.9
  25.0 1.8 pad_maximum_fusion.5
  27.8 1.4 collective-permute-done.2.refs_6_
  29.2 11.6 %collective-permute-done.1.refs_5_ = bf16[144,768]{1,0:T(8,128)(2,1)} collective-permute-done((bf16[144,768]{1,0:T(8,128)(2,1)}, bf16[144,768]{1,0:T(8,128)(2,1)}, u32[]{:S(2)}, u32[]{:S(2)}) %collective-permute-start.1) | collective-permute-done | bytes 221216 | tf_op jit(solution)/shard_map/ppermute | solution.py:717
  41.5 1.4 collective-permute-start.10
  42.9 1.4 collective-permute-done.8.refs_13_
  45.4 7.8 %collective-permute-done.10.refs_15_ = bf16[112,1536]{1,0:T(8,128)(2,1)S(1)} collective-permute-done((bf16[112,1536]{1,0:T(8,128)(2,1)S(1)}, bf16[112,1536]{1,0:T(8,128)(2,1)S(1)}, u32[]{:S(2)}, u32[]{:S(2)}) %collective-permute-start.10) | collective-permute-done | bytes 344096 | tf_op jit(solution)/shard_map/ppermute | solution.py:758
  54.0 3.6 %collective-permute-start.13 = (bf16[128,768]{1,0:T(8,128)(2,1)}, bf16[128,768]{1,0:T(8,128)(2,1)S(1)}, u32[]{:S(2)}, u32[]{:S(2)}) collective-permute-start(bf16[128,768]{1,0:T(8,128)(2,1)} %get-tuple-element.102), channel_id=1, source_target_pairs={{0,24},{8,16},{16,8},{24,0},{1,25},{9,17},{17,9},{25,1},{2,26},{10... | collective-permute-start | bytes 589832 | tf_op jit(solution)/shard_map/ppermute | solution.py:717
  59.2 15.0 %attend.1 = (bf16[1024,384]{1,0:T(8,128)(2,1)}, bf16[1024,384]{1,0:T(8,128)(2,1)}, bf16[1024,384]{1,0:T(8,128)(2,1)}, bf16[1024,384]{1,0:T(8,128)(2,1)}, f32[3,8...) custom-call(s32[3]{0:T(128)S(1)} %pad_add_fusion.refs_0_.where_ref, ...), custom_call_target="tpu_custom_call" | custom-call | flops 1 | bytes 1 | tf_op jit(solution)/shard_map/attend/pallas_call | solution.py:216
  76.2 2.1 convolution_convert_fusion.2.refs_1_
  81.8 14.7 %ffn_forward.1 = (f32[1024,768]{1,0:T(8,128)}, bf16[1024,768]{1,0:T(8,128)(2,1)}, bf16[1024,1024]{1,0:T(8,128)(2,1)}, bf16[1024,1024]{1,0:T(8,128)(2,1)}, bf16[1...) custom-call(bf16[1024,768]{1,0:T(8,128)(2,1)} %get-tuple-element.96.refs_0_, ...), custom_call_target="tpu_custom_call" | custom-call | flops 1 | bytes 1 | tf_op jit(solution)/shard_map/ffn_forward/pallas_call | solution.py:285
  97.9 2.6 collective-permute-done.17.refs_11_
  101.3 1.4 copy-done.1
  102.7 15.7 %ffn_backward.1 = (bf16[128,768]{1,0:T(8,128)(2,1)}, bf16[128,768]{1,0:T(8,128)(2,1)}, bf16[128,768]{1,0:T(8,128)(2,1)}, bf16[128,768]{1,0:T(8,128)(2,1)}, f32[1...) custom-call(s32[3]{0:T(128)S(1)} %pad_add_fusion.refs_0_.where_ref, ...), custom_call_target="tpu_custom_call" | custom-call | flops 1 | bytes 1 | tf_op jit(solution)/shard_map/ffn_backward/pallas_call | solution.py:361
  118.7 3.5 %convolution_convert_fusion.4.down_ref = bf16[1024,768]{1,0:T(8,128)(2,1)S(1)} fusion(bf16[1024,1024]{1,0:T(8,128)(2,1)S(1)} %copy-done.20, bf16[1024,768]{1,0:T(8,128)(2,1)} %get-tuple-element.124), kind=kOutput, calls=%fused_computation.14 | convolution fusion | flops 1611399168 | bytes 5242880 | tf_op jit(solution)/shard_map/dot_general | solution.py:19
  122.2 3.7 %convolution_convert_fusion.1.gu_ref = bf16[768,2048]{1,0:T(8,128)(2,1)S(1)} fusion(bf16[1024,768]{1,0:T(8,128)(2,1)S(1)} %copy-done.22, bf16[1024,2048]{1,0:T(8,128)(2,1)S(1)} %copy-done.19), kind=kOutput, calls=%fused_computation.6 | convolution fusion | flops 3222798336 | bytes 8912896 | tf_op jit(solution)/shard_map/dot_general | solution.py:19
  126.0 2.7 arrange.1
  130.0 5.7 %norm_back.1 = (bf16[1024,768]{1,0:T(8,128)(2,1)}, f32[4,128,768]{2,1,0:T(8,128)}, f32[1,768]{1,0:T(1,128)}) custom-call(s32[1]{0:T(128)} %bitcast.2.rank_ref.refs_0_, f32[1024,768]{1,0:T(8,128)} %get-tuple-element.105.refs_1_.sum_ref, f32[1024,768]{1,0:T(8,128)} %get-tuple-element.118.grad_ref, bf16[1024,768]{1,0:T(8,128)(2,1)S(1)} %copy-done.3, ...), custom_call_target="tpu_custom_call" | custom-call | flops 1 | bytes 1 | tf_op jit(solution)/shard_map/norm_back/pallas_call | solution.py:402
  135.7 2.3 convolution_convert_fusion.5
  139.9 2.4 collective-permute-start.22
  143.4 15.7 %attend_back.1 = bf16[1024,1152]{1,0:T(8,128)(2,1)} custom-call(f32[1,1024]{1,0:T(1,128)} %get-tuple-element.117.refs_0_, bf16[1024,768]{1,0:T(8,128)(2,1)} %get-tuple-element.130.refs_1_, bf16[384,768]{1,0:T(8,128)(2,1)} %copy-done.9, bf16[1024,384]{1,0:T(8,128)(2,1)} %get-tuple-element.131.refs_3_, bf16[1024,384]{1,0:T(8,128)(2,1)} %get-tuple-element.132.refs_4_, ...), custom_call_target="tpu_custom_call" | custom-call | flops 1 | bytes 1 | tf_op jit(solution)/shard_map/attend_back/pallas_call | solution.py:640
  159.1 3.9 %convolution_convert_fusion = bf16[768,1152]{1,0:T(8,128)(2,1)S(1)} fusion(bf16[1024,768]{1,0:T(8,128)(2,1)S(1)} %copy-done.12, bf16[1024,1152]{1,0:T(8,128)(2,1)} %attend_back.1), kind=kOutput, calls=%fused_computation.5 | convolution fusion | flops 1812824064 | bytes 5701632 | tf_op jit(solution)/shard_map/dot_general | solution.py:19
  163.4 1.6 collective-permute-start.31
  166.3 2.2 convolution_convert_fusion.3.refs_2_
  171.7 1.7 collective-permute-start.27
  173.4 2.0 collective-permute-start.28
  176.2 8.2 %collective-permute-done.30 = bf16[96,1536]{1,0:T(8,128)(2,1)S(1)} collective-permute-done((bf16[96,1536]{1,0:T(8,128)(2,1)S(1)}, bf16[96,1536]{1,0:T(8,128)(2,1)S(1)}, u32[]{:S(2)}, u32[]{:S(2)}) %collective-permute-start.30) | collective-permute-done | bytes 294944 | tf_op jit(solution)/shard_map/ppermute | solution.py:773
  184.4 6.1 %collective-permute-done.28.refs_2_ = bf16[128,768]{1,0:T(8,128)(2,1)S(1)} collective-permute-done((bf16[128,768]{1,0:T(8,128)(2,1)S(1)}, bf16[128,768]{1,0:T(8,128)(2,1)S(1)}, u32[]{:S(2)}, u32[]{:S(2)}) %collective-permute-start.28) | collective-permute-done | bytes 196640 | tf_op jit(solution)/shard_map/ppermute | solution.py:717
  191.9 1.4 collective-permute-start.32
  194.2 14.0 %collective-permute-done.32 = bf16[208,1536]{1,0:T(8,128)(2,1)S(1)} collective-permute-done((bf16[208,1536]{1,0:T(8,128)(2,1)}, bf16[208,1536]{1,0:T(8,128)(2,1)S(1)}, u32[]{:S(2)}, u32[]{:S(2)}) %collective-permute-start.32) | collective-permute-done | bytes 639008 | tf_op jit(solution)/shard_map/ppermute | solution.py:782
  208.3 1.3 fusion.1
  209.6 3.8 %collective-permute-start.34 = (bf16[208,768]{1,0:T(8,128)(2,1)S(1)}, bf16[208,768]{1,0:T(8,128)(2,1)S(1)}, u32[]{:S(2)}, u32[]{:S(2)}) collective-permute-start(bf16[208,768]{1,0:T(8,128)(2,1)S(1)} %constant_dynamic-slice_fusion.1), channel_id=1, source_target_pairs={{0,8},{8,0},{16,24},{24,16},{1,9},{9,1},{17,25},{25,17},{2,10},{10... | collective-permute-start | bytes 958472 | tf_op jit(solution)/shard_map/ppermute | solution.py:717
  213.4 13.9 %collective-permute-done.34 = bf16[208,768]{1,0:T(8,128)(2,1)S(1)} collective-permute-done((bf16[208,768]{1,0:T(8,128)(2,1)S(1)}, bf16[208,768]{1,0:T(8,128)(2,1)S(1)}, u32[]{:S(2)}, u32[]{:S(2)}) %collective-permute-start.34) | collective-permute-done | bytes 319520 | tf_op jit(solution)/shard_map/ppermute | solution.py:717
  227.3 2.4 reduce-scatter.5.cloned.1.call-done
  229.9 1.6 collective-permute-start.35
  231.5 6.6 %collective-permute-done.35 = bf16[208,384]{1,0:T(8,128)(2,1)S(1)} collective-permute-done((bf16[208,384]{1,0:T(8,128)(2,1)S(1)}, bf16[208,384]{1,0:T(8,128)(2,1)S(1)}, u32[]{:S(2)}, u32[]{:S(2)}) %collective-permute-start.35) | collective-permute-done | bytes 159776 | tf_op jit(solution)/shard_map/ppermute | solution.py:717
  238.3 18.1 %collective-permute-done.36 = bf16[208,384]{1,0:T(8,128)(2,1)S(1)} collective-permute-done((bf16[208,384]{1,0:T(8,128)(2,1)S(1)}, bf16[208,384]{1,0:T(8,128)(2,1)S(1)}, u32[]{:S(2)}, u32[]{:S(2)}) %collective-permute-start.36) | collective-permute-done | bytes 159776 | tf_op jit(solution)/shard_map/ppermute | solution.py:717
  256.6 15.0 %collective-permute-done.37 = bf16[208,768]{1,0:T(8,128)(2,1)S(1)} collective-permute-done((bf16[208,768]{1,0:T(8,128)(2,1)S(1)}, bf16[208,768]{1,0:T(8,128)(2,1)S(1)}, u32[]{:S(2)}, u32[]{:S(2)}) %collective-permute-start.37) | collective-permute-done | bytes 319520 | tf_op jit(solution)/shard_map/ppermute | solution.py:717
  272.0 1.5 stack.30
  273.4 1.5 stack.31
  274.9 1.5 join.1
  276.4 1.7 copy-done
  278.1 2.4 join_all.1
  (175 shorter events, 27.7 us)
Async XLA Ops:
  7.2 74.6 %all-gather.5.cloned.1.call-start = ((), (), s32[]{:S(2)}) async-start(), calls=%async_computation.3 | async-start | bytes 5898240 | tf_op jit(solution)/shard_map/all_gather | solution.py:821
  10.1 181.7 %reduce-scatter.7.cloned.1.call-start = ((), (), s32[]{:S(2)}) async-start(), calls=%async_computation.5 | async-start | bytes 5898240
  14.1 27.3 %collective-permute-start.7 = (bf16[208,1536]{1,0:T(8,128)(2,1)}, bf16[208,1536]{1,0:T(8,128)(2,1)S(1)}, u32[]{:S(2)}, u32[]{:S(2)}) collective-permute-start(bf16[208,1536]{1,0:T(8,128)(2,1)} %get-tuple-element.95.refs_11_), channel_id=1, source_target_pairs={{0,1},{1,0},{2,3},{3,2},{4,5},{5,4},{6,7},{7,6},{8,9},{9,8},{10,11... | collective-permute-start | bytes 1916936 | tf_op jit(solution)/shard_map/ppermute | solution.py:755
  17.1 27.1 %collective-permute-start.8 = (bf16[208,1536]{1,0:T(8,128)(2,1)}, bf16[208,1536]{1,0:T(8,128)(2,1)S(1)}, u32[]{:S(2)}, u32[]{:S(2)}) collective-permute-start(bf16[208,1536]{1,0:T(8,128)(2,1)} %get-tuple-element.95.refs_11_), channel_id=1, source_target_pairs={{0,2},{2,0},{1,3},{3,1},{4,6},{6,4},{5,7},{7,5},{8,10},{10,8},{9,1... | collective-permute-start | bytes 1916936 | tf_op jit(solution)/shard_map/ppermute | solution.py:756
  18.6 10.6 %collective-permute-start.2 = (bf16[144,768]{1,0:T(8,128)(2,1)}, bf16[144,768]{1,0:T(8,128)(2,1)}, u32[]{:S(2)}, u32[]{:S(2)}) collective-permute-start(bf16[144,768]{1,0:T(8,128)(2,1)} %get-tuple-element.93), channel_id=1, source_target_pairs={{0,24},{8,16},{16,8},{24,0},{1,25},{9,17},{17,9},{25,1},{2,26},{10... | collective-permute-start | bytes 663560 | tf_op jit(solution)/shard_map/ppermute | solution.py:717
  22.3 18.6 %collective-permute-start.1 = (bf16[144,768]{1,0:T(8,128)(2,1)}, bf16[144,768]{1,0:T(8,128)(2,1)}, u32[]{:S(2)}, u32[]{:S(2)}) collective-permute-start(bf16[144,768]{1,0:T(8,128)(2,1)} %get-tuple-element.91), channel_id=1, source_target_pairs={{0,16},{8,24},{16,0},{24,8},{1,17},{9,25},{17,1},{25,9},{2,18},{10... | collective-permute-start | bytes 663560 | tf_op jit(solution)/shard_map/ppermute | solution.py:717
  22.3 31.7 %collective-permute-start = (bf16[144,768]{1,0:T(8,128)(2,1)}, bf16[144,768]{1,0:T(8,128)(2,1)}, u32[]{:S(2)}, u32[]{:S(2)}) collective-permute-start(bf16[144,768]{1,0:T(8,128)(2,1)} %get-tuple-element.89), channel_id=1, source_target_pairs={{0,8},{8,0},{16,24},{24,16},{1,9},{9,1},{17,25},{25,17},{2,10},{10... | collective-permute-start | bytes 663560 | tf_op jit(solution)/shard_map/ppermute | solution.py:717
  29.2 24.8 %collective-permute-start.3 = (bf16[144,768]{1,0:T(8,128)(2,1)S(1)}, bf16[144,768]{1,0:T(8,128)(2,1)}, u32[]{:S(2)}, u32[]{:S(2)}) collective-permute-start(bf16[144,768]{1,0:T(8,128)(2,1)S(1)} %copy-done.15), channel_id=1, source_target_pairs={{0,4},{4,0},{1,5},{5,1},{2,6},{6,2},{3,7},{7,3},{8,12},{12,8},{9,1... | collective-permute-start | bytes 663560 | tf_op jit(solution)/shard_map/ppermute | solution.py:731
  40.8 16.8 %collective-permute-start.6 = (bf16[144,768]{1,0:T(8,128)(2,1)}, bf16[144,768]{1,0:T(8,128)(2,1)}, u32[]{:S(2)}, u32[]{:S(2)}) collective-permute-start(bf16[144,768]{1,0:T(8,128)(2,1)} %collective-permute-done.2.refs_6_), channel_id=1, source_target_pairs={{0,4},{4,0},{1,5},{5,1},{2,6},{6,2},{3,7},{7,3},{8,12},{12,8},{9,1... | collective-permute-start | bytes 663560 | tf_op jit(solution)/shard_map/ppermute | solution.py:731
  41.5 17.0 %copy-start.10 = (bf16[208,1536]{1,0:T(8,128)(2,1)}, bf16[208,1536]{1,0:T(8,128)(2,1)S(1)}, u32[]{:S(2)}) copy-start(bf16[208,1536]{1,0:T(8,128)(2,1)S(1)} %collective-permute-done.7.refs_12_) | copy-start | bytes 1916932
  41.5 11.7 %collective-permute-start.10 = (bf16[112,1536]{1,0:T(8,128)(2,1)S(1)}, bf16[112,1536]{1,0:T(8,128)(2,1)S(1)}, u32[]{:S(2)}, u32[]{:S(2)}) collective-permute-start(bf16[112,1536]{1,0:T(8,128)(2,1)S(1)} %slice.96), channel_id=1, source_target_pairs={{0,2},{2,0},{1,3},{3,1},{4,6},{6,4},{5,7},{7,5},{8,10},{10,8},{9,1... | collective-permute-start | bytes 1032200 | tf_op jit(solution)/shard_map/ppermute | solution.py:758
  44.3 8.9 %collective-permute-start.9 = (bf16[96,1536]{1,0:T(8,128)(2,1)S(1)}, bf16[96,1536]{1,0:T(8,128)(2,1)S(1)}, u32[]{:S(2)}, u32[]{:S(2)}) collective-permute-start(bf16[96,1536]{1,0:T(8,128)(2,1)S(1)} %slice.95), channel_id=1, source_target_pairs={{0,1},{1,0},{2,3},{3,2},{4,5},{5,4},{6,7},{7,6},{8,9},{9,8},{10,11... | collective-permute-start | bytes 884744 | tf_op jit(solution)/shard_map/ppermute | solution.py:757
  53.2 4.4 %collective-permute-start.5 = (bf16[144,768]{1,0:T(8,128)(2,1)}, bf16[144,768]{1,0:T(8,128)(2,1)}, u32[]{:S(2)}, u32[]{:S(2)}) collective-permute-start(bf16[144,768]{1,0:T(8,128)(2,1)} %collective-permute-done.1.refs_5_), channel_id=1, source_target_pairs={{0,4},{4,0},{1,5},{5,1},{2,6},{6,2},{3,7},{7,3},{8,12},{12,8},{9,1... | collective-permute-start | bytes 663560 | tf_op jit(solution)/shard_map/ppermute | solution.py:731
  53.4 21.9 %collective-permute-start.14 = (bf16[384,384]{1,0:T(8,128)(2,1)S(1)}, bf16[384,384]{1,0:T(8,128)(2,1)S(1)}, u32[]{:S(2)}, u32[]{:S(2)}) collective-permute-start(bf16[384,384]{1,0:T(8,128)(2,1)S(1)} %get-tuple-element.171), channel_id=1, source_target_pairs={{0,4},{4,0},{1,5},{5,1},{2,6},{6,2},{3,7},{7,3},{8,12},{12,8},{9,1... | collective-permute-start | bytes 884744 | tf_op jit(solution)/shard_map/ppermute | solution.py:864
  53.9 4.5 %collective-permute-start.4 = (bf16[144,768]{1,0:T(8,128)(2,1)}, bf16[144,768]{1,0:T(8,128)(2,1)S(1)}, u32[]{:S(2)}, u32[]{:S(2)}) collective-permute-start(bf16[144,768]{1,0:T(8,128)(2,1)} %collective-permute-done.refs_4_), channel_id=1, source_target_pairs={{0,4},{4,0},{1,5},{5,1},{2,6},{6,2},{3,7},{7,3},{8,12},{12,8},{9,1... | collective-permute-start | bytes 663560 | tf_op jit(solution)/shard_map/ppermute | solution.py:731
  54.0 20.1 %collective-permute-start.13 = (bf16[128,768]{1,0:T(8,128)(2,1)}, bf16[128,768]{1,0:T(8,128)(2,1)S(1)}, u32[]{:S(2)}, u32[]{:S(2)}) collective-permute-start(bf16[128,768]{1,0:T(8,128)(2,1)} %get-tuple-element.102), channel_id=1, source_target_pairs={{0,24},{8,16},{16,8},{24,0},{1,25},{9,17},{17,9},{25,1},{2,26},{10... | collective-permute-start | bytes 589832 | tf_op jit(solution)/shard_map/ppermute | solution.py:717
  57.6 17.6 %collective-permute-start.12 = (bf16[128,768]{1,0:T(8,128)(2,1)}, bf16[128,768]{1,0:T(8,128)(2,1)}, u32[]{:S(2)}, u32[]{:S(2)}) collective-permute-start(bf16[128,768]{1,0:T(8,128)(2,1)} %get-tuple-element.100), channel_id=1, source_target_pairs={{0,16},{8,24},{16,0},{24,8},{1,17},{9,25},{17,1},{25,9},{2,18},{10... | collective-permute-start | bytes 589832 | tf_op jit(solution)/shard_map/ppermute | solution.py:717
  57.6 17.6 %collective-permute-start.11 = (bf16[128,768]{1,0:T(8,128)(2,1)}, bf16[128,768]{1,0:T(8,128)(2,1)}, u32[]{:S(2)}, u32[]{:S(2)}) collective-permute-start(bf16[128,768]{1,0:T(8,128)(2,1)} %get-tuple-element.98), channel_id=1, source_target_pairs={{0,8},{8,0},{16,24},{24,16},{1,9},{9,1},{17,25},{25,17},{2,10},{10... | collective-permute-start | bytes 589832 | tf_op jit(solution)/shard_map/ppermute | solution.py:717
  78.3 3.5 %collective-permute-start.15 = (bf16[1024,768]{1,0:T(8,128)(2,1)S(1)}, bf16[1024,768]{1,0:T(8,128)(2,1)S(1)}, u32[]{:S(2)}, u32[]{:S(2)}) collective-permute-start(bf16[1024,768]{1,0:T(8,128)(2,1)S(1)} %convolution_convert_fusion.2.refs_1_), channel_id=1, source_target_pairs={{0,4},{4,0},{1,5},{5,1},{2,6},{6,2},{3,7},{7,3},{8,12},{12,8},{9,1... | collective-permute-start | bytes 4718600 | tf_op jit(solution)/shard_map/ppermute | solution.py:745
  81.8 15.0 %copy-start.4 = (bf16[128,768]{1,0:T(8,128)(2,1)S(1)}, bf16[128,768]{1,0:T(8,128)(2,1)}, u32[]{:S(2)}) copy-start(bf16[128,768]{1,0:T(8,128)(2,1)} %get-tuple-element.109.refs_7_) | copy-start | bytes 589828
  96.5 4.8 %collective-permute-start.16 = (bf16[1024,768]{1,0:T(8,128)(2,1)}, bf16[1024,768]{1,0:T(8,128)(2,1)S(1)}, u32[]{:S(2)}, u32[]{:S(2)}) collective-permute-start(bf16[1024,768]{1,0:T(8,128)(2,1)} %get-tuple-element.106.refs_2_), channel_id=1, source_target_pairs={{0,4},{4,0},{1,5},{5,1},{2,6},{6,2},{3,7},{7,3},{8,12},{12,8},{9,1... | collective-permute-start | bytes 4718600 | tf_op jit(solution)/shard_map/ppermute | solution.py:745
  96.8 3.7 %collective-permute-start.17 = (bf16[128,768]{1,0:T(8,128)(2,1)S(1)}, bf16[128,768]{1,0:T(8,128)(2,1)S(1)}, u32[]{:S(2)}, u32[]{:S(2)}) collective-permute-start(bf16[128,768]{1,0:T(8,128)(2,1)S(1)} %copy-done.4), channel_id=1, source_target_pairs={{0,4},{4,0},{1,5},{5,1},{2,6},{6,2},{3,7},{7,3},{8,12},{12,8},{9,1... | collective-permute-start | bytes 589832 | tf_op jit(solution)/shard_map/ppermute | solution.py:731
  97.1 3.7 %collective-permute-start.18 = (bf16[128,768]{1,0:T(8,128)(2,1)}, bf16[128,768]{1,0:T(8,128)(2,1)S(1)}, u32[]{:S(2)}, u32[]{:S(2)}) collective-permute-start(bf16[128,768]{1,0:T(8,128)(2,1)} %collective-permute-done.11.refs_8_), channel_id=1, source_target_pairs={{0,4},{4,0},{1,5},{5,1},{2,6},{6,2},{3,7},{7,3},{8,12},{12,8},{9,1... | collective-permute-start | bytes 589832 | tf_op jit(solution)/shard_map/ppermute | solution.py:731
  97.3 4.0 %collective-permute-start.19 = (bf16[128,768]{1,0:T(8,128)(2,1)}, bf16[128,768]{1,0:T(8,128)(2,1)S(1)}, u32[]{:S(2)}, u32[]{:S(2)}) collective-permute-start(bf16[128,768]{1,0:T(8,128)(2,1)} %collective-permute-done.12.refs_9_), channel_id=1, source_target_pairs={{0,4},{4,0},{1,5},{5,1},{2,6},{6,2},{3,7},{7,3},{8,12},{12,8},{9,1... | collective-permute-start | bytes 589832 | tf_op jit(solution)/shard_map/ppermute | solution.py:731
  97.6 3.7 %collective-permute-start.20 = (bf16[128,768]{1,0:T(8,128)(2,1)S(1)}, bf16[128,768]{1,0:T(8,128)(2,1)S(1)}, u32[]{:S(2)}, u32[]{:S(2)}) collective-permute-start(bf16[128,768]{1,0:T(8,128)(2,1)S(1)} %collective-permute-done.13.refs_10_), channel_id=1, source_target_pairs={{0,4},{4,0},{1,5},{5,1},{2,6},{6,2},{3,7},{7,3},{8,12},{12,8},{9,1... | collective-permute-start | bytes 589832 | tf_op jit(solution)/shard_map/ppermute | solution.py:731
  102.7 16.0 %copy-start.20 = (bf16[1024,1024]{1,0:T(8,128)(2,1)S(1)}, bf16[1024,1024]{1,0:T(8,128)(2,1)}, u32[]{:S(2)}) copy-start(bf16[1024,1024]{1,0:T(8,128)(2,1)} %get-tuple-element.123) | copy-start | bytes 6291460
  118.5 7.5 %collective-permute-start.24 = (bf16[1024,768]{1,0:T(8,128)(2,1)}, bf16[1024,768]{1,0:T(8,128)(2,1)S(1)}, u32[]{:S(2)}, u32[]{:S(2)}) collective-permute-start(bf16[1024,768]{1,0:T(8,128)(2,1)} %get-tuple-element.125.own_ref), channel_id=1, source_target_pairs={{0,4},{4,0},{1,5},{5,1},{2,6},{6,2},{3,7},{7,3},{8,12},{12,8},{9,1... | collective-permute-start | bytes 4718600 | tf_op jit(solution)/shard_map/ppermute | solution.py:745
  128.6 101.1 %reduce-scatter.5.cloned.1.call-start = ((), (), s32[]{:S(2)}) async-start(), calls=%async_computation.2 | async-start | bytes 1474560 | tf_op jit(solution)/shard_map/reduce_scatter | solution.py:944
  138.1 5.1 %collective-permute-start.25 = (bf16[384,384]{1,0:T(8,128)(2,1)S(1)}, bf16[384,384]{1,0:T(8,128)(2,1)S(1)}, u32[]{:S(2)}, u32[]{:S(2)}) collective-permute-start(bf16[384,384]{1,0:T(8,128)(2,1)S(1)} %get-tuple-element.169), channel_id=1, source_target_pairs={{0,4},{4,0},{1,5},{5,1},{2,6},{6,2},{3,7},{7,3},{8,12},{12,8},{9,1... | collective-permute-start | bytes 884744 | tf_op jit(solution)/shard_map/ppermute | solution.py:903
  138.6 20.5 %collective-permute-start.21 = (bf16[128,768]{1,0:T(8,128)(2,1)S(1)}, bf16[128,768]{1,0:T(8,128)(2,1)S(1)}, u32[]{:S(2)}, u32[]{:S(2)}) collective-permute-start(bf16[128,768]{1,0:T(8,128)(2,1)S(1)} %copy-done.25), channel_id=1, source_target_pairs={{0,8},{8,0},{16,24},{24,16},{1,9},{9,1},{17,25},{25,17},{2,10},{10... | collective-permute-start | bytes 589832 | tf_op jit(solution)/shard_map/ppermute | solution.py:717
  139.9 19.2 %collective-permute-start.22 = (bf16[128,768]{1,0:T(8,128)(2,1)S(1)}, bf16[128,768]{1,0:T(8,128)(2,1)S(1)}, u32[]{:S(2)}, u32[]{:S(2)}) collective-permute-start(bf16[128,768]{1,0:T(8,128)(2,1)S(1)} %copy-done.24), channel_id=1, source_target_pairs={{0,16},{8,24},{16,0},{24,8},{1,17},{9,25},{17,1},{25,9},{2,18},{10... | collective-permute-start | bytes 589832 | tf_op jit(solution)/shard_map/ppermute | solution.py:717
  142.3 16.8 %collective-permute-start.23 = (bf16[128,768]{1,0:T(8,128)(2,1)S(1)}, bf16[128,768]{1,0:T(8,128)(2,1)S(1)}, u32[]{:S(2)}, u32[]{:S(2)}) collective-permute-start(bf16[128,768]{1,0:T(8,128)(2,1)S(1)} %copy-done.23), channel_id=1, source_target_pairs={{0,24},{8,16},{16,8},{24,0},{1,25},{9,17},{17,9},{25,1},{2,26},{10... | collective-permute-start | bytes 589832 | tf_op jit(solution)/shard_map/ppermute | solution.py:717
  143.4 15.7 %copy-start.12 = (bf16[1024,768]{1,0:T(8,128)(2,1)S(1)}, bf16[1024,768]{1,0:T(8,128)(2,1)}, u32[]{:S(2)}) copy-start(bf16[1024,768]{1,0:T(8,128)(2,1)} %get-tuple-element.96.refs_0_) | copy-start | bytes 4718596
  163.4 21.0 %collective-permute-start.31 = (bf16[112,1536]{1,0:T(8,128)(2,1)S(1)}, bf16[112,1536]{1,0:T(8,128)(2,1)S(1)}, u32[]{:S(2)}, u32[]{:S(2)}) collective-permute-start(bf16[112,1536]{1,0:T(8,128)(2,1)S(1)} %slice_bitcast_fusion.2), channel_id=1, source_target_pairs={{0,2},{2,0},{1,3},{3,1},{4,6},{6,4},{5,7},{7,5},{8,10},{10,8},{9,1... | collective-permute-start | bytes 1032200 | tf_op jit(solution)/shard_map/ppermute | solution.py:773
  168.6 2.4 collective-permute-start.26
  168.7 15.7 %collective-permute-start.30 = (bf16[96,1536]{1,0:T(8,128)(2,1)S(1)}, bf16[96,1536]{1,0:T(8,128)(2,1)S(1)}, u32[]{:S(2)}, u32[]{:S(2)}) collective-permute-start(bf16[96,1536]{1,0:T(8,128)(2,1)S(1)} %slice_bitcast_fusion.5), channel_id=1, source_target_pairs={{0,1},{1,0},{2,3},{3,2},{4,5},{5,4},{6,7},{7,6},{8,9},{9,8},{10,11... | collective-permute-start | bytes 884744 | tf_op jit(solution)/shard_map/ppermute | solution.py:773
  171.7 12.7 %collective-permute-start.27 = (bf16[128,768]{1,0:T(8,128)(2,1)S(1)}, bf16[128,768]{1,0:T(8,128)(2,1)S(1)}, u32[]{:S(2)}, u32[]{:S(2)}) collective-permute-start(bf16[128,768]{1,0:T(8,128)(2,1)S(1)} %get-tuple-element.143), channel_id=1, source_target_pairs={{0,8},{8,0},{16,24},{24,16},{1,9},{9,1},{17,25},{25,17},{2,10},{10... | collective-permute-start | bytes 589832 | tf_op jit(solution)/shard_map/ppermute | solution.py:717
  173.4 17.1 %collective-permute-start.28 = (bf16[128,768]{1,0:T(8,128)(2,1)S(1)}, bf16[128,768]{1,0:T(8,128)(2,1)S(1)}, u32[]{:S(2)}, u32[]{:S(2)}) collective-permute-start(bf16[128,768]{1,0:T(8,128)(2,1)S(1)} %get-tuple-element.144), channel_id=1, source_target_pairs={{0,16},{8,24},{16,0},{24,8},{1,17},{9,25},{17,1},{25,9},{2,18},{10... | collective-permute-start | bytes 589832 | tf_op jit(solution)/shard_map/ppermute | solution.py:717
  175.4 15.1 %collective-permute-start.29 = (bf16[128,768]{1,0:T(8,128)(2,1)S(1)}, bf16[128,768]{1,0:T(8,128)(2,1)S(1)}, u32[]{:S(2)}, u32[]{:S(2)}) collective-permute-start(bf16[128,768]{1,0:T(8,128)(2,1)S(1)} %get-tuple-element.145), channel_id=1, source_target_pairs={{0,24},{8,16},{16,8},{24,0},{1,25},{9,17},{17,9},{25,1},{2,26},{10... | collective-permute-start | bytes 589832 | tf_op jit(solution)/shard_map/ppermute | solution.py:717
  191.8 84.6 %all-gather.7.cloned.1.call-start = ((), (), s32[]{:S(2)}) async-start(), calls=%async_computation.4 | async-start | bytes 2654208 | tf_op jit(solution)/shard_map/all_gather | solution.py:947
  191.9 16.4 %collective-permute-start.32 = (bf16[208,1536]{1,0:T(8,128)(2,1)}, bf16[208,1536]{1,0:T(8,128)(2,1)S(1)}, u32[]{:S(2)}, u32[]{:S(2)}) collective-permute-start(bf16[208,1536]{1,0:T(8,128)(2,1)} %pad_maximum_fusion.2), channel_id=1, source_target_pairs={{0,1},{1,0},{2,3},{3,2},{4,5},{5,4},{6,7},{7,6},{8,9},{9,8},{10,11... | collective-permute-start | bytes 1916936 | tf_op jit(solution)/shard_map/ppermute | solution.py:782
  193.3 15.0 %collective-permute-start.33 = (bf16[208,1536]{1,0:T(8,128)(2,1)S(1)}, bf16[208,1536]{1,0:T(8,128)(2,1)S(1)}, u32[]{:S(2)}, u32[]{:S(2)}) collective-permute-start(bf16[208,1536]{1,0:T(8,128)(2,1)S(1)} %pad_maximum_fusion.3), channel_id=1, source_target_pairs={{0,2},{2,0},{1,3},{3,1},{4,6},{6,4},{5,7},{7,5},{8,10},{10,8},{9,1... | collective-permute-start | bytes 1916936 | tf_op jit(solution)/shard_map/ppermute | solution.py:782
  209.6 17.7 %collective-permute-start.34 = (bf16[208,768]{1,0:T(8,128)(2,1)S(1)}, bf16[208,768]{1,0:T(8,128)(2,1)S(1)}, u32[]{:S(2)}, u32[]{:S(2)}) collective-permute-start(bf16[208,768]{1,0:T(8,128)(2,1)S(1)} %constant_dynamic-slice_fusion.1), channel_id=1, source_target_pairs={{0,8},{8,0},{16,24},{24,16},{1,9},{9,1},{17,25},{25,17},{2,10},{10... | collective-permute-start | bytes 958472 | tf_op jit(solution)/shard_map/ppermute | solution.py:717
  229.9 8.1 %collective-permute-start.35 = (bf16[208,384]{1,0:T(8,128)(2,1)S(1)}, bf16[208,384]{1,0:T(8,128)(2,1)S(1)}, u32[]{:S(2)}, u32[]{:S(2)}) collective-permute-start(bf16[208,384]{1,0:T(8,128)(2,1)S(1)} %constant_dynamic-slice_fusion), channel_id=1, source_target_pairs={{0,16},{8,24},{16,0},{24,8},{1,17},{9,25},{17,1},{25,9},{2,18},{10... | collective-permute-start | bytes 479240 | tf_op jit(solution)/shard_map/ppermute | solution.py:717
  238.1 18.3 %collective-permute-start.36 = (bf16[208,384]{1,0:T(8,128)(2,1)S(1)}, bf16[208,384]{1,0:T(8,128)(2,1)S(1)}, u32[]{:S(2)}, u32[]{:S(2)}) collective-permute-start(bf16[208,384]{1,0:T(8,128)(2,1)S(1)} %add_convert_fusion.1), channel_id=1, source_target_pairs={{0,16},{8,24},{16,0},{24,8},{1,17},{9,25},{17,1},{25,9},{2,18},{10... | collective-permute-start | bytes 479240 | tf_op jit(solution)/shard_map/ppermute | solution.py:717
  256.4 15.5 %copy-start.5 = (bf16[128,768]{1,0:T(8,128)(2,1)S(1)}, bf16[128,768]{1,0:T(8,128)(2,1)}, u32[]{:S(2)}) copy-start(bf16[128,768]{1,0:T(8,128)(2,1)} %get-tuple-element.113.refs_0_) | copy-start | bytes 589828
  256.5 15.1 %collective-permute-start.37 = (bf16[208,768]{1,0:T(8,128)(2,1)S(1)}, bf16[208,768]{1,0:T(8,128)(2,1)S(1)}, u32[]{:S(2)}, u32[]{:S(2)}) collective-permute-start(bf16[208,768]{1,0:T(8,128)(2,1)S(1)} %pad_maximum_fusion.7), channel_id=1, source_target_pairs={{0,8},{8,0},{16,24},{24,16},{1,9},{9,1},{17,25},{25,17},{2,10},{10... | collective-permute-start | bytes 958472 | tf_op jit(solution)/shard_map/ppermute | solution.py:717
  271.8 3.1 %collective-permute-start.38 = (bf16[208,1536]{1,0:T(8,128)(2,1)S(1)}, bf16[208,1536]{1,0:T(8,128)(2,1)S(1)}, u32[]{:S(2)}, u32[]{:S(2)}) collective-permute-start(bf16[208,1536]{1,0:T(8,128)(2,1)S(1)} %pad_maximum_fusion.4.refs_1_), channel_id=1, source_target_pairs={{0,4},{4,0},{1,5},{5,1},{2,6},{6,2},{3,7},{7,3},{8,12},{12,8},{9,1... | collective-permute-start | bytes 1916936 | tf_op jit(solution)/shard_map/ppermute | solution.py:981
  (23 other events, 90.2 us)
Sparse Core Ops, SparseCore 0:
  10.4 71.0 all-gather.4
  128.7 63.0 reduce-scatter.6
  194.1 35.5 reduce-scatter.4
  231.2 39.5 all-gather.6

commit v2 on v1

--- a/solution.py
+++ b/solution.py
@@ -192,6 +192,10 @@
     return [pltpu.with_memory_space_constraint(a, pltpu.HBM) for a in arrays]
 
 
+def vmem(*arrays):
+    return [pltpu.with_memory_space_constraint(a, pltpu.VMEM) for a in arrays]
+
+
 def whole_specs(*arrays):
     return [pl.BlockSpec(a.shape, lambda *_, n=a.ndim: (0,) * n, pipeline_mode=pl.Buffered(1))
             for a in arrays]
@@ -237,42 +241,34 @@
 
 def forward_kernel(x_ref, own_ref, got_ref, gain_ref, stack_ref, sum_ref, low_ref, hidden_ref,
                    gate_ref, silu_ref, part_ref, gu, down, sems, *, shard, part_rows):
-    step = pl.program_id(0)
+    step, block = pl.program_id(0), x_ref.shape[0]
     ff = down.shape[0]
-    chunks = ff // 256
-    copies = stack_copies(gu, down, stack_ref, sems, shard, part_rows)
-    order = [n * chunks + c for c in range(chunks) for n in range(2)]
-    order += list(range(2 * chunks, len(copies)))
-
-    def wait_for(numbers):
-        @pl.when(step == 0)
-        def _():
-            for number in numbers:
-                for copy in copies[number]:
-                    copy.wait()
 
     @pl.when(step == 0)
     def _():
-        for number in order:
-            for copy in copies[number]:
+        copies = stack_copies(gu, down, stack_ref, sems, shard, part_rows)
+        for group in copies:
+            for copy in group:
                 copy.start()
-
+        for group in copies:
+            for copy in group:
+                copy.wait()
+
+    rows = pl.ds(pl.multiple_of(step * block, block), block)
     total = x_ref[...].astype(F32) + own_ref[...].astype(F32) + got_ref[...].astype(F32)
-    sum_ref[...] = total
+    sum_ref[rows, :] = total
     middle_low = (unit_of(total)[0] * gain_ref[...]).astype(BF)
-    low_ref[...] = middle_low
-    for c in range(chunks):
-        wait_for([c, chunks + c])
-        cols = slice(c * 256, (c + 1) * 256)
+    low_ref[rows, :] = middle_low
+    for c in range(0, ff, 256):
+        cols = slice(c, c + 256)
         gate = dot(middle_low, gu[:, cols])
-        up = dot(middle_low, gu[:, ff + c * 256:ff + (c + 1) * 256])
+        up = dot(middle_low, gu[:, ff + c:ff + c + 256])
         sigmoid = jax.nn.sigmoid(gate)
         silu = gate * sigmoid
-        hidden_ref[:, cols] = (silu * up).astype(BF)
-        gate_ref[:, cols] = (up * sigmoid * (1.0 + gate * (1.0 - sigmoid))).astype(BF)
-        silu_ref[:, cols] = silu.astype(BF)
-    wait_for(range(2 * chunks, len(copies)))
-    part_ref[...] = dot(hidden_ref[...], down[...]).astype(BF)
+        hidden_ref[rows, cols] = (silu * up).astype(BF)
+        gate_ref[rows, cols] = (up * sigmoid * (1.0 + gate * (1.0 - sigmoid))).astype(BF)
+        silu_ref[rows, cols] = silu.astype(BF)
+    part_ref[...] = dot(hidden_ref[rows, :], down[...]).astype(BF)
 
 
 HBM_SPEC = pl.BlockSpec(memory_space=pltpu.HBM)
@@ -281,138 +277,136 @@
 def forward(x, own, got, gain, stack, shard, part_rows, ff, block):
     tokens, width = x.shape
     row = lambda cols: pl.BlockSpec((block, cols), lambda i: (i, 0))
-    x, stack = hbm(x, stack)
+    x, own, got, stack = hbm(x, own, got, stack)
     return pl.pallas_call(
         lambda *refs: forward_kernel(*refs, shard=shard, part_rows=part_rows),
         grid=(tokens // block,),
         in_specs=[row(width), row(width), row(width)] + whole_specs(gain) + [HBM_SPEC],
-        out_specs=[row(width), row(width), row(ff), row(ff), row(ff), row(width)],
-        out_shape=[pltpu.HBM((tokens, width), F32), pltpu.HBM((tokens, width), BF)]
-        + [pltpu.HBM((tokens, ff), BF)] * 3 + [pltpu.HBM((tokens, width), BF)],
-        scratch_shapes=[pltpu.VMEM((width, 2 * ff), BF), pltpu.VMEM((ff, width), BF),
-                        pltpu.SemaphoreType.DMA(((2 * ff + width) // 256, stack.shape[0]))],
-        compiler_params=pltpu.CompilerParams(vmem_limit_bytes=28 << 20),
+        out_specs=[VMEM_SPEC] * 5 + [row(width)] + [VMEM_SPEC] * 2,
+        out_shape=[pltpu.VMEM((tokens, width), F32), pltpu.VMEM((tokens, width), BF)]
+        + [pltpu.VMEM((tokens, ff), BF)] * 3 + [jax.ShapeDtypeStruct((tokens, width), BF)]
+        + [pltpu.VMEM((width, 2 * ff), BF), pltpu.VMEM((ff, width), BF)],
+        scratch_shapes=[pltpu.SemaphoreType.DMA(((2 * ff + width) // 256, stack.shape[0]))],
+        compiler_params=pltpu.CompilerParams(vmem_limit_bytes=16 << 20),
         cost_estimate=SMALL_COST,
         name="ffn_forward",
     )(x, own, got, gain, stack)
 
 
-def backward_kernel(where_ref, sum_ref, own_ref, got_ref, gate_ref, silu_ref, gains_ref, *refs,
-                    cot_count, shard, part_rows, groups, ranks):
-    cot_refs, stack_ref, refs = refs[:cot_count], refs[cot_count], refs[cot_count + 1:]
+def backward_kernel(where_ref, sum_ref, own_ref, got_ref, gate_ref, silu_ref, gains_ref, gu, down,
+                    *refs, cot_count, groups, ranks):
+    cot_refs, refs = refs[:cot_count], refs[cot_count:]
     out_refs, refs = refs[:groups], refs[groups:]
-    grad_ref, low_ref, gu_grad_ref, part_ref, gain_ref, gu, down, cot_ref, rows_ref, sems = refs
+    low_ref, gu_grad_ref, part_ref, gain_ref, cot_ref, rows_ref = refs
     step = pl.program_id(0)
-    copies = stack_copies(gu, down, stack_ref, sems, shard, part_rows)
-    chunks = gu.shape[1] // 256
-
-    def wait_for(numbers):
-        @pl.when(step == 0)
-        def _():
-            for number in numbers:
-                for copy in copies[number]:
-                    copy.wait()
+    block, span = rows_ref.shape[0], out_refs[0].shape[0]
 
     @pl.when(step == 0)
     def _():
-        for group in copies[chunks:] + copies[:chunks]:
-            for copy in group:
-                copy.start()
         place_tokens(cot_ref, cot_refs, where_ref, ranks)
         gain_ref[...] = jnp.zeros_like(gain_ref)
 
+    rows = pl.ds(pl.multiple_of(step * block, block), block)
     gain_two = gains_ref[1:2, :]
-    middle = unit_of(sum_ref[...])[0] * gains_ref[0:1, :]
+    middle = unit_of(sum_ref[rows, :])[0] * gains_ref[0:1, :]
     unit, factor = unit_of(middle + own_ref[...].astype(F32) + got_ref[...].astype(F32))
-    block, span = rows_ref.shape[0], out_refs[0].shape[0]
     rows_ref[...] = unit * gain_two
+    cot = cot_ref[rows, :].astype(F32)
+    gain_ref[...] += jnp.sum(cot * unit, axis=0, keepdims=True)
+    scaled = cot * gain_two
+    grad_low = (factor * (scaled - unit * jnp.mean(scaled * unit, axis=1, keepdims=True))).astype(BF)
+    low_ref[rows, :] = grad_low
+    ff = down.shape[0]
+    for c in range(0, ff, 256):
+        cols = slice(c, c + 256)
+        hidden_grad = dot(grad_low, down[cols, :], ((1,), (1,)))
+        gu_grad_ref[rows, cols] = (hidden_grad * gate_ref[rows, cols].astype(F32)).astype(BF)
+        gu_grad_ref[rows, ff + c:ff + c + 256] = (
+            hidden_grad * silu_ref[rows, cols].astype(F32)).astype(BF)
+    part_ref[...] = dot(gu_grad_ref[rows, :], gu[...], ((1,), (1,))).astype(BF)
     kept = rows_ref[pl.ds(pl.multiple_of(where_ref[2] * span, span), span), :].astype(BF)
     for k, out_ref in enumerate(out_refs):
         @pl.when(step == (where_ref[1] ^ k))
         def _(out_ref=out_ref):
             out_ref[...] = kept
-    cot = cot_ref[pl.ds(pl.multiple_of(step * block, block), block), :].astype(F32)
-    gain_ref[...] += jnp.sum(cot * unit, axis=0, keepdims=True)
-    scaled = cot * gain_two
-    grad = factor * (scaled - unit * jnp.mean(scaled * unit, axis=1, keepdims=True))
-    grad_ref[...] = grad
-    grad_low = grad.astype(BF)
-    low_ref[...] = grad_low
-    ff = down.shape[0]
-    wait_for(range(chunks, len(copies)))
-    for c in range(0, ff, 256):
-        hidden_grad = dot(grad_low, down[c:c + 256, :], ((1,), (1,)))
-        gu_grad_ref[:, c:c + 256] = (hidden_grad * gate_ref[:, c:c + 256].astype(F32)).astype(BF)
-        gu_grad_ref[:, ff + c:ff + c + 256] = (
-            hidden_grad * silu_ref[:, c:c + 256].astype(F32)).astype(BF)
-    wait_for(range(chunks))
-    part_ref[...] = dot(gu_grad_ref[...], gu[...], ((1,), (1,))).astype(BF)
-
-
-def backward(where, total, own, got, gate, silu, gains, cot, stack, shard, part_rows, block,
-             groups, ranks):
+
+
+def backward(where, total, own, got, gate, silu, gains, gu, down, cot, block, groups, ranks):
     tokens, width = total.shape
     ff = gate.shape[1]
     kernel = lambda *refs: backward_kernel(
-        *refs, cot_count=len(cot), shard=shard, part_rows=part_rows, groups=groups, ranks=ranks)
-    row = lambda cols: pl.BlockSpec((block, cols), lambda i: (i, 0))
+        *refs, cot_count=len(cot), groups=groups, ranks=ranks)
+    row = pl.BlockSpec((block, width), lambda i: (i, 0))
     slab = pl.BlockSpec((block // ranks, width), lambda i: (0, 0))
-    total, gate, silu, stack = hbm(total, gate, silu, stack)
+    total, gate, silu, gu, down = vmem(total, gate, silu, gu, down)
+    cot = hbm(*cot)
     return pl.pallas_call(
         kernel,
         grid=(tokens // block,),
-        in_specs=[SMEM_SPEC] + [row(width)] * 3 + [row(ff)] * 2
-        + whole_specs(gains, *cot) + [HBM_SPEC],
-        out_specs=[slab] * groups + [row(width), row(width), row(2 * ff), row(width),
+        in_specs=[SMEM_SPEC, VMEM_SPEC, row, row, VMEM_SPEC, VMEM_SPEC] + whole_specs(gains)
+        + [VMEM_SPEC] * 2 + whole_specs(*cot),
+        out_specs=[slab] * groups + [VMEM_SPEC, VMEM_SPEC, row,
                                      pl.BlockSpec((1, width), lambda i: (0, 0))],
         out_shape=[pltpu.HBM((block // ranks, width), BF)] * groups
-        + [pltpu.HBM((tokens, width), F32), pltpu.HBM((tokens, width), BF),
-           pltpu.HBM((tokens, 2 * ff), BF), pltpu.HBM((tokens, width), BF),
-           pltpu.HBM((1, width), F32)],
-        scratch_shapes=[pltpu.VMEM((width, 2 * ff), BF), pltpu.VMEM((ff, width), BF),
-                        pltpu.VMEM((tokens, width), BF), pltpu.VMEM((block, width), F32),
-                        pltpu.SemaphoreType.DMA(((2 * ff + width) // 256, stack.shape[0]))],
-        compiler_params=pltpu.CompilerParams(vmem_limit_bytes=32 << 20),
+        + [pltpu.VMEM((tokens, width), BF), pltpu.VMEM((tokens, 2 * ff), BF),
+           jax.ShapeDtypeStruct((tokens, width), BF), pltpu.HBM((1, width), F32)],
+        scratch_shapes=[pltpu.VMEM((tokens, width), BF), pltpu.VMEM((block, width), F32)],
+        compiler_params=pltpu.CompilerParams(vmem_limit_bytes=20 << 20),
         cost_estimate=SMALL_COST,
         name="ffn_backward",
-    )(where, total, own, got, gate, silu, gains, *cot, stack)
-
-
-def norm_back_kernel(rank_ref, sum_ref, grad_ref, own_ref, got_ref, gain_ref,
-                     low_ref, keep_ref, gain_grad_ref, rows_ref):
-    @pl.when(pl.program_id(0) == 0)
+    )(where, total, own, got, gate, silu, gains, gu, down, *cot)
+
+
+def norm_back_kernel(rank_ref, sum_ref, grad_ref, own_ref, got_ref, gain_ref, other_ref,
+                     low_ref, keep_ref, out_ref, rows_ref, gain_grad_ref):
+    step, block = pl.program_id(0), rows_ref.shape[0]
+
+    @pl.when(step == 0)
     def _():
         gain_grad_ref[...] = jnp.zeros_like(gain_grad_ref)
 
-    unit, factor = unit_of(sum_ref[...])
-    grad = grad_ref[...] + own_ref[...].astype(F32) + got_ref[...].astype(F32)
+    rows = pl.ds(pl.multiple_of(step * block, block), block)
+    unit, factor = unit_of(sum_ref[rows, :])
+    grad = (grad_ref[...].astype(F32) + own_ref[...].astype(F32)) + got_ref[...].astype(F32)
     gain_grad_ref[...] += jnp.sum(grad * unit, axis=0, keepdims=True)
     scaled = grad * gain_ref[...]
     branch_grad = factor * (scaled - unit * jnp.mean(scaled * unit, axis=1, keepdims=True))
-    low_ref[...] = branch_grad.astype(BF)
+    low_ref[rows, :] = branch_grad.astype(BF)
     rows_ref[...] = branch_grad
     span = keep_ref.shape[1]
     keep_ref[0] = rows_ref[pl.ds(pl.multiple_of(rank_ref[0] * span, span), span), :]
 
-
-def norm_back(rank, total, grad, own, got, gain, block, span):
+    @pl.when(step == pl.num_programs(0) - 1)
+    def _():
+        out_ref[...] = jnp.zeros_like(out_ref)
+        shard = gain_ref.shape[1] // out_ref.shape[0]
+        first = lax.broadcasted_iota(jnp.int32, (16, shard), 0)
+        for j in range(out_ref.shape[0]):
+            lanes = slice(j * shard, (j + 1) * shard)
+            one = jnp.broadcast_to(gain_grad_ref[:, lanes], (16, shard))
+            two = jnp.broadcast_to(other_ref[:, lanes], (16, shard))
+            out_ref[j, :, 0:shard] = jnp.where(
+                first == 0, one, jnp.where(first == 1, two, 0.0)).astype(BF)
+
+
+def norm_back(rank, total, grad, own, got, gain, other_grad, fsdp, cols, block, span):
     tokens, width = total.shape
     row = pl.BlockSpec((block, width), lambda i: (i, 0))
-    total, grad = hbm(total, grad)
+    inputs = vmem(total) + hbm(grad, own, got)
     return pl.pallas_call(
         norm_back_kernel,
         grid=(tokens // block,),
-        in_specs=[SMEM_SPEC, row, row, row, row] + whole_specs(gain),
-        out_specs=[row, pl.BlockSpec((1, span, width), lambda i: (i, 0, 0)),
-                   pl.BlockSpec((1, width), lambda i: (0, 0))],
-        out_shape=[pltpu.HBM((tokens, width), BF),
+        in_specs=[SMEM_SPEC, VMEM_SPEC, row, row, row] + whole_specs(gain, other_grad),
+        out_specs=[VMEM_SPEC, pl.BlockSpec((1, span, width), lambda i: (i, 0, 0)),
+                   pl.BlockSpec((fsdp, 16, cols), lambda i: (0, 0, 0))],
+        out_shape=[pltpu.VMEM((tokens, width), BF),
                    pltpu.HBM((tokens // block, span, width), F32),
-                   pltpu.HBM((1, width), F32)],
-        scratch_shapes=[pltpu.VMEM((block, width), F32)],
+                   pltpu.HBM((fsdp, 16, cols), BF)],
+        scratch_shapes=[pltpu.VMEM((block, width), F32), pltpu.VMEM((1, width), F32)],
         compiler_params=pltpu.CompilerParams(vmem_limit_bytes=16 << 20),
         cost_estimate=SMALL_COST,
         name="norm_back",
-    )(rank, total, grad, own, got, gain)
+    )(rank, *inputs, gain, other_grad)
 
 
 def pick(rank, parts):
@@ -587,39 +581,35 @@
     for low in range(0, tokens, block):
         rows = pl.ds(low, block)
         grad_ref[rows, :] = dot(g_ref[rows, :], w_out_ref[...], ((1,), (1,))).astype(BF)
-    for low in range(0, tokens, block):
-        begin = first_key(low, block, window)
-        end = low + block
+    small = block // 2
+    for low in range(0, tokens, small):
+        begin = first_key(low, small, window)
+        end = low + small
         count = end - begin
         q = q_ref[low:end, :] * jnp.asarray(scale, BF)
         grad = grad_ref[low:end, :]
         product = (grad.astype(F32) * att_ref[low:end, :].astype(F32)).T
+        zero = jnp.zeros_like(q)
+        q_two = jnp.concatenate([jnp.where(first, q, zero), jnp.where(first, zero, q)], axis=0)
+        grad_two = jnp.concatenate(
+            [jnp.where(first, grad, zero), jnp.where(first, zero, grad)], axis=0)
         k = k_ref[begin:end, :]
-        v = v_ref[begin:end, :]
-        zero = jnp.zeros_like(k)
-        k_two = jnp.concatenate([jnp.where(first, k, zero), jnp.where(first, zero, k)], axis=0)
-        v_two = jnp.concatenate([jnp.where(first, v, zero), jnp.where(first, zero, v)], axis=0)
-        scores = dot(k_two, q, ((1,), (1,)))
-        prob_grad = dot(v_two, grad, ((1,), (1,)))
-        key_index = lax.broadcasted_iota(jnp.int32, (count, block), 0) + begin
-        query_index = lax.broadcasted_iota(jnp.int32, (count, block), 1) + low
+        scores = dot(k, q_two, ((1,), (1,)))
+        prob_grad = dot(v_ref[begin:end, :], grad_two, ((1,), (1,)))
+        key_index = lax.broadcasted_iota(jnp.int32, (count, small), 0) + begin
+        query_index = lax.broadcasted_iota(jnp.int32, (count, small), 1) + low
         visible = (key_index.astype(F32) >= starts[:, low:end]) & (key_index <= query_index)
-        weights_low, score_low = [], []
-        for head in range(2):
-            part = slice(head * count, (head + 1) * count)
-            weights = jnp.where(
-                visible, jnp.exp(scores[part] - lse_ref[0, head:head + 1, low:end]), 0.0)
-            row_dots = jnp.sum(
-                product[head * head_size:(head + 1) * head_size], axis=0, keepdims=True)
-            weights_low.append(weights.astype(BF))
-            score_low.append((weights * (prob_grad[part] - row_dots)).astype(BF))
-        weights_low = jnp.concatenate(weights_low, axis=0)
-        score_low = jnp.concatenate(score_low, axis=0)
-        v_part = dot(weights_low, grad)
-        k_part = dot(score_low, q)
-        v_sum[begin:end, :] += jnp.where(first, v_part[:count], v_part[count:])
-        k_sum[begin:end, :] += jnp.where(first, k_part[:count], k_part[count:])
-        dq = dot(score_low, k_two, ((0,), (0,))) * scale
+        visible = jnp.concatenate([visible, visible], axis=1)
+        lse = jnp.concatenate([lse_ref[0, h:h + 1, low:end] for h in range(2)], axis=1)
+        row_dots = jnp.concatenate(
+            [jnp.sum(product[h * head_size:(h + 1) * head_size], axis=0, keepdims=True)
+             for h in range(2)], axis=1)
+        weights = jnp.where(visible, jnp.exp(scores - lse), 0.0)
+        score_low = (weights * (prob_grad - row_dots)).astype(BF)
+        v_sum[begin:end, :] += dot(weights.astype(BF), grad_two)
+        k_sum[begin:end, :] += dot(score_low, q_two)
+        dq = dot(score_low, k, ((0,), (0,))) * scale
+        dq = jnp.where(first, dq[:small], dq[small:])
         d_ref[low:end, :lanes] = (
             dq * cos_ref[low:end, :] - turn(dq, half) * sin_ref[low:end, :]).astype(BF)
     for low in range(0, tokens, block):
@@ -636,17 +626,18 @@
     kernel = lambda *refs: attend_back_kernel(
         *refs, block=256, window=window, scale=1.0 / math.sqrt(head_size), head_size=head_size)
     column = pl.BlockSpec((tokens, lanes), lambda p: (0, p))
-    inputs = hbm(seg, g, w_out, q, k, v, att, lse, cosine, sine)
+    inputs = hbm(seg) + vmem(g) + hbm(w_out, q, k, v, att, lse, cosine, sine)
     return pl.pallas_call(
         kernel,
         grid=(pairs,),
-        in_specs=whole_specs(seg, g) + [
+        in_specs=whole_specs(seg) + [
+            VMEM_SPEC,
             pl.BlockSpec((lanes, width), lambda p: (p, 0)),
             column, column, column, column,
             pl.BlockSpec((1, 8, tokens), lambda p: (p, 0, 0)),
         ] + whole_specs(cosine, sine),
         out_specs=pl.BlockSpec((tokens, 3 * lanes), lambda p: (0, p)),
-        out_shape=pltpu.HBM((tokens, 3 * lanes * pairs), BF),
+        out_shape=jax.ShapeDtypeStruct((tokens, 3 * lanes * pairs), BF),
         scratch_shapes=[
             pltpu.VMEM((tokens, lanes), BF),
             pltpu.VMEM((tokens, lanes), F32),
@@ -696,10 +687,12 @@
 
 def join_all(parts, moves, shapes):
     groups, ranks, rows, cols = parts.shape
+    parts, = hbm(parts)
     return pl.pallas_call(
         lambda *refs: join_all_kernel(*refs, moves=moves),
-        in_specs=[VMEM_SPEC],
-        out_specs=[VMEM_SPEC] * len(shapes),
+        grid=(1,),
+        in_specs=whole_specs(parts),
+        out_specs=[pl.BlockSpec(shape, lambda i: (0, 0)) for shape in shapes],
         out_shape=[jax.ShapeDtypeStruct(shape, F32) for shape in shapes],
         scratch_shapes=[pltpu.VMEM((ranks, groups * rows, cols), BF)],
         compiler_params=pltpu.CompilerParams(vmem_limit_bytes=32 << 20),
@@ -858,6 +851,7 @@
             out_cols = whole[:, :shard, 3 * lanes_all:].reshape(width, own_cols)
             qkv_refs = [whole[:, :shard, :3 * lanes_all].reshape(width, 3 * lanes_all)]
         gains = gains.astype(F32)
+        gain_one = gains[0:1]
         if ranks == 2:
             give = lax.dynamic_slice_in_dim(out_cols, (1 - rank) * own_cols, own_cols, 0)
             keep = lax.dynamic_slice_in_dim(out_cols, rank * own_cols, own_cols, 0)
@@ -871,7 +865,7 @@
         w_out_even = jnp.pad(w_out_own, ((0, spare), (0, 0)))
 
         q, k, v, att, lse, w_qkv, x, seg = attend(
-            where, cosine, sine, token_refs, ranks, qkv_refs, small_pieces, shard, lanes_all,
+            where, after(cosine, gains, gain_one), sine, token_refs, ranks, qkv_refs, small_pieces, shard, lanes_all,
             window, head_size, width)
         if square:
             cot_slabs, att = between(cot_slabs, att)
@@ -879,13 +873,12 @@
         cot_refs = both_ranks(where, cot_slabs, span)
         if ranks != 2:
             cot_refs = cot_refs[:1]
-        total, middle_low, hidden_low, gate_back, silu, part = forward(
-            x, own, got, gains[0:1], stack_all, shard, part_rows, half_ff, block)
+        total, middle_low, hidden_low, gate_back, silu, part, gu, down = forward(
+            x, own, got, gain_one, stack_all, shard, part_rows, half_ff, block)
         own, got = exchange(part)
 
-        *out_slabs, ffn_grad, ffn_grad_low, gu_grad_low, part, gain_ffn_grad = backward(
-            where, total, own, got, gate_back, silu, gains, cot_refs, stack_all, shard, part_rows,
-            block, groups, ranks)
+        *out_slabs, ffn_grad_low, gu_grad_low, part, gain_ffn_grad = backward(
+            where, total, own, got, gate_back, silu, gains, gu, down, cot_refs, block, groups, ranks)
         own, got = exchange(part)
         gu_w_grad = dot(middle_low, gu_grad_low, ((0,), (0,))).astype(BF)
         if ranks == 2:
@@ -894,8 +887,9 @@
         stack_grad = arrange(gu_w_grad, down_w_grad, fsdp)
         stack_owned = lax.psum_scatter(stack_grad, F, scatter_dimension=0, tiled=False)
         own = after(own, stack_grad)
-        branch_grad_low, branch_keep, gain_attn_grad = norm_back(
-            where[2:], total, ffn_grad, own, got, gains[0:1], block, span)
+        branch_grad_low, branch_keep, gain_grads = norm_back(
+            where[2:], total, ffn_grad_low, own, got, gain_one, gain_ffn_grad,
+            fsdp, small_cols, block, span)
         out_w_grad = dot(att, branch_grad_low, ((0,), (0,)))[:own_cols].astype(BF)
         if ranks == 2:
             give = lax.dynamic_slice_in_dim(out_w_grad, (1 - rank) * own_cols, own_cols, 1)
@@ -906,10 +900,7 @@
         else:
             rows = out_w_grad.reshape(own_cols, ranks, own_cols).transpose(1, 0, 2)
             out_cols_grad = lax.all_to_all(rows, "r", 0, 0, tiled=True).reshape(width, own_cols)
-        gain_grads = jnp.concatenate([gain_attn_grad, gain_ffn_grad], axis=0).astype(BF)
-        gain_grads = gain_grads.reshape(2, fsdp, shard).transpose(1, 0, 2)
-        gain_grads = jnp.pad(gain_grads, ((0, 0), (0, 14), (0, small_cols - shard)))
-        branch_grad_low = after(branch_grad_low, out_cols_grad, gain_grads)
+        branch_grad_low = after(branch_grad_low, out_cols_grad)
         d_qkv = attend_back(
             seg, branch_grad_low, w_out_even, q, k, v, att, lse, cosine, sine, window, head_size)
         if square:
@@ -933,17 +924,17 @@
             part = lax.psum(part, "r")
             got = jnp.zeros_like(branch_keep, BF)
         grad_slabs = list(finish(where, branch_keep, part, got, ranks))
+        grad_slabs = spread(grad_slabs)
         if pairs:
-            grad_slabs, small_one = between(spread(grad_slabs), small_one)
-        else:
-            grad_slabs = spread(grad_slabs)
-        if pairs:
+            grad_slabs[:3], small_one = between(grad_slabs[:3], small_one)
             terms = second_terms(small_grad, *small_one)
-            small_two = round_two(*terms)
+            small_two, output, grad_slabs[3] = lax.optimization_barrier(
+                (round_two(*terms), output, grad_slabs[3]))
+            input_grad = stack(where, grad_slabs)
             stack_owned = after(stack_owned, *terms)
             quarter = lax.psum_scatter(stack_owned, "m", scatter_dimension=0, tiled=True)
             give, keep = halve(add(take(small_grad, 0), *small_two), 1, 1)
-            got, quarter = lax.optimization_barrier((hop(give, 1), quarter))
+            got, quarter, input_grad = lax.optimization_barrier((hop(give, 1), quarter, input_grad))
             stack_parts = lax.all_gather(quarter, ("m", "r"), axis=0)
             stack_parts = stack_parts.reshape((groups, ranks) + quarter.shape)
             give, keep = halve(add(keep, got), 2, 1)
@@ -953,7 +944,7 @@
         else:
             stack_sum = lax.psum(stack_owned, "m")
             small_sum = reduce(small_grad)
-        input_grad = stack(where, grad_slabs)
+            input_grad = stack(where, grad_slabs)
         if pairs:
             everything = slice(None)
             chunks = 2 * half_ff // 256

time: 288 us -> 274 us (0.951)
  Pallas kernels: 83.2 us -> 75.6 us
  matrix products: 17.7 us -> 13.4 us
  local copies, waits for them, and re-layouts: 11.8 us -> 8.7 us
    ppermute x2, waiting for transfers between devices: 14.1 us -> 6.23 us  [round_two(): return (lax.ppermute(to_x, 'x', swap), lax.ppermute(to_y, 'y', swap))]
    unnamed x5, waiting for transfers between devices: 0.25 us -> 5.54 us
    dot_general x6, matrix products: 17.7 us -> 13.4 us  [dot(): lax.dot_general(left, right, (dims, ((), ())), preferred_element_type=F32)]
    ppermute x16, starting transfers between devices: 23.3 us -> 27.2 us  [hop(): return lax.ppermute(value, 'm', [(i, i ^ k) for i in range(groups)])]
    pallas_call x3, Pallas kernels: 33.8 us -> 30.1 us  [the longest x1 13.7 us: attend_back(): pl.pallas_call(kernel, grid=(pairs,), in_specs=whole_specs(seg) + [VMEM_S...]
    ppermute x1, waiting for transfers between devices: 8.18 us -> 4.56 us  [round_one(): lax.ppermute(far[:rows], 'x', swap)]
    pallas_call x1, Pallas kernels: 14.7 us -> 11.2 us  [forward(): pl.pallas_call(lambda *refs: forward_kernel(*refs, shard=shard, part_rows...]
    ppermute x3, waiting for transfers between devices: 0.27 us -> 3.53 us  [exchange(): return (part, lax.ppermute(part, 'r', swap))]
  transfers between devices with their start and end apart: 43 -> 43, of which waited for: 20 -> 24; matrix products, arithmetic and copies ran while one was open for 11% -> 9% of each run, Pallas kernels for 16% -> 16%
where the time goes in v2:
time: 274 us; the launch traced here: 273 us
  waiting for transfers between devices  111 us (41%)
  Pallas kernels  75.6 us (28%)
  starting transfers between devices  41.3 us (15%)
  between operations  14.6 us (5%)
  matrix products  13.4 us (5%)
  local copies, waits for them, and re-layouts  8.7 us (3%)
  other arithmetic  8.05 us (3%)
    ppermute x16, waiting for transfers between devices, hop(): return lax.ppermute(value, 'm', [(i, i ^ k) for i in range(groups)])  75.2 us
    ppermute x16, starting transfers between devices, hop(): return lax.ppermute(value, 'm', [(i, i ^ k) for i in range(groups)])  27.2 us
    pallas_call x1, Pallas kernels, attend(): pl.pallas_call(kernel, grid=(pairs,), in_specs=[SMEM_SPEC] + whole_specs(...  15 us
    pallas_call x1, Pallas kernels, attend_back(): pl.pallas_call(kernel, grid=(pairs,), in_specs=whole_specs(seg) + [VMEM_S...  13.7 us
    dot_general x6, matrix products, dot(): lax.dot_general(left, right, (dims, ((), ())), preferred_element_type=F32)  13.4 us
    pallas_call x1, Pallas kernels, backward(): pl.pallas_call(kernel, grid=(tokens // block,), in_specs=[SMEM_SPEC, VMEM...  12.4 us
    pallas_call x1, Pallas kernels, forward(): pl.pallas_call(lambda *refs: forward_kernel(*refs, shard=shard, part_rows...  11.2 us
    ppermute x1, waiting for transfers between devices, gather_rows(): far_b = lax.ppermute(from_x[rows:], 'y', swap)  7.7 us
  transfers between devices with their start and end apart: 43, of which 24 were waited for; matrix products, arithmetic and copies ran while one was open for 9% of the time, Pallas kernels for 16%

profile of v2, /device:TPU:0, one launch (start us, length us, event | category | flops | bytes accessed | tf_op | source)
XLA Modules:
  0.0 273.0 jit_solution(3437350966800511470)
XLA Ops:
  7.3 2.8 %pack.1 = bf16[2304,256]{1,0:T(8,128)(2,1)} custom-call(s32[3]{0:T(128)S(1)} %pad_add_fusion.refs_0_.where_ref, bf16[192,2048]{1,0:T(8,128)(2,1)} %refs_1_.2, bf16[192,2048]{1,0:T(8,128)(2,1)} %refs_2_.2, bf16[512,768]{1,0:T(8,128)(2,1)} %refs_3_.2), custom_call_target="tpu_custom_call" | custom-call | flops 1 | bytes 1 | tf_op jit(solution)/shard_map/pack/pallas_call | solution.py:490
  10.8 3.4 %pack_small.1 = (bf16[208,1536]{1,0:T(8,128)(2,1)}, bf16[144,768]{1,0:T(8,128)(2,1)}, bf16[144,768]{1,0:T(8,128)(2,1)}, bf16[144,768]{1,0:T(8,128)(2,1)}, bf16[1...) custom-call(s32[3]{0:T(128)S(1)} %pad_add_fusion.refs_0_.where_ref, ...), custom_call_target="tpu_custom_call" | custom-call | flops 1 | bytes 1 | tf_op jit(solution)/shard_map/pack_small/pallas_call | solution.py:454
  14.2 3.0 %collective-permute-start = (bf16[208,1536]{1,0:T(8,128)(2,1)}, bf16[208,1536]{1,0:T(8,128)(2,1)S(1)}, u32[]{:S(2)}, u32[]{:S(2)}) collective-permute-start(bf16[208,1536]{1,0:T(8,128)(2,1)} %get-tuple-element.94.refs_11_), channel_id=1, source_target_pairs={{0,1},{1,0},{2,3},{3,2},{4,5},{5,4},{6,7},{7,6},{8,9},{9,8},{10,11... | collective-permute-start | bytes 1916936 | tf_op jit(solution)/shard_map/ppermute | solution.py:748
  17.2 1.5 collective-permute-start.1
  18.7 3.6 %collective-permute-start.5 = (bf16[144,768]{1,0:T(8,128)(2,1)}, bf16[144,768]{1,0:T(8,128)(2,1)}, u32[]{:S(2)}, u32[]{:S(2)}) collective-permute-start(bf16[144,768]{1,0:T(8,128)(2,1)} %get-tuple-element.101), channel_id=1, source_target_pairs={{0,24},{8,16},{16,8},{24,0},{1,25},{9,17},{17,9},{25,1},{2,26},{10... | collective-permute-start | bytes 663560 | tf_op jit(solution)/shard_map/ppermute | solution.py:710
  23.1 1.9 fusion.9
  25.1 1.8 pad_maximum_fusion.5
  29.3 11.6 %collective-permute-done.4.refs_5_ = bf16[144,768]{1,0:T(8,128)(2,1)} collective-permute-done((bf16[144,768]{1,0:T(8,128)(2,1)}, bf16[144,768]{1,0:T(8,128)(2,1)}, u32[]{:S(2)}, u32[]{:S(2)}) %collective-permute-start.4) | collective-permute-done | bytes 221216 | tf_op jit(solution)/shard_map/ppermute | solution.py:710
  41.6 1.4 collective-permute-start.2
  43.0 1.4 collective-permute-done.1.refs_13_
  45.5 7.7 %collective-permute-done.2.refs_15_ = bf16[112,1536]{1,0:T(8,128)(2,1)S(1)} collective-permute-done((bf16[112,1536]{1,0:T(8,128)(2,1)S(1)}, bf16[112,1536]{1,0:T(8,128)(2,1)S(1)}, u32[]{:S(2)}, u32[]{:S(2)}) %collective-permute-start.2) | collective-permute-done | bytes 344096 | tf_op jit(solution)/shard_map/ppermute | solution.py:751
  54.2 3.7 %collective-permute-start.13 = (bf16[128,768]{1,0:T(8,128)(2,1)}, bf16[128,768]{1,0:T(8,128)(2,1)S(1)}, u32[]{:S(2)}, u32[]{:S(2)}) collective-permute-start(bf16[128,768]{1,0:T(8,128)(2,1)} %get-tuple-element.109), channel_id=1, source_target_pairs={{0,24},{8,16},{16,8},{24,0},{1,25},{9,17},{17,9},{25,1},{2,26},{10... | collective-permute-start | bytes 589832 | tf_op jit(solution)/shard_map/ppermute | solution.py:710
  58.9 15.0 %attend.1 = (bf16[1024,384]{1,0:T(8,128)(2,1)}, bf16[1024,384]{1,0:T(8,128)(2,1)}, bf16[1024,384]{1,0:T(8,128)(2,1)}, bf16[1024,384]{1,0:T(8,128)(2,1)}, f32[3,8...) custom-call(s32[3]{0:T(128)S(1)} %pad_add_fusion.refs_0_.where_ref, ...), custom_call_target="tpu_custom_call" | custom-call | flops 1 | bytes 1 | tf_op jit(solution)/shard_map/attend/pallas_call | solution.py:220
  75.9 2.3 convolution_convert_fusion.2.refs_1_
  78.3 3.5 %collective-permute-done.15.refs_2_ = bf16[1024,768]{1,0:T(8,128)(2,1)} collective-permute-done((bf16[1024,768]{1,0:T(8,128)(2,1)S(1)}, bf16[1024,768]{1,0:T(8,128)(2,1)}, u32[]{:S(2)}, u32[]{:S(2)}) %collective-permute-start.15) | collective-permute-done | bytes 1572896 | tf_op jit(solution)/shard_map/ppermute | solution.py:738
  81.8 11.2 %ffn_forward.1 = (f32[1024,768]{1,0:T(8,128)S(1)}, bf16[1024,768]{1,0:T(8,128)(2,1)S(1)}, bf16[1024,1024]{1,0:T(8,128)(2,1)S(1)}, bf16[1024,1024]{1,0:T(8,128)(2...) custom-call(bf16[1024,768]{1,0:T(8,128)(2,1)} %get-tuple-element.103, ...), custom_call_target="tpu_custom_call" | custom-call | flops 1 | bytes 1 | tf_op jit(solution)/shard_map/ffn_forward/pallas_call | solution.py:281
  94.3 2.5 collective-permute-done.17.refs_13_
  98.4 12.4 %ffn_backward.1 = (bf16[128,768]{1,0:T(8,128)(2,1)}, bf16[128,768]{1,0:T(8,128)(2,1)}, bf16[128,768]{1,0:T(8,128)(2,1)}, bf16[128,768]{1,0:T(8,128)(2,1)}, bf16[...) custom-call(s32[3]{0:T(128)S(1)} %pad_add_fusion.refs_0_.where_ref, ...), custom_call_target="tpu_custom_call" | custom-call | flops 1 | bytes 1 | tf_op jit(solution)/shard_map/ffn_backward/pallas_call | solution.py:343
  111.0 1.9 convolution_convert_fusion.4.down_ref
  112.9 3.9 %convolution_convert_fusion.1.gu_ref = bf16[768,2048]{1,0:T(8,128)(2,1)S(1)} fusion(bf16[1024,768]{1,0:T(8,128)(2,1)S(1)} %get-tuple-element.128, bf16[1024,2048]{1,0:T(8,128)(2,1)S(1)} %get-tuple-element.129), kind=kOutput, calls=%fused_computation.6 | convolution fusion | flops 3222798336 | bytes 8912896 | tf_op jit(solution)/shard_map/dot_general | solution.py:19
  117.9 2.6 arrange.1
  121.2 5.3 %norm_back.1 = (bf16[1024,768]{1,0:T(8,128)(2,1)S(1)}, f32[4,128,768]{2,1,0:T(8,128)}, bf16[4,16,1536]{2,1,0:T(8,128)(2,1)}) custom-call(s32[1]{0:T(128)} %bitcast.2.rank_ref.refs_0_, f32[1024,768]{1,0:T(8,128)S(1)} %get-tuple-element.112.refs_1_.sum_ref, bf16[1024,768]{1,0:T(8,128)(2,1)} %copy-done.3, bf16[1024,768]{1,0:T(8,128)(2,1)} %copy-done.4, ...), custom_call_target="tpu_custom_call" | custom-call | flops 1 | bytes 1 | tf_op jit(solution)/shard_map/norm_back/pallas_call | solution.py:396
  129.2 2.4 collective-permute-start.22
  132.6 1.4 copy-done.1
  134.1 13.7 %attend_back.1 = bf16[1024,1152]{1,0:T(8,128)(2,1)S(1)} custom-call(f32[1,1024]{1,0:T(1,128)} %get-tuple-element.125.refs_0_, bf16[1024,768]{1,0:T(8,128)(2,1)S(1)} %copy-done.1, bf16[384,768]{1,0:T(8,128)(2,1)} %copy-done.9, bf16[1024,384]{1,0:T(8,128)(2,1)} %get-tuple-element.137.refs_3_, bf16[1024,384]{1,0:T(8,128)(2,1)} %get-tuple-element.138.refs_4_, ...), custom_call_target="tpu_custom_call" | custom-call | flops 1 | bytes 1 | tf_op jit(solution)/shard_map/attend_back/pallas_call | solution.py:630
  147.8 2.2 convolution_convert_fusion
  151.7 1.6 collective-permute-start.30
  153.3 2.2 convolution_convert_fusion.3.refs_2_
  156.3 1.7 collective-permute-done.26.refs_3_
  158.8 2.2 collective-permute-start.27
  162.4 4.6 %collective-permute-done.29 = bf16[96,1536]{1,0:T(8,128)(2,1)S(1)} collective-permute-done((bf16[96,1536]{1,0:T(8,128)(2,1)S(1)}, bf16[96,1536]{1,0:T(8,128)(2,1)S(1)}, u32[]{:S(2)}, u32[]{:S(2)}) %collective-permute-start.29) | collective-permute-done | bytes 294944 | tf_op jit(solution)/shard_map/ppermute | solution.py:766
  166.9 3.3 %collective-permute-done.27.refs_1_ = bf16[128,768]{1,0:T(8,128)(2,1)S(1)} collective-permute-done((bf16[128,768]{1,0:T(8,128)(2,1)S(1)}, bf16[128,768]{1,0:T(8,128)(2,1)S(1)}, u32[]{:S(2)}, u32[]{:S(2)}) %collective-permute-start.27) | collective-permute-done | bytes 196640 | tf_op jit(solution)/shard_map/ppermute | solution.py:710
  170.2 2.6 collective-permute-done.28.refs_2_
  173.9 5.5 %reduce-scatter.7.cloned.1.call-done = bf16[1,2304,256]{2,1,0:T(8,128)(2,1)} async-done(((bf16[4,2304,256]{2,1,0:T(8,128)(2,1)}), bf16[1,2304,256]{2,1,0:T(8,128)(2,1)}) %reduce-scatter.7.cloned.1.call-update) | async-done | bytes 1179664
  181.2 3.3 %collective-permute-start.33 = (bf16[128,768]{1,0:T(8,128)(2,1)S(1)}, bf16[128,768]{1,0:T(8,128)(2,1)S(1)}, u32[]{:S(2)}, u32[]{:S(2)}) collective-permute-start(bf16[128,768]{1,0:T(8,128)(2,1)S(1)} %get-tuple-element.154), channel_id=1, source_target_pairs={{0,24},{8,16},{16,8},{24,0},{1,25},{9,17},{17,9},{25,1},{2,26},{10... | collective-permute-start | bytes 589832 | tf_op jit(solution)/shard_map/ppermute | solution.py:710
  184.5 1.5 stack.30
  186.0 4.5 %collective-permute-done.33.refs_3_ = bf16[128,768]{1,0:T(8,128)(2,1)S(1)} collective-permute-done((bf16[128,768]{1,0:T(8,128)(2,1)S(1)}, bf16[128,768]{1,0:T(8,128)(2,1)S(1)}, u32[]{:S(2)}, u32[]{:S(2)}) %collective-permute-start.33) | collective-permute-done | bytes 196640 | tf_op jit(solution)/shard_map/ppermute | solution.py:710
  190.4 5.4 %collective-permute-done.32 = bf16[208,1536]{1,0:T(8,128)(2,1)S(1)} collective-permute-done((bf16[208,1536]{1,0:T(8,128)(2,1)S(1)}, bf16[208,1536]{1,0:T(8,128)(2,1)S(1)}, u32[]{:S(2)}, u32[]{:S(2)}) %collective-permute-start.32) | collective-permute-done | bytes 639008 | tf_op jit(solution)/shard_map/ppermute | solution.py:775
  196.7 1.5 fusion.1
  198.2 6.9 %collective-permute-start.34 = (bf16[208,768]{1,0:T(8,128)(2,1)S(1)}, bf16[208,768]{1,0:T(8,128)(2,1)S(1)}, u32[]{:S(2)}, u32[]{:S(2)}) collective-permute-start(bf16[208,768]{1,0:T(8,128)(2,1)S(1)} %constant_dynamic-slice_fusion.1), channel_id=1, source_target_pairs={{0,8},{8,0},{16,24},{24,16},{1,9},{9,1},{17,25},{25,17},{2,10},{10... | collective-permute-start | bytes 958472 | tf_op jit(solution)/shard_map/ppermute | solution.py:710
  205.1 1.5 stack.31
  206.6 11.2 %collective-permute-done.34 = bf16[208,768]{1,0:T(8,128)(2,1)S(1)} collective-permute-done((bf16[208,768]{1,0:T(8,128)(2,1)S(1)}, bf16[208,768]{1,0:T(8,128)(2,1)S(1)}, u32[]{:S(2)}, u32[]{:S(2)}) %collective-permute-start.34) | collective-permute-done | bytes 319520 | tf_op jit(solution)/shard_map/ppermute | solution.py:710
  218.1 9.1 %collective-permute-done.35 = bf16[208,384]{1,0:T(8,128)(2,1)S(1)} collective-permute-done((bf16[208,384]{1,0:T(8,128)(2,1)S(1)}, bf16[208,384]{1,0:T(8,128)(2,1)S(1)}, u32[]{:S(2)}, u32[]{:S(2)}) %collective-permute-start.35) | collective-permute-done | bytes 159776 | tf_op jit(solution)/shard_map/ppermute | solution.py:710
  227.3 19.2 %collective-permute-done.36 = bf16[208,384]{1,0:T(8,128)(2,1)S(1)} collective-permute-done((bf16[208,384]{1,0:T(8,128)(2,1)S(1)}, bf16[208,384]{1,0:T(8,128)(2,1)S(1)}, u32[]{:S(2)}, u32[]{:S(2)}) %collective-permute-start.36) | collective-permute-done | bytes 159776 | tf_op jit(solution)/shard_map/ppermute | solution.py:710
  246.7 12.0 %collective-permute-done.37 = bf16[208,768]{1,0:T(8,128)(2,1)S(1)} collective-permute-done((bf16[208,768]{1,0:T(8,128)(2,1)S(1)}, bf16[208,768]{1,0:T(8,128)(2,1)S(1)}, u32[]{:S(2)}, u32[]{:S(2)}) %collective-permute-start.37) | collective-permute-done | bytes 319520 | tf_op jit(solution)/shard_map/ppermute | solution.py:710
  258.9 2.1 collective-permute-done.38.refs_2_
  261.0 1.5 join.1
  262.5 4.0 %join_all.1 = (f32[192,2048]{1,0:T(8,128)}, f32[192,2048]{1,0:T(8,128)}, f32[512,768]{1,0:T(8,128)}) custom-call(bf16[4,2,576,256]{3,2,1,0:T(8,128)(2,1)} %bitcast.69), custom_call_target="tpu_custom_call" | custom-call | flops 1 | bytes 1 | tf_op jit(solution)/shard_map/join_all/pallas_call | solution.py:691
  (183 shorter events, 27.0 us)
Async XLA Ops:
  7.2 74.6 %all-gather.5.cloned.1.call-start = ((), (), s32[]{:S(2)}) async-start(), calls=%async_computation.3 | async-start | bytes 5898240 | tf_op jit(solution)/shard_map/all_gather | solution.py:814
  10.1 169.3 %reduce-scatter.7.cloned.1.call-start = ((), (), s32[]{:S(2)}) async-start(), calls=%async_computation.5 | async-start | bytes 5898240
  14.2 27.3 %collective-permute-start = (bf16[208,1536]{1,0:T(8,128)(2,1)}, bf16[208,1536]{1,0:T(8,128)(2,1)S(1)}, u32[]{:S(2)}, u32[]{:S(2)}) collective-permute-start(bf16[208,1536]{1,0:T(8,128)(2,1)} %get-tuple-element.94.refs_11_), channel_id=1, source_target_pairs={{0,1},{1,0},{2,3},{3,2},{4,5},{5,4},{6,7},{7,6},{8,9},{9,8},{10,11... | collective-permute-start | bytes 1916936 | tf_op jit(solution)/shard_map/ppermute | solution.py:748
  17.2 27.2 %collective-permute-start.1 = (bf16[208,1536]{1,0:T(8,128)(2,1)}, bf16[208,1536]{1,0:T(8,128)(2,1)S(1)}, u32[]{:S(2)}, u32[]{:S(2)}) collective-permute-start(bf16[208,1536]{1,0:T(8,128)(2,1)} %get-tuple-element.94.refs_11_), channel_id=1, source_target_pairs={{0,2},{2,0},{1,3},{3,1},{4,6},{6,4},{5,7},{7,5},{8,10},{10,8},{9,1... | collective-permute-start | bytes 1916936 | tf_op jit(solution)/shard_map/ppermute | solution.py:749
  18.7 10.6 %collective-permute-start.5 = (bf16[144,768]{1,0:T(8,128)(2,1)}, bf16[144,768]{1,0:T(8,128)(2,1)}, u32[]{:S(2)}, u32[]{:S(2)}) collective-permute-start(bf16[144,768]{1,0:T(8,128)(2,1)} %get-tuple-element.101), channel_id=1, source_target_pairs={{0,24},{8,16},{16,8},{24,0},{1,25},{9,17},{17,9},{25,1},{2,26},{10... | collective-permute-start | bytes 663560 | tf_op jit(solution)/shard_map/ppermute | solution.py:710
  22.3 18.6 %collective-permute-start.4 = (bf16[144,768]{1,0:T(8,128)(2,1)}, bf16[144,768]{1,0:T(8,128)(2,1)}, u32[]{:S(2)}, u32[]{:S(2)}) collective-permute-start(bf16[144,768]{1,0:T(8,128)(2,1)} %get-tuple-element.99), channel_id=1, source_target_pairs={{0,16},{8,24},{16,0},{24,8},{1,17},{9,25},{17,1},{25,9},{2,18},{10... | collective-permute-start | bytes 663560 | tf_op jit(solution)/shard_map/ppermute | solution.py:710
  22.3 18.6 %collective-permute-start.3 = (bf16[144,768]{1,0:T(8,128)(2,1)}, bf16[144,768]{1,0:T(8,128)(2,1)}, u32[]{:S(2)}, u32[]{:S(2)}) collective-permute-start(bf16[144,768]{1,0:T(8,128)(2,1)} %get-tuple-element.97), channel_id=1, source_target_pairs={{0,8},{8,0},{16,24},{24,16},{1,9},{9,1},{17,25},{25,17},{2,10},{10... | collective-permute-start | bytes 663560 | tf_op jit(solution)/shard_map/ppermute | solution.py:710
  29.3 25.0 %collective-permute-start.6 = (bf16[144,768]{1,0:T(8,128)(2,1)S(1)}, bf16[144,768]{1,0:T(8,128)(2,1)S(1)}, u32[]{:S(2)}, u32[]{:S(2)}) collective-permute-start(bf16[144,768]{1,0:T(8,128)(2,1)S(1)} %copy-done.18), channel_id=1, source_target_pairs={{0,4},{4,0},{1,5},{5,1},{2,6},{6,2},{3,7},{7,3},{8,12},{12,8},{9,1... | collective-permute-start | bytes 663560 | tf_op jit(solution)/shard_map/ppermute | solution.py:724
  40.8 17.1 %collective-permute-start.9 = (bf16[144,768]{1,0:T(8,128)(2,1)}, bf16[144,768]{1,0:T(8,128)(2,1)}, u32[]{:S(2)}, u32[]{:S(2)}) collective-permute-start(bf16[144,768]{1,0:T(8,128)(2,1)} %collective-permute-done.5.refs_6_), channel_id=1, source_target_pairs={{0,4},{4,0},{1,5},{5,1},{2,6},{6,2},{3,7},{7,3},{8,12},{12,8},{9,1... | collective-permute-start | bytes 663560 | tf_op jit(solution)/shard_map/ppermute | solution.py:724
  40.8 17.1 %collective-permute-start.8 = (bf16[144,768]{1,0:T(8,128)(2,1)}, bf16[144,768]{1,0:T(8,128)(2,1)}, u32[]{:S(2)}, u32[]{:S(2)}) collective-permute-start(bf16[144,768]{1,0:T(8,128)(2,1)} %collective-permute-done.4.refs_5_), channel_id=1, source_target_pairs={{0,4},{4,0},{1,5},{5,1},{2,6},{6,2},{3,7},{7,3},{8,12},{12,8},{9,1... | collective-permute-start | bytes 663560 | tf_op jit(solution)/shard_map/ppermute | solution.py:724
  41.5 11.8 %copy-start.10 = (bf16[208,1536]{1,0:T(8,128)(2,1)}, bf16[208,1536]{1,0:T(8,128)(2,1)S(1)}, u32[]{:S(2)}) copy-start(bf16[208,1536]{1,0:T(8,128)(2,1)S(1)} %collective-permute-done.refs_12_) | copy-start | bytes 1916932
  41.6 11.7 %collective-permute-start.2 = (bf16[112,1536]{1,0:T(8,128)(2,1)S(1)}, bf16[112,1536]{1,0:T(8,128)(2,1)S(1)}, u32[]{:S(2)}, u32[]{:S(2)}) collective-permute-start(bf16[112,1536]{1,0:T(8,128)(2,1)S(1)} %slice.96), channel_id=1, source_target_pairs={{0,2},{2,0},{1,3},{3,1},{4,6},{6,4},{5,7},{7,5},{8,10},{10,8},{9,1... | collective-permute-start | bytes 1032200 | tf_op jit(solution)/shard_map/ppermute | solution.py:751
  44.4 8.9 %collective-permute-start.10 = (bf16[96,1536]{1,0:T(8,128)(2,1)S(1)}, bf16[96,1536]{1,0:T(8,128)(2,1)S(1)}, u32[]{:S(2)}, u32[]{:S(2)}) collective-permute-start(bf16[96,1536]{1,0:T(8,128)(2,1)S(1)} %slice.99), channel_id=1, source_target_pairs={{0,1},{1,0},{2,3},{3,2},{4,5},{5,4},{6,7},{7,6},{8,9},{9,8},{10,11... | collective-permute-start | bytes 884744 | tf_op jit(solution)/shard_map/ppermute | solution.py:750
  53.2 5.6 %collective-permute-start.7 = (bf16[144,768]{1,0:T(8,128)(2,1)}, bf16[144,768]{1,0:T(8,128)(2,1)}, u32[]{:S(2)}, u32[]{:S(2)}) collective-permute-start(bf16[144,768]{1,0:T(8,128)(2,1)} %collective-permute-done.3.refs_4_), channel_id=1, source_target_pairs={{0,4},{4,0},{1,5},{5,1},{2,6},{6,2},{3,7},{7,3},{8,12},{12,8},{9,1... | collective-permute-start | bytes 663560 | tf_op jit(solution)/shard_map/ppermute | solution.py:724
  53.4 21.6 %collective-permute-start.14 = (bf16[384,384]{1,0:T(8,128)(2,1)S(1)}, bf16[384,384]{1,0:T(8,128)(2,1)S(1)}, u32[]{:S(2)}, u32[]{:S(2)}) collective-permute-start(bf16[384,384]{1,0:T(8,128)(2,1)S(1)} %get-tuple-element.183), channel_id=1, source_target_pairs={{0,4},{4,0},{1,5},{5,1},{2,6},{6,2},{3,7},{7,3},{8,12},{12,8},{9,1... | collective-permute-start | bytes 884744 | tf_op jit(solution)/shard_map/ppermute | solution.py:858
  54.2 19.7 %collective-permute-start.13 = (bf16[128,768]{1,0:T(8,128)(2,1)}, bf16[128,768]{1,0:T(8,128)(2,1)S(1)}, u32[]{:S(2)}, u32[]{:S(2)}) collective-permute-start(bf16[128,768]{1,0:T(8,128)(2,1)} %get-tuple-element.109), channel_id=1, source_target_pairs={{0,24},{8,16},{16,8},{24,0},{1,25},{9,17},{17,9},{25,1},{2,26},{10... | collective-permute-start | bytes 589832 | tf_op jit(solution)/shard_map/ppermute | solution.py:710
  57.9 17.1 %collective-permute-start.12 = (bf16[128,768]{1,0:T(8,128)(2,1)}, bf16[128,768]{1,0:T(8,128)(2,1)S(1)}, u32[]{:S(2)}, u32[]{:S(2)}) collective-permute-start(bf16[128,768]{1,0:T(8,128)(2,1)} %get-tuple-element.107), channel_id=1, source_target_pairs={{0,16},{8,24},{16,0},{24,8},{1,17},{9,25},{17,1},{25,9},{2,18},{10... | collective-permute-start | bytes 589832 | tf_op jit(solution)/shard_map/ppermute | solution.py:710
  57.9 17.1 %collective-permute-start.11 = (bf16[128,768]{1,0:T(8,128)(2,1)}, bf16[128,768]{1,0:T(8,128)(2,1)S(1)}, u32[]{:S(2)}, u32[]{:S(2)}) collective-permute-start(bf16[128,768]{1,0:T(8,128)(2,1)} %get-tuple-element.105), channel_id=1, source_target_pairs={{0,8},{8,0},{16,24},{24,16},{1,9},{9,1},{17,25},{25,17},{2,10},{10... | collective-permute-start | bytes 589832 | tf_op jit(solution)/shard_map/ppermute | solution.py:710
  73.9 20.3 %copy-start.21 = (bf16[128,768]{1,0:T(8,128)(2,1)}, bf16[128,768]{1,0:T(8,128)(2,1)S(1)}, u32[]{:S(2)}) copy-start(bf16[128,768]{1,0:T(8,128)(2,1)S(1)} %collective-permute-done.13.refs_12_) | copy-start | bytes 589828
  75.0 18.8 %copy-start.22 = (bf16[128,768]{1,0:T(8,128)(2,1)}, bf16[128,768]{1,0:T(8,128)(2,1)S(1)}, u32[]{:S(2)}) copy-start(bf16[128,768]{1,0:T(8,128)(2,1)S(1)} %collective-permute-done.12.refs_11_) | copy-start | bytes 589828
  78.2 3.6 %collective-permute-start.15 = (bf16[1024,768]{1,0:T(8,128)(2,1)S(1)}, bf16[1024,768]{1,0:T(8,128)(2,1)}, u32[]{:S(2)}, u32[]{:S(2)}) collective-permute-start(bf16[1024,768]{1,0:T(8,128)(2,1)S(1)} %convolution_convert_fusion.2.refs_1_), channel_id=1, source_target_pairs={{0,4},{4,0},{1,5},{5,1},{2,6},{6,2},{3,7},{7,3},{8,12},{12,8},{9,1... | collective-permute-start | bytes 4718600 | tf_op jit(solution)/shard_map/ppermute | solution.py:738
  81.8 11.8 %copy-start.24 = (bf16[128,768]{1,0:T(8,128)(2,1)S(1)}, bf16[128,768]{1,0:T(8,128)(2,1)}, u32[]{:S(2)}) copy-start(bf16[128,768]{1,0:T(8,128)(2,1)} %copy-done.23) | copy-start | bytes 589828
  93.1 4.6 %collective-permute-start.16 = (bf16[1024,768]{1,0:T(8,128)(2,1)S(1)}, bf16[1024,768]{1,0:T(8,128)(2,1)S(1)}, u32[]{:S(2)}, u32[]{:S(2)}) collective-permute-start(bf16[1024,768]{1,0:T(8,128)(2,1)S(1)} %get-tuple-element.113.refs_2_), channel_id=1, source_target_pairs={{0,4},{4,0},{1,5},{5,1},{2,6},{6,2},{3,7},{7,3},{8,12},{12,8},{9,1... | collective-permute-start | bytes 4718600 | tf_op jit(solution)/shard_map/ppermute | solution.py:738
  93.3 3.6 %collective-permute-start.17 = (bf16[128,768]{1,0:T(8,128)(2,1)S(1)}, bf16[128,768]{1,0:T(8,128)(2,1)S(1)}, u32[]{:S(2)}, u32[]{:S(2)}) collective-permute-start(bf16[128,768]{1,0:T(8,128)(2,1)S(1)} %copy-done.20), channel_id=1, source_target_pairs={{0,4},{4,0},{1,5},{5,1},{2,6},{6,2},{3,7},{7,3},{8,12},{12,8},{9,1... | collective-permute-start | bytes 589832 | tf_op jit(solution)/shard_map/ppermute | solution.py:724
  93.7 3.5 %collective-permute-start.18 = (bf16[128,768]{1,0:T(8,128)(2,1)S(1)}, bf16[128,768]{1,0:T(8,128)(2,1)S(1)}, u32[]{:S(2)}, u32[]{:S(2)}) collective-permute-start(bf16[128,768]{1,0:T(8,128)(2,1)S(1)} %copy-done.24), channel_id=1, source_target_pairs={{0,4},{4,0},{1,5},{5,1},{2,6},{6,2},{3,7},{7,3},{8,12},{12,8},{9,1... | collective-permute-start | bytes 589832 | tf_op jit(solution)/shard_map/ppermute | solution.py:724
  93.8 3.6 %collective-permute-start.19 = (bf16[128,768]{1,0:T(8,128)(2,1)S(1)}, bf16[128,768]{1,0:T(8,128)(2,1)S(1)}, u32[]{:S(2)}, u32[]{:S(2)}) collective-permute-start(bf16[128,768]{1,0:T(8,128)(2,1)S(1)} %collective-permute-done.12.refs_11_), channel_id=1, source_target_pairs={{0,4},{4,0},{1,5},{5,1},{2,6},{6,2},{3,7},{7,3},{8,12},{12,8},{9,1... | collective-permute-start | bytes 589832 | tf_op jit(solution)/shard_map/ppermute | solution.py:724
  94.2 3.5 %collective-permute-start.20 = (bf16[128,768]{1,0:T(8,128)(2,1)S(1)}, bf16[128,768]{1,0:T(8,128)(2,1)S(1)}, u32[]{:S(2)}, u32[]{:S(2)}) collective-permute-start(bf16[128,768]{1,0:T(8,128)(2,1)S(1)} %collective-permute-done.13.refs_12_), channel_id=1, source_target_pairs={{0,4},{4,0},{1,5},{5,1},{2,6},{6,2},{3,7},{7,3},{8,12},{12,8},{9,1... | collective-permute-start | bytes 589832 | tf_op jit(solution)/shard_map/ppermute | solution.py:724
  110.8 6.0 %collective-permute-start.24 = (bf16[1024,768]{1,0:T(8,128)(2,1)S(1)}, bf16[1024,768]{1,0:T(8,128)(2,1)S(1)}, u32[]{:S(2)}, u32[]{:S(2)}) collective-permute-start(bf16[1024,768]{1,0:T(8,128)(2,1)S(1)} %get-tuple-element.132.own_ref), channel_id=1, source_target_pairs={{0,4},{4,0},{1,5},{5,1},{2,6},{6,2},{3,7},{7,3},{8,12},{12,8},{9,1... | collective-permute-start | bytes 4718600 | tf_op jit(solution)/shard_map/ppermute | solution.py:738
  120.6 97.2 %reduce-scatter.5.cloned.1.call-start = ((), (), s32[]{:S(2)}) async-start(), calls=%async_computation.2 | async-start | bytes 1474560 | tf_op jit(solution)/shard_map/reduce_scatter | solution.py:935
  127.7 4.8 %collective-permute-start.25 = (bf16[384,384]{1,0:T(8,128)(2,1)S(1)}, bf16[384,384]{1,0:T(8,128)(2,1)S(1)}, u32[]{:S(2)}, u32[]{:S(2)}) collective-permute-start(bf16[384,384]{1,0:T(8,128)(2,1)S(1)} %get-tuple-element.181), channel_id=1, source_target_pairs={{0,4},{4,0},{1,5},{5,1},{2,6},{6,2},{3,7},{7,3},{8,12},{12,8},{9,1... | collective-permute-start | bytes 884744 | tf_op jit(solution)/shard_map/ppermute | solution.py:897
  128.0 19.7 %collective-permute-start.21 = (bf16[128,768]{1,0:T(8,128)(2,1)S(1)}, bf16[128,768]{1,0:T(8,128)(2,1)S(1)}, u32[]{:S(2)}, u32[]{:S(2)}) collective-permute-start(bf16[128,768]{1,0:T(8,128)(2,1)S(1)} %copy-done.32), channel_id=1, source_target_pairs={{0,8},{8,0},{16,24},{24,16},{1,9},{9,1},{17,25},{25,17},{2,10},{10... | collective-permute-start | bytes 589832 | tf_op jit(solution)/shard_map/ppermute | solution.py:710
  129.2 18.6 %collective-permute-start.22 = (bf16[128,768]{1,0:T(8,128)(2,1)S(1)}, bf16[128,768]{1,0:T(8,128)(2,1)S(1)}, u32[]{:S(2)}, u32[]{:S(2)}) collective-permute-start(bf16[128,768]{1,0:T(8,128)(2,1)S(1)} %copy-done.31), channel_id=1, source_target_pairs={{0,16},{8,24},{16,0},{24,8},{1,17},{9,25},{17,1},{25,9},{2,18},{10... | collective-permute-start | bytes 589832 | tf_op jit(solution)/shard_map/ppermute | solution.py:710
  131.7 16.1 %collective-permute-start.23 = (bf16[128,768]{1,0:T(8,128)(2,1)S(1)}, bf16[128,768]{1,0:T(8,128)(2,1)S(1)}, u32[]{:S(2)}, u32[]{:S(2)}) collective-permute-start(bf16[128,768]{1,0:T(8,128)(2,1)S(1)} %copy-done.30), channel_id=1, source_target_pairs={{0,24},{8,16},{16,8},{24,0},{1,25},{9,17},{17,9},{25,1},{2,26},{10... | collective-permute-start | bytes 589832 | tf_op jit(solution)/shard_map/ppermute | solution.py:710
  134.1 13.8 %copy-start.13 = (bf16[1024,768]{1,0:T(8,128)(2,1)S(1)}, bf16[1024,768]{1,0:T(8,128)(2,1)}, u32[]{:S(2)}) copy-start(bf16[1024,768]{1,0:T(8,128)(2,1)} %get-tuple-element.103.refs_0_) | copy-start | bytes 4718596
  151.7 15.2 %collective-permute-start.30 = (bf16[112,1536]{1,0:T(8,128)(2,1)S(1)}, bf16[112,1536]{1,0:T(8,128)(2,1)S(1)}, u32[]{:S(2)}, u32[]{:S(2)}) collective-permute-start(bf16[112,1536]{1,0:T(8,128)(2,1)S(1)} %slice_bitcast_fusion.1), channel_id=1, source_target_pairs={{0,2},{2,0},{1,3},{3,1},{4,6},{6,4},{5,7},{7,5},{8,10},{10,8},{9,1... | collective-permute-start | bytes 1032200 | tf_op jit(solution)/shard_map/ppermute | solution.py:766
  155.6 2.4 collective-permute-start.26
  155.7 11.2 %collective-permute-start.29 = (bf16[96,1536]{1,0:T(8,128)(2,1)S(1)}, bf16[96,1536]{1,0:T(8,128)(2,1)S(1)}, u32[]{:S(2)}, u32[]{:S(2)}) collective-permute-start(bf16[96,1536]{1,0:T(8,128)(2,1)S(1)} %slice_bitcast_fusion.4), channel_id=1, source_target_pairs={{0,1},{1,0},{2,3},{3,2},{4,5},{5,4},{6,7},{7,6},{8,9},{9,8},{10,11... | collective-permute-start | bytes 884744 | tf_op jit(solution)/shard_map/ppermute | solution.py:766
  158.8 11.4 %collective-permute-start.27 = (bf16[128,768]{1,0:T(8,128)(2,1)S(1)}, bf16[128,768]{1,0:T(8,128)(2,1)S(1)}, u32[]{:S(2)}, u32[]{:S(2)}) collective-permute-start(bf16[128,768]{1,0:T(8,128)(2,1)S(1)} %get-tuple-element.146), channel_id=1, source_target_pairs={{0,8},{8,0},{16,24},{24,16},{1,9},{9,1},{17,25},{25,17},{2,10},{10... | collective-permute-start | bytes 589832 | tf_op jit(solution)/shard_map/ppermute | solution.py:710
  161.0 11.8 %collective-permute-start.28 = (bf16[128,768]{1,0:T(8,128)(2,1)S(1)}, bf16[128,768]{1,0:T(8,128)(2,1)S(1)}, u32[]{:S(2)}, u32[]{:S(2)}) collective-permute-start(bf16[128,768]{1,0:T(8,128)(2,1)S(1)} %get-tuple-element.147), channel_id=1, source_target_pairs={{0,16},{8,24},{16,0},{24,8},{1,17},{9,25},{17,1},{25,9},{2,18},{10... | collective-permute-start | bytes 589832 | tf_op jit(solution)/shard_map/ppermute | solution.py:710
  179.4 83.1 %all-gather.7.cloned.1.call-start = ((), (), s32[]{:S(2)}) async-start(), calls=%async_computation.4 | async-start | bytes 2654208 | tf_op jit(solution)/shard_map/all_gather | solution.py:938
  179.5 16.4 %collective-permute-start.32 = (bf16[208,1536]{1,0:T(8,128)(2,1)S(1)}, bf16[208,1536]{1,0:T(8,128)(2,1)S(1)}, u32[]{:S(2)}, u32[]{:S(2)}) collective-permute-start(bf16[208,1536]{1,0:T(8,128)(2,1)S(1)} %pad_maximum_fusion.3), channel_id=1, source_target_pairs={{0,2},{2,0},{1,3},{3,1},{4,6},{6,4},{5,7},{7,5},{8,10},{10,8},{9,1... | collective-permute-start | bytes 1916936 | tf_op jit(solution)/shard_map/ppermute | solution.py:775
  180.3 16.4 %collective-permute-start.31 = (bf16[208,1536]{1,0:T(8,128)(2,1)}, bf16[208,1536]{1,0:T(8,128)(2,1)}, u32[]{:S(2)}, u32[]{:S(2)}) collective-permute-start(bf16[208,1536]{1,0:T(8,128)(2,1)} %pad_maximum_fusion.2), channel_id=1, source_target_pairs={{0,1},{1,0},{2,3},{3,2},{4,5},{5,4},{6,7},{7,6},{8,9},{9,8},{10,11... | collective-permute-start | bytes 1916936 | tf_op jit(solution)/shard_map/ppermute | solution.py:775
  181.2 9.3 %collective-permute-start.33 = (bf16[128,768]{1,0:T(8,128)(2,1)S(1)}, bf16[128,768]{1,0:T(8,128)(2,1)S(1)}, u32[]{:S(2)}, u32[]{:S(2)}) collective-permute-start(bf16[128,768]{1,0:T(8,128)(2,1)S(1)} %get-tuple-element.154), channel_id=1, source_target_pairs={{0,24},{8,16},{16,8},{24,0},{1,25},{9,17},{17,9},{25,1},{2,26},{10... | collective-permute-start | bytes 589832 | tf_op jit(solution)/shard_map/ppermute | solution.py:710
  198.2 19.6 %collective-permute-start.34 = (bf16[208,768]{1,0:T(8,128)(2,1)S(1)}, bf16[208,768]{1,0:T(8,128)(2,1)S(1)}, u32[]{:S(2)}, u32[]{:S(2)}) collective-permute-start(bf16[208,768]{1,0:T(8,128)(2,1)S(1)} %constant_dynamic-slice_fusion.1), channel_id=1, source_target_pairs={{0,8},{8,0},{16,24},{24,16},{1,9},{9,1},{17,25},{25,17},{2,10},{10... | collective-permute-start | bytes 958472 | tf_op jit(solution)/shard_map/ppermute | solution.py:710
  218.0 9.2 %collective-permute-start.35 = (bf16[208,384]{1,0:T(8,128)(2,1)S(1)}, bf16[208,384]{1,0:T(8,128)(2,1)S(1)}, u32[]{:S(2)}, u32[]{:S(2)}) collective-permute-start(bf16[208,384]{1,0:T(8,128)(2,1)S(1)} %constant_dynamic-slice_fusion), channel_id=1, source_target_pairs={{0,16},{8,24},{16,0},{24,8},{1,17},{9,25},{17,1},{25,9},{2,18},{10... | collective-permute-start | bytes 479240 | tf_op jit(solution)/shard_map/ppermute | solution.py:710
  227.2 19.3 %collective-permute-start.36 = (bf16[208,384]{1,0:T(8,128)(2,1)S(1)}, bf16[208,384]{1,0:T(8,128)(2,1)S(1)}, u32[]{:S(2)}, u32[]{:S(2)}) collective-permute-start(bf16[208,384]{1,0:T(8,128)(2,1)S(1)} %add_convert_fusion.1), channel_id=1, source_target_pairs={{0,16},{8,24},{16,0},{24,8},{1,17},{9,25},{17,1},{25,9},{2,18},{10... | collective-permute-start | bytes 479240 | tf_op jit(solution)/shard_map/ppermute | solution.py:710
  246.6 12.0 %collective-permute-start.37 = (bf16[208,768]{1,0:T(8,128)(2,1)S(1)}, bf16[208,768]{1,0:T(8,128)(2,1)S(1)}, u32[]{:S(2)}, u32[]{:S(2)}) collective-permute-start(bf16[208,768]{1,0:T(8,128)(2,1)S(1)} %pad_maximum_fusion.7), channel_id=1, source_target_pairs={{0,8},{8,0},{16,24},{24,16},{1,9},{9,1},{17,25},{25,17},{2,10},{10... | collective-permute-start | bytes 958472 | tf_op jit(solution)/shard_map/ppermute | solution.py:710
  258.8 2.1 collective-permute-start.38
  (30 other events, 101.4 us)
Sparse Core Ops, SparseCore 0:
  10.4 71.0 all-gather.4
  120.7 58.6 reduce-scatter.6
  181.7 33.5 reduce-scatter.4
  217.9 36.8 all-gather.6

commit v3 on v2

--- a/solution.py
+++ b/solution.py
@@ -97,40 +97,6 @@
                 down.at[j * part_rows:(j + 1) * part_rows, c * 256:(c + 1) * 256],
                 sems.at[chunks + c, j]) for j in range(members)])
     return groups
-
-
-def place_tokens(target, refs, where_ref, ranks):
-    if len(refs) == 1:
-        target[...] = refs[0][...]
-        return
-    groups = len(refs) // ranks
-    span = target.shape[0] // (groups * ranks)
-    for n, ref in enumerate(refs):
-        rank = where_ref[2] if n < groups else 1 - where_ref[2]
-        chunk = (where_ref[1] ^ (n % groups)) * ranks + rank
-        target[pl.ds(pl.multiple_of(chunk * span, span), span), :] = ref[0:span, :]
-
-
-def place_segments(target, refs, where_ref, ranks):
-    groups = len(refs) // ranks
-    span = target.shape[1] // (groups * ranks)
-    for n, ref in enumerate(refs):
-        rank = where_ref[2] if n < groups else 1 - where_ref[2]
-        chunk = (where_ref[1] ^ (n % groups)) * ranks + rank
-        row = ref[span:span + 16, 0:span].astype(F32)[0:1, :]
-        target[:, pl.ds(pl.multiple_of(chunk * span, span), span)] = row
-
-
-def place_stack(gu, down, stack_ref, shard, part_rows):
-    chunks = gu.shape[1] // 256
-    for j in range(stack_ref.shape[0]):
-        for c in range(chunks):
-            gu[j * shard:(j + 1) * shard, c * 256:(c + 1) * 256] = (
-                stack_ref[j, c * shard:(c + 1) * shard, :])
-        for c in range(down.shape[1] // 256):
-            at = chunks * shard + c * part_rows
-            down[j * part_rows:(j + 1) * part_rows, c * 256:(c + 1) * 256] = (
-                stack_ref[j, at:at + part_rows, :])
 
 
 def attend_kernel(where_ref, cos_ref, sin_ref, *refs, pieces, token_count, ranks, shard, block,
@@ -339,7 +305,6 @@
     row = pl.BlockSpec((block, width), lambda i: (i, 0))
     slab = pl.BlockSpec((block // ranks, width), lambda i: (0, 0))
     total, gate, silu, gu, down = vmem(total, gate, silu, gu, down)
-    cot = hbm(*cot)
     return pl.pallas_call(
         kernel,
         grid=(tokens // block,),
@@ -349,7 +314,7 @@
                                      pl.BlockSpec((1, width), lambda i: (0, 0))],
         out_shape=[pltpu.HBM((block // ranks, width), BF)] * groups
         + [pltpu.VMEM((tokens, width), BF), pltpu.VMEM((tokens, 2 * ff), BF),
-           jax.ShapeDtypeStruct((tokens, width), BF), pltpu.HBM((1, width), F32)],
+           pltpu.HBM((tokens, width), BF), pltpu.HBM((1, width), F32)],
         scratch_shapes=[pltpu.VMEM((tokens, width), BF), pltpu.VMEM((block, width), F32)],
         compiler_params=pltpu.CompilerParams(vmem_limit_bytes=20 << 20),
         cost_estimate=SMALL_COST,
@@ -676,13 +641,21 @@
 
 
 def join_all_kernel(all_ref, *refs, moves):
-    out_refs, whole_ref = refs[:-1], refs[-1]
+    outs = (len(refs) - 2) // 2
+    out_refs, whole_ref, blocks, sems = refs[:outs], refs[outs], refs[outs + 1:-1], refs[-1]
     groups, ranks, rows, _ = all_ref.shape
     for h in range(ranks):
         for m in range(groups):
             whole_ref[h, m * rows:(m + 1) * rows, :] = all_ref[m, h]
-    for out, half, (rows, cols), (to_rows, to_cols) in moves:
-        out_refs[out][to_rows, to_cols] = whole_ref[half, rows, cols].astype(F32)
+    copies = []
+    for n in range(outs):
+        for out, half, (rows, cols), (to_rows, to_cols) in moves:
+            if out == n:
+                blocks[out][to_rows, to_cols] = whole_ref[half, rows, cols].astype(F32)
+        copies.append(pltpu.make_async_copy(blocks[n], out_refs[n], sems.at[n]))
+        copies[-1].start()
+    for copy in copies:
+        copy.wait()
 
 
 def join_all(parts, moves, shapes):
@@ -692,10 +665,12 @@
         lambda *refs: join_all_kernel(*refs, moves=moves),
         grid=(1,),
         in_specs=whole_specs(parts),
-        out_specs=[pl.BlockSpec(shape, lambda i: (0, 0)) for shape in shapes],
-        out_shape=[jax.ShapeDtypeStruct(shape, F32) for shape in shapes],
-        scratch_shapes=[pltpu.VMEM((ranks, groups * rows, cols), BF)],
-        compiler_params=pltpu.CompilerParams(vmem_limit_bytes=32 << 20),
+        out_specs=[HBM_SPEC] * len(shapes),
+        out_shape=[pltpu.HBM(shape, F32) for shape in shapes],
+        scratch_shapes=[pltpu.VMEM((ranks, groups * rows, cols), BF)]
+        + [pltpu.VMEM(shape, F32) for shape in shapes]
+        + [pltpu.SemaphoreType.DMA((len(shapes),))],
+        compiler_params=pltpu.CompilerParams(vmem_limit_bytes=24 << 20),
         cost_estimate=SMALL_COST,
         name="join_all",
     )(parts)
@@ -807,6 +782,8 @@
         spare = lanes_all - own_cols
         block = span * ranks
         f_index = lax.axis_index(F)
+        own_at, other_at, other_rank = (
+            at.astype(jnp.uint32) for at in (rank * own_cols, (1 - rank) * own_cols, 1 - rank))
         where = jnp.stack([f_index, lax.axis_index("m"), rank])
         small_cols = 3 * lanes_all + own_cols
         gains_in = jnp.pad(jnp.stack([gain_attn, gain_ffn]), ((0, 14), (0, 0)))
@@ -864,8 +841,10 @@
             w_out_own = jnp.concatenate([pieces[i] for i in range(ranks)], axis=1)
         w_out_even = jnp.pad(w_out_own, ((0, spare), (0, 0)))
 
+        cosine, gains, gain_one, own_at, other_at, other_rank = lax.optimization_barrier(
+            (cosine, gains, gain_one, own_at, other_at, other_rank))
         q, k, v, att, lse, w_qkv, x, seg = attend(
-            where, after(cosine, gains, gain_one), sine, token_refs, ranks, qkv_refs, small_pieces, shard, lanes_all,
+            where, cosine, sine, token_refs, ranks, qkv_refs, small_pieces, shard, lanes_all,
             window, head_size, width)
         if square:
             cot_slabs, att = between(cot_slabs, att)
@@ -886,14 +865,14 @@
         down_w_grad = dot(hidden_low, ffn_grad_low, ((0,), (0,))).astype(BF)
         stack_grad = arrange(gu_w_grad, down_w_grad, fsdp)
         stack_owned = lax.psum_scatter(stack_grad, F, scatter_dimension=0, tiled=False)
-        own = after(own, stack_grad)
+        own, got = after(own, stack_grad), after(got, stack_grad)
         branch_grad_low, branch_keep, gain_grads = norm_back(
             where[2:], total, ffn_grad_low, own, got, gain_one, gain_ffn_grad,
             fsdp, small_cols, block, span)
         out_w_grad = dot(att, branch_grad_low, ((0,), (0,)))[:own_cols].astype(BF)
         if ranks == 2:
-            give = lax.dynamic_slice_in_dim(out_w_grad, (1 - rank) * own_cols, own_cols, 1)
-            keep = lax.dynamic_slice_in_dim(out_w_grad, rank * own_cols, own_cols, 1)
+            give = lax.dynamic_slice_in_dim(out_w_grad, other_at, own_cols, 1)
+            keep = lax.dynamic_slice_in_dim(out_w_grad, own_at, own_cols, 1)
             got = lax.ppermute(give, "r", swap)
             out_cols_grad = jnp.where(rank == 0, jnp.concatenate([keep, got], 0),
                                       jnp.concatenate([got, keep], 0))
@@ -918,7 +897,7 @@
         part = dot(d_qkv, w_qkv, ((1,), (1,))).astype(BF)
         if ranks == 2:
             rows = part.reshape(groups, ranks, span, width)
-            give = lax.dynamic_index_in_dim(rows, 1 - rank, 1, keepdims=False)
+            give = lax.dynamic_index_in_dim(rows, other_rank, 1, keepdims=False)
             got = lax.ppermute(give, "r", swap)
         else:
             part = lax.psum(part, "r")
@@ -968,8 +947,10 @@
                 (4 + n, (slice(shard + n, shard + n + 1), slice(0, shard))) for n in range(2)]
             gate_w, up_w, down_grad = join_all(
                 stack_parts, stack_moves, [(shard, ff)] * 2 + [(down_rows, width)])
+            small_got, gate_w, up_w, down_grad = lax.optimization_barrier(
+                (lax.ppermute(small_sum, "r", swap), gate_w, up_w, down_grad))
             query_w, key_w, value_w, out_w, gain_a, gain_f = join(
-                rank, small_sum, lax.ppermute(small_sum, "r", swap), small_moves, small_plain,
+                rank, small_sum, small_got, small_moves, small_plain,
                 [(shard, width)] * 4 + [(1, shard)] * 2)
         else:
             at = 2 * half_ff // 256 * shard

time: 274 us -> 269 us (0.982)
  local copies, waits for them, and re-layouts: 8.7 us -> 4.78 us
    unnamed x70 -> x52, local copies, waits for them, and re-layouts: 6.11 us -> 1.97 us
    ppermute x1, waiting for transfers between devices: 4.56 us -> 1.66 us  [round_one(): lax.ppermute(far[:rows], 'x', swap)]
  transfers between devices with their start and end apart: 43 -> 43, of which waited for: 24 -> 24; matrix products, arithmetic and copies ran while one was open for 9% -> 9% of each run, Pallas kernels for 16% -> 17%
where the time goes in v3:
time: 269 us
  waiting for transfers between devices  109 us (41%)
  Pallas kernels  75.4 us (28%)
  starting transfers between devices  43.3 us (16%)
  between operations  14.5 us (5%)
  matrix products  13.5 us (5%)
  other arithmetic  8.81 us (3%)
  local copies, waits for them, and re-layouts  4.78 us (2%)
    ppermute x16, waiting for transfers between devices, hop(): return lax.ppermute(value, 'm', [(i, i ^ k) for i in range(groups)])  76.9 us
    ppermute x16, starting transfers between devices, hop(): return lax.ppermute(value, 'm', [(i, i ^ k) for i in range(groups)])  28.5 us
    pallas_call x1, Pallas kernels, attend(): pl.pallas_call(kernel, grid=(pairs,), in_specs=[SMEM_SPEC] + whole_specs(...  15 us
    pallas_call x1, Pallas kernels, attend_back(): pl.pallas_call(kernel, grid=(pairs,), in_specs=whole_specs(seg) + [VMEM_S...  13.9 us
    dot_general x6, matrix products, dot(): lax.dot_general(left, right, (dims, ((), ())), preferred_element_type=F32)  13.5 us
    pallas_call x1, Pallas kernels, backward(): pl.pallas_call(kernel, grid=(tokens // block,), in_specs=[SMEM_SPEC, VMEM...  11.8 us
    pallas_call x1, Pallas kernels, forward(): pl.pallas_call(lambda *refs: forward_kernel(*refs, shard=shard, part_rows...  11.5 us
    ppermute x1, waiting for transfers between devices, gather_rows(): far_b = lax.ppermute(from_x[rows:], 'y', swap)  7.7 us
  transfers between devices with their start and end apart: 43, of which 24 were waited for; matrix products, arithmetic and copies ran while one was open for 9% of the time, Pallas kernels for 17%

profile of v3, /device:TPU:0, one launch (start us, length us, event | category | flops | bytes accessed | tf_op | source)
XLA Modules:
  0.0 268.9 jit_solution(8319582196828398305)
XLA Ops:
  7.3 2.8 %pack.1 = bf16[2304,256]{1,0:T(8,128)(2,1)} custom-call(s32[3]{0:T(128)S(1)} %pad_add_fusion.refs_0_.where_ref, bf16[192,2048]{1,0:T(8,128)(2,1)} %refs_1_.2, bf16[192,2048]{1,0:T(8,128)(2,1)} %refs_2_.2, bf16[512,768]{1,0:T(8,128)(2,1)} %refs_3_.2), custom_call_target="tpu_custom_call" | custom-call | flops 1 | bytes 1 | tf_op jit(solution)/shard_map/pack/pallas_call | solution.py:455
  10.8 3.4 %pack_small.1 = (bf16[208,1536]{1,0:T(8,128)(2,1)}, bf16[144,768]{1,0:T(8,128)(2,1)}, bf16[144,768]{1,0:T(8,128)(2,1)}, bf16[144,768]{1,0:T(8,128)(2,1)}, bf16[1...) custom-call(s32[3]{0:T(128)S(1)} %pad_add_fusion.refs_0_.where_ref, ...), custom_call_target="tpu_custom_call" | custom-call | flops 1 | bytes 1 | tf_op jit(solution)/shard_map/pack_small/pallas_call | solution.py:419
  14.2 3.0 %collective-permute-start = (bf16[208,1536]{1,0:T(8,128)(2,1)}, bf16[208,1536]{1,0:T(8,128)(2,1)S(1)}, u32[]{:S(2)}, u32[]{:S(2)}) collective-permute-start(bf16[208,1536]{1,0:T(8,128)(2,1)} %get-tuple-element.104.refs_11_), channel_id=1, source_target_pairs={{0,1},{1,0},{2,3},{3,2},{4,5},{5,4},{6,7},{7,6},{8,9},{9,8},{10,11... | collective-permute-start | bytes 1916936 | tf_op jit(solution)/shard_map/ppermute | solution.py:723
  17.2 1.5 collective-permute-start.1
  18.7 3.6 %collective-permute-start.5 = (bf16[144,768]{1,0:T(8,128)(2,1)}, bf16[144,768]{1,0:T(8,128)(2,1)S(1)}, u32[]{:S(2)}, u32[]{:S(2)}) collective-permute-start(bf16[144,768]{1,0:T(8,128)(2,1)} %get-tuple-element.111), channel_id=1, source_target_pairs={{0,24},{8,16},{16,8},{24,0},{1,25},{9,17},{17,9},{25,1},{2,26},{10... | collective-permute-start | bytes 663560 | tf_op jit(solution)/shard_map/ppermute | solution.py:685
  23.1 1.9 fusion.9
  29.4 11.5 %collective-permute-done.4.refs_5_ = bf16[144,768]{1,0:T(8,128)(2,1)} collective-permute-done((bf16[144,768]{1,0:T(8,128)(2,1)}, bf16[144,768]{1,0:T(8,128)(2,1)}, u32[]{:S(2)}, u32[]{:S(2)}) %collective-permute-start.4) | collective-permute-done | bytes 221216 | tf_op jit(solution)/shard_map/ppermute | solution.py:685
  41.6 1.4 collective-permute-start.2
  43.0 1.4 collective-permute-done.1.refs_13_
  45.5 7.7 %collective-permute-done.2.refs_15_ = bf16[112,1536]{1,0:T(8,128)(2,1)S(1)} collective-permute-done((bf16[112,1536]{1,0:T(8,128)(2,1)S(1)}, bf16[112,1536]{1,0:T(8,128)(2,1)S(1)}, u32[]{:S(2)}, u32[]{:S(2)}) %collective-permute-start.2) | collective-permute-done | bytes 344096 | tf_op jit(solution)/shard_map/ppermute | solution.py:726
  54.2 3.7 %collective-permute-start.13 = (bf16[128,768]{1,0:T(8,128)(2,1)}, bf16[128,768]{1,0:T(8,128)(2,1)S(1)}, u32[]{:S(2)}, u32[]{:S(2)}) collective-permute-start(bf16[128,768]{1,0:T(8,128)(2,1)} %get-tuple-element.119), channel_id=1, source_target_pairs={{0,24},{8,16},{16,8},{24,0},{1,25},{9,17},{17,9},{25,1},{2,26},{10... | collective-permute-start | bytes 589832 | tf_op jit(solution)/shard_map/ppermute | solution.py:685
  59.3 15.0 %attend.1 = (bf16[1024,384]{1,0:T(8,128)(2,1)}, bf16[1024,384]{1,0:T(8,128)(2,1)}, bf16[1024,384]{1,0:T(8,128)(2,1)}, bf16[1024,384]{1,0:T(8,128)(2,1)}, f32[3,8...) custom-call(s32[3]{0:T(128)S(1)} %pad_add_fusion.refs_0_.where_ref, ...), custom_call_target="tpu_custom_call" | custom-call | flops 1 | bytes 1 | tf_op jit(solution)/shard_map/attend/pallas_call | solution.py:186
  75.2 2.3 convolution_convert_fusion.2.refs_1_
  77.6 3.5 %collective-permute-done.15.refs_2_ = bf16[1024,768]{1,0:T(8,128)(2,1)} collective-permute-done((bf16[1024,768]{1,0:T(8,128)(2,1)S(1)}, bf16[1024,768]{1,0:T(8,128)(2,1)}, u32[]{:S(2)}, u32[]{:S(2)}) %collective-permute-start.15) | collective-permute-done | bytes 1572896 | tf_op jit(solution)/shard_map/ppermute | solution.py:713
  81.5 11.5 %ffn_forward.1 = (f32[1024,768]{1,0:T(8,128)S(1)}, bf16[1024,768]{1,0:T(8,128)(2,1)S(1)}, bf16[1024,1024]{1,0:T(8,128)(2,1)S(1)}, bf16[1024,1024]{1,0:T(8,128)(2...) custom-call(bf16[1024,768]{1,0:T(8,128)(2,1)} %get-tuple-element.113, ...), custom_call_target="tpu_custom_call" | custom-call | flops 1 | bytes 1 | tf_op jit(solution)/shard_map/ffn_forward/pallas_call | solution.py:247
  94.2 2.6 collective-permute-done.17.refs_13_
  97.7 11.8 %ffn_backward.1 = (bf16[128,768]{1,0:T(8,128)(2,1)}, bf16[128,768]{1,0:T(8,128)(2,1)}, bf16[128,768]{1,0:T(8,128)(2,1)}, bf16[128,768]{1,0:T(8,128)(2,1)}, bf16[...) custom-call(s32[3]{0:T(128)S(1)} %pad_add_fusion.refs_0_.where_ref, ...), custom_call_target="tpu_custom_call" | custom-call | flops 1 | bytes 1 | tf_op jit(solution)/shard_map/ffn_backward/pallas_call | solution.py:308
  109.6 1.9 convolution_convert_fusion.4.down_ref
  111.5 3.9 %convolution_convert_fusion.1.gu_ref = bf16[768,2048]{1,0:T(8,128)(2,1)S(1)} fusion(bf16[1024,768]{1,0:T(8,128)(2,1)S(1)} %get-tuple-element.140, bf16[1024,2048]{1,0:T(8,128)(2,1)S(1)} %get-tuple-element.141), kind=kOutput, calls=%fused_computation.6 | convolution fusion | flops 3222798336 | bytes 8912896 | tf_op jit(solution)/shard_map/dot_general | solution.py:19
  115.4 2.6 arrange.1
  118.8 5.3 %norm_back.1 = (bf16[1024,768]{1,0:T(8,128)(2,1)S(1)}, f32[4,128,768]{2,1,0:T(8,128)}, bf16[4,16,1536]{2,1,0:T(8,128)(2,1)}) custom-call(s32[1]{0:T(128)} %bitcast.2.rank_ref.refs_0_, f32[1024,768]{1,0:T(8,128)S(1)} %get-tuple-element.123.refs_1_.sum_ref, bf16[1024,768]{1,0:T(8,128)(2,1)} %copy-done.1, bf16[1024,768]{1,0:T(8,128)(2,1)} %get-tuple-element.144.own_ref, ...), custom_call_target="tpu_custom_call" | custom-call | flops 1 | bytes 1 | tf_op jit(solution)/shard_map/norm_back/pallas_call | solution.py:361
  125.6 1.5 collective-permute-start.21
  127.1 2.5 collective-permute-start.22
  130.2 13.9 %attend_back.1 = bf16[1024,1152]{1,0:T(8,128)(2,1)S(1)} custom-call(f32[1,1024]{1,0:T(1,128)} %get-tuple-element.137.refs_0_, bf16[1024,768]{1,0:T(8,128)(2,1)S(1)} %get-tuple-element.151.refs_1_, bf16[384,768]{1,0:T(8,128)(2,1)} %copy-done.9, bf16[1024,384]{1,0:T(8,128)(2,1)} %get-tuple-element.152.refs_3_, bf16[1024,384]{1,0:T(8,128)(2,1)} %get-tuple-element.153.refs_4_, ...), custom_call_target="tpu_custom_call" | custom-call | flops 1 | bytes 1 | tf_op jit(solution)/shard_map/attend_back/pallas_call | solution.py:595
  144.2 2.3 convolution_convert_fusion
  148.1 1.5 collective-permute-start.30
  149.7 2.2 convolution_convert_fusion.3.refs_2_
  153.0 1.3 collective-permute-done.26.refs_3_
  155.1 3.8 %collective-permute-start.27 = (bf16[128,768]{1,0:T(8,128)(2,1)S(1)}, bf16[128,768]{1,0:T(8,128)(2,1)S(1)}, u32[]{:S(2)}, u32[]{:S(2)}) collective-permute-start(bf16[128,768]{1,0:T(8,128)(2,1)S(1)} %get-tuple-element.162), channel_id=1, source_target_pairs={{0,8},{8,0},{16,24},{24,16},{1,9},{9,1},{17,25},{25,17},{2,10},{10... | collective-permute-start | bytes 589832 | tf_op jit(solution)/shard_map/ppermute | solution.py:685
  159.9 1.7 collective-permute-done.29
  161.6 6.5 %collective-permute-done.27.refs_1_ = bf16[128,768]{1,0:T(8,128)(2,1)S(1)} collective-permute-done((bf16[128,768]{1,0:T(8,128)(2,1)S(1)}, bf16[128,768]{1,0:T(8,128)(2,1)S(1)}, u32[]{:S(2)}, u32[]{:S(2)}) %collective-permute-start.27) | collective-permute-done | bytes 196640 | tf_op jit(solution)/shard_map/ppermute | solution.py:685
  168.1 2.6 collective-permute-done.28.refs_2_
  171.8 5.5 %reduce-scatter.7.cloned.1.call-done = bf16[1,2304,256]{2,1,0:T(8,128)(2,1)} async-done(((bf16[4,2304,256]{2,1,0:T(8,128)(2,1)}), bf16[1,2304,256]{2,1,0:T(8,128)(2,1)}) %reduce-scatter.7.cloned.1.call-update) | async-done | bytes 1179664
  177.3 1.4 collective-permute-start.32
  179.4 3.3 %collective-permute-start.33 = (bf16[128,768]{1,0:T(8,128)(2,1)S(1)}, bf16[128,768]{1,0:T(8,128)(2,1)S(1)}, u32[]{:S(2)}, u32[]{:S(2)}) collective-permute-start(bf16[128,768]{1,0:T(8,128)(2,1)S(1)} %get-tuple-element.170), channel_id=1, source_target_pairs={{0,24},{8,16},{16,8},{24,0},{1,25},{9,17},{17,9},{25,1},{2,26},{10... | collective-permute-start | bytes 589832 | tf_op jit(solution)/shard_map/ppermute | solution.py:685
  182.8 1.5 stack.30
  184.2 4.0 %collective-permute-done.33.refs_3_ = bf16[128,768]{1,0:T(8,128)(2,1)S(1)} collective-permute-done((bf16[128,768]{1,0:T(8,128)(2,1)S(1)}, bf16[128,768]{1,0:T(8,128)(2,1)S(1)}, u32[]{:S(2)}, u32[]{:S(2)}) %collective-permute-start.33) | collective-permute-done | bytes 196640 | tf_op jit(solution)/shard_map/ppermute | solution.py:685
  188.3 5.2 %collective-permute-done.32 = bf16[208,1536]{1,0:T(8,128)(2,1)S(1)} collective-permute-done((bf16[208,1536]{1,0:T(8,128)(2,1)S(1)}, bf16[208,1536]{1,0:T(8,128)(2,1)S(1)}, u32[]{:S(2)}, u32[]{:S(2)}) %collective-permute-start.32) | collective-permute-done | bytes 639008 | tf_op jit(solution)/shard_map/ppermute | solution.py:750
  193.5 1.4 collective-permute-done.31
  194.9 1.5 fusion.1
  196.5 6.7 %collective-permute-start.34 = (bf16[208,768]{1,0:T(8,128)(2,1)S(1)}, bf16[208,768]{1,0:T(8,128)(2,1)S(1)}, u32[]{:S(2)}, u32[]{:S(2)}) collective-permute-start(bf16[208,768]{1,0:T(8,128)(2,1)S(1)} %constant_dynamic-slice_fusion.1), channel_id=1, source_target_pairs={{0,8},{8,0},{16,24},{24,16},{1,9},{9,1},{17,25},{25,17},{2,10},{10... | collective-permute-start | bytes 958472 | tf_op jit(solution)/shard_map/ppermute | solution.py:685
  203.2 1.5 stack.31
  204.6 11.2 %collective-permute-done.34 = bf16[208,768]{1,0:T(8,128)(2,1)S(1)} collective-permute-done((bf16[208,768]{1,0:T(8,128)(2,1)S(1)}, bf16[208,768]{1,0:T(8,128)(2,1)S(1)}, u32[]{:S(2)}, u32[]{:S(2)}) %collective-permute-start.34) | collective-permute-done | bytes 319520 | tf_op jit(solution)/shard_map/ppermute | solution.py:685
  216.1 9.0 %collective-permute-done.35 = bf16[208,384]{1,0:T(8,128)(2,1)S(1)} collective-permute-done((bf16[208,384]{1,0:T(8,128)(2,1)S(1)}, bf16[208,384]{1,0:T(8,128)(2,1)S(1)}, u32[]{:S(2)}, u32[]{:S(2)}) %collective-permute-start.35) | collective-permute-done | bytes 159776 | tf_op jit(solution)/shard_map/ppermute | solution.py:685
  225.2 19.2 %collective-permute-done.36 = bf16[208,384]{1,0:T(8,128)(2,1)S(1)} collective-permute-done((bf16[208,384]{1,0:T(8,128)(2,1)S(1)}, bf16[208,384]{1,0:T(8,128)(2,1)S(1)}, u32[]{:S(2)}, u32[]{:S(2)}) %collective-permute-start.36) | collective-permute-done | bytes 159776 | tf_op jit(solution)/shard_map/ppermute | solution.py:685
  244.6 12.0 %collective-permute-done.37 = bf16[208,768]{1,0:T(8,128)(2,1)S(1)} collective-permute-done((bf16[208,768]{1,0:T(8,128)(2,1)S(1)}, bf16[208,768]{1,0:T(8,128)(2,1)S(1)}, u32[]{:S(2)}, u32[]{:S(2)}) %collective-permute-start.37) | collective-permute-done | bytes 319520 | tf_op jit(solution)/shard_map/ppermute | solution.py:685
  256.9 4.0 %join_all.1 = (f32[192,2048]{1,0:T(8,128)}, f32[192,2048]{1,0:T(8,128)}, f32[512,768]{1,0:T(8,128)}) custom-call(bf16[4,2,576,256]{3,2,1,0:T(8,128)(2,1)} %bitcast.69), custom_call_target="tpu_custom_call" | custom-call | flops 1 | bytes 1 | tf_op jit(solution)/shard_map/join_all/pallas_call | solution.py:664
  260.9 1.5 join.1
  (166 shorter events, 23.6 us)
Async XLA Ops:
  7.2 74.4 %all-gather.5.cloned.1.call-start = ((), (), s32[]{:S(2)}) async-start(), calls=%async_computation.3 | async-start | bytes 5898240 | tf_op jit(solution)/shard_map/all_gather | solution.py:791
  10.1 167.2 %reduce-scatter.7.cloned.1.call-start = ((), (), s32[]{:S(2)}) async-start(), calls=%async_computation.5 | async-start | bytes 5898240
  14.2 27.3 %collective-permute-start = (bf16[208,1536]{1,0:T(8,128)(2,1)}, bf16[208,1536]{1,0:T(8,128)(2,1)S(1)}, u32[]{:S(2)}, u32[]{:S(2)}) collective-permute-start(bf16[208,1536]{1,0:T(8,128)(2,1)} %get-tuple-element.104.refs_11_), channel_id=1, source_target_pairs={{0,1},{1,0},{2,3},{3,2},{4,5},{5,4},{6,7},{7,6},{8,9},{9,8},{10,11... | collective-permute-start | bytes 1916936 | tf_op jit(solution)/shard_map/ppermute | solution.py:723
  17.2 27.2 %collective-permute-start.1 = (bf16[208,1536]{1,0:T(8,128)(2,1)}, bf16[208,1536]{1,0:T(8,128)(2,1)S(1)}, u32[]{:S(2)}, u32[]{:S(2)}) collective-permute-start(bf16[208,1536]{1,0:T(8,128)(2,1)} %get-tuple-element.104.refs_11_), channel_id=1, source_target_pairs={{0,2},{2,0},{1,3},{3,1},{4,6},{6,4},{5,7},{7,5},{8,10},{10,8},{9,1... | collective-permute-start | bytes 1916936 | tf_op jit(solution)/shard_map/ppermute | solution.py:724
  18.7 10.6 %collective-permute-start.5 = (bf16[144,768]{1,0:T(8,128)(2,1)}, bf16[144,768]{1,0:T(8,128)(2,1)S(1)}, u32[]{:S(2)}, u32[]{:S(2)}) collective-permute-start(bf16[144,768]{1,0:T(8,128)(2,1)} %get-tuple-element.111), channel_id=1, source_target_pairs={{0,24},{8,16},{16,8},{24,0},{1,25},{9,17},{17,9},{25,1},{2,26},{10... | collective-permute-start | bytes 663560 | tf_op jit(solution)/shard_map/ppermute | solution.py:685
  22.3 18.6 %collective-permute-start.4 = (bf16[144,768]{1,0:T(8,128)(2,1)}, bf16[144,768]{1,0:T(8,128)(2,1)}, u32[]{:S(2)}, u32[]{:S(2)}) collective-permute-start(bf16[144,768]{1,0:T(8,128)(2,1)} %get-tuple-element.109), channel_id=1, source_target_pairs={{0,16},{8,24},{16,0},{24,8},{1,17},{9,25},{17,1},{25,9},{2,18},{10... | collective-permute-start | bytes 663560 | tf_op jit(solution)/shard_map/ppermute | solution.py:685
  22.3 18.6 %collective-permute-start.3 = (bf16[144,768]{1,0:T(8,128)(2,1)}, bf16[144,768]{1,0:T(8,128)(2,1)}, u32[]{:S(2)}, u32[]{:S(2)}) collective-permute-start(bf16[144,768]{1,0:T(8,128)(2,1)} %get-tuple-element.107), channel_id=1, source_target_pairs={{0,8},{8,0},{16,24},{24,16},{1,9},{9,1},{17,25},{25,17},{2,10},{10... | collective-permute-start | bytes 663560 | tf_op jit(solution)/shard_map/ppermute | solution.py:685
  29.3 24.1 %copy-start.18 = (bf16[144,768]{1,0:T(8,128)(2,1)}, bf16[144,768]{1,0:T(8,128)(2,1)S(1)}, u32[]{:S(2)}) copy-start(bf16[144,768]{1,0:T(8,128)(2,1)S(1)} %collective-permute-done.5.refs_6_) | copy-start | bytes 663556
  29.3 25.0 %collective-permute-start.6 = (bf16[144,768]{1,0:T(8,128)(2,1)S(1)}, bf16[144,768]{1,0:T(8,128)(2,1)S(1)}, u32[]{:S(2)}, u32[]{:S(2)}) collective-permute-start(bf16[144,768]{1,0:T(8,128)(2,1)S(1)} %copy-done.17), channel_id=1, source_target_pairs={{0,4},{4,0},{1,5},{5,1},{2,6},{6,2},{3,7},{7,3},{8,12},{12,8},{9,1... | collective-permute-start | bytes 663560 | tf_op jit(solution)/shard_map/ppermute | solution.py:699
  40.8 17.1 %collective-permute-start.9 = (bf16[144,768]{1,0:T(8,128)(2,1)S(1)}, bf16[144,768]{1,0:T(8,128)(2,1)}, u32[]{:S(2)}, u32[]{:S(2)}) collective-permute-start(bf16[144,768]{1,0:T(8,128)(2,1)S(1)} %collective-permute-done.5.refs_6_), channel_id=1, source_target_pairs={{0,4},{4,0},{1,5},{5,1},{2,6},{6,2},{3,7},{7,3},{8,12},{12,8},{9,1... | collective-permute-start | bytes 663560 | tf_op jit(solution)/shard_map/ppermute | solution.py:699
  40.9 17.1 %collective-permute-start.8 = (bf16[144,768]{1,0:T(8,128)(2,1)}, bf16[144,768]{1,0:T(8,128)(2,1)}, u32[]{:S(2)}, u32[]{:S(2)}) collective-permute-start(bf16[144,768]{1,0:T(8,128)(2,1)} %collective-permute-done.4.refs_5_), channel_id=1, source_target_pairs={{0,4},{4,0},{1,5},{5,1},{2,6},{6,2},{3,7},{7,3},{8,12},{12,8},{9,1... | collective-permute-start | bytes 663560 | tf_op jit(solution)/shard_map/ppermute | solution.py:699
  41.5 11.8 %copy-start.10 = (bf16[208,1536]{1,0:T(8,128)(2,1)}, bf16[208,1536]{1,0:T(8,128)(2,1)S(1)}, u32[]{:S(2)}) copy-start(bf16[208,1536]{1,0:T(8,128)(2,1)S(1)} %collective-permute-done.refs_12_) | copy-start | bytes 1916932
  41.6 11.7 %collective-permute-start.2 = (bf16[112,1536]{1,0:T(8,128)(2,1)S(1)}, bf16[112,1536]{1,0:T(8,128)(2,1)S(1)}, u32[]{:S(2)}, u32[]{:S(2)}) collective-permute-start(bf16[112,1536]{1,0:T(8,128)(2,1)S(1)} %slice.96), channel_id=1, source_target_pairs={{0,2},{2,0},{1,3},{3,1},{4,6},{6,4},{5,7},{7,5},{8,10},{10,8},{9,1... | collective-permute-start | bytes 1032200 | tf_op jit(solution)/shard_map/ppermute | solution.py:726
  44.4 8.9 %collective-permute-start.10 = (bf16[96,1536]{1,0:T(8,128)(2,1)S(1)}, bf16[96,1536]{1,0:T(8,128)(2,1)S(1)}, u32[]{:S(2)}, u32[]{:S(2)}) collective-permute-start(bf16[96,1536]{1,0:T(8,128)(2,1)S(1)} %slice.99), channel_id=1, source_target_pairs={{0,1},{1,0},{2,3},{3,2},{4,5},{5,4},{6,7},{7,6},{8,9},{9,8},{10,11... | collective-permute-start | bytes 884744 | tf_op jit(solution)/shard_map/ppermute | solution.py:725
  53.2 6.0 %collective-permute-start.7 = (bf16[144,768]{1,0:T(8,128)(2,1)}, bf16[144,768]{1,0:T(8,128)(2,1)}, u32[]{:S(2)}, u32[]{:S(2)}) collective-permute-start(bf16[144,768]{1,0:T(8,128)(2,1)} %collective-permute-done.3.refs_4_), channel_id=1, source_target_pairs={{0,4},{4,0},{1,5},{5,1},{2,6},{6,2},{3,7},{7,3},{8,12},{12,8},{9,1... | collective-permute-start | bytes 663560 | tf_op jit(solution)/shard_map/ppermute | solution.py:699
  53.4 21.6 %collective-permute-start.14 = (bf16[384,384]{1,0:T(8,128)(2,1)S(1)}, bf16[384,384]{1,0:T(8,128)(2,1)S(1)}, u32[]{:S(2)}, u32[]{:S(2)}) collective-permute-start(bf16[384,384]{1,0:T(8,128)(2,1)S(1)} %get-tuple-element.203), channel_id=1, source_target_pairs={{0,4},{4,0},{1,5},{5,1},{2,6},{6,2},{3,7},{7,3},{8,12},{12,8},{9,1... | collective-permute-start | bytes 884744 | tf_op jit(solution)/shard_map/ppermute | solution.py:835
  54.2 20.1 %collective-permute-start.13 = (bf16[128,768]{1,0:T(8,128)(2,1)}, bf16[128,768]{1,0:T(8,128)(2,1)S(1)}, u32[]{:S(2)}, u32[]{:S(2)}) collective-permute-start(bf16[128,768]{1,0:T(8,128)(2,1)} %get-tuple-element.119), channel_id=1, source_target_pairs={{0,24},{8,16},{16,8},{24,0},{1,25},{9,17},{17,9},{25,1},{2,26},{10... | collective-permute-start | bytes 589832 | tf_op jit(solution)/shard_map/ppermute | solution.py:685
  57.9 17.1 %collective-permute-start.12 = (bf16[128,768]{1,0:T(8,128)(2,1)}, bf16[128,768]{1,0:T(8,128)(2,1)S(1)}, u32[]{:S(2)}, u32[]{:S(2)}) collective-permute-start(bf16[128,768]{1,0:T(8,128)(2,1)} %get-tuple-element.117), channel_id=1, source_target_pairs={{0,16},{8,24},{16,0},{24,8},{1,17},{9,25},{17,1},{25,9},{2,18},{10... | collective-permute-start | bytes 589832 | tf_op jit(solution)/shard_map/ppermute | solution.py:685
  57.9 17.1 %collective-permute-start.11 = (bf16[128,768]{1,0:T(8,128)(2,1)}, bf16[128,768]{1,0:T(8,128)(2,1)S(1)}, u32[]{:S(2)}, u32[]{:S(2)}) collective-permute-start(bf16[128,768]{1,0:T(8,128)(2,1)} %get-tuple-element.115), channel_id=1, source_target_pairs={{0,8},{8,0},{16,24},{24,16},{1,9},{9,1},{17,25},{25,17},{2,10},{10... | collective-permute-start | bytes 589832 | tf_op jit(solution)/shard_map/ppermute | solution.py:685
  77.5 3.6 %collective-permute-start.15 = (bf16[1024,768]{1,0:T(8,128)(2,1)S(1)}, bf16[1024,768]{1,0:T(8,128)(2,1)}, u32[]{:S(2)}, u32[]{:S(2)}) collective-permute-start(bf16[1024,768]{1,0:T(8,128)(2,1)S(1)} %convolution_convert_fusion.2.refs_1_), channel_id=1, source_target_pairs={{0,4},{4,0},{1,5},{5,1},{2,6},{6,2},{3,7},{7,3},{8,12},{12,8},{9,1... | collective-permute-start | bytes 4718600 | tf_op jit(solution)/shard_map/ppermute | solution.py:713
  81.5 12.1 %copy-start.4 = (bf16[128,768]{1,0:T(8,128)(2,1)S(1)}, bf16[128,768]{1,0:T(8,128)(2,1)}, u32[]{:S(2)}) copy-start(bf16[128,768]{1,0:T(8,128)(2,1)} %copy-done.3) | copy-start | bytes 589828
  93.0 4.6 %collective-permute-start.16 = (bf16[1024,768]{1,0:T(8,128)(2,1)S(1)}, bf16[1024,768]{1,0:T(8,128)(2,1)S(1)}, u32[]{:S(2)}, u32[]{:S(2)}) collective-permute-start(bf16[1024,768]{1,0:T(8,128)(2,1)S(1)} %get-tuple-element.124.refs_2_), channel_id=1, source_target_pairs={{0,4},{4,0},{1,5},{5,1},{2,6},{6,2},{3,7},{7,3},{8,12},{12,8},{9,1... | collective-permute-start | bytes 4718600 | tf_op jit(solution)/shard_map/ppermute | solution.py:713
  93.1 3.7 %collective-permute-start.17 = (bf16[128,768]{1,0:T(8,128)(2,1)S(1)}, bf16[128,768]{1,0:T(8,128)(2,1)S(1)}, u32[]{:S(2)}, u32[]{:S(2)}) collective-permute-start(bf16[128,768]{1,0:T(8,128)(2,1)S(1)} %copy-done.2), channel_id=1, source_target_pairs={{0,4},{4,0},{1,5},{5,1},{2,6},{6,2},{3,7},{7,3},{8,12},{12,8},{9,1... | collective-permute-start | bytes 589832 | tf_op jit(solution)/shard_map/ppermute | solution.py:699
  93.6 3.5 %collective-permute-start.18 = (bf16[128,768]{1,0:T(8,128)(2,1)S(1)}, bf16[128,768]{1,0:T(8,128)(2,1)S(1)}, u32[]{:S(2)}, u32[]{:S(2)}) collective-permute-start(bf16[128,768]{1,0:T(8,128)(2,1)S(1)} %copy-done.4), channel_id=1, source_target_pairs={{0,4},{4,0},{1,5},{5,1},{2,6},{6,2},{3,7},{7,3},{8,12},{12,8},{9,1... | collective-permute-start | bytes 589832 | tf_op jit(solution)/shard_map/ppermute | solution.py:699
  93.7 3.7 %collective-permute-start.19 = (bf16[128,768]{1,0:T(8,128)(2,1)S(1)}, bf16[128,768]{1,0:T(8,128)(2,1)S(1)}, u32[]{:S(2)}, u32[]{:S(2)}) collective-permute-start(bf16[128,768]{1,0:T(8,128)(2,1)S(1)} %collective-permute-done.12.refs_11_), channel_id=1, source_target_pairs={{0,4},{4,0},{1,5},{5,1},{2,6},{6,2},{3,7},{7,3},{8,12},{12,8},{9,1... | collective-permute-start | bytes 589832 | tf_op jit(solution)/shard_map/ppermute | solution.py:699
  94.1 3.5 %collective-permute-start.20 = (bf16[128,768]{1,0:T(8,128)(2,1)S(1)}, bf16[128,768]{1,0:T(8,128)(2,1)S(1)}, u32[]{:S(2)}, u32[]{:S(2)}) collective-permute-start(bf16[128,768]{1,0:T(8,128)(2,1)S(1)} %collective-permute-done.13.refs_12_), channel_id=1, source_target_pairs={{0,4},{4,0},{1,5},{5,1},{2,6},{6,2},{3,7},{7,3},{8,12},{12,8},{9,1... | collective-permute-start | bytes 589832 | tf_op jit(solution)/shard_map/ppermute | solution.py:699
  109.4 6.0 %collective-permute-start.24 = (bf16[1024,768]{1,0:T(8,128)(2,1)}, bf16[1024,768]{1,0:T(8,128)(2,1)}, u32[]{:S(2)}, u32[]{:S(2)}) collective-permute-start(bf16[1024,768]{1,0:T(8,128)(2,1)} %get-tuple-element.144.own_ref), channel_id=1, source_target_pairs={{0,4},{4,0},{1,5},{5,1},{2,6},{6,2},{3,7},{7,3},{8,12},{12,8},{9,1... | collective-permute-start | bytes 4718600 | tf_op jit(solution)/shard_map/ppermute | solution.py:713
  118.1 97.7 %reduce-scatter.5.cloned.1.call-start = ((), (), s32[]{:S(2)}) async-start(), calls=%async_computation.2 | async-start | bytes 1474560 | tf_op jit(solution)/shard_map/reduce_scatter | solution.py:914
  125.2 4.8 %collective-permute-start.25 = (bf16[384,384]{1,0:T(8,128)(2,1)S(1)}, bf16[384,384]{1,0:T(8,128)(2,1)S(1)}, u32[]{:S(2)}, u32[]{:S(2)}) collective-permute-start(bf16[384,384]{1,0:T(8,128)(2,1)S(1)} %get-tuple-element.201), channel_id=1, source_target_pairs={{0,4},{4,0},{1,5},{5,1},{2,6},{6,2},{3,7},{7,3},{8,12},{12,8},{9,1... | collective-permute-start | bytes 884744 | tf_op jit(solution)/shard_map/ppermute | solution.py:876
  125.6 18.5 %collective-permute-start.21 = (bf16[128,768]{1,0:T(8,128)(2,1)S(1)}, bf16[128,768]{1,0:T(8,128)(2,1)S(1)}, u32[]{:S(2)}, u32[]{:S(2)}) collective-permute-start(bf16[128,768]{1,0:T(8,128)(2,1)S(1)} %copy-done.23), channel_id=1, source_target_pairs={{0,8},{8,0},{16,24},{24,16},{1,9},{9,1},{17,25},{25,17},{2,10},{10... | collective-permute-start | bytes 589832 | tf_op jit(solution)/shard_map/ppermute | solution.py:685
  127.1 17.1 %collective-permute-start.22 = (bf16[128,768]{1,0:T(8,128)(2,1)S(1)}, bf16[128,768]{1,0:T(8,128)(2,1)S(1)}, u32[]{:S(2)}, u32[]{:S(2)}) collective-permute-start(bf16[128,768]{1,0:T(8,128)(2,1)S(1)} %copy-done.22), channel_id=1, source_target_pairs={{0,16},{8,24},{16,0},{24,8},{1,17},{9,25},{17,1},{25,9},{2,18},{10... | collective-permute-start | bytes 589832 | tf_op jit(solution)/shard_map/ppermute | solution.py:685
  129.5 14.7 %collective-permute-start.23 = (bf16[128,768]{1,0:T(8,128)(2,1)S(1)}, bf16[128,768]{1,0:T(8,128)(2,1)S(1)}, u32[]{:S(2)}, u32[]{:S(2)}) collective-permute-start(bf16[128,768]{1,0:T(8,128)(2,1)S(1)} %copy-done.21), channel_id=1, source_target_pairs={{0,24},{8,16},{16,8},{24,0},{1,25},{9,17},{17,9},{25,1},{2,26},{10... | collective-permute-start | bytes 589832 | tf_op jit(solution)/shard_map/ppermute | solution.py:685
  130.2 14.0 %copy-start.12 = (bf16[1024,768]{1,0:T(8,128)(2,1)S(1)}, bf16[1024,768]{1,0:T(8,128)(2,1)}, u32[]{:S(2)}) copy-start(bf16[1024,768]{1,0:T(8,128)(2,1)} %get-tuple-element.113.refs_0_) | copy-start | bytes 4718596
  148.1 13.4 %collective-permute-start.30 = (bf16[112,1536]{1,0:T(8,128)(2,1)S(1)}, bf16[112,1536]{1,0:T(8,128)(2,1)S(1)}, u32[]{:S(2)}, u32[]{:S(2)}) collective-permute-start(bf16[112,1536]{1,0:T(8,128)(2,1)S(1)} %slice_bitcast_fusion.1), channel_id=1, source_target_pairs={{0,2},{2,0},{1,3},{3,1},{4,6},{6,4},{5,7},{7,5},{8,10},{10,8},{9,1... | collective-permute-start | bytes 1032200 | tf_op jit(solution)/shard_map/ppermute | solution.py:741
  152.0 2.4 collective-permute-start.26
  152.1 9.5 %collective-permute-start.29 = (bf16[96,1536]{1,0:T(8,128)(2,1)S(1)}, bf16[96,1536]{1,0:T(8,128)(2,1)S(1)}, u32[]{:S(2)}, u32[]{:S(2)}) collective-permute-start(bf16[96,1536]{1,0:T(8,128)(2,1)S(1)} %slice_bitcast_fusion.4), channel_id=1, source_target_pairs={{0,1},{1,0},{2,3},{3,2},{4,5},{5,4},{6,7},{7,6},{8,9},{9,8},{10,11... | collective-permute-start | bytes 884744 | tf_op jit(solution)/shard_map/ppermute | solution.py:741
  155.1 13.0 %collective-permute-start.27 = (bf16[128,768]{1,0:T(8,128)(2,1)S(1)}, bf16[128,768]{1,0:T(8,128)(2,1)S(1)}, u32[]{:S(2)}, u32[]{:S(2)}) collective-permute-start(bf16[128,768]{1,0:T(8,128)(2,1)S(1)} %get-tuple-element.162), channel_id=1, source_target_pairs={{0,8},{8,0},{16,24},{24,16},{1,9},{9,1},{17,25},{25,17},{2,10},{10... | collective-permute-start | bytes 589832 | tf_op jit(solution)/shard_map/ppermute | solution.py:685
  158.9 11.8 %collective-permute-start.28 = (bf16[128,768]{1,0:T(8,128)(2,1)S(1)}, bf16[128,768]{1,0:T(8,128)(2,1)S(1)}, u32[]{:S(2)}, u32[]{:S(2)}) collective-permute-start(bf16[128,768]{1,0:T(8,128)(2,1)S(1)} %get-tuple-element.163), channel_id=1, source_target_pairs={{0,16},{8,24},{16,0},{24,8},{1,17},{9,25},{17,1},{25,9},{2,18},{10... | collective-permute-start | bytes 589832 | tf_op jit(solution)/shard_map/ppermute | solution.py:685
  170.8 11.9 %copy-start.5 = (bf16[128,768]{1,0:T(8,128)(2,1)S(1)}, bf16[128,768]{1,0:T(8,128)(2,1)}, u32[]{:S(2)}) copy-start(bf16[128,768]{1,0:T(8,128)(2,1)} %get-tuple-element.166.refs_0_) | copy-start | bytes 589828
  177.3 79.6 %all-gather.7.cloned.1.call-start = ((), (), s32[]{:S(2)}) async-start(), calls=%async_computation.4 | async-start | bytes 2654208 | tf_op jit(solution)/shard_map/all_gather | solution.py:917
  177.3 16.2 %collective-permute-start.32 = (bf16[208,1536]{1,0:T(8,128)(2,1)S(1)}, bf16[208,1536]{1,0:T(8,128)(2,1)S(1)}, u32[]{:S(2)}, u32[]{:S(2)}) collective-permute-start(bf16[208,1536]{1,0:T(8,128)(2,1)S(1)} %pad_maximum_fusion.3), channel_id=1, source_target_pairs={{0,2},{2,0},{1,3},{3,1},{4,6},{6,4},{5,7},{7,5},{8,10},{10,8},{9,1... | collective-permute-start | bytes 1916936 | tf_op jit(solution)/shard_map/ppermute | solution.py:750
  178.8 16.2 %collective-permute-start.31 = (bf16[208,1536]{1,0:T(8,128)(2,1)}, bf16[208,1536]{1,0:T(8,128)(2,1)}, u32[]{:S(2)}, u32[]{:S(2)}) collective-permute-start(bf16[208,1536]{1,0:T(8,128)(2,1)} %pad_maximum_fusion.2), channel_id=1, source_target_pairs={{0,1},{1,0},{2,3},{3,2},{4,5},{5,4},{6,7},{7,6},{8,9},{9,8},{10,11... | collective-permute-start | bytes 1916936 | tf_op jit(solution)/shard_map/ppermute | solution.py:750
  179.4 8.8 %collective-permute-start.33 = (bf16[128,768]{1,0:T(8,128)(2,1)S(1)}, bf16[128,768]{1,0:T(8,128)(2,1)S(1)}, u32[]{:S(2)}, u32[]{:S(2)}) collective-permute-start(bf16[128,768]{1,0:T(8,128)(2,1)S(1)} %get-tuple-element.170), channel_id=1, source_target_pairs={{0,24},{8,16},{16,8},{24,0},{1,25},{9,17},{17,9},{25,1},{2,26},{10... | collective-permute-start | bytes 589832 | tf_op jit(solution)/shard_map/ppermute | solution.py:685
  196.5 19.3 %collective-permute-start.34 = (bf16[208,768]{1,0:T(8,128)(2,1)S(1)}, bf16[208,768]{1,0:T(8,128)(2,1)S(1)}, u32[]{:S(2)}, u32[]{:S(2)}) collective-permute-start(bf16[208,768]{1,0:T(8,128)(2,1)S(1)} %constant_dynamic-slice_fusion.1), channel_id=1, source_target_pairs={{0,8},{8,0},{16,24},{24,16},{1,9},{9,1},{17,25},{25,17},{2,10},{10... | collective-permute-start | bytes 958472 | tf_op jit(solution)/shard_map/ppermute | solution.py:685
  216.0 9.1 %collective-permute-start.35 = (bf16[208,384]{1,0:T(8,128)(2,1)S(1)}, bf16[208,384]{1,0:T(8,128)(2,1)S(1)}, u32[]{:S(2)}, u32[]{:S(2)}) collective-permute-start(bf16[208,384]{1,0:T(8,128)(2,1)S(1)} %constant_dynamic-slice_fusion), channel_id=1, source_target_pairs={{0,16},{8,24},{16,0},{24,8},{1,17},{9,25},{17,1},{25,9},{2,18},{10... | collective-permute-start | bytes 479240 | tf_op jit(solution)/shard_map/ppermute | solution.py:685
  225.2 19.3 %collective-permute-start.36 = (bf16[208,384]{1,0:T(8,128)(2,1)S(1)}, bf16[208,384]{1,0:T(8,128)(2,1)S(1)}, u32[]{:S(2)}, u32[]{:S(2)}) collective-permute-start(bf16[208,384]{1,0:T(8,128)(2,1)S(1)} %add_convert_fusion.1), channel_id=1, source_target_pairs={{0,16},{8,24},{16,0},{24,8},{1,17},{9,25},{17,1},{25,9},{2,18},{10... | collective-permute-start | bytes 479240 | tf_op jit(solution)/shard_map/ppermute | solution.py:685
  244.5 12.1 %collective-permute-start.37 = (bf16[208,768]{1,0:T(8,128)(2,1)S(1)}, bf16[208,768]{1,0:T(8,128)(2,1)S(1)}, u32[]{:S(2)}, u32[]{:S(2)}) collective-permute-start(bf16[208,768]{1,0:T(8,128)(2,1)S(1)} %pad_maximum_fusion.7), channel_id=1, source_target_pairs={{0,8},{8,0},{16,24},{24,16},{1,9},{9,1},{17,25},{25,17},{2,10},{10... | collective-permute-start | bytes 958472 | tf_op jit(solution)/shard_map/ppermute | solution.py:685
  256.8 4.1 %collective-permute-start.38 = (bf16[208,1536]{1,0:T(8,128)(2,1)S(1)}, bf16[208,1536]{1,0:T(8,128)(2,1)S(1)}, u32[]{:S(2)}, u32[]{:S(2)}) collective-permute-start(bf16[208,1536]{1,0:T(8,128)(2,1)S(1)} %pad_maximum_fusion.4.refs_1_), channel_id=1, source_target_pairs={{0,4},{4,0},{1,5},{5,1},{2,6},{6,2},{3,7},{7,3},{8,12},{12,8},{9,1... | collective-permute-start | bytes 1916936 | tf_op jit(solution)/shard_map/ppermute | solution.py:951
  (21 other events, 84.5 us)
Sparse Core Ops, SparseCore 0:
  10.4 71.0 all-gather.4
  118.2 58.9 reduce-scatter.6
  179.6 33.7 reduce-scatter.4
  216.0 37.0 all-gather.6

commit v4 on v3

--- a/solution.py
+++ b/solution.py
@@ -77,7 +77,7 @@
     for n, ref in enumerate(refs):
         rank = where_ref[2] if n < groups else 1 - where_ref[2]
         chunk = (where_ref[1] ^ (n % groups)) * ranks + rank
-        row = ref[span:span + 16, 0:span].astype(F32)[0:1, :]
+        row = ref[span:span + 8, 0:span].astype(F32)[0:1, :]
         target[:, pl.ds(pl.multiple_of(chunk * span, span), span)] = row
 
 
@@ -345,11 +345,11 @@
     def _():
         out_ref[...] = jnp.zeros_like(out_ref)
         shard = gain_ref.shape[1] // out_ref.shape[0]
-        first = lax.broadcasted_iota(jnp.int32, (16, shard), 0)
+        first = lax.broadcasted_iota(jnp.int32, (8, shard), 0)
         for j in range(out_ref.shape[0]):
             lanes = slice(j * shard, (j + 1) * shard)
-            one = jnp.broadcast_to(gain_grad_ref[:, lanes], (16, shard))
-            two = jnp.broadcast_to(other_ref[:, lanes], (16, shard))
+            one = jnp.broadcast_to(gain_grad_ref[:, lanes], (8, shard))
+            two = jnp.broadcast_to(other_ref[:, lanes], (8, shard))
             out_ref[j, :, 0:shard] = jnp.where(
                 first == 0, one, jnp.where(first == 1, two, 0.0)).astype(BF)
 
@@ -363,10 +363,10 @@
         grid=(tokens // block,),
         in_specs=[SMEM_SPEC, VMEM_SPEC, row, row, row] + whole_specs(gain, other_grad),
         out_specs=[VMEM_SPEC, pl.BlockSpec((1, span, width), lambda i: (i, 0, 0)),
-                   pl.BlockSpec((fsdp, 16, cols), lambda i: (0, 0, 0))],
+                   pl.BlockSpec((fsdp, 8, cols), lambda i: (0, 0, 0))],
         out_shape=[pltpu.VMEM((tokens, width), BF),
                    pltpu.HBM((tokens // block, span, width), F32),
-                   pltpu.HBM((fsdp, 16, cols), BF)],
+                   pltpu.HBM((fsdp, 8, cols), BF)],
         scratch_shapes=[pltpu.VMEM((block, width), F32), pltpu.VMEM((1, width), F32)],
         compiler_params=pltpu.CompilerParams(vmem_limit_bytes=16 << 20),
         cost_estimate=SMALL_COST,
@@ -406,7 +406,7 @@
         ref[0:span, :] = tokens_ref[m ^ k, 0]
         ref[span:, :] = jnp.zeros_like(ref[span:, :])
         row = seg_ref[pl.ds(m ^ k, 1), :].astype(F32)
-        ref[span:, 0:span] = jnp.broadcast_to(row, (16, span)).astype(BF)
+        ref[span:, 0:span] = jnp.broadcast_to(row, (8, span)).astype(BF)
 
 
 def pack_small(where, query, key, value, out, gains, tokens, segments, cot, ranks, lanes,
@@ -415,7 +415,7 @@
     groups, _, span, _ = tokens.shape
     cols = 3 * lanes_all + width // ranks
     inputs = hbm(query, key, value, out, gains, tokens, segments, cot)
-    shapes = [(shard + 16, cols)] + [(span + 16, width)] * groups + [(span, width)] * groups
+    shapes = [(shard + 8, cols)] + [(span + 8, width)] * groups + [(span, width)] * groups
     return pl.pallas_call(
         lambda *refs: pack_small_kernel(*refs, ranks=ranks, lanes=lanes, lanes_all=lanes_all),
         grid=(1,),
@@ -465,30 +465,42 @@
     )(where, *inputs)
 
 
-def arrange_kernel(gu_ref, down_ref, out_ref):
-    shard, part = gu_ref.shape[0], down_ref.shape[0]
+def arrange_kernel(gu_ref, hidden_ref, grad_ref, out_ref, down, sems):
+    fsdp = out_ref.shape[0]
+    shard, part = gu_ref.shape[0] // fsdp, hidden_ref.shape[1] // fsdp
     chunks = gu_ref.shape[1] // 256
+    copies = []
+
+    def send(source, j, low, rows):
+        copies.append(pltpu.make_async_copy(
+            source, out_ref.at[j, low:low + rows, :], sems.at[len(copies)]))
+        copies[-1].start()
+
     for c in range(chunks):
-        out_ref[0, c * shard:(c + 1) * shard, :] = gu_ref[:, c * 256:(c + 1) * 256]
-    for c in range(down_ref.shape[1] // 256):
-        at = chunks * shard + c * part
-        out_ref[0, at:at + part, :] = down_ref[:, c * 256:(c + 1) * 256]
-
-
-def arrange(gu, down, fsdp):
-    shard, part = gu.shape[0] // fsdp, down.shape[0] // fsdp
-    rows = gu.shape[1] // 256 * shard + down.shape[1] // 256 * part
+        for j in range(fsdp):
+            send(gu_ref.at[j * shard:(j + 1) * shard, c * 256:(c + 1) * 256], j, c * shard, shard)
+    for c in range(grad_ref.shape[1] // 256):
+        down[c] = dot(hidden_ref[...], grad_ref[:, c * 256:(c + 1) * 256], ((0,), (0,))).astype(BF)
+        for j in range(fsdp):
+            send(down.at[c, j * part:(j + 1) * part, :], j, chunks * shard + c * part, part)
+    for copy in copies:
+        copy.wait()
+
+
+def arrange(gu, hidden, grad, fsdp):
+    shard, ff, width = gu.shape[0] // fsdp, hidden.shape[1], grad.shape[1]
+    rows = gu.shape[1] // 256 * shard + width // 256 * (ff // fsdp)
     return pl.pallas_call(
         arrange_kernel,
-        grid=(fsdp,),
-        in_specs=[pl.BlockSpec((shard, gu.shape[1]), lambda j: (j, 0)),
-                  pl.BlockSpec((part, down.shape[1]), lambda j: (j, 0))],
-        out_specs=pl.BlockSpec((1, rows, 256), lambda j: (j, 0, 0)),
+        in_specs=[VMEM_SPEC] * 3,
+        out_specs=HBM_SPEC,
         out_shape=pltpu.HBM((fsdp, rows, 256), BF),
-        compiler_params=pltpu.CompilerParams(vmem_limit_bytes=24 << 20),
+        scratch_shapes=[pltpu.VMEM((width // 256, ff, 256), BF),
+                        pltpu.SemaphoreType.DMA(((gu.shape[1] + width) // 256 * fsdp,))],
+        compiler_params=pltpu.CompilerParams(vmem_limit_bytes=16 << 20),
         cost_estimate=SMALL_COST,
         name="arrange",
-    )(gu, down)
+    )(*vmem(gu, hidden, grad))
 
 
 def finish_kernel(where_ref, keep_ref, part_ref, got_ref, *out_refs, ranks):
@@ -786,7 +798,7 @@
             at.astype(jnp.uint32) for at in (rank * own_cols, (1 - rank) * own_cols, 1 - rank))
         where = jnp.stack([f_index, lax.axis_index("m"), rank])
         small_cols = 3 * lanes_all + own_cols
-        gains_in = jnp.pad(jnp.stack([gain_attn, gain_ffn]), ((0, 14), (0, 0)))
+        gains_in = jnp.pad(jnp.stack([gain_attn, gain_ffn]), ((0, 6), (0, 0)))
         stack_own = pack(where, w_gate, w_up, w_down, fsdp, ranks)
         stack_all = lax.all_gather(stack_own, F, axis=0)
         cosine, sine = rotary_tables(seq_tokens, head_size, 2)
@@ -823,7 +835,7 @@
             small_pieces = [(o, f, min(n, shard - f)) for o, f, n in small_pieces]
             qkv_refs = small_refs
         else:
-            whole = small_refs[0].reshape(fsdp, shard + 16, small_cols)
+            whole = small_refs[0].reshape(fsdp, shard + 8, small_cols)
             gains = whole[:, shard:shard + 2, :shard].transpose(1, 0, 2).reshape(2, width)
             out_cols = whole[:, :shard, 3 * lanes_all:].reshape(width, own_cols)
             qkv_refs = [whole[:, :shard, :3 * lanes_all].reshape(width, 3 * lanes_all)]
@@ -862,8 +874,7 @@
         gu_w_grad = dot(middle_low, gu_grad_low, ((0,), (0,))).astype(BF)
         if ranks == 2:
             got, gu_w_grad = lax.optimization_barrier((got, gu_w_grad))
-        down_w_grad = dot(hidden_low, ffn_grad_low, ((0,), (0,))).astype(BF)
-        stack_grad = arrange(gu_w_grad, down_w_grad, fsdp)
+        stack_grad = arrange(gu_w_grad, hidden_low, ffn_grad_low, fsdp)
         stack_owned = lax.psum_scatter(stack_grad, F, scatter_dimension=0, tiled=False)
         own, got = after(own, stack_grad), after(got, stack_grad)
         branch_grad_low, branch_keep, gain_grads = norm_back(

time: 269 us -> 268 us (level)
    dot_general x6 -> x5, matrix products: 13.5 us -> 11.6 us  [dot(): lax.dot_general(left, right, (dims, ((), ())), preferred_element_type=F32)]
  transfers between devices with their start and end apart: 43 -> 43, of which waited for: 24 -> 24; matrix products, arithmetic and copies ran while one was open for 9% -> 8% of each run, Pallas kernels for 17% -> 17%
where the time goes in v4:
time: 268 us
  waiting for transfers between devices  108 us (40%)
  Pallas kernels  76.6 us (29%)
  starting transfers between devices  43.6 us (16%)
  between operations  14.5 us (5%)
  matrix products  11.6 us (4%)
  other arithmetic  8.12 us (3%)
  local copies, waits for them, and re-layouts  4.76 us (2%)
    ppermute x16, waiting for transfers between devices, hop(): return lax.ppermute(value, 'm', [(i, i ^ k) for i in range(groups)])  75.3 us
    ppermute x16, starting transfers between devices, hop(): return lax.ppermute(value, 'm', [(i, i ^ k) for i in range(groups)])  28.9 us
    pallas_call x1, Pallas kernels, attend(): pl.pallas_call(kernel, grid=(pairs,), in_specs=[SMEM_SPEC] + whole_specs(...  15 us
    pallas_call x1, Pallas kernels, attend_back(): pl.pallas_call(kernel, grid=(pairs,), in_specs=whole_specs(seg) + [VMEM_S...  13.9 us
    pallas_call x1, Pallas kernels, backward(): pl.pallas_call(kernel, grid=(tokens // block,), in_specs=[SMEM_SPEC, VMEM...  11.8 us
    dot_general x5, matrix products, dot(): lax.dot_general(left, right, (dims, ((), ())), preferred_element_type=F32)  11.6 us
    pallas_call x1, Pallas kernels, forward(): pl.pallas_call(lambda *refs: forward_kernel(*refs, shard=shard, part_rows...  11.5 us
    ppermute x1, waiting for transfers between devices, gather_rows(): far_b = lax.ppermute(from_x[rows:], 'y', swap)  7.71 us
  transfers between devices with their start and end apart: 43, of which 24 were waited for; matrix products, arithmetic and copies ran while one was open for 8% of the time, Pallas kernels for 17%

profile of v4, /device:TPU:0, one launch (start us, length us, event | category | flops | bytes accessed | tf_op | source)
XLA Modules:
  0.0 267.5 jit_solution(7394551813491304684)
XLA Ops:
  7.3 2.8 %pack.1 = bf16[2304,256]{1,0:T(8,128)(2,1)} custom-call(s32[3]{0:T(128)S(1)} %pad_add_fusion.refs_0_.where_ref, bf16[192,2048]{1,0:T(8,128)(2,1)} %refs_1_.2, bf16[192,2048]{1,0:T(8,128)(2,1)} %refs_2_.2, bf16[512,768]{1,0:T(8,128)(2,1)} %refs_3_.2), custom_call_target="tpu_custom_call" | custom-call | flops 1 | bytes 1 | tf_op jit(solution)/shard_map/pack/pallas_call | solution.py:455
  10.8 3.4 %pack_small.1 = (bf16[200,1536]{1,0:T(8,128)(2,1)}, bf16[136,768]{1,0:T(8,128)(2,1)}, bf16[136,768]{1,0:T(8,128)(2,1)}, bf16[136,768]{1,0:T(8,128)(2,1)}, bf16[1...) custom-call(s32[3]{0:T(128)S(1)} %pad_add_fusion.refs_0_.where_ref, ...), custom_call_target="tpu_custom_call" | custom-call | flops 1 | bytes 1 | tf_op jit(solution)/shard_map/pack_small/pallas_call | solution.py:419
  14.2 3.0 %collective-permute-start = (bf16[200,1536]{1,0:T(8,128)(2,1)}, bf16[200,1536]{1,0:T(8,128)(2,1)S(1)}, u32[]{:S(2)}, u32[]{:S(2)}) collective-permute-start(bf16[200,1536]{1,0:T(8,128)(2,1)} %get-tuple-element.104.refs_11_), channel_id=1, source_target_pairs={{0,1},{1,0},{2,3},{3,2},{4,5},{5,4},{6,7},{7,6},{8,9},{9,8},{10,11... | collective-permute-start | bytes 1843208 | tf_op jit(solution)/shard_map/ppermute | solution.py:735
  17.1 1.5 collective-permute-start.1
  18.7 3.6 %collective-permute-start.5 = (bf16[136,768]{1,0:T(8,128)(2,1)}, bf16[136,768]{1,0:T(8,128)(2,1)}, u32[]{:S(2)}, u32[]{:S(2)}) collective-permute-start(bf16[136,768]{1,0:T(8,128)(2,1)} %get-tuple-element.111), channel_id=1, source_target_pairs={{0,24},{8,16},{16,8},{24,0},{1,25},{9,17},{17,9},{25,1},{2,26},{10... | collective-permute-start | bytes 626696 | tf_op jit(solution)/shard_map/ppermute | solution.py:697
  23.1 1.9 fusion.9
  25.0 1.3 pad_maximum_fusion.5.refs_1_.refs_8_
  29.2 10.5 %collective-permute-done.4.refs_5_ = bf16[136,768]{1,0:T(8,128)(2,1)} collective-permute-done((bf16[136,768]{1,0:T(8,128)(2,1)}, bf16[136,768]{1,0:T(8,128)(2,1)}, u32[]{:S(2)}, u32[]{:S(2)}) %collective-permute-start.4) | collective-permute-done | bytes 208928 | tf_op jit(solution)/shard_map/ppermute | solution.py:697
  40.4 1.4 collective-permute-start.2
  41.8 1.4 collective-permute-done.1.refs_13_
  44.4 7.7 %collective-permute-done.2.refs_15_ = bf16[104,1536]{1,0:T(8,128)(2,1)S(1)} collective-permute-done((bf16[104,1536]{1,0:T(8,128)(2,1)S(1)}, bf16[104,1536]{1,0:T(8,128)(2,1)S(1)}, u32[]{:S(2)}, u32[]{:S(2)}) %collective-permute-start.2) | collective-permute-done | bytes 319520 | tf_op jit(solution)/shard_map/ppermute | solution.py:738
  53.1 3.7 %collective-permute-start.13 = (bf16[128,768]{1,0:T(8,128)(2,1)S(1)}, bf16[128,768]{1,0:T(8,128)(2,1)S(1)}, u32[]{:S(2)}, u32[]{:S(2)}) collective-permute-start(bf16[128,768]{1,0:T(8,128)(2,1)S(1)} %copy-done.20), channel_id=1, source_target_pairs={{0,24},{8,16},{16,8},{24,0},{1,25},{9,17},{17,9},{25,1},{2,26},{10... | collective-permute-start | bytes 589832 | tf_op jit(solution)/shard_map/ppermute | solution.py:697
  57.8 15.0 %attend.1 = (bf16[1024,384]{1,0:T(8,128)(2,1)}, bf16[1024,384]{1,0:T(8,128)(2,1)}, bf16[1024,384]{1,0:T(8,128)(2,1)}, bf16[1024,384]{1,0:T(8,128)(2,1)}, f32[3,8...) custom-call(s32[3]{0:T(128)S(1)} %pad_add_fusion.refs_0_.where_ref, ...), custom_call_target="tpu_custom_call" | custom-call | flops 1 | bytes 1 | tf_op jit(solution)/shard_map/attend/pallas_call | solution.py:186
  73.9 2.3 convolution_convert_fusion.2.refs_1_
  76.3 3.5 %collective-permute-done.15.refs_2_ = bf16[1024,768]{1,0:T(8,128)(2,1)} collective-permute-done((bf16[1024,768]{1,0:T(8,128)(2,1)S(1)}, bf16[1024,768]{1,0:T(8,128)(2,1)}, u32[]{:S(2)}, u32[]{:S(2)}) %collective-permute-start.15) | collective-permute-done | bytes 1572896 | tf_op jit(solution)/shard_map/ppermute | solution.py:725
  79.9 1.7 all-gather.5.cloned.1.call-done
  81.5 11.5 %ffn_forward.1 = (f32[1024,768]{1,0:T(8,128)S(1)}, bf16[1024,768]{1,0:T(8,128)(2,1)S(1)}, bf16[1024,1024]{1,0:T(8,128)(2,1)S(1)}, bf16[1024,1024]{1,0:T(8,128)(2...) custom-call(bf16[1024,768]{1,0:T(8,128)(2,1)} %get-tuple-element.113, ...), custom_call_target="tpu_custom_call" | custom-call | flops 1 | bytes 1 | tf_op jit(solution)/shard_map/ffn_forward/pallas_call | solution.py:247
  94.2 2.6 collective-permute-done.17.refs_13_
  97.6 11.8 %ffn_backward.1 = (bf16[128,768]{1,0:T(8,128)(2,1)}, bf16[128,768]{1,0:T(8,128)(2,1)}, bf16[128,768]{1,0:T(8,128)(2,1)}, bf16[128,768]{1,0:T(8,128)(2,1)}, bf16[...) custom-call(s32[3]{0:T(128)S(1)} %pad_add_fusion.refs_0_.where_ref, ...), custom_call_target="tpu_custom_call" | custom-call | flops 1 | bytes 1 | tf_op jit(solution)/shard_map/ffn_backward/pallas_call | solution.py:308
  109.6 3.9 %convolution_convert_fusion.1.gu_ref = bf16[768,2048]{1,0:T(8,128)(2,1)S(1)} fusion(bf16[1024,768]{1,0:T(8,128)(2,1)S(1)} %get-tuple-element.140, bf16[1024,2048]{1,0:T(8,128)(2,1)S(1)} %get-tuple-element.141), kind=kOutput, calls=%fused_computation.6 | convolution fusion | flops 3222798336 | bytes 8912896 | tf_op jit(solution)/shard_map/dot_general | solution.py:19
  113.5 3.9 %arrange.1 = bf16[4,2304,256]{2,1,0:T(8,128)(2,1)} custom-call(bf16[768,2048]{1,0:T(8,128)(2,1)S(1)} %convolution_convert_fusion.1.gu_ref, bf16[1024,1024]{1,0:T(8,128)(2,1)S(1)} %get-tuple-element.143.hidden_ref, bf16[1024,768]{1,0:T(8,128)(2,1)S(1)} %get-tuple-element.138.grad_ref), custom_call_target="tpu_custom_call" | custom-call | flops 1 | bytes 1 | tf_op jit(solution)/shard_map/arrange/pallas_call | solution.py:493
  118.1 5.2 %norm_back.1 = (bf16[1024,768]{1,0:T(8,128)(2,1)S(1)}, f32[4,128,768]{2,1,0:T(8,128)}, bf16[4,8,1536]{2,1,0:T(8,128)(2,1)}) custom-call(s32[1]{0:T(128)} %bitcast.2.rank_ref.refs_0_, f32[1024,768]{1,0:T(8,128)S(1)} %get-tuple-element.123.refs_1_.sum_ref, bf16[1024,768]{1,0:T(8,128)(2,1)} %copy-done, bf16[1024,768]{1,0:T(8,128)(2,1)} %get-tuple-element.144.own_ref, ...), custom_call_target="tpu_custom_call" | custom-call | flops 1 | bytes 1 | tf_op jit(solution)/shard_map/norm_back/pallas_call | solution.py:361
  124.9 1.5 collective-permute-start.21
  126.4 2.4 collective-permute-start.22
  129.5 13.9 %attend_back.1 = bf16[1024,1152]{1,0:T(8,128)(2,1)S(1)} custom-call(f32[1,1024]{1,0:T(1,128)} %get-tuple-element.137.refs_0_, bf16[1024,768]{1,0:T(8,128)(2,1)S(1)} %get-tuple-element.151.refs_1_, bf16[384,768]{1,0:T(8,128)(2,1)} %copy-done.9, bf16[1024,384]{1,0:T(8,128)(2,1)} %get-tuple-element.152.refs_3_, bf16[1024,384]{1,0:T(8,128)(2,1)} %get-tuple-element.153.refs_4_, ...), custom_call_target="tpu_custom_call" | custom-call | flops 1 | bytes 1 | tf_op jit(solution)/shard_map/attend_back/pallas_call | solution.py:607
  143.5 2.3 convolution_convert_fusion
  147.4 1.5 collective-permute-start.30
  148.9 2.2 convolution_convert_fusion.3.refs_2_
  152.3 1.3 collective-permute-done.26.refs_3_
  154.4 3.8 %collective-permute-start.27 = (bf16[128,768]{1,0:T(8,128)(2,1)S(1)}, bf16[128,768]{1,0:T(8,128)(2,1)S(1)}, u32[]{:S(2)}, u32[]{:S(2)}) collective-permute-start(bf16[128,768]{1,0:T(8,128)(2,1)S(1)} %get-tuple-element.162), channel_id=1, source_target_pairs={{0,8},{8,0},{16,24},{24,16},{1,9},{9,1},{17,25},{25,17},{2,10},{10... | collective-permute-start | bytes 589832 | tf_op jit(solution)/shard_map/ppermute | solution.py:697
  159.2 1.7 collective-permute-done.29
  160.8 6.5 %collective-permute-done.27.refs_1_ = bf16[128,768]{1,0:T(8,128)(2,1)S(1)} collective-permute-done((bf16[128,768]{1,0:T(8,128)(2,1)S(1)}, bf16[128,768]{1,0:T(8,128)(2,1)S(1)}, u32[]{:S(2)}, u32[]{:S(2)}) %collective-permute-start.27) | collective-permute-done | bytes 196640 | tf_op jit(solution)/shard_map/ppermute | solution.py:697
  167.4 2.6 collective-permute-done.28.refs_2_
  170.3 6.3 %reduce-scatter.7.cloned.1.call-done = bf16[1,2304,256]{2,1,0:T(8,128)(2,1)} async-done(((bf16[4,2304,256]{2,1,0:T(8,128)(2,1)}), bf16[1,2304,256]{2,1,0:T(8,128)(2,1)}) %reduce-scatter.7.cloned.1.call-update) | async-done | bytes 1179664
  176.6 1.4 collective-permute-start.32
  178.7 3.4 %collective-permute-start.33 = (bf16[128,768]{1,0:T(8,128)(2,1)S(1)}, bf16[128,768]{1,0:T(8,128)(2,1)S(1)}, u32[]{:S(2)}, u32[]{:S(2)}) collective-permute-start(bf16[128,768]{1,0:T(8,128)(2,1)S(1)} %get-tuple-element.170), channel_id=1, source_target_pairs={{0,24},{8,16},{16,8},{24,0},{1,25},{9,17},{17,9},{25,1},{2,26},{10... | collective-permute-start | bytes 589832 | tf_op jit(solution)/shard_map/ppermute | solution.py:697
  182.0 1.5 stack.30
  183.5 4.0 %collective-permute-done.33.refs_3_ = bf16[128,768]{1,0:T(8,128)(2,1)S(1)} collective-permute-done((bf16[128,768]{1,0:T(8,128)(2,1)S(1)}, bf16[128,768]{1,0:T(8,128)(2,1)S(1)}, u32[]{:S(2)}, u32[]{:S(2)}) %collective-permute-start.33) | collective-permute-done | bytes 196640 | tf_op jit(solution)/shard_map/ppermute | solution.py:697
  187.5 4.9 %collective-permute-done.32 = bf16[200,1536]{1,0:T(8,128)(2,1)} collective-permute-done((bf16[200,1536]{1,0:T(8,128)(2,1)S(1)}, bf16[200,1536]{1,0:T(8,128)(2,1)}, u32[]{:S(2)}, u32[]{:S(2)}) %collective-permute-start.32) | collective-permute-done | bytes 614432 | tf_op jit(solution)/shard_map/ppermute | solution.py:762
  193.4 1.7 fusion.1
  195.2 7.4 %collective-permute-start.34 = (bf16[200,768]{1,0:T(8,128)(2,1)S(1)}, bf16[200,768]{1,0:T(8,128)(2,1)S(1)}, u32[]{:S(2)}, u32[]{:S(2)}) collective-permute-start(bf16[200,768]{1,0:T(8,128)(2,1)S(1)} %constant_dynamic-slice_fusion.1), channel_id=1, source_target_pairs={{0,8},{8,0},{16,24},{24,16},{1,9},{9,1},{17,25},{25,17},{2,10},{10... | collective-permute-start | bytes 921608 | tf_op jit(solution)/shard_map/ppermute | solution.py:697
  202.6 1.5 stack.31
  204.0 10.8 %collective-permute-done.34 = bf16[200,768]{1,0:T(8,128)(2,1)S(1)} collective-permute-done((bf16[200,768]{1,0:T(8,128)(2,1)S(1)}, bf16[200,768]{1,0:T(8,128)(2,1)S(1)}, u32[]{:S(2)}, u32[]{:S(2)}) %collective-permute-start.34) | collective-permute-done | bytes 307232 | tf_op jit(solution)/shard_map/ppermute | solution.py:697
  215.1 8.6 %collective-permute-done.35 = bf16[200,384]{1,0:T(8,128)(2,1)S(1)} collective-permute-done((bf16[200,384]{1,0:T(8,128)(2,1)S(1)}, bf16[200,384]{1,0:T(8,128)(2,1)S(1)}, u32[]{:S(2)}, u32[]{:S(2)}) %collective-permute-start.35) | collective-permute-done | bytes 153632 | tf_op jit(solution)/shard_map/ppermute | solution.py:697
  223.9 19.1 %collective-permute-done.36 = bf16[200,384]{1,0:T(8,128)(2,1)S(1)} collective-permute-done((bf16[200,384]{1,0:T(8,128)(2,1)S(1)}, bf16[200,384]{1,0:T(8,128)(2,1)S(1)}, u32[]{:S(2)}, u32[]{:S(2)}) %collective-permute-start.36) | collective-permute-done | bytes 153632 | tf_op jit(solution)/shard_map/ppermute | solution.py:697
  243.2 12.0 %collective-permute-done.37 = bf16[200,768]{1,0:T(8,128)(2,1)S(1)} collective-permute-done((bf16[200,768]{1,0:T(8,128)(2,1)S(1)}, bf16[200,768]{1,0:T(8,128)(2,1)S(1)}, u32[]{:S(2)}, u32[]{:S(2)}) %collective-permute-start.37) | collective-permute-done | bytes 307232 | tf_op jit(solution)/shard_map/ppermute | solution.py:697
  255.5 4.0 %join_all.1 = (f32[192,2048]{1,0:T(8,128)}, f32[192,2048]{1,0:T(8,128)}, f32[512,768]{1,0:T(8,128)}) custom-call(bf16[4,2,576,256]{3,2,1,0:T(8,128)(2,1)} %bitcast.67), custom_call_target="tpu_custom_call" | custom-call | flops 1 | bytes 1 | tf_op jit(solution)/shard_map/join_all/pallas_call | solution.py:676
  259.5 1.5 join.1
  (165 shorter events, 21.9 us)
Async XLA Ops:
  7.2 74.4 %all-gather.5.cloned.1.call-start = ((), (), s32[]{:S(2)}) async-start(), calls=%async_computation.3 | async-start | bytes 5898240 | tf_op jit(solution)/shard_map/all_gather | solution.py:803
  10.1 166.4 %reduce-scatter.7.cloned.1.call-start = ((), (), s32[]{:S(2)}) async-start(), calls=%async_computation.5 | async-start | bytes 5898240
  14.2 26.3 %collective-permute-start = (bf16[200,1536]{1,0:T(8,128)(2,1)}, bf16[200,1536]{1,0:T(8,128)(2,1)S(1)}, u32[]{:S(2)}, u32[]{:S(2)}) collective-permute-start(bf16[200,1536]{1,0:T(8,128)(2,1)} %get-tuple-element.104.refs_11_), channel_id=1, source_target_pairs={{0,1},{1,0},{2,3},{3,2},{4,5},{5,4},{6,7},{7,6},{8,9},{9,8},{10,11... | collective-permute-start | bytes 1843208 | tf_op jit(solution)/shard_map/ppermute | solution.py:735
  17.1 26.1 %collective-permute-start.1 = (bf16[200,1536]{1,0:T(8,128)(2,1)}, bf16[200,1536]{1,0:T(8,128)(2,1)S(1)}, u32[]{:S(2)}, u32[]{:S(2)}) collective-permute-start(bf16[200,1536]{1,0:T(8,128)(2,1)} %get-tuple-element.104.refs_11_), channel_id=1, source_target_pairs={{0,2},{2,0},{1,3},{3,1},{4,6},{6,4},{5,7},{7,5},{8,10},{10,8},{9,1... | collective-permute-start | bytes 1843208 | tf_op jit(solution)/shard_map/ppermute | solution.py:736
  18.7 10.6 %collective-permute-start.5 = (bf16[136,768]{1,0:T(8,128)(2,1)}, bf16[136,768]{1,0:T(8,128)(2,1)}, u32[]{:S(2)}, u32[]{:S(2)}) collective-permute-start(bf16[136,768]{1,0:T(8,128)(2,1)} %get-tuple-element.111), channel_id=1, source_target_pairs={{0,24},{8,16},{16,8},{24,0},{1,25},{9,17},{17,9},{25,1},{2,26},{10... | collective-permute-start | bytes 626696 | tf_op jit(solution)/shard_map/ppermute | solution.py:697
  22.3 17.5 %collective-permute-start.4 = (bf16[136,768]{1,0:T(8,128)(2,1)}, bf16[136,768]{1,0:T(8,128)(2,1)}, u32[]{:S(2)}, u32[]{:S(2)}) collective-permute-start(bf16[136,768]{1,0:T(8,128)(2,1)} %get-tuple-element.109), channel_id=1, source_target_pairs={{0,16},{8,24},{16,0},{24,8},{1,17},{9,25},{17,1},{25,9},{2,18},{10... | collective-permute-start | bytes 626696 | tf_op jit(solution)/shard_map/ppermute | solution.py:697
  22.3 17.5 %collective-permute-start.3 = (bf16[136,768]{1,0:T(8,128)(2,1)}, bf16[136,768]{1,0:T(8,128)(2,1)}, u32[]{:S(2)}, u32[]{:S(2)}) collective-permute-start(bf16[136,768]{1,0:T(8,128)(2,1)} %get-tuple-element.107), channel_id=1, source_target_pairs={{0,8},{8,0},{16,24},{24,16},{1,9},{9,1},{17,25},{25,17},{2,10},{10... | collective-permute-start | bytes 626696 | tf_op jit(solution)/shard_map/ppermute | solution.py:697
  29.2 23.9 %collective-permute-start.6 = (bf16[136,768]{1,0:T(8,128)(2,1)}, bf16[136,768]{1,0:T(8,128)(2,1)}, u32[]{:S(2)}, u32[]{:S(2)}) collective-permute-start(bf16[136,768]{1,0:T(8,128)(2,1)} %get-tuple-element.106.refs_3_), channel_id=1, source_target_pairs={{0,4},{4,0},{1,5},{5,1},{2,6},{6,2},{3,7},{7,3},{8,12},{12,8},{9,1... | collective-permute-start | bytes 626696 | tf_op jit(solution)/shard_map/ppermute | solution.py:711
  39.8 17.1 %collective-permute-start.9 = (bf16[136,768]{1,0:T(8,128)(2,1)}, bf16[136,768]{1,0:T(8,128)(2,1)}, u32[]{:S(2)}, u32[]{:S(2)}) collective-permute-start(bf16[136,768]{1,0:T(8,128)(2,1)} %collective-permute-done.5.refs_6_), channel_id=1, source_target_pairs={{0,4},{4,0},{1,5},{5,1},{2,6},{6,2},{3,7},{7,3},{8,12},{12,8},{9,1... | collective-permute-start | bytes 626696 | tf_op jit(solution)/shard_map/ppermute | solution.py:711
  39.8 17.1 %collective-permute-start.8 = (bf16[136,768]{1,0:T(8,128)(2,1)}, bf16[136,768]{1,0:T(8,128)(2,1)}, u32[]{:S(2)}, u32[]{:S(2)}) collective-permute-start(bf16[136,768]{1,0:T(8,128)(2,1)} %collective-permute-done.4.refs_5_), channel_id=1, source_target_pairs={{0,4},{4,0},{1,5},{5,1},{2,6},{6,2},{3,7},{7,3},{8,12},{12,8},{9,1... | collective-permute-start | bytes 626696 | tf_op jit(solution)/shard_map/ppermute | solution.py:711
  40.4 11.7 %collective-permute-start.2 = (bf16[104,1536]{1,0:T(8,128)(2,1)S(1)}, bf16[104,1536]{1,0:T(8,128)(2,1)S(1)}, u32[]{:S(2)}, u32[]{:S(2)}) collective-permute-start(bf16[104,1536]{1,0:T(8,128)(2,1)S(1)} %slice.96), channel_id=1, source_target_pairs={{0,2},{2,0},{1,3},{3,1},{4,6},{6,4},{5,7},{7,5},{8,10},{10,8},{9,1... | collective-permute-start | bytes 958472 | tf_op jit(solution)/shard_map/ppermute | solution.py:738
  43.2 13.6 %copy-start.19 = (bf16[128,768]{1,0:T(8,128)(2,1)S(1)}, bf16[128,768]{1,0:T(8,128)(2,1)}, u32[]{:S(2)}) copy-start(bf16[128,768]{1,0:T(8,128)(2,1)} %get-tuple-element.117) | copy-start | bytes 589828
  43.3 13.6 %copy-start.18 = (bf16[128,768]{1,0:T(8,128)(2,1)S(1)}, bf16[128,768]{1,0:T(8,128)(2,1)}, u32[]{:S(2)}) copy-start(bf16[128,768]{1,0:T(8,128)(2,1)} %get-tuple-element.115) | copy-start | bytes 589828
  43.3 8.9 %collective-permute-start.10 = (bf16[96,1536]{1,0:T(8,128)(2,1)S(1)}, bf16[96,1536]{1,0:T(8,128)(2,1)S(1)}, u32[]{:S(2)}, u32[]{:S(2)}) collective-permute-start(bf16[96,1536]{1,0:T(8,128)(2,1)S(1)} %slice.99), channel_id=1, source_target_pairs={{0,1},{1,0},{2,3},{3,2},{4,5},{5,4},{6,7},{7,6},{8,9},{9,8},{10,11... | collective-permute-start | bytes 884744 | tf_op jit(solution)/shard_map/ppermute | solution.py:737
  52.1 5.6 %collective-permute-start.7 = (bf16[136,768]{1,0:T(8,128)(2,1)}, bf16[136,768]{1,0:T(8,128)(2,1)}, u32[]{:S(2)}, u32[]{:S(2)}) collective-permute-start(bf16[136,768]{1,0:T(8,128)(2,1)} %collective-permute-done.3.refs_4_), channel_id=1, source_target_pairs={{0,4},{4,0},{1,5},{5,1},{2,6},{6,2},{3,7},{7,3},{8,12},{12,8},{9,1... | collective-permute-start | bytes 626696 | tf_op jit(solution)/shard_map/ppermute | solution.py:711
  52.3 21.4 %collective-permute-start.14 = (bf16[384,384]{1,0:T(8,128)(2,1)S(1)}, bf16[384,384]{1,0:T(8,128)(2,1)S(1)}, u32[]{:S(2)}, u32[]{:S(2)}) collective-permute-start(bf16[384,384]{1,0:T(8,128)(2,1)S(1)} %get-tuple-element.203), channel_id=1, source_target_pairs={{0,4},{4,0},{1,5},{5,1},{2,6},{6,2},{3,7},{7,3},{8,12},{12,8},{9,1... | collective-permute-start | bytes 884744 | tf_op jit(solution)/shard_map/ppermute | solution.py:847
  53.1 19.6 %collective-permute-start.13 = (bf16[128,768]{1,0:T(8,128)(2,1)S(1)}, bf16[128,768]{1,0:T(8,128)(2,1)S(1)}, u32[]{:S(2)}, u32[]{:S(2)}) collective-permute-start(bf16[128,768]{1,0:T(8,128)(2,1)S(1)} %copy-done.20), channel_id=1, source_target_pairs={{0,24},{8,16},{16,8},{24,0},{1,25},{9,17},{17,9},{25,1},{2,26},{10... | collective-permute-start | bytes 589832 | tf_op jit(solution)/shard_map/ppermute | solution.py:697
  56.8 16.9 %collective-permute-start.12 = (bf16[128,768]{1,0:T(8,128)(2,1)S(1)}, bf16[128,768]{1,0:T(8,128)(2,1)S(1)}, u32[]{:S(2)}, u32[]{:S(2)}) collective-permute-start(bf16[128,768]{1,0:T(8,128)(2,1)S(1)} %copy-done.19), channel_id=1, source_target_pairs={{0,16},{8,24},{16,0},{24,8},{1,17},{9,25},{17,1},{25,9},{2,18},{10... | collective-permute-start | bytes 589832 | tf_op jit(solution)/shard_map/ppermute | solution.py:697
  56.8 16.9 %collective-permute-start.11 = (bf16[128,768]{1,0:T(8,128)(2,1)S(1)}, bf16[128,768]{1,0:T(8,128)(2,1)S(1)}, u32[]{:S(2)}, u32[]{:S(2)}) collective-permute-start(bf16[128,768]{1,0:T(8,128)(2,1)S(1)} %copy-done.18), channel_id=1, source_target_pairs={{0,8},{8,0},{16,24},{24,16},{1,9},{9,1},{17,25},{25,17},{2,10},{10... | collective-permute-start | bytes 589832 | tf_op jit(solution)/shard_map/ppermute | solution.py:697
  76.2 3.6 %collective-permute-start.15 = (bf16[1024,768]{1,0:T(8,128)(2,1)S(1)}, bf16[1024,768]{1,0:T(8,128)(2,1)}, u32[]{:S(2)}, u32[]{:S(2)}) collective-permute-start(bf16[1024,768]{1,0:T(8,128)(2,1)S(1)} %convolution_convert_fusion.2.refs_1_), channel_id=1, source_target_pairs={{0,4},{4,0},{1,5},{5,1},{2,6},{6,2},{3,7},{7,3},{8,12},{12,8},{9,1... | collective-permute-start | bytes 4718600 | tf_op jit(solution)/shard_map/ppermute | solution.py:725
  81.5 12.1 %copy-start.4 = (bf16[128,768]{1,0:T(8,128)(2,1)S(1)}, bf16[128,768]{1,0:T(8,128)(2,1)}, u32[]{:S(2)}) copy-start(bf16[128,768]{1,0:T(8,128)(2,1)} %copy-done.3) | copy-start | bytes 589828
  93.0 4.6 %collective-permute-start.16 = (bf16[1024,768]{1,0:T(8,128)(2,1)S(1)}, bf16[1024,768]{1,0:T(8,128)(2,1)S(1)}, u32[]{:S(2)}, u32[]{:S(2)}) collective-permute-start(bf16[1024,768]{1,0:T(8,128)(2,1)S(1)} %get-tuple-element.124.refs_2_), channel_id=1, source_target_pairs={{0,4},{4,0},{1,5},{5,1},{2,6},{6,2},{3,7},{7,3},{8,12},{12,8},{9,1... | collective-permute-start | bytes 4718600 | tf_op jit(solution)/shard_map/ppermute | solution.py:725
  93.1 3.7 %collective-permute-start.17 = (bf16[128,768]{1,0:T(8,128)(2,1)S(1)}, bf16[128,768]{1,0:T(8,128)(2,1)S(1)}, u32[]{:S(2)}, u32[]{:S(2)}) collective-permute-start(bf16[128,768]{1,0:T(8,128)(2,1)S(1)} %copy-done.2), channel_id=1, source_target_pairs={{0,4},{4,0},{1,5},{5,1},{2,6},{6,2},{3,7},{7,3},{8,12},{12,8},{9,1... | collective-permute-start | bytes 589832 | tf_op jit(solution)/shard_map/ppermute | solution.py:711
  93.6 3.5 %collective-permute-start.18 = (bf16[128,768]{1,0:T(8,128)(2,1)S(1)}, bf16[128,768]{1,0:T(8,128)(2,1)S(1)}, u32[]{:S(2)}, u32[]{:S(2)}) collective-permute-start(bf16[128,768]{1,0:T(8,128)(2,1)S(1)} %copy-done.4), channel_id=1, source_target_pairs={{0,4},{4,0},{1,5},{5,1},{2,6},{6,2},{3,7},{7,3},{8,12},{12,8},{9,1... | collective-permute-start | bytes 589832 | tf_op jit(solution)/shard_map/ppermute | solution.py:711
  93.7 3.7 %collective-permute-start.19 = (bf16[128,768]{1,0:T(8,128)(2,1)S(1)}, bf16[128,768]{1,0:T(8,128)(2,1)S(1)}, u32[]{:S(2)}, u32[]{:S(2)}) collective-permute-start(bf16[128,768]{1,0:T(8,128)(2,1)S(1)} %collective-permute-done.12.refs_11_), channel_id=1, source_target_pairs={{0,4},{4,0},{1,5},{5,1},{2,6},{6,2},{3,7},{7,3},{8,12},{12,8},{9,1... | collective-permute-start | bytes 589832 | tf_op jit(solution)/shard_map/ppermute | solution.py:711
  94.1 3.5 %collective-permute-start.20 = (bf16[128,768]{1,0:T(8,128)(2,1)S(1)}, bf16[128,768]{1,0:T(8,128)(2,1)S(1)}, u32[]{:S(2)}, u32[]{:S(2)}) collective-permute-start(bf16[128,768]{1,0:T(8,128)(2,1)S(1)} %collective-permute-done.13.refs_12_), channel_id=1, source_target_pairs={{0,4},{4,0},{1,5},{5,1},{2,6},{6,2},{3,7},{7,3},{8,12},{12,8},{9,1... | collective-permute-start | bytes 589832 | tf_op jit(solution)/shard_map/ppermute | solution.py:711
  109.4 4.1 %collective-permute-start.24 = (bf16[1024,768]{1,0:T(8,128)(2,1)}, bf16[1024,768]{1,0:T(8,128)(2,1)}, u32[]{:S(2)}, u32[]{:S(2)}) collective-permute-start(bf16[1024,768]{1,0:T(8,128)(2,1)} %get-tuple-element.144.own_ref), channel_id=1, source_target_pairs={{0,4},{4,0},{1,5},{5,1},{2,6},{6,2},{3,7},{7,3},{8,12},{12,8},{9,1... | collective-permute-start | bytes 4718600 | tf_op jit(solution)/shard_map/ppermute | solution.py:725
  117.4 97.4 %reduce-scatter.5.cloned.1.call-start = ((), (), s32[]{:S(2)}) async-start(), calls=%async_computation.2 | async-start | bytes 1474560 | tf_op jit(solution)/shard_map/reduce_scatter | solution.py:925
  124.4 4.8 %collective-permute-start.25 = (bf16[384,384]{1,0:T(8,128)(2,1)S(1)}, bf16[384,384]{1,0:T(8,128)(2,1)S(1)}, u32[]{:S(2)}, u32[]{:S(2)}) collective-permute-start(bf16[384,384]{1,0:T(8,128)(2,1)S(1)} %get-tuple-element.201), channel_id=1, source_target_pairs={{0,4},{4,0},{1,5},{5,1},{2,6},{6,2},{3,7},{7,3},{8,12},{12,8},{9,1... | collective-permute-start | bytes 884744 | tf_op jit(solution)/shard_map/ppermute | solution.py:887
  124.9 18.5 %collective-permute-start.21 = (bf16[128,768]{1,0:T(8,128)(2,1)S(1)}, bf16[128,768]{1,0:T(8,128)(2,1)S(1)}, u32[]{:S(2)}, u32[]{:S(2)}) collective-permute-start(bf16[128,768]{1,0:T(8,128)(2,1)S(1)} %copy-done.23), channel_id=1, source_target_pairs={{0,8},{8,0},{16,24},{24,16},{1,9},{9,1},{17,25},{25,17},{2,10},{10... | collective-permute-start | bytes 589832 | tf_op jit(solution)/shard_map/ppermute | solution.py:697
  126.4 17.1 %collective-permute-start.22 = (bf16[128,768]{1,0:T(8,128)(2,1)S(1)}, bf16[128,768]{1,0:T(8,128)(2,1)S(1)}, u32[]{:S(2)}, u32[]{:S(2)}) collective-permute-start(bf16[128,768]{1,0:T(8,128)(2,1)S(1)} %copy-done.22), channel_id=1, source_target_pairs={{0,16},{8,24},{16,0},{24,8},{1,17},{9,25},{17,1},{25,9},{2,18},{10... | collective-permute-start | bytes 589832 | tf_op jit(solution)/shard_map/ppermute | solution.py:697
  128.8 14.7 %collective-permute-start.23 = (bf16[128,768]{1,0:T(8,128)(2,1)S(1)}, bf16[128,768]{1,0:T(8,128)(2,1)S(1)}, u32[]{:S(2)}, u32[]{:S(2)}) collective-permute-start(bf16[128,768]{1,0:T(8,128)(2,1)S(1)} %copy-done.21), channel_id=1, source_target_pairs={{0,24},{8,16},{16,8},{24,0},{1,25},{9,17},{17,9},{25,1},{2,26},{10... | collective-permute-start | bytes 589832 | tf_op jit(solution)/shard_map/ppermute | solution.py:697
  129.5 14.0 %copy-start.12 = (bf16[1024,768]{1,0:T(8,128)(2,1)S(1)}, bf16[1024,768]{1,0:T(8,128)(2,1)}, u32[]{:S(2)}) copy-start(bf16[1024,768]{1,0:T(8,128)(2,1)} %get-tuple-element.113.refs_0_) | copy-start | bytes 4718596
  147.4 13.4 %collective-permute-start.30 = (bf16[104,1536]{1,0:T(8,128)(2,1)S(1)}, bf16[104,1536]{1,0:T(8,128)(2,1)S(1)}, u32[]{:S(2)}, u32[]{:S(2)}) collective-permute-start(bf16[104,1536]{1,0:T(8,128)(2,1)S(1)} %slice_bitcast_fusion.1), channel_id=1, source_target_pairs={{0,2},{2,0},{1,3},{3,1},{4,6},{6,4},{5,7},{7,5},{8,10},{10,8},{9,1... | collective-permute-start | bytes 958472 | tf_op jit(solution)/shard_map/ppermute | solution.py:753
  151.3 2.4 collective-permute-start.26
  151.4 9.5 %collective-permute-start.29 = (bf16[96,1536]{1,0:T(8,128)(2,1)S(1)}, bf16[96,1536]{1,0:T(8,128)(2,1)S(1)}, u32[]{:S(2)}, u32[]{:S(2)}) collective-permute-start(bf16[96,1536]{1,0:T(8,128)(2,1)S(1)} %slice_bitcast_fusion.4), channel_id=1, source_target_pairs={{0,1},{1,0},{2,3},{3,2},{4,5},{5,4},{6,7},{7,6},{8,9},{9,8},{10,11... | collective-permute-start | bytes 884744 | tf_op jit(solution)/shard_map/ppermute | solution.py:753
  154.4 13.0 %collective-permute-start.27 = (bf16[128,768]{1,0:T(8,128)(2,1)S(1)}, bf16[128,768]{1,0:T(8,128)(2,1)S(1)}, u32[]{:S(2)}, u32[]{:S(2)}) collective-permute-start(bf16[128,768]{1,0:T(8,128)(2,1)S(1)} %get-tuple-element.162), channel_id=1, source_target_pairs={{0,8},{8,0},{16,24},{24,16},{1,9},{9,1},{17,25},{25,17},{2,10},{10... | collective-permute-start | bytes 589832 | tf_op jit(solution)/shard_map/ppermute | solution.py:697
  158.2 11.8 %collective-permute-start.28 = (bf16[128,768]{1,0:T(8,128)(2,1)S(1)}, bf16[128,768]{1,0:T(8,128)(2,1)S(1)}, u32[]{:S(2)}, u32[]{:S(2)}) collective-permute-start(bf16[128,768]{1,0:T(8,128)(2,1)S(1)} %get-tuple-element.163), channel_id=1, source_target_pairs={{0,16},{8,24},{16,0},{24,8},{1,17},{9,25},{17,1},{25,9},{2,18},{10... | collective-permute-start | bytes 589832 | tf_op jit(solution)/shard_map/ppermute | solution.py:697
  170.1 11.9 %copy-start.5 = (bf16[128,768]{1,0:T(8,128)(2,1)S(1)}, bf16[128,768]{1,0:T(8,128)(2,1)}, u32[]{:S(2)}) copy-start(bf16[128,768]{1,0:T(8,128)(2,1)} %get-tuple-element.166.refs_0_) | copy-start | bytes 589828
  176.6 78.9 %all-gather.7.cloned.1.call-start = ((), (), s32[]{:S(2)}) async-start(), calls=%async_computation.4 | async-start | bytes 2654208 | tf_op jit(solution)/shard_map/all_gather | solution.py:928
  176.6 15.8 %collective-permute-start.32 = (bf16[200,1536]{1,0:T(8,128)(2,1)S(1)}, bf16[200,1536]{1,0:T(8,128)(2,1)}, u32[]{:S(2)}, u32[]{:S(2)}) collective-permute-start(bf16[200,1536]{1,0:T(8,128)(2,1)S(1)} %pad_maximum_fusion.3), channel_id=1, source_target_pairs={{0,2},{2,0},{1,3},{3,1},{4,6},{6,4},{5,7},{7,5},{8,10},{10,8},{9,1... | collective-permute-start | bytes 1843208 | tf_op jit(solution)/shard_map/ppermute | solution.py:762
  178.0 15.4 %collective-permute-start.31 = (bf16[200,1536]{1,0:T(8,128)(2,1)S(1)}, bf16[200,1536]{1,0:T(8,128)(2,1)}, u32[]{:S(2)}, u32[]{:S(2)}) collective-permute-start(bf16[200,1536]{1,0:T(8,128)(2,1)S(1)} %pad_maximum_fusion.2), channel_id=1, source_target_pairs={{0,1},{1,0},{2,3},{3,2},{4,5},{5,4},{6,7},{7,6},{8,9},{9,8},{10,11... | collective-permute-start | bytes 1843208 | tf_op jit(solution)/shard_map/ppermute | solution.py:762
  178.7 8.8 %collective-permute-start.33 = (bf16[128,768]{1,0:T(8,128)(2,1)S(1)}, bf16[128,768]{1,0:T(8,128)(2,1)S(1)}, u32[]{:S(2)}, u32[]{:S(2)}) collective-permute-start(bf16[128,768]{1,0:T(8,128)(2,1)S(1)} %get-tuple-element.170), channel_id=1, source_target_pairs={{0,24},{8,16},{16,8},{24,0},{1,25},{9,17},{17,9},{25,1},{2,26},{10... | collective-permute-start | bytes 589832 | tf_op jit(solution)/shard_map/ppermute | solution.py:697
  195.2 19.7 %collective-permute-start.34 = (bf16[200,768]{1,0:T(8,128)(2,1)S(1)}, bf16[200,768]{1,0:T(8,128)(2,1)S(1)}, u32[]{:S(2)}, u32[]{:S(2)}) collective-permute-start(bf16[200,768]{1,0:T(8,128)(2,1)S(1)} %constant_dynamic-slice_fusion.1), channel_id=1, source_target_pairs={{0,8},{8,0},{16,24},{24,16},{1,9},{9,1},{17,25},{25,17},{2,10},{10... | collective-permute-start | bytes 921608 | tf_op jit(solution)/shard_map/ppermute | solution.py:697
  215.1 8.7 %collective-permute-start.35 = (bf16[200,384]{1,0:T(8,128)(2,1)S(1)}, bf16[200,384]{1,0:T(8,128)(2,1)S(1)}, u32[]{:S(2)}, u32[]{:S(2)}) collective-permute-start(bf16[200,384]{1,0:T(8,128)(2,1)S(1)} %constant_dynamic-slice_fusion), channel_id=1, source_target_pairs={{0,16},{8,24},{16,0},{24,8},{1,17},{9,25},{17,1},{25,9},{2,18},{10... | collective-permute-start | bytes 460808 | tf_op jit(solution)/shard_map/ppermute | solution.py:697
  223.8 19.2 %collective-permute-start.36 = (bf16[200,384]{1,0:T(8,128)(2,1)S(1)}, bf16[200,384]{1,0:T(8,128)(2,1)S(1)}, u32[]{:S(2)}, u32[]{:S(2)}) collective-permute-start(bf16[200,384]{1,0:T(8,128)(2,1)S(1)} %add_convert_fusion.1), channel_id=1, source_target_pairs={{0,16},{8,24},{16,0},{24,8},{1,17},{9,25},{17,1},{25,9},{2,18},{10... | collective-permute-start | bytes 460808 | tf_op jit(solution)/shard_map/ppermute | solution.py:697
  243.1 12.1 %collective-permute-start.37 = (bf16[200,768]{1,0:T(8,128)(2,1)S(1)}, bf16[200,768]{1,0:T(8,128)(2,1)S(1)}, u32[]{:S(2)}, u32[]{:S(2)}) collective-permute-start(bf16[200,768]{1,0:T(8,128)(2,1)S(1)} %pad_maximum_fusion.7), channel_id=1, source_target_pairs={{0,8},{8,0},{16,24},{24,16},{1,9},{9,1},{17,25},{25,17},{2,10},{10... | collective-permute-start | bytes 921608 | tf_op jit(solution)/shard_map/ppermute | solution.py:697
  255.4 4.1 %collective-permute-start.38 = (bf16[200,1536]{1,0:T(8,128)(2,1)S(1)}, bf16[200,1536]{1,0:T(8,128)(2,1)S(1)}, u32[]{:S(2)}, u32[]{:S(2)}) collective-permute-start(bf16[200,1536]{1,0:T(8,128)(2,1)S(1)} %pad_maximum_fusion.4.refs_1_), channel_id=1, source_target_pairs={{0,4},{4,0},{1,5},{5,1},{2,6},{6,2},{3,7},{7,3},{8,12},{12,8},{9,1... | collective-permute-start | bytes 1843208 | tf_op jit(solution)/shard_map/ppermute | solution.py:962
  (21 other events, 102.0 us)
Sparse Core Ops, SparseCore 0:
  10.4 71.0 all-gather.4
  117.5 58.9 reduce-scatter.6
  178.8 33.6 reduce-scatter.4
  215.0 37.5 all-gather.6

commit v5 on v4

--- a/solution.py
+++ b/solution.py
@@ -77,7 +77,7 @@
     for n, ref in enumerate(refs):
         rank = where_ref[2] if n < groups else 1 - where_ref[2]
         chunk = (where_ref[1] ^ (n % groups)) * ranks + rank
-        row = ref[span:span + 8, 0:span].astype(F32)[0:1, :]
+        row = ref[span:span + 16, 0:span].astype(F32)[0:1, :]
         target[:, pl.ds(pl.multiple_of(chunk * span, span), span)] = row
 
 
@@ -345,11 +345,11 @@
     def _():
         out_ref[...] = jnp.zeros_like(out_ref)
         shard = gain_ref.shape[1] // out_ref.shape[0]
-        first = lax.broadcasted_iota(jnp.int32, (8, shard), 0)
+        first = lax.broadcasted_iota(jnp.int32, (16, shard), 0)
         for j in range(out_ref.shape[0]):
             lanes = slice(j * shard, (j + 1) * shard)
-            one = jnp.broadcast_to(gain_grad_ref[:, lanes], (8, shard))
-            two = jnp.broadcast_to(other_ref[:, lanes], (8, shard))
+            one = jnp.broadcast_to(gain_grad_ref[:, lanes], (16, shard))
+            two = jnp.broadcast_to(other_ref[:, lanes], (16, shard))
             out_ref[j, :, 0:shard] = jnp.where(
                 first == 0, one, jnp.where(first == 1, two, 0.0)).astype(BF)
 
@@ -363,10 +363,10 @@
         grid=(tokens // block,),
         in_specs=[SMEM_SPEC, VMEM_SPEC, row, row, row] + whole_specs(gain, other_grad),
         out_specs=[VMEM_SPEC, pl.BlockSpec((1, span, width), lambda i: (i, 0, 0)),
-                   pl.BlockSpec((fsdp, 8, cols), lambda i: (0, 0, 0))],
+                   pl.BlockSpec((fsdp, 16, cols), lambda i: (0, 0, 0))],
         out_shape=[pltpu.VMEM((tokens, width), BF),
                    pltpu.HBM((tokens // block, span, width), F32),
-                   pltpu.HBM((fsdp, 8, cols), BF)],
+                   pltpu.HBM((fsdp, 16, cols), BF)],
         scratch_shapes=[pltpu.VMEM((block, width), F32), pltpu.VMEM((1, width), F32)],
         compiler_params=pltpu.CompilerParams(vmem_limit_bytes=16 << 20),
         cost_estimate=SMALL_COST,
@@ -406,7 +406,7 @@
         ref[0:span, :] = tokens_ref[m ^ k, 0]
         ref[span:, :] = jnp.zeros_like(ref[span:, :])
         row = seg_ref[pl.ds(m ^ k, 1), :].astype(F32)
-        ref[span:, 0:span] = jnp.broadcast_to(row, (8, span)).astype(BF)
+        ref[span:, 0:span] = jnp.broadcast_to(row, (16, span)).astype(BF)
 
 
 def pack_small(where, query, key, value, out, gains, tokens, segments, cot, ranks, lanes,
@@ -415,7 +415,7 @@
     groups, _, span, _ = tokens.shape
     cols = 3 * lanes_all + width // ranks
     inputs = hbm(query, key, value, out, gains, tokens, segments, cot)
-    shapes = [(shard + 8, cols)] + [(span + 8, width)] * groups + [(span, width)] * groups
+    shapes = [(shard + 16, cols)] + [(span + 16, width)] * groups + [(span, width)] * groups
     return pl.pallas_call(
         lambda *refs: pack_small_kernel(*refs, ranks=ranks, lanes=lanes, lanes_all=lanes_all),
         grid=(1,),
@@ -798,7 +798,7 @@
             at.astype(jnp.uint32) for at in (rank * own_cols, (1 - rank) * own_cols, 1 - rank))
         where = jnp.stack([f_index, lax.axis_index("m"), rank])
         small_cols = 3 * lanes_all + own_cols
-        gains_in = jnp.pad(jnp.stack([gain_attn, gain_ffn]), ((0, 6), (0, 0)))
+        gains_in = jnp.pad(jnp.stack([gain_attn, gain_ffn]), ((0, 14), (0, 0)))
         stack_own = pack(where, w_gate, w_up, w_down, fsdp, ranks)
         stack_all = lax.all_gather(stack_own, F, axis=0)
         cosine, sine = rotary_tables(seq_tokens, head_size, 2)
@@ -835,7 +835,7 @@
             small_pieces = [(o, f, min(n, shard - f)) for o, f, n in small_pieces]
             qkv_refs = small_refs
         else:
-            whole = small_refs[0].reshape(fsdp, shard + 8, small_cols)
+            whole = small_refs[0].reshape(fsdp, shard + 16, small_cols)
             gains = whole[:, shard:shard + 2, :shard].transpose(1, 0, 2).reshape(2, width)
             out_cols = whole[:, :shard, 3 * lanes_all:].reshape(width, own_cols)
             qkv_refs = [whole[:, :shard, :3 * lanes_all].reshape(width, 3 * lanes_all)]

time: 268 us -> 269 us (level)
  transfers between devices with their start and end apart: 43 -> 43, of which waited for: 24 -> 24; matrix products, arithmetic and copies ran while one was open for 8% -> 9% of each run, Pallas kernels for 17% -> 17%
where the time goes in v5:
time: 269 us; the launch traced here: 268 us
  waiting for transfers between devices  109 us (41%)
  Pallas kernels  76.7 us (29%)
  starting transfers between devices  42.9 us (16%)
  between operations  14.5 us (5%)
  matrix products  11.5 us (4%)
  other arithmetic  8.81 us (3%)
  local copies, waits for them, and re-layouts  4.77 us (2%)
    ppermute x16, waiting for transfers between devices, hop(): return lax.ppermute(value, 'm', [(i, i ^ k) for i in range(groups)])  77.1 us
    ppermute x16, starting transfers between devices, hop(): return lax.ppermute(value, 'm', [(i, i ^ k) for i in range(groups)])  28.2 us
    pallas_call x1, Pallas kernels, attend(): pl.pallas_call(kernel, grid=(pairs,), in_specs=[SMEM_SPEC] + whole_specs(...  15 us
    pallas_call x1, Pallas kernels, attend_back(): pl.pallas_call(kernel, grid=(pairs,), in_specs=whole_specs(seg) + [VMEM_S...  13.9 us
    pallas_call x1, Pallas kernels, backward(): pl.pallas_call(kernel, grid=(tokens // block,), in_specs=[SMEM_SPEC, VMEM...  11.8 us
    dot_general x5, matrix products, dot(): lax.dot_general(left, right, (dims, ((), ())), preferred_element_type=F32)  11.5 us
    pallas_call x1, Pallas kernels, forward(): pl.pallas_call(lambda *refs: forward_kernel(*refs, shard=shard, part_rows...  11.5 us
    ppermute x1, waiting for transfers between devices, gather_rows(): far_b = lax.ppermute(from_x[rows:], 'y', swap)  7.7 us
  transfers between devices with their start and end apart: 43, of which 24 were waited for; matrix products, arithmetic and copies ran while one was open for 9% of the time, Pallas kernels for 17%

profile of v5, /device:TPU:0, one launch (start us, length us, event | category | flops | bytes accessed | tf_op | source)
XLA Modules:
  0.0 268.2 jit_solution(2889797782029471455)
XLA Ops:
  7.3 2.8 %pack.1 = bf16[2304,256]{1,0:T(8,128)(2,1)} custom-call(s32[3]{0:T(128)S(1)} %pad_add_fusion.refs_0_.where_ref, bf16[192,2048]{1,0:T(8,128)(2,1)} %refs_1_.2, bf16[192,2048]{1,0:T(8,128)(2,1)} %refs_2_.2, bf16[512,768]{1,0:T(8,128)(2,1)} %refs_3_.2), custom_call_target="tpu_custom_call" | custom-call | flops 1 | bytes 1 | tf_op jit(solution)/shard_map/pack/pallas_call | solution.py:455
  10.8 3.4 %pack_small.1 = (bf16[208,1536]{1,0:T(8,128)(2,1)}, bf16[144,768]{1,0:T(8,128)(2,1)}, bf16[144,768]{1,0:T(8,128)(2,1)}, bf16[144,768]{1,0:T(8,128)(2,1)}, bf16[1...) custom-call(s32[3]{0:T(128)S(1)} %pad_add_fusion.refs_0_.where_ref, ...), custom_call_target="tpu_custom_call" | custom-call | flops 1 | bytes 1 | tf_op jit(solution)/shard_map/pack_small/pallas_call | solution.py:419
  14.2 3.0 %collective-permute-start = (bf16[208,1536]{1,0:T(8,128)(2,1)}, bf16[208,1536]{1,0:T(8,128)(2,1)S(1)}, u32[]{:S(2)}, u32[]{:S(2)}) collective-permute-start(bf16[208,1536]{1,0:T(8,128)(2,1)} %get-tuple-element.104.refs_11_), channel_id=1, source_target_pairs={{0,1},{1,0},{2,3},{3,2},{4,5},{5,4},{6,7},{7,6},{8,9},{9,8},{10,11... | collective-permute-start | bytes 1916936 | tf_op jit(solution)/shard_map/ppermute | solution.py:735
  17.2 1.5 collective-permute-start.1
  18.7 3.6 %collective-permute-start.5 = (bf16[144,768]{1,0:T(8,128)(2,1)}, bf16[144,768]{1,0:T(8,128)(2,1)S(1)}, u32[]{:S(2)}, u32[]{:S(2)}) collective-permute-start(bf16[144,768]{1,0:T(8,128)(2,1)} %get-tuple-element.111), channel_id=1, source_target_pairs={{0,24},{8,16},{16,8},{24,0},{1,25},{9,17},{17,9},{25,1},{2,26},{10... | collective-permute-start | bytes 663560 | tf_op jit(solution)/shard_map/ppermute | solution.py:697
  23.1 1.9 fusion.9
  25.0 1.3 pad_maximum_fusion.5.refs_1_.refs_8_
  29.4 11.4 %collective-permute-done.4.refs_5_ = bf16[144,768]{1,0:T(8,128)(2,1)S(1)} collective-permute-done((bf16[144,768]{1,0:T(8,128)(2,1)}, bf16[144,768]{1,0:T(8,128)(2,1)S(1)}, u32[]{:S(2)}, u32[]{:S(2)}) %collective-permute-start.4) | collective-permute-done | bytes 221216 | tf_op jit(solution)/shard_map/ppermute | solution.py:697
  41.6 1.4 collective-permute-start.2
  43.0 1.4 collective-permute-done.1.refs_13_
  45.5 7.7 %collective-permute-done.2.refs_15_ = bf16[112,1536]{1,0:T(8,128)(2,1)S(1)} collective-permute-done((bf16[112,1536]{1,0:T(8,128)(2,1)S(1)}, bf16[112,1536]{1,0:T(8,128)(2,1)S(1)}, u32[]{:S(2)}, u32[]{:S(2)}) %collective-permute-start.2) | collective-permute-done | bytes 344096 | tf_op jit(solution)/shard_map/ppermute | solution.py:738
  54.2 3.7 %collective-permute-start.13 = (bf16[128,768]{1,0:T(8,128)(2,1)}, bf16[128,768]{1,0:T(8,128)(2,1)S(1)}, u32[]{:S(2)}, u32[]{:S(2)}) collective-permute-start(bf16[128,768]{1,0:T(8,128)(2,1)} %get-tuple-element.119), channel_id=1, source_target_pairs={{0,24},{8,16},{16,8},{24,0},{1,25},{9,17},{17,9},{25,1},{2,26},{10... | collective-permute-start | bytes 589832 | tf_op jit(solution)/shard_map/ppermute | solution.py:697
  58.9 15.0 %attend.1 = (bf16[1024,384]{1,0:T(8,128)(2,1)}, bf16[1024,384]{1,0:T(8,128)(2,1)}, bf16[1024,384]{1,0:T(8,128)(2,1)}, bf16[1024,384]{1,0:T(8,128)(2,1)}, f32[3,8...) custom-call(s32[3]{0:T(128)S(1)} %pad_add_fusion.refs_0_.where_ref, ...), custom_call_target="tpu_custom_call" | custom-call | flops 1 | bytes 1 | tf_op jit(solution)/shard_map/attend/pallas_call | solution.py:186
  75.2 2.3 convolution_convert_fusion.2.refs_1_
  77.6 3.5 %collective-permute-done.15.refs_2_ = bf16[1024,768]{1,0:T(8,128)(2,1)} collective-permute-done((bf16[1024,768]{1,0:T(8,128)(2,1)S(1)}, bf16[1024,768]{1,0:T(8,128)(2,1)}, u32[]{:S(2)}, u32[]{:S(2)}) %collective-permute-start.15) | collective-permute-done | bytes 1572896 | tf_op jit(solution)/shard_map/ppermute | solution.py:725
  81.6 11.5 %ffn_forward.1 = (f32[1024,768]{1,0:T(8,128)S(1)}, bf16[1024,768]{1,0:T(8,128)(2,1)S(1)}, bf16[1024,1024]{1,0:T(8,128)(2,1)S(1)}, bf16[1024,1024]{1,0:T(8,128)(2...) custom-call(bf16[1024,768]{1,0:T(8,128)(2,1)} %get-tuple-element.113, ...), custom_call_target="tpu_custom_call" | custom-call | flops 1 | bytes 1 | tf_op jit(solution)/shard_map/ffn_forward/pallas_call | solution.py:247
  94.2 2.6 collective-permute-done.17.refs_13_
  97.7 11.8 %ffn_backward.1 = (bf16[128,768]{1,0:T(8,128)(2,1)}, bf16[128,768]{1,0:T(8,128)(2,1)}, bf16[128,768]{1,0:T(8,128)(2,1)}, bf16[128,768]{1,0:T(8,128)(2,1)}, bf16[...) custom-call(s32[3]{0:T(128)S(1)} %pad_add_fusion.refs_0_.where_ref, ...), custom_call_target="tpu_custom_call" | custom-call | flops 1 | bytes 1 | tf_op jit(solution)/shard_map/ffn_backward/pallas_call | solution.py:308
  109.6 3.9 %convolution_convert_fusion.1.gu_ref = bf16[768,2048]{1,0:T(8,128)(2,1)S(1)} fusion(bf16[1024,768]{1,0:T(8,128)(2,1)S(1)} %get-tuple-element.140, bf16[1024,2048]{1,0:T(8,128)(2,1)S(1)} %get-tuple-element.141), kind=kOutput, calls=%fused_computation.6 | convolution fusion | flops 3222798336 | bytes 8912896 | tf_op jit(solution)/shard_map/dot_general | solution.py:19
  113.5 3.9 %arrange.1 = bf16[4,2304,256]{2,1,0:T(8,128)(2,1)} custom-call(bf16[768,2048]{1,0:T(8,128)(2,1)S(1)} %convolution_convert_fusion.1.gu_ref, bf16[1024,1024]{1,0:T(8,128)(2,1)S(1)} %get-tuple-element.143.hidden_ref, bf16[1024,768]{1,0:T(8,128)(2,1)S(1)} %get-tuple-element.138.grad_ref), custom_call_target="tpu_custom_call" | custom-call | flops 1 | bytes 1 | tf_op jit(solution)/shard_map/arrange/pallas_call | solution.py:493
  118.1 5.3 %norm_back.1 = (bf16[1024,768]{1,0:T(8,128)(2,1)S(1)}, f32[4,128,768]{2,1,0:T(8,128)}, bf16[4,16,1536]{2,1,0:T(8,128)(2,1)}) custom-call(s32[1]{0:T(128)} %bitcast.2.rank_ref.refs_0_, f32[1024,768]{1,0:T(8,128)S(1)} %get-tuple-element.123.refs_1_.sum_ref, bf16[1024,768]{1,0:T(8,128)(2,1)} %copy-done, bf16[1024,768]{1,0:T(8,128)(2,1)} %get-tuple-element.144.own_ref, ...), custom_call_target="tpu_custom_call" | custom-call | flops 1 | bytes 1 | tf_op jit(solution)/shard_map/norm_back/pallas_call | solution.py:361
  124.9 1.5 collective-permute-start.21
  126.4 2.4 collective-permute-start.22
  129.6 13.9 %attend_back.1 = bf16[1024,1152]{1,0:T(8,128)(2,1)S(1)} custom-call(f32[1,1024]{1,0:T(1,128)} %get-tuple-element.137.refs_0_, bf16[1024,768]{1,0:T(8,128)(2,1)S(1)} %get-tuple-element.151.refs_1_, bf16[384,768]{1,0:T(8,128)(2,1)} %copy-done.9, bf16[1024,384]{1,0:T(8,128)(2,1)} %get-tuple-element.152.refs_3_, bf16[1024,384]{1,0:T(8,128)(2,1)} %get-tuple-element.153.refs_4_, ...), custom_call_target="tpu_custom_call" | custom-call | flops 1 | bytes 1 | tf_op jit(solution)/shard_map/attend_back/pallas_call | solution.py:607
  143.5 2.3 convolution_convert_fusion
  147.5 1.5 collective-permute-start.30
  149.0 2.2 convolution_convert_fusion.3.refs_2_
  152.4 1.3 collective-permute-done.26.refs_3_
  154.5 3.8 %collective-permute-start.27 = (bf16[128,768]{1,0:T(8,128)(2,1)S(1)}, bf16[128,768]{1,0:T(8,128)(2,1)S(1)}, u32[]{:S(2)}, u32[]{:S(2)}) collective-permute-start(bf16[128,768]{1,0:T(8,128)(2,1)S(1)} %get-tuple-element.162), channel_id=1, source_target_pairs={{0,8},{8,0},{16,24},{24,16},{1,9},{9,1},{17,25},{25,17},{2,10},{10... | collective-permute-start | bytes 589832 | tf_op jit(solution)/shard_map/ppermute | solution.py:697
  159.2 1.7 collective-permute-done.29
  160.9 6.5 %collective-permute-done.27.refs_1_ = bf16[128,768]{1,0:T(8,128)(2,1)S(1)} collective-permute-done((bf16[128,768]{1,0:T(8,128)(2,1)S(1)}, bf16[128,768]{1,0:T(8,128)(2,1)S(1)}, u32[]{:S(2)}, u32[]{:S(2)}) %collective-permute-start.27) | collective-permute-done | bytes 196640 | tf_op jit(solution)/shard_map/ppermute | solution.py:697
  167.4 2.6 collective-permute-done.28.refs_2_
  171.1 5.4 %reduce-scatter.7.cloned.1.call-done = bf16[1,2304,256]{2,1,0:T(8,128)(2,1)} async-done(((bf16[4,2304,256]{2,1,0:T(8,128)(2,1)}), bf16[1,2304,256]{2,1,0:T(8,128)(2,1)}) %reduce-scatter.7.cloned.1.call-update) | async-done | bytes 1179664
  176.6 1.4 collective-permute-start.32
  178.7 3.3 %collective-permute-start.33 = (bf16[128,768]{1,0:T(8,128)(2,1)S(1)}, bf16[128,768]{1,0:T(8,128)(2,1)S(1)}, u32[]{:S(2)}, u32[]{:S(2)}) collective-permute-start(bf16[128,768]{1,0:T(8,128)(2,1)S(1)} %get-tuple-element.170), channel_id=1, source_target_pairs={{0,24},{8,16},{16,8},{24,0},{1,25},{9,17},{17,9},{25,1},{2,26},{10... | collective-permute-start | bytes 589832 | tf_op jit(solution)/shard_map/ppermute | solution.py:697
  182.0 1.5 stack.30
  183.5 4.0 %collective-permute-done.33.refs_3_ = bf16[128,768]{1,0:T(8,128)(2,1)S(1)} collective-permute-done((bf16[128,768]{1,0:T(8,128)(2,1)S(1)}, bf16[128,768]{1,0:T(8,128)(2,1)S(1)}, u32[]{:S(2)}, u32[]{:S(2)}) %collective-permute-start.33) | collective-permute-done | bytes 196640 | tf_op jit(solution)/shard_map/ppermute | solution.py:697
  187.5 5.3 %collective-permute-done.32 = bf16[208,1536]{1,0:T(8,128)(2,1)S(1)} collective-permute-done((bf16[208,1536]{1,0:T(8,128)(2,1)S(1)}, bf16[208,1536]{1,0:T(8,128)(2,1)S(1)}, u32[]{:S(2)}, u32[]{:S(2)}) %collective-permute-start.32) | collective-permute-done | bytes 639008 | tf_op jit(solution)/shard_map/ppermute | solution.py:762
  192.8 1.4 collective-permute-done.31
  194.2 1.5 fusion.1
  195.8 6.7 %collective-permute-start.34 = (bf16[208,768]{1,0:T(8,128)(2,1)S(1)}, bf16[208,768]{1,0:T(8,128)(2,1)S(1)}, u32[]{:S(2)}, u32[]{:S(2)}) collective-permute-start(bf16[208,768]{1,0:T(8,128)(2,1)S(1)} %constant_dynamic-slice_fusion.1), channel_id=1, source_target_pairs={{0,8},{8,0},{16,24},{24,16},{1,9},{9,1},{17,25},{25,17},{2,10},{10... | collective-permute-start | bytes 958472 | tf_op jit(solution)/shard_map/ppermute | solution.py:697
  202.4 1.5 stack.31
  203.9 11.2 %collective-permute-done.34 = bf16[208,768]{1,0:T(8,128)(2,1)S(1)} collective-permute-done((bf16[208,768]{1,0:T(8,128)(2,1)S(1)}, bf16[208,768]{1,0:T(8,128)(2,1)S(1)}, u32[]{:S(2)}, u32[]{:S(2)}) %collective-permute-start.34) | collective-permute-done | bytes 319520 | tf_op jit(solution)/shard_map/ppermute | solution.py:697
  215.4 8.9 %collective-permute-done.35 = bf16[208,384]{1,0:T(8,128)(2,1)S(1)} collective-permute-done((bf16[208,384]{1,0:T(8,128)(2,1)S(1)}, bf16[208,384]{1,0:T(8,128)(2,1)S(1)}, u32[]{:S(2)}, u32[]{:S(2)}) %collective-permute-start.35) | collective-permute-done | bytes 159776 | tf_op jit(solution)/shard_map/ppermute | solution.py:697
  224.4 19.3 %collective-permute-done.36 = bf16[208,384]{1,0:T(8,128)(2,1)S(1)} collective-permute-done((bf16[208,384]{1,0:T(8,128)(2,1)S(1)}, bf16[208,384]{1,0:T(8,128)(2,1)S(1)}, u32[]{:S(2)}, u32[]{:S(2)}) %collective-permute-start.36) | collective-permute-done | bytes 159776 | tf_op jit(solution)/shard_map/ppermute | solution.py:697
  243.9 12.0 %collective-permute-done.37 = bf16[208,768]{1,0:T(8,128)(2,1)S(1)} collective-permute-done((bf16[208,768]{1,0:T(8,128)(2,1)S(1)}, bf16[208,768]{1,0:T(8,128)(2,1)S(1)}, u32[]{:S(2)}, u32[]{:S(2)}) %collective-permute-start.37) | collective-permute-done | bytes 319520 | tf_op jit(solution)/shard_map/ppermute | solution.py:697
  256.2 4.0 %join_all.1 = (f32[192,2048]{1,0:T(8,128)}, f32[192,2048]{1,0:T(8,128)}, f32[512,768]{1,0:T(8,128)}) custom-call(bf16[4,2,576,256]{3,2,1,0:T(8,128)(2,1)} %bitcast.67), custom_call_target="tpu_custom_call" | custom-call | flops 1 | bytes 1 | tf_op jit(solution)/shard_map/join_all/pallas_call | solution.py:676
  260.2 1.5 join.1
  (165 shorter events, 22.4 us)
Async XLA Ops:
  7.2 74.4 %all-gather.5.cloned.1.call-start = ((), (), s32[]{:S(2)}) async-start(), calls=%async_computation.3 | async-start | bytes 5898240 | tf_op jit(solution)/shard_map/all_gather | solution.py:803
  10.1 166.5 %reduce-scatter.7.cloned.1.call-start = ((), (), s32[]{:S(2)}) async-start(), calls=%async_computation.5 | async-start | bytes 5898240
  14.2 27.3 %collective-permute-start = (bf16[208,1536]{1,0:T(8,128)(2,1)}, bf16[208,1536]{1,0:T(8,128)(2,1)S(1)}, u32[]{:S(2)}, u32[]{:S(2)}) collective-permute-start(bf16[208,1536]{1,0:T(8,128)(2,1)} %get-tuple-element.104.refs_11_), channel_id=1, source_target_pairs={{0,1},{1,0},{2,3},{3,2},{4,5},{5,4},{6,7},{7,6},{8,9},{9,8},{10,11... | collective-permute-start | bytes 1916936 | tf_op jit(solution)/shard_map/ppermute | solution.py:735
  17.2 27.2 %collective-permute-start.1 = (bf16[208,1536]{1,0:T(8,128)(2,1)}, bf16[208,1536]{1,0:T(8,128)(2,1)S(1)}, u32[]{:S(2)}, u32[]{:S(2)}) collective-permute-start(bf16[208,1536]{1,0:T(8,128)(2,1)} %get-tuple-element.104.refs_11_), channel_id=1, source_target_pairs={{0,2},{2,0},{1,3},{3,1},{4,6},{6,4},{5,7},{7,5},{8,10},{10,8},{9,1... | collective-permute-start | bytes 1916936 | tf_op jit(solution)/shard_map/ppermute | solution.py:736
  18.7 10.6 %collective-permute-start.5 = (bf16[144,768]{1,0:T(8,128)(2,1)}, bf16[144,768]{1,0:T(8,128)(2,1)S(1)}, u32[]{:S(2)}, u32[]{:S(2)}) collective-permute-start(bf16[144,768]{1,0:T(8,128)(2,1)} %get-tuple-element.111), channel_id=1, source_target_pairs={{0,24},{8,16},{16,8},{24,0},{1,25},{9,17},{17,9},{25,1},{2,26},{10... | collective-permute-start | bytes 663560 | tf_op jit(solution)/shard_map/ppermute | solution.py:697
  22.3 18.4 %collective-permute-start.4 = (bf16[144,768]{1,0:T(8,128)(2,1)}, bf16[144,768]{1,0:T(8,128)(2,1)S(1)}, u32[]{:S(2)}, u32[]{:S(2)}) collective-permute-start(bf16[144,768]{1,0:T(8,128)(2,1)} %get-tuple-element.109), channel_id=1, source_target_pairs={{0,16},{8,24},{16,0},{24,8},{1,17},{9,25},{17,1},{25,9},{2,18},{10... | collective-permute-start | bytes 663560 | tf_op jit(solution)/shard_map/ppermute | solution.py:697
  22.3 18.5 %collective-permute-start.3 = (bf16[144,768]{1,0:T(8,128)(2,1)}, bf16[144,768]{1,0:T(8,128)(2,1)}, u32[]{:S(2)}, u32[]{:S(2)}) collective-permute-start(bf16[144,768]{1,0:T(8,128)(2,1)} %get-tuple-element.107), channel_id=1, source_target_pairs={{0,8},{8,0},{16,24},{24,16},{1,9},{9,1},{17,25},{25,17},{2,10},{10... | collective-permute-start | bytes 663560 | tf_op jit(solution)/shard_map/ppermute | solution.py:697
  29.3 24.1 %copy-start.18 = (bf16[144,768]{1,0:T(8,128)(2,1)}, bf16[144,768]{1,0:T(8,128)(2,1)S(1)}, u32[]{:S(2)}) copy-start(bf16[144,768]{1,0:T(8,128)(2,1)S(1)} %collective-permute-done.5.refs_6_) | copy-start | bytes 663556
  29.3 25.0 %collective-permute-start.6 = (bf16[144,768]{1,0:T(8,128)(2,1)S(1)}, bf16[144,768]{1,0:T(8,128)(2,1)}, u32[]{:S(2)}, u32[]{:S(2)}) collective-permute-start(bf16[144,768]{1,0:T(8,128)(2,1)S(1)} %copy-done.17), channel_id=1, source_target_pairs={{0,4},{4,0},{1,5},{5,1},{2,6},{6,2},{3,7},{7,3},{8,12},{12,8},{9,1... | collective-permute-start | bytes 663560 | tf_op jit(solution)/shard_map/ppermute | solution.py:711
  40.7 12.6 %copy-start.19 = (bf16[144,768]{1,0:T(8,128)(2,1)}, bf16[144,768]{1,0:T(8,128)(2,1)S(1)}, u32[]{:S(2)}) copy-start(bf16[144,768]{1,0:T(8,128)(2,1)S(1)} %collective-permute-done.4.refs_5_) | copy-start | bytes 663556
  40.7 17.2 %collective-permute-start.9 = (bf16[144,768]{1,0:T(8,128)(2,1)S(1)}, bf16[144,768]{1,0:T(8,128)(2,1)}, u32[]{:S(2)}, u32[]{:S(2)}) collective-permute-start(bf16[144,768]{1,0:T(8,128)(2,1)S(1)} %collective-permute-done.5.refs_6_), channel_id=1, source_target_pairs={{0,4},{4,0},{1,5},{5,1},{2,6},{6,2},{3,7},{7,3},{8,12},{12,8},{9,1... | collective-permute-start | bytes 663560 | tf_op jit(solution)/shard_map/ppermute | solution.py:711
  40.8 17.2 %collective-permute-start.8 = (bf16[144,768]{1,0:T(8,128)(2,1)S(1)}, bf16[144,768]{1,0:T(8,128)(2,1)}, u32[]{:S(2)}, u32[]{:S(2)}) collective-permute-start(bf16[144,768]{1,0:T(8,128)(2,1)S(1)} %collective-permute-done.4.refs_5_), channel_id=1, source_target_pairs={{0,4},{4,0},{1,5},{5,1},{2,6},{6,2},{3,7},{7,3},{8,12},{12,8},{9,1... | collective-permute-start | bytes 663560 | tf_op jit(solution)/shard_map/ppermute | solution.py:711
  41.6 11.7 %collective-permute-start.2 = (bf16[112,1536]{1,0:T(8,128)(2,1)S(1)}, bf16[112,1536]{1,0:T(8,128)(2,1)S(1)}, u32[]{:S(2)}, u32[]{:S(2)}) collective-permute-start(bf16[112,1536]{1,0:T(8,128)(2,1)S(1)} %slice.96), channel_id=1, source_target_pairs={{0,2},{2,0},{1,3},{3,1},{4,6},{6,4},{5,7},{7,5},{8,10},{10,8},{9,1... | collective-permute-start | bytes 1032200 | tf_op jit(solution)/shard_map/ppermute | solution.py:738
  44.4 8.9 %collective-permute-start.10 = (bf16[96,1536]{1,0:T(8,128)(2,1)S(1)}, bf16[96,1536]{1,0:T(8,128)(2,1)S(1)}, u32[]{:S(2)}, u32[]{:S(2)}) collective-permute-start(bf16[96,1536]{1,0:T(8,128)(2,1)S(1)} %slice.99), channel_id=1, source_target_pairs={{0,1},{1,0},{2,3},{3,2},{4,5},{5,4},{6,7},{7,6},{8,9},{9,8},{10,11... | collective-permute-start | bytes 884744 | tf_op jit(solution)/shard_map/ppermute | solution.py:737
  53.2 5.7 %collective-permute-start.7 = (bf16[144,768]{1,0:T(8,128)(2,1)}, bf16[144,768]{1,0:T(8,128)(2,1)}, u32[]{:S(2)}, u32[]{:S(2)}) collective-permute-start(bf16[144,768]{1,0:T(8,128)(2,1)} %collective-permute-done.3.refs_4_), channel_id=1, source_target_pairs={{0,4},{4,0},{1,5},{5,1},{2,6},{6,2},{3,7},{7,3},{8,12},{12,8},{9,1... | collective-permute-start | bytes 663560 | tf_op jit(solution)/shard_map/ppermute | solution.py:711
  53.4 21.6 %collective-permute-start.14 = (bf16[384,384]{1,0:T(8,128)(2,1)S(1)}, bf16[384,384]{1,0:T(8,128)(2,1)S(1)}, u32[]{:S(2)}, u32[]{:S(2)}) collective-permute-start(bf16[384,384]{1,0:T(8,128)(2,1)S(1)} %get-tuple-element.203), channel_id=1, source_target_pairs={{0,4},{4,0},{1,5},{5,1},{2,6},{6,2},{3,7},{7,3},{8,12},{12,8},{9,1... | collective-permute-start | bytes 884744 | tf_op jit(solution)/shard_map/ppermute | solution.py:847
  54.2 19.7 %collective-permute-start.13 = (bf16[128,768]{1,0:T(8,128)(2,1)}, bf16[128,768]{1,0:T(8,128)(2,1)S(1)}, u32[]{:S(2)}, u32[]{:S(2)}) collective-permute-start(bf16[128,768]{1,0:T(8,128)(2,1)} %get-tuple-element.119), channel_id=1, source_target_pairs={{0,24},{8,16},{16,8},{24,0},{1,25},{9,17},{17,9},{25,1},{2,26},{10... | collective-permute-start | bytes 589832 | tf_op jit(solution)/shard_map/ppermute | solution.py:697
  57.9 17.1 %collective-permute-start.12 = (bf16[128,768]{1,0:T(8,128)(2,1)}, bf16[128,768]{1,0:T(8,128)(2,1)S(1)}, u32[]{:S(2)}, u32[]{:S(2)}) collective-permute-start(bf16[128,768]{1,0:T(8,128)(2,1)} %get-tuple-element.117), channel_id=1, source_target_pairs={{0,16},{8,24},{16,0},{24,8},{1,17},{9,25},{17,1},{25,9},{2,18},{10... | collective-permute-start | bytes 589832 | tf_op jit(solution)/shard_map/ppermute | solution.py:697
  57.9 17.1 %collective-permute-start.11 = (bf16[128,768]{1,0:T(8,128)(2,1)}, bf16[128,768]{1,0:T(8,128)(2,1)S(1)}, u32[]{:S(2)}, u32[]{:S(2)}) collective-permute-start(bf16[128,768]{1,0:T(8,128)(2,1)} %get-tuple-element.115), channel_id=1, source_target_pairs={{0,8},{8,0},{16,24},{24,16},{1,9},{9,1},{17,25},{25,17},{2,10},{10... | collective-permute-start | bytes 589832 | tf_op jit(solution)/shard_map/ppermute | solution.py:697
  77.5 3.6 %collective-permute-start.15 = (bf16[1024,768]{1,0:T(8,128)(2,1)S(1)}, bf16[1024,768]{1,0:T(8,128)(2,1)}, u32[]{:S(2)}, u32[]{:S(2)}) collective-permute-start(bf16[1024,768]{1,0:T(8,128)(2,1)S(1)} %convolution_convert_fusion.2.refs_1_), channel_id=1, source_target_pairs={{0,4},{4,0},{1,5},{5,1},{2,6},{6,2},{3,7},{7,3},{8,12},{12,8},{9,1... | collective-permute-start | bytes 4718600 | tf_op jit(solution)/shard_map/ppermute | solution.py:725
  81.6 12.1 %copy-start.4 = (bf16[128,768]{1,0:T(8,128)(2,1)S(1)}, bf16[128,768]{1,0:T(8,128)(2,1)}, u32[]{:S(2)}) copy-start(bf16[128,768]{1,0:T(8,128)(2,1)} %copy-done.3) | copy-start | bytes 589828
  93.1 4.6 %collective-permute-start.16 = (bf16[1024,768]{1,0:T(8,128)(2,1)S(1)}, bf16[1024,768]{1,0:T(8,128)(2,1)S(1)}, u32[]{:S(2)}, u32[]{:S(2)}) collective-permute-start(bf16[1024,768]{1,0:T(8,128)(2,1)S(1)} %get-tuple-element.124.refs_2_), channel_id=1, source_target_pairs={{0,4},{4,0},{1,5},{5,1},{2,6},{6,2},{3,7},{7,3},{8,12},{12,8},{9,1... | collective-permute-start | bytes 4718600 | tf_op jit(solution)/shard_map/ppermute | solution.py:725
  93.2 3.7 %collective-permute-start.17 = (bf16[128,768]{1,0:T(8,128)(2,1)S(1)}, bf16[128,768]{1,0:T(8,128)(2,1)S(1)}, u32[]{:S(2)}, u32[]{:S(2)}) collective-permute-start(bf16[128,768]{1,0:T(8,128)(2,1)S(1)} %copy-done.2), channel_id=1, source_target_pairs={{0,4},{4,0},{1,5},{5,1},{2,6},{6,2},{3,7},{7,3},{8,12},{12,8},{9,1... | collective-permute-start | bytes 589832 | tf_op jit(solution)/shard_map/ppermute | solution.py:711
  93.6 3.5 %collective-permute-start.18 = (bf16[128,768]{1,0:T(8,128)(2,1)S(1)}, bf16[128,768]{1,0:T(8,128)(2,1)S(1)}, u32[]{:S(2)}, u32[]{:S(2)}) collective-permute-start(bf16[128,768]{1,0:T(8,128)(2,1)S(1)} %copy-done.4), channel_id=1, source_target_pairs={{0,4},{4,0},{1,5},{5,1},{2,6},{6,2},{3,7},{7,3},{8,12},{12,8},{9,1... | collective-permute-start | bytes 589832 | tf_op jit(solution)/shard_map/ppermute | solution.py:711
  93.7 3.7 %collective-permute-start.19 = (bf16[128,768]{1,0:T(8,128)(2,1)S(1)}, bf16[128,768]{1,0:T(8,128)(2,1)S(1)}, u32[]{:S(2)}, u32[]{:S(2)}) collective-permute-start(bf16[128,768]{1,0:T(8,128)(2,1)S(1)} %collective-permute-done.12.refs_11_), channel_id=1, source_target_pairs={{0,4},{4,0},{1,5},{5,1},{2,6},{6,2},{3,7},{7,3},{8,12},{12,8},{9,1... | collective-permute-start | bytes 589832 | tf_op jit(solution)/shard_map/ppermute | solution.py:711
  94.2 3.5 %collective-permute-start.20 = (bf16[128,768]{1,0:T(8,128)(2,1)S(1)}, bf16[128,768]{1,0:T(8,128)(2,1)S(1)}, u32[]{:S(2)}, u32[]{:S(2)}) collective-permute-start(bf16[128,768]{1,0:T(8,128)(2,1)S(1)} %collective-permute-done.13.refs_12_), channel_id=1, source_target_pairs={{0,4},{4,0},{1,5},{5,1},{2,6},{6,2},{3,7},{7,3},{8,12},{12,8},{9,1... | collective-permute-start | bytes 589832 | tf_op jit(solution)/shard_map/ppermute | solution.py:711
  109.4 4.1 %collective-permute-start.24 = (bf16[1024,768]{1,0:T(8,128)(2,1)}, bf16[1024,768]{1,0:T(8,128)(2,1)}, u32[]{:S(2)}, u32[]{:S(2)}) collective-permute-start(bf16[1024,768]{1,0:T(8,128)(2,1)} %get-tuple-element.144.own_ref), channel_id=1, source_target_pairs={{0,4},{4,0},{1,5},{5,1},{2,6},{6,2},{3,7},{7,3},{8,12},{12,8},{9,1... | collective-permute-start | bytes 4718600 | tf_op jit(solution)/shard_map/ppermute | solution.py:725
  117.4 97.7 %reduce-scatter.5.cloned.1.call-start = ((), (), s32[]{:S(2)}) async-start(), calls=%async_computation.2 | async-start | bytes 1474560 | tf_op jit(solution)/shard_map/reduce_scatter | solution.py:925
  124.5 4.8 %collective-permute-start.25 = (bf16[384,384]{1,0:T(8,128)(2,1)S(1)}, bf16[384,384]{1,0:T(8,128)(2,1)S(1)}, u32[]{:S(2)}, u32[]{:S(2)}) collective-permute-start(bf16[384,384]{1,0:T(8,128)(2,1)S(1)} %get-tuple-element.201), channel_id=1, source_target_pairs={{0,4},{4,0},{1,5},{5,1},{2,6},{6,2},{3,7},{7,3},{8,12},{12,8},{9,1... | collective-permute-start | bytes 884744 | tf_op jit(solution)/shard_map/ppermute | solution.py:887
  124.9 18.5 %collective-permute-start.21 = (bf16[128,768]{1,0:T(8,128)(2,1)S(1)}, bf16[128,768]{1,0:T(8,128)(2,1)S(1)}, u32[]{:S(2)}, u32[]{:S(2)}) collective-permute-start(bf16[128,768]{1,0:T(8,128)(2,1)S(1)} %copy-done.23), channel_id=1, source_target_pairs={{0,8},{8,0},{16,24},{24,16},{1,9},{9,1},{17,25},{25,17},{2,10},{10... | collective-permute-start | bytes 589832 | tf_op jit(solution)/shard_map/ppermute | solution.py:697
  126.4 17.1 %collective-permute-start.22 = (bf16[128,768]{1,0:T(8,128)(2,1)S(1)}, bf16[128,768]{1,0:T(8,128)(2,1)S(1)}, u32[]{:S(2)}, u32[]{:S(2)}) collective-permute-start(bf16[128,768]{1,0:T(8,128)(2,1)S(1)} %copy-done.22), channel_id=1, source_target_pairs={{0,16},{8,24},{16,0},{24,8},{1,17},{9,25},{17,1},{25,9},{2,18},{10... | collective-permute-start | bytes 589832 | tf_op jit(solution)/shard_map/ppermute | solution.py:697
  128.9 14.7 %collective-permute-start.23 = (bf16[128,768]{1,0:T(8,128)(2,1)S(1)}, bf16[128,768]{1,0:T(8,128)(2,1)S(1)}, u32[]{:S(2)}, u32[]{:S(2)}) collective-permute-start(bf16[128,768]{1,0:T(8,128)(2,1)S(1)} %copy-done.21), channel_id=1, source_target_pairs={{0,24},{8,16},{16,8},{24,0},{1,25},{9,17},{17,9},{25,1},{2,26},{10... | collective-permute-start | bytes 589832 | tf_op jit(solution)/shard_map/ppermute | solution.py:697
  129.5 14.0 %copy-start.12 = (bf16[1024,768]{1,0:T(8,128)(2,1)S(1)}, bf16[1024,768]{1,0:T(8,128)(2,1)}, u32[]{:S(2)}) copy-start(bf16[1024,768]{1,0:T(8,128)(2,1)} %get-tuple-element.113.refs_0_) | copy-start | bytes 4718596
  147.5 13.4 %collective-permute-start.30 = (bf16[112,1536]{1,0:T(8,128)(2,1)S(1)}, bf16[112,1536]{1,0:T(8,128)(2,1)S(1)}, u32[]{:S(2)}, u32[]{:S(2)}) collective-permute-start(bf16[112,1536]{1,0:T(8,128)(2,1)S(1)} %slice_bitcast_fusion.1), channel_id=1, source_target_pairs={{0,2},{2,0},{1,3},{3,1},{4,6},{6,4},{5,7},{7,5},{8,10},{10,8},{9,1... | collective-permute-start | bytes 1032200 | tf_op jit(solution)/shard_map/ppermute | solution.py:753
  151.3 2.4 collective-permute-start.26
  151.4 9.5 %collective-permute-start.29 = (bf16[96,1536]{1,0:T(8,128)(2,1)S(1)}, bf16[96,1536]{1,0:T(8,128)(2,1)S(1)}, u32[]{:S(2)}, u32[]{:S(2)}) collective-permute-start(bf16[96,1536]{1,0:T(8,128)(2,1)S(1)} %slice_bitcast_fusion.4), channel_id=1, source_target_pairs={{0,1},{1,0},{2,3},{3,2},{4,5},{5,4},{6,7},{7,6},{8,9},{9,8},{10,11... | collective-permute-start | bytes 884744 | tf_op jit(solution)/shard_map/ppermute | solution.py:753
  154.5 12.9 %collective-permute-start.27 = (bf16[128,768]{1,0:T(8,128)(2,1)S(1)}, bf16[128,768]{1,0:T(8,128)(2,1)S(1)}, u32[]{:S(2)}, u32[]{:S(2)}) collective-permute-start(bf16[128,768]{1,0:T(8,128)(2,1)S(1)} %get-tuple-element.162), channel_id=1, source_target_pairs={{0,8},{8,0},{16,24},{24,16},{1,9},{9,1},{17,25},{25,17},{2,10},{10... | collective-permute-start | bytes 589832 | tf_op jit(solution)/shard_map/ppermute | solution.py:697
  158.2 11.8 %collective-permute-start.28 = (bf16[128,768]{1,0:T(8,128)(2,1)S(1)}, bf16[128,768]{1,0:T(8,128)(2,1)S(1)}, u32[]{:S(2)}, u32[]{:S(2)}) collective-permute-start(bf16[128,768]{1,0:T(8,128)(2,1)S(1)} %get-tuple-element.163), channel_id=1, source_target_pairs={{0,16},{8,24},{16,0},{24,8},{1,17},{9,25},{17,1},{25,9},{2,18},{10... | collective-permute-start | bytes 589832 | tf_op jit(solution)/shard_map/ppermute | solution.py:697
  170.2 11.9 %copy-start.5 = (bf16[128,768]{1,0:T(8,128)(2,1)S(1)}, bf16[128,768]{1,0:T(8,128)(2,1)}, u32[]{:S(2)}) copy-start(bf16[128,768]{1,0:T(8,128)(2,1)} %get-tuple-element.166.refs_0_) | copy-start | bytes 589828
  176.6 79.6 %all-gather.7.cloned.1.call-start = ((), (), s32[]{:S(2)}) async-start(), calls=%async_computation.4 | async-start | bytes 2654208 | tf_op jit(solution)/shard_map/all_gather | solution.py:928
  176.6 16.2 %collective-permute-start.32 = (bf16[208,1536]{1,0:T(8,128)(2,1)S(1)}, bf16[208,1536]{1,0:T(8,128)(2,1)S(1)}, u32[]{:S(2)}, u32[]{:S(2)}) collective-permute-start(bf16[208,1536]{1,0:T(8,128)(2,1)S(1)} %pad_maximum_fusion.3), channel_id=1, source_target_pairs={{0,2},{2,0},{1,3},{3,1},{4,6},{6,4},{5,7},{7,5},{8,10},{10,8},{9,1... | collective-permute-start | bytes 1916936 | tf_op jit(solution)/shard_map/ppermute | solution.py:762
  178.0 16.1 %collective-permute-start.31 = (bf16[208,1536]{1,0:T(8,128)(2,1)}, bf16[208,1536]{1,0:T(8,128)(2,1)}, u32[]{:S(2)}, u32[]{:S(2)}) collective-permute-start(bf16[208,1536]{1,0:T(8,128)(2,1)} %pad_maximum_fusion.2), channel_id=1, source_target_pairs={{0,1},{1,0},{2,3},{3,2},{4,5},{5,4},{6,7},{7,6},{8,9},{9,8},{10,11... | collective-permute-start | bytes 1916936 | tf_op jit(solution)/shard_map/ppermute | solution.py:762
  178.7 8.8 %collective-permute-start.33 = (bf16[128,768]{1,0:T(8,128)(2,1)S(1)}, bf16[128,768]{1,0:T(8,128)(2,1)S(1)}, u32[]{:S(2)}, u32[]{:S(2)}) collective-permute-start(bf16[128,768]{1,0:T(8,128)(2,1)S(1)} %get-tuple-element.170), channel_id=1, source_target_pairs={{0,24},{8,16},{16,8},{24,0},{1,25},{9,17},{17,9},{25,1},{2,26},{10... | collective-permute-start | bytes 589832 | tf_op jit(solution)/shard_map/ppermute | solution.py:697
  195.8 19.4 %collective-permute-start.34 = (bf16[208,768]{1,0:T(8,128)(2,1)S(1)}, bf16[208,768]{1,0:T(8,128)(2,1)S(1)}, u32[]{:S(2)}, u32[]{:S(2)}) collective-permute-start(bf16[208,768]{1,0:T(8,128)(2,1)S(1)} %constant_dynamic-slice_fusion.1), channel_id=1, source_target_pairs={{0,8},{8,0},{16,24},{24,16},{1,9},{9,1},{17,25},{25,17},{2,10},{10... | collective-permute-start | bytes 958472 | tf_op jit(solution)/shard_map/ppermute | solution.py:697
  215.3 9.0 %collective-permute-start.35 = (bf16[208,384]{1,0:T(8,128)(2,1)S(1)}, bf16[208,384]{1,0:T(8,128)(2,1)S(1)}, u32[]{:S(2)}, u32[]{:S(2)}) collective-permute-start(bf16[208,384]{1,0:T(8,128)(2,1)S(1)} %constant_dynamic-slice_fusion), channel_id=1, source_target_pairs={{0,16},{8,24},{16,0},{24,8},{1,17},{9,25},{17,1},{25,9},{2,18},{10... | collective-permute-start | bytes 479240 | tf_op jit(solution)/shard_map/ppermute | solution.py:697
  224.4 19.4 %collective-permute-start.36 = (bf16[208,384]{1,0:T(8,128)(2,1)S(1)}, bf16[208,384]{1,0:T(8,128)(2,1)S(1)}, u32[]{:S(2)}, u32[]{:S(2)}) collective-permute-start(bf16[208,384]{1,0:T(8,128)(2,1)S(1)} %add_convert_fusion.1), channel_id=1, source_target_pairs={{0,16},{8,24},{16,0},{24,8},{1,17},{9,25},{17,1},{25,9},{2,18},{10... | collective-permute-start | bytes 479240 | tf_op jit(solution)/shard_map/ppermute | solution.py:697
  243.8 12.1 %collective-permute-start.37 = (bf16[208,768]{1,0:T(8,128)(2,1)S(1)}, bf16[208,768]{1,0:T(8,128)(2,1)S(1)}, u32[]{:S(2)}, u32[]{:S(2)}) collective-permute-start(bf16[208,768]{1,0:T(8,128)(2,1)S(1)} %pad_maximum_fusion.7), channel_id=1, source_target_pairs={{0,8},{8,0},{16,24},{24,16},{1,9},{9,1},{17,25},{25,17},{2,10},{10... | collective-permute-start | bytes 958472 | tf_op jit(solution)/shard_map/ppermute | solution.py:697
  256.1 4.1 %collective-permute-start.38 = (bf16[208,1536]{1,0:T(8,128)(2,1)S(1)}, bf16[208,1536]{1,0:T(8,128)(2,1)S(1)}, u32[]{:S(2)}, u32[]{:S(2)}) collective-permute-start(bf16[208,1536]{1,0:T(8,128)(2,1)S(1)} %pad_maximum_fusion.4.refs_1_), channel_id=1, source_target_pairs={{0,4},{4,0},{1,5},{5,1},{2,6},{6,2},{3,7},{7,3},{8,12},{12,8},{9,1... | collective-permute-start | bytes 1916936 | tf_op jit(solution)/shard_map/ppermute | solution.py:962
  (21 other events, 93.9 us)
Sparse Core Ops, SparseCore 0:
  10.4 71.0 all-gather.4
  117.6 58.9 reduce-scatter.6
  178.9 33.7 reduce-scatter.4
  215.3 37.0 all-gather.6

commit v6 on v5

--- a/solution.py
+++ b/solution.py
@@ -865,7 +865,7 @@
         if ranks != 2:
             cot_refs = cot_refs[:1]
         total, middle_low, hidden_low, gate_back, silu, part, gu, down = forward(
-            x, own, got, gain_one, stack_all, shard, part_rows, half_ff, block)
+            x, own, got, gain_one, stack_all, shard, part_rows, half_ff, 512)
         own, got = exchange(part)
 
         *out_slabs, ffn_grad_low, gu_grad_low, part, gain_ffn_grad = backward(

time: 269 us -> 268 us (level)
  no operation moved by 1% of the time
where the time goes in v6:
time: 268 us
  waiting for transfers between devices  109 us (41%)
  Pallas kernels  76.5 us (29%)
  starting transfers between devices  42.9 us (16%)
  between operations  14.5 us (5%)
  matrix products  11.4 us (4%)
  other arithmetic  8.81 us (3%)
  local copies, waits for them, and re-layouts  4.77 us (2%)
    ppermute x16, waiting for transfers between devices, hop(): return lax.ppermute(value, 'm', [(i, i ^ k) for i in range(groups)])  77.3 us
    ppermute x16, starting transfers between devices, hop(): return lax.ppermute(value, 'm', [(i, i ^ k) for i in range(groups)])  28.3 us
    pallas_call x1, Pallas kernels, attend(): pl.pallas_call(kernel, grid=(pairs,), in_specs=[SMEM_SPEC] + whole_specs(...  15 us
    pallas_call x1, Pallas kernels, attend_back(): pl.pallas_call(kernel, grid=(pairs,), in_specs=whole_specs(seg) + [VMEM_S...  13.8 us
    pallas_call x1, Pallas kernels, backward(): pl.pallas_call(kernel, grid=(tokens // block,), in_specs=[SMEM_SPEC, VMEM...  11.8 us
    dot_general x5, matrix products, dot(): lax.dot_general(left, right, (dims, ((), ())), preferred_element_type=F32)  11.4 us
    pallas_call x1, Pallas kernels, forward(): pl.pallas_call(lambda *refs: forward_kernel(*refs, shard=shard, part_rows...  11.3 us
    ppermute x1, waiting for transfers between devices, gather_rows(): far_b = lax.ppermute(from_x[rows:], 'y', swap)  7.7 us
  transfers between devices with their start and end apart: 43, of which 24 were waited for; matrix products, arithmetic and copies ran while one was open for 9% of the time, Pallas kernels for 17%

profile of v6, /device:TPU:0, one launch (start us, length us, event | category | flops | bytes accessed | tf_op | source)
XLA Modules:
  0.0 268.0 jit_solution(13267350012396917938)
XLA Ops:
  7.3 2.8 %pack.1 = bf16[2304,256]{1,0:T(8,128)(2,1)} custom-call(s32[3]{0:T(128)S(1)} %pad_add_fusion.refs_0_.where_ref, bf16[192,2048]{1,0:T(8,128)(2,1)} %refs_1_.2, bf16[192,2048]{1,0:T(8,128)(2,1)} %refs_2_.2, bf16[512,768]{1,0:T(8,128)(2,1)} %refs_3_.2), custom_call_target="tpu_custom_call" | custom-call | flops 1 | bytes 1 | tf_op jit(solution)/shard_map/pack/pallas_call | solution.py:455
  10.8 3.4 %pack_small.1 = (bf16[208,1536]{1,0:T(8,128)(2,1)}, bf16[144,768]{1,0:T(8,128)(2,1)}, bf16[144,768]{1,0:T(8,128)(2,1)}, bf16[144,768]{1,0:T(8,128)(2,1)}, bf16[1...) custom-call(s32[3]{0:T(128)S(1)} %pad_add_fusion.refs_0_.where_ref, ...), custom_call_target="tpu_custom_call" | custom-call | flops 1 | bytes 1 | tf_op jit(solution)/shard_map/pack_small/pallas_call | solution.py:419
  14.2 3.0 %collective-permute-start = (bf16[208,1536]{1,0:T(8,128)(2,1)}, bf16[208,1536]{1,0:T(8,128)(2,1)S(1)}, u32[]{:S(2)}, u32[]{:S(2)}) collective-permute-start(bf16[208,1536]{1,0:T(8,128)(2,1)} %get-tuple-element.104.refs_11_), channel_id=1, source_target_pairs={{0,1},{1,0},{2,3},{3,2},{4,5},{5,4},{6,7},{7,6},{8,9},{9,8},{10,11... | collective-permute-start | bytes 1916936 | tf_op jit(solution)/shard_map/ppermute | solution.py:735
  17.2 1.5 collective-permute-start.1
  18.7 3.6 %collective-permute-start.5 = (bf16[144,768]{1,0:T(8,128)(2,1)}, bf16[144,768]{1,0:T(8,128)(2,1)S(1)}, u32[]{:S(2)}, u32[]{:S(2)}) collective-permute-start(bf16[144,768]{1,0:T(8,128)(2,1)} %get-tuple-element.111), channel_id=1, source_target_pairs={{0,24},{8,16},{16,8},{24,0},{1,25},{9,17},{17,9},{25,1},{2,26},{10... | collective-permute-start | bytes 663560 | tf_op jit(solution)/shard_map/ppermute | solution.py:697
  23.1 1.9 fusion.9
  25.0 1.3 pad_maximum_fusion.5.refs_1_.refs_8_
  29.4 11.4 %collective-permute-done.4.refs_5_ = bf16[144,768]{1,0:T(8,128)(2,1)S(1)} collective-permute-done((bf16[144,768]{1,0:T(8,128)(2,1)}, bf16[144,768]{1,0:T(8,128)(2,1)S(1)}, u32[]{:S(2)}, u32[]{:S(2)}) %collective-permute-start.4) | collective-permute-done | bytes 221216 | tf_op jit(solution)/shard_map/ppermute | solution.py:697
  41.6 1.4 collective-permute-start.2
  43.0 1.4 collective-permute-done.1.refs_13_
  45.5 7.7 %collective-permute-done.2.refs_15_ = bf16[112,1536]{1,0:T(8,128)(2,1)S(1)} collective-permute-done((bf16[112,1536]{1,0:T(8,128)(2,1)S(1)}, bf16[112,1536]{1,0:T(8,128)(2,1)S(1)}, u32[]{:S(2)}, u32[]{:S(2)}) %collective-permute-start.2) | collective-permute-done | bytes 344096 | tf_op jit(solution)/shard_map/ppermute | solution.py:738
  54.2 3.7 %collective-permute-start.13 = (bf16[128,768]{1,0:T(8,128)(2,1)}, bf16[128,768]{1,0:T(8,128)(2,1)S(1)}, u32[]{:S(2)}, u32[]{:S(2)}) collective-permute-start(bf16[128,768]{1,0:T(8,128)(2,1)} %get-tuple-element.119), channel_id=1, source_target_pairs={{0,24},{8,16},{16,8},{24,0},{1,25},{9,17},{17,9},{25,1},{2,26},{10... | collective-permute-start | bytes 589832 | tf_op jit(solution)/shard_map/ppermute | solution.py:697
  58.9 15.0 %attend.1 = (bf16[1024,384]{1,0:T(8,128)(2,1)}, bf16[1024,384]{1,0:T(8,128)(2,1)}, bf16[1024,384]{1,0:T(8,128)(2,1)}, bf16[1024,384]{1,0:T(8,128)(2,1)}, f32[3,8...) custom-call(s32[3]{0:T(128)S(1)} %pad_add_fusion.refs_0_.where_ref, ...), custom_call_target="tpu_custom_call" | custom-call | flops 1 | bytes 1 | tf_op jit(solution)/shard_map/attend/pallas_call | solution.py:186
  75.2 2.3 convolution_convert_fusion.2.refs_1_
  77.6 3.5 %collective-permute-done.15.refs_2_ = bf16[1024,768]{1,0:T(8,128)(2,1)} collective-permute-done((bf16[1024,768]{1,0:T(8,128)(2,1)S(1)}, bf16[1024,768]{1,0:T(8,128)(2,1)}, u32[]{:S(2)}, u32[]{:S(2)}) %collective-permute-start.15) | collective-permute-done | bytes 1572896 | tf_op jit(solution)/shard_map/ppermute | solution.py:725
  81.6 11.3 %ffn_forward.1 = (f32[1024,768]{1,0:T(8,128)S(1)}, bf16[1024,768]{1,0:T(8,128)(2,1)S(1)}, bf16[1024,1024]{1,0:T(8,128)(2,1)S(1)}, bf16[1024,1024]{1,0:T(8,128)(2...) custom-call(bf16[1024,768]{1,0:T(8,128)(2,1)} %get-tuple-element.113, ...), custom_call_target="tpu_custom_call" | custom-call | flops 1 | bytes 1 | tf_op jit(solution)/shard_map/ffn_forward/pallas_call | solution.py:247
  94.1 2.6 collective-permute-done.17.refs_13_
  97.5 11.8 %ffn_backward.1 = (bf16[128,768]{1,0:T(8,128)(2,1)}, bf16[128,768]{1,0:T(8,128)(2,1)}, bf16[128,768]{1,0:T(8,128)(2,1)}, bf16[128,768]{1,0:T(8,128)(2,1)}, bf16[...) custom-call(s32[3]{0:T(128)S(1)} %pad_add_fusion.refs_0_.where_ref, ...), custom_call_target="tpu_custom_call" | custom-call | flops 1 | bytes 1 | tf_op jit(solution)/shard_map/ffn_backward/pallas_call | solution.py:308
  109.4 3.8 %convolution_convert_fusion.1.gu_ref = bf16[768,2048]{1,0:T(8,128)(2,1)S(1)} fusion(bf16[1024,768]{1,0:T(8,128)(2,1)S(1)} %get-tuple-element.140, bf16[1024,2048]{1,0:T(8,128)(2,1)S(1)} %get-tuple-element.141), kind=kOutput, calls=%fused_computation.6 | convolution fusion | flops 3222798336 | bytes 8912896 | tf_op jit(solution)/shard_map/dot_general | solution.py:19
  113.3 3.9 %arrange.1 = bf16[4,2304,256]{2,1,0:T(8,128)(2,1)} custom-call(bf16[768,2048]{1,0:T(8,128)(2,1)S(1)} %convolution_convert_fusion.1.gu_ref, bf16[1024,1024]{1,0:T(8,128)(2,1)S(1)} %get-tuple-element.143.hidden_ref, bf16[1024,768]{1,0:T(8,128)(2,1)S(1)} %get-tuple-element.138.grad_ref), custom_call_target="tpu_custom_call" | custom-call | flops 1 | bytes 1 | tf_op jit(solution)/shard_map/arrange/pallas_call | solution.py:493
  117.8 5.3 %norm_back.1 = (bf16[1024,768]{1,0:T(8,128)(2,1)S(1)}, f32[4,128,768]{2,1,0:T(8,128)}, bf16[4,16,1536]{2,1,0:T(8,128)(2,1)}) custom-call(s32[1]{0:T(128)} %bitcast.2.rank_ref.refs_0_, f32[1024,768]{1,0:T(8,128)S(1)} %get-tuple-element.123.refs_1_.sum_ref, bf16[1024,768]{1,0:T(8,128)(2,1)} %copy-done, bf16[1024,768]{1,0:T(8,128)(2,1)} %get-tuple-element.144.own_ref, ...), custom_call_target="tpu_custom_call" | custom-call | flops 1 | bytes 1 | tf_op jit(solution)/shard_map/norm_back/pallas_call | solution.py:361
  124.6 1.5 collective-permute-start.21
  126.1 2.4 collective-permute-start.22
  129.2 13.8 %attend_back.1 = bf16[1024,1152]{1,0:T(8,128)(2,1)S(1)} custom-call(f32[1,1024]{1,0:T(1,128)} %get-tuple-element.137.refs_0_, bf16[1024,768]{1,0:T(8,128)(2,1)S(1)} %get-tuple-element.151.refs_1_, bf16[384,768]{1,0:T(8,128)(2,1)} %copy-done.9, bf16[1024,384]{1,0:T(8,128)(2,1)} %get-tuple-element.152.refs_3_, bf16[1024,384]{1,0:T(8,128)(2,1)} %get-tuple-element.153.refs_4_, ...), custom_call_target="tpu_custom_call" | custom-call | flops 1 | bytes 1 | tf_op jit(solution)/shard_map/attend_back/pallas_call | solution.py:607
  143.2 2.3 convolution_convert_fusion
  147.1 1.5 collective-permute-start.30
  148.6 2.2 convolution_convert_fusion.3.refs_2_
  152.0 1.3 collective-permute-done.26.refs_3_
  154.1 3.9 %collective-permute-start.27 = (bf16[128,768]{1,0:T(8,128)(2,1)S(1)}, bf16[128,768]{1,0:T(8,128)(2,1)S(1)}, u32[]{:S(2)}, u32[]{:S(2)}) collective-permute-start(bf16[128,768]{1,0:T(8,128)(2,1)S(1)} %get-tuple-element.162), channel_id=1, source_target_pairs={{0,8},{8,0},{16,24},{24,16},{1,9},{9,1},{17,25},{25,17},{2,10},{10... | collective-permute-start | bytes 589832 | tf_op jit(solution)/shard_map/ppermute | solution.py:697
  159.0 1.5 collective-permute-done.29
  160.5 6.6 %collective-permute-done.27.refs_1_ = bf16[128,768]{1,0:T(8,128)(2,1)S(1)} collective-permute-done((bf16[128,768]{1,0:T(8,128)(2,1)S(1)}, bf16[128,768]{1,0:T(8,128)(2,1)S(1)}, u32[]{:S(2)}, u32[]{:S(2)}) %collective-permute-start.27) | collective-permute-done | bytes 196640 | tf_op jit(solution)/shard_map/ppermute | solution.py:697
  167.1 2.6 collective-permute-done.28.refs_2_
  170.9 5.4 %reduce-scatter.7.cloned.1.call-done = bf16[1,2304,256]{2,1,0:T(8,128)(2,1)} async-done(((bf16[4,2304,256]{2,1,0:T(8,128)(2,1)}), bf16[1,2304,256]{2,1,0:T(8,128)(2,1)}) %reduce-scatter.7.cloned.1.call-update) | async-done | bytes 1179664
  176.3 1.4 collective-permute-start.32
  178.4 3.3 %collective-permute-start.33 = (bf16[128,768]{1,0:T(8,128)(2,1)S(1)}, bf16[128,768]{1,0:T(8,128)(2,1)S(1)}, u32[]{:S(2)}, u32[]{:S(2)}) collective-permute-start(bf16[128,768]{1,0:T(8,128)(2,1)S(1)} %get-tuple-element.170), channel_id=1, source_target_pairs={{0,24},{8,16},{16,8},{24,0},{1,25},{9,17},{17,9},{25,1},{2,26},{10... | collective-permute-start | bytes 589832 | tf_op jit(solution)/shard_map/ppermute | solution.py:697
  181.7 1.5 stack.30
  183.2 4.0 %collective-permute-done.33.refs_3_ = bf16[128,768]{1,0:T(8,128)(2,1)S(1)} collective-permute-done((bf16[128,768]{1,0:T(8,128)(2,1)S(1)}, bf16[128,768]{1,0:T(8,128)(2,1)S(1)}, u32[]{:S(2)}, u32[]{:S(2)}) %collective-permute-start.33) | collective-permute-done | bytes 196640 | tf_op jit(solution)/shard_map/ppermute | solution.py:697
  187.2 5.3 %collective-permute-done.32 = bf16[208,1536]{1,0:T(8,128)(2,1)S(1)} collective-permute-done((bf16[208,1536]{1,0:T(8,128)(2,1)S(1)}, bf16[208,1536]{1,0:T(8,128)(2,1)S(1)}, u32[]{:S(2)}, u32[]{:S(2)}) %collective-permute-start.32) | collective-permute-done | bytes 639008 | tf_op jit(solution)/shard_map/ppermute | solution.py:762
  192.5 1.4 collective-permute-done.31
  193.9 1.5 fusion.1
  195.5 6.7 %collective-permute-start.34 = (bf16[208,768]{1,0:T(8,128)(2,1)S(1)}, bf16[208,768]{1,0:T(8,128)(2,1)S(1)}, u32[]{:S(2)}, u32[]{:S(2)}) collective-permute-start(bf16[208,768]{1,0:T(8,128)(2,1)S(1)} %constant_dynamic-slice_fusion.1), channel_id=1, source_target_pairs={{0,8},{8,0},{16,24},{24,16},{1,9},{9,1},{17,25},{25,17},{2,10},{10... | collective-permute-start | bytes 958472 | tf_op jit(solution)/shard_map/ppermute | solution.py:697
  202.1 1.5 stack.31
  203.6 11.2 %collective-permute-done.34 = bf16[208,768]{1,0:T(8,128)(2,1)S(1)} collective-permute-done((bf16[208,768]{1,0:T(8,128)(2,1)S(1)}, bf16[208,768]{1,0:T(8,128)(2,1)S(1)}, u32[]{:S(2)}, u32[]{:S(2)}) %collective-permute-start.34) | collective-permute-done | bytes 319520 | tf_op jit(solution)/shard_map/ppermute | solution.py:697
  215.1 9.0 %collective-permute-done.35 = bf16[208,384]{1,0:T(8,128)(2,1)S(1)} collective-permute-done((bf16[208,384]{1,0:T(8,128)(2,1)S(1)}, bf16[208,384]{1,0:T(8,128)(2,1)S(1)}, u32[]{:S(2)}, u32[]{:S(2)}) %collective-permute-start.35) | collective-permute-done | bytes 159776 | tf_op jit(solution)/shard_map/ppermute | solution.py:697
  224.2 19.2 %collective-permute-done.36 = bf16[208,384]{1,0:T(8,128)(2,1)S(1)} collective-permute-done((bf16[208,384]{1,0:T(8,128)(2,1)S(1)}, bf16[208,384]{1,0:T(8,128)(2,1)S(1)}, u32[]{:S(2)}, u32[]{:S(2)}) %collective-permute-start.36) | collective-permute-done | bytes 159776 | tf_op jit(solution)/shard_map/ppermute | solution.py:697
  243.6 12.0 %collective-permute-done.37 = bf16[208,768]{1,0:T(8,128)(2,1)S(1)} collective-permute-done((bf16[208,768]{1,0:T(8,128)(2,1)S(1)}, bf16[208,768]{1,0:T(8,128)(2,1)S(1)}, u32[]{:S(2)}, u32[]{:S(2)}) %collective-permute-start.37) | collective-permute-done | bytes 319520 | tf_op jit(solution)/shard_map/ppermute | solution.py:697
  255.9 4.0 %join_all.1 = (f32[192,2048]{1,0:T(8,128)}, f32[192,2048]{1,0:T(8,128)}, f32[512,768]{1,0:T(8,128)}) custom-call(bf16[4,2,576,256]{3,2,1,0:T(8,128)(2,1)} %bitcast.67), custom_call_target="tpu_custom_call" | custom-call | flops 1 | bytes 1 | tf_op jit(solution)/shard_map/join_all/pallas_call | solution.py:676
  259.9 1.5 join.1
  (165 shorter events, 22.3 us)
Async XLA Ops:
  7.2 74.4 %all-gather.5.cloned.1.call-start = ((), (), s32[]{:S(2)}) async-start(), calls=%async_computation.3 | async-start | bytes 5898240 | tf_op jit(solution)/shard_map/all_gather | solution.py:803
  10.1 166.2 %reduce-scatter.7.cloned.1.call-start = ((), (), s32[]{:S(2)}) async-start(), calls=%async_computation.5 | async-start | bytes 5898240
  14.2 27.3 %collective-permute-start = (bf16[208,1536]{1,0:T(8,128)(2,1)}, bf16[208,1536]{1,0:T(8,128)(2,1)S(1)}, u32[]{:S(2)}, u32[]{:S(2)}) collective-permute-start(bf16[208,1536]{1,0:T(8,128)(2,1)} %get-tuple-element.104.refs_11_), channel_id=1, source_target_pairs={{0,1},{1,0},{2,3},{3,2},{4,5},{5,4},{6,7},{7,6},{8,9},{9,8},{10,11... | collective-permute-start | bytes 1916936 | tf_op jit(solution)/shard_map/ppermute | solution.py:735
  17.2 27.2 %collective-permute-start.1 = (bf16[208,1536]{1,0:T(8,128)(2,1)}, bf16[208,1536]{1,0:T(8,128)(2,1)S(1)}, u32[]{:S(2)}, u32[]{:S(2)}) collective-permute-start(bf16[208,1536]{1,0:T(8,128)(2,1)} %get-tuple-element.104.refs_11_), channel_id=1, source_target_pairs={{0,2},{2,0},{1,3},{3,1},{4,6},{6,4},{5,7},{7,5},{8,10},{10,8},{9,1... | collective-permute-start | bytes 1916936 | tf_op jit(solution)/shard_map/ppermute | solution.py:736
  18.7 10.6 %collective-permute-start.5 = (bf16[144,768]{1,0:T(8,128)(2,1)}, bf16[144,768]{1,0:T(8,128)(2,1)S(1)}, u32[]{:S(2)}, u32[]{:S(2)}) collective-permute-start(bf16[144,768]{1,0:T(8,128)(2,1)} %get-tuple-element.111), channel_id=1, source_target_pairs={{0,24},{8,16},{16,8},{24,0},{1,25},{9,17},{17,9},{25,1},{2,26},{10... | collective-permute-start | bytes 663560 | tf_op jit(solution)/shard_map/ppermute | solution.py:697
  22.3 18.4 %collective-permute-start.4 = (bf16[144,768]{1,0:T(8,128)(2,1)}, bf16[144,768]{1,0:T(8,128)(2,1)S(1)}, u32[]{:S(2)}, u32[]{:S(2)}) collective-permute-start(bf16[144,768]{1,0:T(8,128)(2,1)} %get-tuple-element.109), channel_id=1, source_target_pairs={{0,16},{8,24},{16,0},{24,8},{1,17},{9,25},{17,1},{25,9},{2,18},{10... | collective-permute-start | bytes 663560 | tf_op jit(solution)/shard_map/ppermute | solution.py:697
  22.3 18.5 %collective-permute-start.3 = (bf16[144,768]{1,0:T(8,128)(2,1)}, bf16[144,768]{1,0:T(8,128)(2,1)}, u32[]{:S(2)}, u32[]{:S(2)}) collective-permute-start(bf16[144,768]{1,0:T(8,128)(2,1)} %get-tuple-element.107), channel_id=1, source_target_pairs={{0,8},{8,0},{16,24},{24,16},{1,9},{9,1},{17,25},{25,17},{2,10},{10... | collective-permute-start | bytes 663560 | tf_op jit(solution)/shard_map/ppermute | solution.py:697
  29.3 24.1 %copy-start.18 = (bf16[144,768]{1,0:T(8,128)(2,1)}, bf16[144,768]{1,0:T(8,128)(2,1)S(1)}, u32[]{:S(2)}) copy-start(bf16[144,768]{1,0:T(8,128)(2,1)S(1)} %collective-permute-done.5.refs_6_) | copy-start | bytes 663556
  29.3 25.0 %collective-permute-start.6 = (bf16[144,768]{1,0:T(8,128)(2,1)S(1)}, bf16[144,768]{1,0:T(8,128)(2,1)}, u32[]{:S(2)}, u32[]{:S(2)}) collective-permute-start(bf16[144,768]{1,0:T(8,128)(2,1)S(1)} %copy-done.17), channel_id=1, source_target_pairs={{0,4},{4,0},{1,5},{5,1},{2,6},{6,2},{3,7},{7,3},{8,12},{12,8},{9,1... | collective-permute-start | bytes 663560 | tf_op jit(solution)/shard_map/ppermute | solution.py:711
  40.7 12.6 %copy-start.19 = (bf16[144,768]{1,0:T(8,128)(2,1)}, bf16[144,768]{1,0:T(8,128)(2,1)S(1)}, u32[]{:S(2)}) copy-start(bf16[144,768]{1,0:T(8,128)(2,1)S(1)} %collective-permute-done.4.refs_5_) | copy-start | bytes 663556
  40.7 17.2 %collective-permute-start.9 = (bf16[144,768]{1,0:T(8,128)(2,1)S(1)}, bf16[144,768]{1,0:T(8,128)(2,1)}, u32[]{:S(2)}, u32[]{:S(2)}) collective-permute-start(bf16[144,768]{1,0:T(8,128)(2,1)S(1)} %collective-permute-done.5.refs_6_), channel_id=1, source_target_pairs={{0,4},{4,0},{1,5},{5,1},{2,6},{6,2},{3,7},{7,3},{8,12},{12,8},{9,1... | collective-permute-start | bytes 663560 | tf_op jit(solution)/shard_map/ppermute | solution.py:711
  40.8 17.2 %collective-permute-start.8 = (bf16[144,768]{1,0:T(8,128)(2,1)S(1)}, bf16[144,768]{1,0:T(8,128)(2,1)}, u32[]{:S(2)}, u32[]{:S(2)}) collective-permute-start(bf16[144,768]{1,0:T(8,128)(2,1)S(1)} %collective-permute-done.4.refs_5_), channel_id=1, source_target_pairs={{0,4},{4,0},{1,5},{5,1},{2,6},{6,2},{3,7},{7,3},{8,12},{12,8},{9,1... | collective-permute-start | bytes 663560 | tf_op jit(solution)/shard_map/ppermute | solution.py:711
  41.6 11.7 %collective-permute-start.2 = (bf16[112,1536]{1,0:T(8,128)(2,1)S(1)}, bf16[112,1536]{1,0:T(8,128)(2,1)S(1)}, u32[]{:S(2)}, u32[]{:S(2)}) collective-permute-start(bf16[112,1536]{1,0:T(8,128)(2,1)S(1)} %slice.96), channel_id=1, source_target_pairs={{0,2},{2,0},{1,3},{3,1},{4,6},{6,4},{5,7},{7,5},{8,10},{10,8},{9,1... | collective-permute-start | bytes 1032200 | tf_op jit(solution)/shard_map/ppermute | solution.py:738
  44.4 8.9 %collective-permute-start.10 = (bf16[96,1536]{1,0:T(8,128)(2,1)S(1)}, bf16[96,1536]{1,0:T(8,128)(2,1)S(1)}, u32[]{:S(2)}, u32[]{:S(2)}) collective-permute-start(bf16[96,1536]{1,0:T(8,128)(2,1)S(1)} %slice.99), channel_id=1, source_target_pairs={{0,1},{1,0},{2,3},{3,2},{4,5},{5,4},{6,7},{7,6},{8,9},{9,8},{10,11... | collective-permute-start | bytes 884744 | tf_op jit(solution)/shard_map/ppermute | solution.py:737
  53.2 5.7 %collective-permute-start.7 = (bf16[144,768]{1,0:T(8,128)(2,1)}, bf16[144,768]{1,0:T(8,128)(2,1)}, u32[]{:S(2)}, u32[]{:S(2)}) collective-permute-start(bf16[144,768]{1,0:T(8,128)(2,1)} %collective-permute-done.3.refs_4_), channel_id=1, source_target_pairs={{0,4},{4,0},{1,5},{5,1},{2,6},{6,2},{3,7},{7,3},{8,12},{12,8},{9,1... | collective-permute-start | bytes 663560 | tf_op jit(solution)/shard_map/ppermute | solution.py:711
  53.4 21.6 %collective-permute-start.14 = (bf16[384,384]{1,0:T(8,128)(2,1)S(1)}, bf16[384,384]{1,0:T(8,128)(2,1)S(1)}, u32[]{:S(2)}, u32[]{:S(2)}) collective-permute-start(bf16[384,384]{1,0:T(8,128)(2,1)S(1)} %get-tuple-element.203), channel_id=1, source_target_pairs={{0,4},{4,0},{1,5},{5,1},{2,6},{6,2},{3,7},{7,3},{8,12},{12,8},{9,1... | collective-permute-start | bytes 884744 | tf_op jit(solution)/shard_map/ppermute | solution.py:847
  54.2 19.7 %collective-permute-start.13 = (bf16[128,768]{1,0:T(8,128)(2,1)}, bf16[128,768]{1,0:T(8,128)(2,1)S(1)}, u32[]{:S(2)}, u32[]{:S(2)}) collective-permute-start(bf16[128,768]{1,0:T(8,128)(2,1)} %get-tuple-element.119), channel_id=1, source_target_pairs={{0,24},{8,16},{16,8},{24,0},{1,25},{9,17},{17,9},{25,1},{2,26},{10... | collective-permute-start | bytes 589832 | tf_op jit(solution)/shard_map/ppermute | solution.py:697
  57.9 17.1 %collective-permute-start.12 = (bf16[128,768]{1,0:T(8,128)(2,1)}, bf16[128,768]{1,0:T(8,128)(2,1)S(1)}, u32[]{:S(2)}, u32[]{:S(2)}) collective-permute-start(bf16[128,768]{1,0:T(8,128)(2,1)} %get-tuple-element.117), channel_id=1, source_target_pairs={{0,16},{8,24},{16,0},{24,8},{1,17},{9,25},{17,1},{25,9},{2,18},{10... | collective-permute-start | bytes 589832 | tf_op jit(solution)/shard_map/ppermute | solution.py:697
  57.9 17.1 %collective-permute-start.11 = (bf16[128,768]{1,0:T(8,128)(2,1)}, bf16[128,768]{1,0:T(8,128)(2,1)S(1)}, u32[]{:S(2)}, u32[]{:S(2)}) collective-permute-start(bf16[128,768]{1,0:T(8,128)(2,1)} %get-tuple-element.115), channel_id=1, source_target_pairs={{0,8},{8,0},{16,24},{24,16},{1,9},{9,1},{17,25},{25,17},{2,10},{10... | collective-permute-start | bytes 589832 | tf_op jit(solution)/shard_map/ppermute | solution.py:697
  77.5 3.6 %collective-permute-start.15 = (bf16[1024,768]{1,0:T(8,128)(2,1)S(1)}, bf16[1024,768]{1,0:T(8,128)(2,1)}, u32[]{:S(2)}, u32[]{:S(2)}) collective-permute-start(bf16[1024,768]{1,0:T(8,128)(2,1)S(1)} %convolution_convert_fusion.2.refs_1_), channel_id=1, source_target_pairs={{0,4},{4,0},{1,5},{5,1},{2,6},{6,2},{3,7},{7,3},{8,12},{12,8},{9,1... | collective-permute-start | bytes 4718600 | tf_op jit(solution)/shard_map/ppermute | solution.py:725
  81.6 11.9 %copy-start.4 = (bf16[128,768]{1,0:T(8,128)(2,1)S(1)}, bf16[128,768]{1,0:T(8,128)(2,1)}, u32[]{:S(2)}) copy-start(bf16[128,768]{1,0:T(8,128)(2,1)} %copy-done.3) | copy-start | bytes 589828
  92.9 4.6 %collective-permute-start.16 = (bf16[1024,768]{1,0:T(8,128)(2,1)S(1)}, bf16[1024,768]{1,0:T(8,128)(2,1)S(1)}, u32[]{:S(2)}, u32[]{:S(2)}) collective-permute-start(bf16[1024,768]{1,0:T(8,128)(2,1)S(1)} %get-tuple-element.124.refs_2_), channel_id=1, source_target_pairs={{0,4},{4,0},{1,5},{5,1},{2,6},{6,2},{3,7},{7,3},{8,12},{12,8},{9,1... | collective-permute-start | bytes 4718600 | tf_op jit(solution)/shard_map/ppermute | solution.py:725
  93.0 3.7 %collective-permute-start.17 = (bf16[128,768]{1,0:T(8,128)(2,1)S(1)}, bf16[128,768]{1,0:T(8,128)(2,1)S(1)}, u32[]{:S(2)}, u32[]{:S(2)}) collective-permute-start(bf16[128,768]{1,0:T(8,128)(2,1)S(1)} %copy-done.2), channel_id=1, source_target_pairs={{0,4},{4,0},{1,5},{5,1},{2,6},{6,2},{3,7},{7,3},{8,12},{12,8},{9,1... | collective-permute-start | bytes 589832 | tf_op jit(solution)/shard_map/ppermute | solution.py:711
  93.5 3.5 %collective-permute-start.18 = (bf16[128,768]{1,0:T(8,128)(2,1)S(1)}, bf16[128,768]{1,0:T(8,128)(2,1)S(1)}, u32[]{:S(2)}, u32[]{:S(2)}) collective-permute-start(bf16[128,768]{1,0:T(8,128)(2,1)S(1)} %copy-done.4), channel_id=1, source_target_pairs={{0,4},{4,0},{1,5},{5,1},{2,6},{6,2},{3,7},{7,3},{8,12},{12,8},{9,1... | collective-permute-start | bytes 589832 | tf_op jit(solution)/shard_map/ppermute | solution.py:711
  93.6 3.7 %collective-permute-start.19 = (bf16[128,768]{1,0:T(8,128)(2,1)S(1)}, bf16[128,768]{1,0:T(8,128)(2,1)S(1)}, u32[]{:S(2)}, u32[]{:S(2)}) collective-permute-start(bf16[128,768]{1,0:T(8,128)(2,1)S(1)} %collective-permute-done.12.refs_11_), channel_id=1, source_target_pairs={{0,4},{4,0},{1,5},{5,1},{2,6},{6,2},{3,7},{7,3},{8,12},{12,8},{9,1... | collective-permute-start | bytes 589832 | tf_op jit(solution)/shard_map/ppermute | solution.py:711
  94.0 3.5 %collective-permute-start.20 = (bf16[128,768]{1,0:T(8,128)(2,1)S(1)}, bf16[128,768]{1,0:T(8,128)(2,1)S(1)}, u32[]{:S(2)}, u32[]{:S(2)}) collective-permute-start(bf16[128,768]{1,0:T(8,128)(2,1)S(1)} %collective-permute-done.13.refs_12_), channel_id=1, source_target_pairs={{0,4},{4,0},{1,5},{5,1},{2,6},{6,2},{3,7},{7,3},{8,12},{12,8},{9,1... | collective-permute-start | bytes 589832 | tf_op jit(solution)/shard_map/ppermute | solution.py:711
  109.3 4.0 %collective-permute-start.24 = (bf16[1024,768]{1,0:T(8,128)(2,1)}, bf16[1024,768]{1,0:T(8,128)(2,1)}, u32[]{:S(2)}, u32[]{:S(2)}) collective-permute-start(bf16[1024,768]{1,0:T(8,128)(2,1)} %get-tuple-element.144.own_ref), channel_id=1, source_target_pairs={{0,4},{4,0},{1,5},{5,1},{2,6},{6,2},{3,7},{7,3},{8,12},{12,8},{9,1... | collective-permute-start | bytes 4718600 | tf_op jit(solution)/shard_map/ppermute | solution.py:725
  117.2 97.7 %reduce-scatter.5.cloned.1.call-start = ((), (), s32[]{:S(2)}) async-start(), calls=%async_computation.2 | async-start | bytes 1474560 | tf_op jit(solution)/shard_map/reduce_scatter | solution.py:925
  124.2 4.7 %collective-permute-start.25 = (bf16[384,384]{1,0:T(8,128)(2,1)S(1)}, bf16[384,384]{1,0:T(8,128)(2,1)S(1)}, u32[]{:S(2)}, u32[]{:S(2)}) collective-permute-start(bf16[384,384]{1,0:T(8,128)(2,1)S(1)} %get-tuple-element.201), channel_id=1, source_target_pairs={{0,4},{4,0},{1,5},{5,1},{2,6},{6,2},{3,7},{7,3},{8,12},{12,8},{9,1... | collective-permute-start | bytes 884744 | tf_op jit(solution)/shard_map/ppermute | solution.py:887
  124.6 18.5 %collective-permute-start.21 = (bf16[128,768]{1,0:T(8,128)(2,1)S(1)}, bf16[128,768]{1,0:T(8,128)(2,1)S(1)}, u32[]{:S(2)}, u32[]{:S(2)}) collective-permute-start(bf16[128,768]{1,0:T(8,128)(2,1)S(1)} %copy-done.23), channel_id=1, source_target_pairs={{0,8},{8,0},{16,24},{24,16},{1,9},{9,1},{17,25},{25,17},{2,10},{10... | collective-permute-start | bytes 589832 | tf_op jit(solution)/shard_map/ppermute | solution.py:697
  126.1 17.1 %collective-permute-start.22 = (bf16[128,768]{1,0:T(8,128)(2,1)S(1)}, bf16[128,768]{1,0:T(8,128)(2,1)S(1)}, u32[]{:S(2)}, u32[]{:S(2)}) collective-permute-start(bf16[128,768]{1,0:T(8,128)(2,1)S(1)} %copy-done.22), channel_id=1, source_target_pairs={{0,16},{8,24},{16,0},{24,8},{1,17},{9,25},{17,1},{25,9},{2,18},{10... | collective-permute-start | bytes 589832 | tf_op jit(solution)/shard_map/ppermute | solution.py:697
  128.5 14.7 %collective-permute-start.23 = (bf16[128,768]{1,0:T(8,128)(2,1)S(1)}, bf16[128,768]{1,0:T(8,128)(2,1)S(1)}, u32[]{:S(2)}, u32[]{:S(2)}) collective-permute-start(bf16[128,768]{1,0:T(8,128)(2,1)S(1)} %copy-done.21), channel_id=1, source_target_pairs={{0,24},{8,16},{16,8},{24,0},{1,25},{9,17},{17,9},{25,1},{2,26},{10... | collective-permute-start | bytes 589832 | tf_op jit(solution)/shard_map/ppermute | solution.py:697
  129.2 14.0 %copy-start.12 = (bf16[1024,768]{1,0:T(8,128)(2,1)S(1)}, bf16[1024,768]{1,0:T(8,128)(2,1)}, u32[]{:S(2)}) copy-start(bf16[1024,768]{1,0:T(8,128)(2,1)} %get-tuple-element.113.refs_0_) | copy-start | bytes 4718596
  147.1 13.4 %collective-permute-start.30 = (bf16[112,1536]{1,0:T(8,128)(2,1)S(1)}, bf16[112,1536]{1,0:T(8,128)(2,1)S(1)}, u32[]{:S(2)}, u32[]{:S(2)}) collective-permute-start(bf16[112,1536]{1,0:T(8,128)(2,1)S(1)} %slice_bitcast_fusion.1), channel_id=1, source_target_pairs={{0,2},{2,0},{1,3},{3,1},{4,6},{6,4},{5,7},{7,5},{8,10},{10,8},{9,1... | collective-permute-start | bytes 1032200 | tf_op jit(solution)/shard_map/ppermute | solution.py:753
  150.9 2.4 collective-permute-start.26
  151.0 9.5 %collective-permute-start.29 = (bf16[96,1536]{1,0:T(8,128)(2,1)S(1)}, bf16[96,1536]{1,0:T(8,128)(2,1)S(1)}, u32[]{:S(2)}, u32[]{:S(2)}) collective-permute-start(bf16[96,1536]{1,0:T(8,128)(2,1)S(1)} %slice_bitcast_fusion.4), channel_id=1, source_target_pairs={{0,1},{1,0},{2,3},{3,2},{4,5},{5,4},{6,7},{7,6},{8,9},{9,8},{10,11... | collective-permute-start | bytes 884744 | tf_op jit(solution)/shard_map/ppermute | solution.py:753
  154.1 13.1 %collective-permute-start.27 = (bf16[128,768]{1,0:T(8,128)(2,1)S(1)}, bf16[128,768]{1,0:T(8,128)(2,1)S(1)}, u32[]{:S(2)}, u32[]{:S(2)}) collective-permute-start(bf16[128,768]{1,0:T(8,128)(2,1)S(1)} %get-tuple-element.162), channel_id=1, source_target_pairs={{0,8},{8,0},{16,24},{24,16},{1,9},{9,1},{17,25},{25,17},{2,10},{10... | collective-permute-start | bytes 589832 | tf_op jit(solution)/shard_map/ppermute | solution.py:697
  158.0 11.8 %collective-permute-start.28 = (bf16[128,768]{1,0:T(8,128)(2,1)S(1)}, bf16[128,768]{1,0:T(8,128)(2,1)S(1)}, u32[]{:S(2)}, u32[]{:S(2)}) collective-permute-start(bf16[128,768]{1,0:T(8,128)(2,1)S(1)} %get-tuple-element.163), channel_id=1, source_target_pairs={{0,16},{8,24},{16,0},{24,8},{1,17},{9,25},{17,1},{25,9},{2,18},{10... | collective-permute-start | bytes 589832 | tf_op jit(solution)/shard_map/ppermute | solution.py:697
  169.9 11.8 %copy-start.5 = (bf16[128,768]{1,0:T(8,128)(2,1)S(1)}, bf16[128,768]{1,0:T(8,128)(2,1)}, u32[]{:S(2)}) copy-start(bf16[128,768]{1,0:T(8,128)(2,1)} %get-tuple-element.166.refs_0_) | copy-start | bytes 589828
  176.3 79.6 %all-gather.7.cloned.1.call-start = ((), (), s32[]{:S(2)}) async-start(), calls=%async_computation.4 | async-start | bytes 2654208 | tf_op jit(solution)/shard_map/all_gather | solution.py:928
  176.3 16.2 %collective-permute-start.32 = (bf16[208,1536]{1,0:T(8,128)(2,1)S(1)}, bf16[208,1536]{1,0:T(8,128)(2,1)S(1)}, u32[]{:S(2)}, u32[]{:S(2)}) collective-permute-start(bf16[208,1536]{1,0:T(8,128)(2,1)S(1)} %pad_maximum_fusion.3), channel_id=1, source_target_pairs={{0,2},{2,0},{1,3},{3,1},{4,6},{6,4},{5,7},{7,5},{8,10},{10,8},{9,1... | collective-permute-start | bytes 1916936 | tf_op jit(solution)/shard_map/ppermute | solution.py:762
  177.8 16.1 %collective-permute-start.31 = (bf16[208,1536]{1,0:T(8,128)(2,1)}, bf16[208,1536]{1,0:T(8,128)(2,1)}, u32[]{:S(2)}, u32[]{:S(2)}) collective-permute-start(bf16[208,1536]{1,0:T(8,128)(2,1)} %pad_maximum_fusion.2), channel_id=1, source_target_pairs={{0,1},{1,0},{2,3},{3,2},{4,5},{5,4},{6,7},{7,6},{8,9},{9,8},{10,11... | collective-permute-start | bytes 1916936 | tf_op jit(solution)/shard_map/ppermute | solution.py:762
  178.4 8.8 %collective-permute-start.33 = (bf16[128,768]{1,0:T(8,128)(2,1)S(1)}, bf16[128,768]{1,0:T(8,128)(2,1)S(1)}, u32[]{:S(2)}, u32[]{:S(2)}) collective-permute-start(bf16[128,768]{1,0:T(8,128)(2,1)S(1)} %get-tuple-element.170), channel_id=1, source_target_pairs={{0,24},{8,16},{16,8},{24,0},{1,25},{9,17},{17,9},{25,1},{2,26},{10... | collective-permute-start | bytes 589832 | tf_op jit(solution)/shard_map/ppermute | solution.py:697
  195.5 19.4 %collective-permute-start.34 = (bf16[208,768]{1,0:T(8,128)(2,1)S(1)}, bf16[208,768]{1,0:T(8,128)(2,1)S(1)}, u32[]{:S(2)}, u32[]{:S(2)}) collective-permute-start(bf16[208,768]{1,0:T(8,128)(2,1)S(1)} %constant_dynamic-slice_fusion.1), channel_id=1, source_target_pairs={{0,8},{8,0},{16,24},{24,16},{1,9},{9,1},{17,25},{25,17},{2,10},{10... | collective-permute-start | bytes 958472 | tf_op jit(solution)/shard_map/ppermute | solution.py:697
  215.0 9.0 %collective-permute-start.35 = (bf16[208,384]{1,0:T(8,128)(2,1)S(1)}, bf16[208,384]{1,0:T(8,128)(2,1)S(1)}, u32[]{:S(2)}, u32[]{:S(2)}) collective-permute-start(bf16[208,384]{1,0:T(8,128)(2,1)S(1)} %constant_dynamic-slice_fusion), channel_id=1, source_target_pairs={{0,16},{8,24},{16,0},{24,8},{1,17},{9,25},{17,1},{25,9},{2,18},{10... | collective-permute-start | bytes 479240 | tf_op jit(solution)/shard_map/ppermute | solution.py:697
  224.1 19.3 %collective-permute-start.36 = (bf16[208,384]{1,0:T(8,128)(2,1)S(1)}, bf16[208,384]{1,0:T(8,128)(2,1)S(1)}, u32[]{:S(2)}, u32[]{:S(2)}) collective-permute-start(bf16[208,384]{1,0:T(8,128)(2,1)S(1)} %add_convert_fusion.1), channel_id=1, source_target_pairs={{0,16},{8,24},{16,0},{24,8},{1,17},{9,25},{17,1},{25,9},{2,18},{10... | collective-permute-start | bytes 479240 | tf_op jit(solution)/shard_map/ppermute | solution.py:697
  243.5 12.1 %collective-permute-start.37 = (bf16[208,768]{1,0:T(8,128)(2,1)S(1)}, bf16[208,768]{1,0:T(8,128)(2,1)S(1)}, u32[]{:S(2)}, u32[]{:S(2)}) collective-permute-start(bf16[208,768]{1,0:T(8,128)(2,1)S(1)} %pad_maximum_fusion.7), channel_id=1, source_target_pairs={{0,8},{8,0},{16,24},{24,16},{1,9},{9,1},{17,25},{25,17},{2,10},{10... | collective-permute-start | bytes 958472 | tf_op jit(solution)/shard_map/ppermute | solution.py:697
  255.8 4.1 %collective-permute-start.38 = (bf16[208,1536]{1,0:T(8,128)(2,1)S(1)}, bf16[208,1536]{1,0:T(8,128)(2,1)S(1)}, u32[]{:S(2)}, u32[]{:S(2)}) collective-permute-start(bf16[208,1536]{1,0:T(8,128)(2,1)S(1)} %pad_maximum_fusion.4.refs_1_), channel_id=1, source_target_pairs={{0,4},{4,0},{1,5},{5,1},{2,6},{6,2},{3,7},{7,3},{8,12},{12,8},{9,1... | collective-permute-start | bytes 1916936 | tf_op jit(solution)/shard_map/ppermute | solution.py:962
  (21 other events, 93.2 us)
Sparse Core Ops, SparseCore 0:
  10.4 71.0 all-gather.4
  117.3 58.9 reduce-scatter.6
  178.6 33.9 reduce-scatter.4
  215.0 37.0 all-gather.6
